TPU v7x, 128 devices: a whole 4x4x4 slice. The times are simulated.
128 devices in a mesh: depth: 32 (over y, z, core), lat: 4 (over x).
Axes of the slice: x: 4, y: 4, z: 4, core: 2. Of those that a mesh axis runs over, the one named last changes fastest.
Arguments:
- density: bfloat16 [32, 16, 512, 2048], P('depth', None, None, 'lat'), may hold values from 0 to 1
- occupancy: int32 [32, 4, 16], P('depth', None, 'lat'), may hold values from 0 to 1, as said below
- shear_offsets: int32 [32, 16], P('depth'), may hold values from 0 to 127, as said below
- frac_lateral: float32 [32, 16], P('depth'), may hold values from 0.05 to 0.95
- frac_vertical: float32 [32, 16], P('depth'), may hold values from 0.05 to 0.95
- extinction: float32 [32, 16], P('depth'), may hold values from 2 to 32
- slab_gain: float32 [32], P('depth'), may hold values from 0.05 to 1
- view_rank: int32 [32], replicated, may hold values from 0 to 31, as said below
Outputs:
- image_color: float32 [512, 2048], P('depth', 'lat')
- image_alpha: float32 [512, 2048], P('depth', 'lat')
Inputs may be any that keep to these rules, and one draw needn't show every extreme that they name: `occupancy`: A block is 1 if occupied; the share of occupied blocks differs from slab to slab. `shear_offsets`: some slice has the offset 128 - 1. `view_rank`: A permutation of the slabs in which every aligned group of a power of two of slabs holds consecutive ranks.
All inputs are finite; a program needn't handle non-finite values.
Results may differ from a plain program's by a relative error of at most 0.00077.
Values may be sent and summed in bfloat16 or wider, within the bound.
No kernel may reach another device: no remote copies, remote signals or barrier semaphores. Data moves between devices by JAX's collectives and lax.ppermute only.
A program may use at most 128 MiB of HBM per device.

v0:
```python
import jax
import jax.numpy as jnp
from jax import lax
from jax.sharding import PartitionSpec as P

SHIFT = 128
BLK = 128


def from_behind(value, axis, steps):
    count = lax.axis_size(axis)
    leading, last = (max(0, -steps), min(count, count - steps))
    return lax.ppermute(value, axis, [(source, source + steps) for source in range(leading, last)])


def partner(value, axis, bit):
    mask = 2**bit
    pairs = [(source, source ^ mask) for source in range(lax.axis_size(axis))]
    return lax.ppermute(value, axis, pairs)


def lateral_weights(offsets, fraction, in_count, out_count):
    source = jnp.arange(in_count, dtype=jnp.int32)[None, :, None]
    target = jnp.arange(out_count, dtype=jnp.int32)[None, None, :]
    shifted = target - offsets[:, None, None]
    first_term = jnp.where(shifted == source, (1.0 - fraction)[:, None, None], 0.0)
    second = jnp.where(shifted - 1 == source, fraction[:, None, None], 0.0)
    return (first_term + second).astype(jnp.bfloat16)


def vertical_weights(fraction, row_count):
    target = jnp.arange(row_count, dtype=jnp.int32)[None, :, None]
    source = jnp.arange(row_count, dtype=jnp.int32)[None, None, :]
    first_term = jnp.where(target == source, (1.0 - fraction)[:, None, None], 0.0)
    second = jnp.where(target - 1 == source, fraction[:, None, None], 0.0)
    return (first_term + second).astype(jnp.bfloat16)


def shade_slices(density_sum, extinction, gain, slice_total):
    row_above = jnp.pad(density_sum, ((0, 0), (1, 0), (0, 0)))[:, :-1, :]
    shading = 0.3 + 0.7 * jax.nn.sigmoid(4.0 * (density_sum - row_above))
    opacity = 1.0 - jnp.exp(-extinction[:, None, None] * density_sum / slice_total)
    emission = opacity * shading * gain
    through = jnp.cumprod(1.0 - opacity, axis=0)
    before = jnp.concatenate([jnp.ones_like(through[:1]), through[:-1]], axis=0)
    return (jnp.sum(emission * before, axis=0), 1.0 - through[-1])


def composite(front_color, front_alpha, back_color, back_alpha):
    return (
        front_color + (1.0 - front_alpha) * back_color,
        front_alpha + (1.0 - front_alpha) * back_alpha,
    )


def shards(
    density, occupancy, shear_offsets, frac_lateral, frac_vertical, extinction, slab_gain, view_rank
):
    slab_voxels = density[0]
    slice_count, row_count, col_count = slab_voxels.shape
    block_rows = row_count // BLK
    block_cols = col_count // BLK
    block_mask = occupancy[0].astype(jnp.bfloat16)
    masked = (
        slab_voxels.reshape(slice_count, block_rows, BLK, block_cols, BLK)
        * block_mask[None, :, None, :, None]
    )
    masked = masked.reshape(slice_count, row_count, col_count)
    lateral_matrix = lateral_weights(
        shear_offsets[0], frac_lateral[0], col_count, col_count + SHIFT
    )
    across = jnp.einsum(
        "srw,swq->srq", masked, lateral_matrix, preferred_element_type=jnp.float32
    ).astype(jnp.bfloat16)
    vertical_matrix = vertical_weights(frac_vertical[0], row_count)
    resampled = jnp.einsum(
        "sij,sjq->siq", vertical_matrix, across, preferred_element_type=jnp.float32
    ).astype(jnp.bfloat16)
    edge_spill = resampled[:, :, col_count:]
    incoming = from_behind(edge_spill, "lat", 1)
    density_sum = resampled[:, :, :col_count].astype(jnp.float32) + jnp.pad(
        incoming.astype(jnp.float32), ((0, 0), (0, 0), (0, col_count - SHIFT))
    )
    slice_total = lax.axis_size("depth") * slice_count
    image_color, image_alpha = shade_slices(density_sum, extinction[0], slab_gain[0], slice_total)
    device_index = lax.axis_index("depth")
    group_size = lax.axis_size("depth")
    piece_rows = row_count // group_size
    my_rank = view_rank[device_index]
    bit_levels = group_size.bit_length() - 1
    held_color = image_color.reshape(group_size, piece_rows, col_count)
    held_alpha = image_alpha.reshape(group_size, piece_rows, col_count)
    for bit_level in range(bit_levels):
        device_bit = device_index >> bit_level & 1
        paired_color = held_color.reshape(held_color.shape[0] // 2, 2, piece_rows, col_count)
        paired_alpha = held_alpha.reshape(held_alpha.shape[0] // 2, 2, piece_rows, col_count)
        keep_color = lax.dynamic_index_in_dim(paired_color, device_bit, 1, keepdims=False)
        keep_alpha = lax.dynamic_index_in_dim(paired_alpha, device_bit, 1, keepdims=False)
        send_color = lax.dynamic_index_in_dim(paired_color, 1 - device_bit, 1, keepdims=False)
        send_alpha = lax.dynamic_index_in_dim(paired_alpha, 1 - device_bit, 1, keepdims=False)
        other_color, other_alpha = partner((send_color, send_alpha), "depth", bit_level)
        in_front = my_rank >> bit_level & 1 == 0
        front_color = jnp.where(in_front, keep_color, other_color)
        front_alpha = jnp.where(in_front, keep_alpha, other_alpha)
        back_color = jnp.where(in_front, other_color, keep_color)
        back_alpha = jnp.where(in_front, other_alpha, keep_alpha)
        held_color, held_alpha = composite(front_color, front_alpha, back_color, back_alpha)
    image_color = held_color.reshape(piece_rows, col_count)
    image_alpha = held_alpha.reshape(piece_rows, col_count)
    return (image_color, image_alpha)


def solution(mesh):
    placed = (
        P("depth", None, None, "lat"),
        P("depth", None, "lat"),
        P("depth", None),
        P("depth", None),
        P("depth", None),
        P("depth", None),
        P("depth"),
        P(),
    )
    return jax.shard_map(
        shards,
        mesh=mesh,
        in_specs=placed,
        out_specs=(P("depth", "lat"), P("depth", "lat")),
        check_vma=False,
    )
```

profile of v0, /device:TPU:0, one launch (start us, length us, event | category | flops | bytes accessed | tf_op | source)
XLA Modules:
  0.0 188.8 jit_solution(16908897201803869929)
XLA Ops:
  0.9 0.7 iota_subtract_fusion
  1.7 0.7 convert_bitcast_fusion
  2.7 0.7 broadcast_subtract_fusion
  3.3 13.3 %fusion.56 = bf16[16,512,640]{2,1,0:T(8,128)(2,1)} fusion(f32[16]{0:T(128)} %bitcast.159, s32[16,640]{1,0:T(8,128)S(1)} %get-tuple-element.13, f32[16]{0:T(128)S(1)} %get-tuple-element.16, s32[16,640]{1,0:T(8,128)S(1)} %get-tuple-element.12, bf16[1,16,512,512]{3,2,1,0:T(8,128)(2,1)} %param.8, bf16[512,512]{1,0:T(8,128)(2,1)S(1)} %bitcast.153), kind=kOutput, calls=%fused_computation.18.clone.clone.clone.2 | convolution fusion | flops 5409603584 | bytes 19480704 | tf_op jit(solution)/shard_map/srw,swq->srq/dot_general | solution.py:72
  16.7 11.1 %fusion.27 = bf16[16,512,640]{2,1,0:T(8,128)(2,1)S(1)} fusion(f32[16]{0:T(128)S(1)} %bitcast.160, f32[16]{0:T(128)S(1)} %get-tuple-element.17, pred[512,512]{1,0:T(8,128)(4,1)S(1)} %get-tuple-element.14, pred[512,512]{1,0:T(8,128)(4,1)S(1)} %get-tuple-element.15, bf16[16,512,640]{2,1,0:T(8,128)(2,1)} %fusion.56), kind=kOutput, calls=%fused_computation.33 | convolution fusion | flops 5390729216 | bytes 21495936 | tf_op jit(solution)/shard_map/sij,sjq->siq/dot_general | solution.py:76
  27.8 3.9 %copy-done = bf16[16,512,640]{2,1,0:T(8,128)(2,1)} copy-done((bf16[16,512,640]{2,1,0:T(8,128)(2,1)}, bf16[16,512,640]{2,1,0:T(8,128)(2,1)S(1)}, u32[]{:S(2)}) %copy-start) | copy-done | bytes 10485784
  31.7 1.7 slice.21
  33.4 3.8 %collective-permute-start = (bf16[16,512,128]{2,1,0:T(8,128)(2,1)}, bf16[16,512,128]{2,1,0:T(8,128)(2,1)S(1)}, u32[]{:S(2)}, u32[]{:S(2)}) collective-permute-start(bf16[16,512,128]{2,1,0:T(8,128)(2,1)} %slice.21), channel_id=1, source_target_pairs={{0,1},{1,2},{2,3},{4,5},{5,6},{6,7},{8,9},{9,10},{10,11},{12,13},{... | collective-permute-start | bytes 6291464 | tf_op jit(solution)/shard_map/ppermute | solution.py:13
  37.9 44.2 %collective-permute-done = bf16[16,512,128]{2,1,0:T(8,128)(2,1)S(1)} collective-permute-done((bf16[16,512,128]{2,1,0:T(8,128)(2,1)}, bf16[16,512,128]{2,1,0:T(8,128)(2,1)S(1)}, u32[]{:S(2)}, u32[]{:S(2)}) %collective-permute-start) | collective-permute-done | bytes 2097184 | tf_op jit(solution)/shard_map/ppermute | solution.py:13
  82.1 10.8 %fusion.6 = f32[16,512,512]{2,1,0:T(8,128)} fusion(f32[16]{0:T(128)S(1)} %negate_bitcast_fusion, bf16[16,512,640]{2,1,0:T(8,128)(2,1)} %copy-done, bf16[16,512,128]{2,1,0:T(8,128)(2,1)S(1)} %collective-permute-done), kind=kOutput, calls=%fused_computation.11 | output fusion | flops 92274688 | bytes 27263040 | tf_op jit(solution)/shard_map/jit(cumprod)/reduce_window | solution.py:44
  92.9 1.3 slice_subtract_fusion
  94.2 13.7 %slice.22 = f32[15,512,512]{2,1,0:T(8,128)} slice(f32[16,512,512]{2,1,0:T(8,128)} %fusion.6), slice={[0:15], [0:512], [0:512]} | slice | bytes 31457280 | tf_op jit(solution)/shard_map/slice | solution.py:45
  107.8 0.9 dynamic-slice_bitcast_fusion
  108.7 11.6 %convert_add_fusion = f32[16,512,512]{2,1,0:T(8,128)} fusion(bf16[16,512,640]{2,1,0:T(8,128)(2,1)} %copy-done, bf16[16,512,128]{2,1,0:T(8,128)(2,1)S(1)} %collective-permute-done), kind=kLoop, calls=%fused_computation.14 | loop fusion | flops 12582912 | bytes 27262976 | tf_op jit(solution)/shard_map/add | solution.py:81
  120.3 23.7 %multiply_reduce_fusion = f32[512,512]{1,0:T(8,128)S(1)} fusion(f32[15,512,512]{2,1,0:T(8,128)} %slice.22, f32[16,512,512]{2,1,0:T(8,128)} %convert_add_fusion, f32[]{:T(128)} %bitcast.139, f32[16]{0:T(128)S(1)} %negate_bitcast_fusion), kind=kLoop, calls=%fused_computation.10 | loop fusion | flops 58458112 | bytes 33554500 | tf_op jit(solution)/shard_map/reduce_sum | solution.py:46
  144.0 0.6 collective-permute-start.1
  144.6 0.6 dynamic_slice.60
  146.1 0.8 copy-done.1
  146.9 1.4 fusion.33
  148.4 2.0 %collective-permute-start.4 = (f32[8,16,512]{2,1,0:T(8,128)S(1)}, f32[8,16,512]{2,1,0:T(8,128)S(1)}, u32[]{:S(2)}, u32[]{:S(2)}) collective-permute-start(f32[8,16,512]{2,1,0:T(8,128)S(1)} %dynamic-slice_bitcast_fusion.2), channel_id=1, source_target_pairs={{0,8},{4,12},{8,0},{12,4},{16,24},{20,28},{24,16},{28,20},{32,40},... | collective-permute-start | bytes 786440 | tf_op jit(solution)/shard_map/ppermute | solution.py:19
  151.3 6.3 %collective-permute-done.4 = f32[8,16,512]{2,1,0:T(8,128)S(1)} collective-permute-done((f32[8,16,512]{2,1,0:T(8,128)S(1)}, f32[8,16,512]{2,1,0:T(8,128)S(1)}, u32[]{:S(2)}, u32[]{:S(2)}) %collective-permute-start.4) | collective-permute-done | bytes 262176 | tf_op jit(solution)/shard_map/ppermute | solution.py:19
  157.6 5.3 %collective-permute-done.3 = f32[8,16,512]{2,1,0:T(8,128)S(1)} collective-permute-done((f32[8,16,512]{2,1,0:T(8,128)S(1)}, f32[8,16,512]{2,1,0:T(8,128)S(1)}, u32[]{:S(2)}, u32[]{:S(2)}) %collective-permute-start.3) | collective-permute-done | bytes 262176 | tf_op jit(solution)/shard_map/ppermute | solution.py:19
  163.0 3.8 %collective-permute-start.6 = (f32[4,16,512]{2,1,0:T(8,128)S(1)}, f32[4,16,512]{2,1,0:T(8,128)S(1)}, u32[]{:S(2)}, u32[]{:S(2)}) collective-permute-start(f32[4,16,512]{2,1,0:T(8,128)S(1)} %dynamic-slice_bitcast_fusion.4), channel_id=1, source_target_pairs={{0,16},{4,20},{8,24},{12,28},{16,0},{20,4},{24,8},{28,12},{32,48},... | collective-permute-start | bytes 393224 | tf_op jit(solution)/shard_map/ppermute | solution.py:19
  167.6 3.1 %collective-permute-done.6 = f32[4,16,512]{2,1,0:T(8,128)S(1)} collective-permute-done((f32[4,16,512]{2,1,0:T(8,128)S(1)}, f32[4,16,512]{2,1,0:T(8,128)S(1)}, u32[]{:S(2)}, u32[]{:S(2)}) %collective-permute-start.6) | collective-permute-done | bytes 131104 | tf_op jit(solution)/shard_map/ppermute | solution.py:19
  170.7 2.7 %collective-permute-done.5 = f32[4,16,512]{2,1,0:T(8,128)S(1)} collective-permute-done((f32[4,16,512]{2,1,0:T(8,128)S(1)}, f32[4,16,512]{2,1,0:T(8,128)S(1)}, u32[]{:S(2)}, u32[]{:S(2)}) %collective-permute-start.5) | collective-permute-done | bytes 131104 | tf_op jit(solution)/shard_map/ppermute | solution.py:19
  173.4 1.7 collective-permute-start.8
  176.2 1.6 collective-permute-done.8
  177.8 1.6 collective-permute-done.7
  179.4 3.3 %collective-permute-start.10 = (f32[1,16,512]{2,1,0:T(8,128)S(1)}, f32[1,16,512]{2,1,0:T(8,128)S(1)}, u32[]{:S(2)}, u32[]{:S(2)}) collective-permute-start(f32[1,16,512]{2,1,0:T(8,128)S(1)} %constant_dynamic-slice_fusion), channel_id=1, source_target_pairs={{0,64},{4,68},{8,72},{12,76},{16,80},{20,84},{24,88},{28,92},{32,9... | collective-permute-start | bytes 98312 | tf_op jit(solution)/shard_map/ppermute | solution.py:19
  183.7 1.2 collective-permute-done.10
  184.9 3.3 %collective-permute-done.9 = f32[1,16,512]{2,1,0:T(8,128)S(1)} collective-permute-done((f32[1,16,512]{2,1,0:T(8,128)S(1)}, f32[1,16,512]{2,1,0:T(8,128)S(1)}, u32[]{:S(2)}, u32[]{:S(2)}) %collective-permute-start.9) | collective-permute-done | bytes 32800 | tf_op jit(solution)/shard_map/ppermute | solution.py:19
  188.2 0.6 add_bitcast_fusion
  (32 shorter events, 2.3 us)
Async XLA Ops:
  3.3 13.3 %copy-start.2 = (f32[1,16]{1,0:T(1,128)S(1)}, f32[1,16]{1,0:T(1,128)}, u32[]{:S(2)}) copy-start(f32[1,16]{1,0:T(1,128)} %param.12) | copy-start | bytes 196
  16.7 21.2 %copy-start.3 = (f32[1,16]{1,0:T(1,128)S(1)}, f32[1,16]{1,0:T(1,128)}, u32[]{:S(2)}) copy-start(f32[1,16]{1,0:T(1,128)} %param.13) | copy-start | bytes 196
  27.8 3.9 %copy-start = (bf16[16,512,640]{2,1,0:T(8,128)(2,1)}, bf16[16,512,640]{2,1,0:T(8,128)(2,1)S(1)}, u32[]{:S(2)}) copy-start(bf16[16,512,640]{2,1,0:T(8,128)(2,1)S(1)} %fusion.27) | copy-start | bytes 31457284
  33.4 48.7 %collective-permute-start = (bf16[16,512,128]{2,1,0:T(8,128)(2,1)}, bf16[16,512,128]{2,1,0:T(8,128)(2,1)S(1)}, u32[]{:S(2)}, u32[]{:S(2)}) collective-permute-start(bf16[16,512,128]{2,1,0:T(8,128)(2,1)} %slice.21), channel_id=1, source_target_pairs={{0,1},{1,2},{2,3},{4,5},{5,6},{6,7},{8,9},{9,10},{10,11},{12,13},{... | collective-permute-start | bytes 6291464 | tf_op jit(solution)/shard_map/ppermute | solution.py:13
  108.7 37.1 %collective-permute-start.2 = (f32[16,16,512]{2,1,0:T(8,128)}, f32[16,16,512]{2,1,0:T(8,128)}, u32[]{:S(2)}, u32[]{:S(2)}) collective-permute-start(f32[16,16,512]{2,1,0:T(8,128)} %dynamic-slice_bitcast_fusion), channel_id=1, source_target_pairs={{0,4},{4,0},{8,12},{12,8},{16,20},{20,16},{24,28},{28,24},{32,36},... | collective-permute-start | bytes 1572872 | tf_op jit(solution)/shard_map/ppermute | solution.py:19
  120.3 24.3 %copy-start.4 = (s32[32]{0:T(128)S(1)}, s32[32]{0:T(128)}, u32[]{:S(2)}) copy-start(s32[32]{0:T(128)} %param.15) | copy-start | bytes 388
  144.0 2.1 %collective-permute-start.1 = (f32[16,16,512]{2,1,0:T(8,128)S(1)}, f32[16,16,512]{2,1,0:T(8,128)S(1)}, u32[]{:S(2)}, u32[]{:S(2)}) collective-permute-start(f32[16,16,512]{2,1,0:T(8,128)S(1)} %dynamic-slice_bitcast_fusion.1), channel_id=1, source_target_pairs={{0,4},{4,0},{8,12},{12,8},{16,20},{20,16},{24,28},{28,24},{32,36},... | collective-permute-start | bytes 1572872 | tf_op jit(solution)/shard_map/ppermute | solution.py:19
  146.1 0.8 copy-start.1
  148.4 9.2 %collective-permute-start.4 = (f32[8,16,512]{2,1,0:T(8,128)S(1)}, f32[8,16,512]{2,1,0:T(8,128)S(1)}, u32[]{:S(2)}, u32[]{:S(2)}) collective-permute-start(f32[8,16,512]{2,1,0:T(8,128)S(1)} %dynamic-slice_bitcast_fusion.2), channel_id=1, source_target_pairs={{0,8},{4,12},{8,0},{12,4},{16,24},{20,28},{24,16},{28,20},{32,40},... | collective-permute-start | bytes 786440 | tf_op jit(solution)/shard_map/ppermute | solution.py:19
  150.4 12.4 %collective-permute-start.3 = (f32[8,16,512]{2,1,0:T(8,128)S(1)}, f32[8,16,512]{2,1,0:T(8,128)S(1)}, u32[]{:S(2)}, u32[]{:S(2)}) collective-permute-start(f32[8,16,512]{2,1,0:T(8,128)S(1)} %dynamic-slice_bitcast_fusion.3), channel_id=1, source_target_pairs={{0,8},{4,12},{8,0},{12,4},{16,24},{20,28},{24,16},{28,20},{32,40},... | collective-permute-start | bytes 786440 | tf_op jit(solution)/shard_map/ppermute | solution.py:19
  163.0 7.7 %collective-permute-start.6 = (f32[4,16,512]{2,1,0:T(8,128)S(1)}, f32[4,16,512]{2,1,0:T(8,128)S(1)}, u32[]{:S(2)}, u32[]{:S(2)}) collective-permute-start(f32[4,16,512]{2,1,0:T(8,128)S(1)} %dynamic-slice_bitcast_fusion.4), channel_id=1, source_target_pairs={{0,16},{4,20},{8,24},{12,28},{16,0},{20,4},{24,8},{28,12},{32,48},... | collective-permute-start | bytes 393224 | tf_op jit(solution)/shard_map/ppermute | solution.py:19
  166.8 6.6 %collective-permute-start.5 = (f32[4,16,512]{2,1,0:T(8,128)S(1)}, f32[4,16,512]{2,1,0:T(8,128)S(1)}, u32[]{:S(2)}, u32[]{:S(2)}) collective-permute-start(f32[4,16,512]{2,1,0:T(8,128)S(1)} %dynamic-slice_bitcast_fusion.5), channel_id=1, source_target_pairs={{0,16},{4,20},{8,24},{12,28},{16,0},{20,4},{24,8},{28,12},{32,48},... | collective-permute-start | bytes 393224 | tf_op jit(solution)/shard_map/ppermute | solution.py:19
  173.4 4.3 %collective-permute-start.8 = (f32[2,16,512]{2,1,0:T(8,128)S(1)}, f32[2,16,512]{2,1,0:T(8,128)S(1)}, u32[]{:S(2)}, u32[]{:S(2)}) collective-permute-start(f32[2,16,512]{2,1,0:T(8,128)S(1)} %dynamic-slice_bitcast_fusion.6), channel_id=1, source_target_pairs={{0,32},{4,36},{8,40},{12,44},{16,48},{20,52},{24,56},{28,60},{32,0... | collective-permute-start | bytes 196616 | tf_op jit(solution)/shard_map/ppermute | solution.py:19
  175.1 4.3 %collective-permute-start.7 = (f32[2,16,512]{2,1,0:T(8,128)S(1)}, f32[2,16,512]{2,1,0:T(8,128)S(1)}, u32[]{:S(2)}, u32[]{:S(2)}) collective-permute-start(f32[2,16,512]{2,1,0:T(8,128)S(1)} %dynamic-slice_bitcast_fusion.7), channel_id=1, source_target_pairs={{0,32},{4,36},{8,40},{12,44},{16,48},{20,52},{24,56},{28,60},{32,0... | collective-permute-start | bytes 196616 | tf_op jit(solution)/shard_map/ppermute | solution.py:19
  179.4 5.5 %collective-permute-start.10 = (f32[1,16,512]{2,1,0:T(8,128)S(1)}, f32[1,16,512]{2,1,0:T(8,128)S(1)}, u32[]{:S(2)}, u32[]{:S(2)}) collective-permute-start(f32[1,16,512]{2,1,0:T(8,128)S(1)} %constant_dynamic-slice_fusion), channel_id=1, source_target_pairs={{0,64},{4,68},{8,72},{12,76},{16,80},{20,84},{24,88},{28,92},{32,9... | collective-permute-start | bytes 98312 | tf_op jit(solution)/shard_map/ppermute | solution.py:19
  182.8 5.4 %collective-permute-start.9 = (f32[1,16,512]{2,1,0:T(8,128)S(1)}, f32[1,16,512]{2,1,0:T(8,128)S(1)}, u32[]{:S(2)}, u32[]{:S(2)}) collective-permute-start(f32[1,16,512]{2,1,0:T(8,128)S(1)} %constant_dynamic-slice_fusion.1), channel_id=1, source_target_pairs={{0,64},{4,68},{8,72},{12,76},{16,80},{20,84},{24,88},{28,92},{32,9... | collective-permute-start | bytes 98312 | tf_op jit(solution)/shard_map/ppermute | solution.py:19
where the time goes:
time: 190 us; the launch traced here: 189 us
  waiting for transfers between devices  69.5 us (37%)
  other arithmetic  52 us (27%)
  matrix products  24.5 us (13%)
  local copies, waits for them, and re-layouts  22 us (12%)
  starting transfers between devices  16.2 us (9%)
  between operations  4.73 us (2%)
    ppermute x1, waiting for transfers between devices, from_behind(): lax.ppermute(value, axis, [(source, source + steps) for source in range(l...  44.2 us
    ppermute x10, waiting for transfers between devices, partner(): return lax.ppermute(value, axis, pairs)  25.3 us
    reduce_sum x1, other arithmetic, shade_slices(): return (jnp.sum(emission * before, axis=0), 1.0 - through[-1])  23.7 us
    slice x1, local copies, waits for them, and re-layouts, shade_slices(): before = jnp.concatenate([jnp.ones_like(through[:1]), through[:-1]], axis=0)  13.7 us
    dot_general x1, matrix products, shards(): jnp.einsum('srw,swq->srq', masked, lateral_matrix, preferred_element_type...  13.3 us
    ppermute x10, starting transfers between devices, partner(): return lax.ppermute(value, axis, pairs)  12.4 us
    add x1, other arithmetic, shards(): resampled[:, :, :col_count].astype(jnp.float32)  11.6 us
    dot_general x1, matrix products, shards(): jnp.einsum('sij,sjq->siq', vertical_matrix, across, preferred_element_typ...  11.1 us
  transfers between devices with their start and end apart: 11, of which 10 were waited for; matrix products, arithmetic and copies ran while one was open for 19% of the time, Pallas kernels for 0%

commit v1 on v0

v1 whole, which is shorter than its diff:
```python
import functools
import math

import jax
import jax.numpy as jnp
from jax import lax
from jax.experimental import pallas as pl
from jax.experimental.pallas import tpu as pltpu
from jax.sharding import PartitionSpec as P

SHIFT = 128
BLK = 128
HALF = SHIFT // 2
LANES = 128
PIECE = 16
WIRE = jnp.float32
LOG2E = math.log2(math.e)
SMEM = pltpu.SMEM
F32 = jnp.float32
BF16 = jnp.bfloat16


def rounded(scalar, shape):
    return jnp.full(shape, scalar, F32).astype(BF16).astype(F32)


def tap(distance, offset, fraction):
    second = jnp.where(distance == offset + 1, fraction, 0.0)
    return jnp.where(distance == offset, 1.0 - fraction, second)


def strips_kernel(occ, x_first, x_last, to_left, to_right):
    chunk = pl.program_id(0)
    half = x_first.shape[2] // 2
    k = lax.broadcasted_iota(jnp.int32, (2 * LANES, LANES), 0)
    n = lax.broadcasted_iota(jnp.int32, (2 * LANES, LANES), 1)
    take = jnp.where(n < HALF, n, n + HALF)
    for ref, out, first, column in (
        (x_first, to_left, 0, 0),
        (x_last, to_right, HALF, occ.shape[2] - 1),
    ):
        low = occ[0, 2 * chunk, column].astype(F32)
        high = occ[0, 2 * chunk + 1, column].astype(F32)
        if first == 0:
            source = take
            pick = jnp.where(k == source, jnp.where(n < HALF, low, high), 0.0)
        else:
            source = jnp.where(n < HALF, n + LANES + HALF, n)
            pick = jnp.where(k == source, jnp.where(n < HALF, high, low), 0.0)
        pick = pick.astype(BF16)
        for s in range(ref.shape[1]):
            rows = jnp.concatenate([ref[0, s, :half], ref[0, s, half:]], axis=1)
            out[0, s] = jnp.dot(rows, pick, preferred_element_type=F32).astype(BF16)


def edge_strips(density, occupancy, chunks):
    _, slices, rows, cols = density.shape
    step = rows // chunks
    shape = jax.ShapeDtypeStruct((chunks, slices, step // 2, LANES), BF16)
    last = cols // LANES - 1
    return pl.pallas_call(
        strips_kernel,
        grid=(chunks,),
        in_specs=[
            pl.BlockSpec(memory_space=SMEM),
            pl.BlockSpec((1, slices, step, LANES), lambda c: (0, 0, c, 0)),
            pl.BlockSpec((1, slices, step, LANES), lambda c: (0, 0, c, last)),
        ],
        out_specs=[pl.BlockSpec((1, slices, step // 2, LANES), lambda c: (c, 0, 0, 0))] * 2,
        out_shape=[shape, shape],
        name="edge_strips",
    )(occupancy, density, density)


def shade(s, x, base, state, refs, first_row):
    frac_vertical, extinction, slice_total = refs
    through_ref, sum_ref = state
    rows = x.shape[0]
    v0 = 2.0 * rounded(1.0 - frac_vertical[0, s], (1, LANES))
    v1 = 2.0 * rounded(frac_vertical[0, s], (1, LANES))
    density = v0 * x + v1 * pltpu.roll(x, 1, 0)
    above = pltpu.roll(density, 1, 0)
    density, above = density[8:], above[8:]
    rate = extinction[0, s] * (-LOG2E / (2.0 * slice_total))
    kept = jnp.exp2(rate * density)
    slope = jnp.tanh(density - above)
    through = through_ref[base : base + rows - 8]
    after = through * kept
    through_ref[base : base + rows - 8] = after
    sum_ref[base : base + rows - 8] += (through - after) * slope


def finish(state, gain, swap, out_keep, out_send, tile):
    through_ref, sum_ref = state
    rows = out_keep.shape[1] * 2
    base = tile * rows
    alphas, colors = [], []
    for p in range(rows // PIECE):
        at = slice(base + p * PIECE, base + (p + 1) * PIECE)
        alpha = 1.0 - through_ref[at]
        alphas.append(alpha)
        colors.append(gain * (0.65 * alpha + 0.35 * sum_ref[at]))
    lanes = slice(tile * LANES, (tile + 1) * LANES)
    for q in range(rows // PIECE // 2):
        at = slice(q * PIECE, (q + 1) * PIECE)
        for i, values in enumerate((colors, alphas)):
            even, odd = values[2 * q], values[2 * q + 1]
            out_keep[i, at, lanes] = jnp.where(swap, odd, even)
            out_send[i, at, lanes] = jnp.where(swap, even, odd).astype(out_send.dtype)


def interior_kernel(
    slice_total, occ, offset, frac_lateral, frac_vertical, extinction, gain,
    x_ref, lead_ref, out_keep, out_send, weights, through_ref, sum_ref,
):
    block = pl.program_id(0)
    slices, rows = x_ref.shape[1], x_ref.shape[2]
    tiles = x_ref.shape[3] // LANES

    @pl.when(block == 0)
    def _():
        k = lax.broadcasted_iota(jnp.int32, (2 * LANES, LANES), 0)
        n = lax.broadcasted_iota(jnp.int32, (2 * LANES, LANES), 1)

        def build(s, _):
            weights[s] = tap(LANES + n - k, offset[0, s], frac_lateral[0, s]).astype(BF16)
            return 0

        lax.fori_loop(0, slices, build, 0)

    through_ref[...] = jnp.ones_like(through_ref)
    sum_ref[...] = jnp.zeros_like(sum_ref)
    inside = jnp.where(block > 0, 1, 0)
    above = jnp.maximum(block - 1, 0)
    mask = [jnp.full((1, LANES), occ[0, block, t], F32).astype(BF16) for t in range(tiles)]
    lead_mask = [
        jnp.full((1, LANES), occ[0, above, t] * inside, F32).astype(BF16) for t in range(tiles)
    ]
    state = (through_ref, sum_ref)

    def one(s, _):
        parts = []
        for t in range(tiles):
            lanes = slice(t * LANES, (t + 1) * LANES)
            parts.append(
                jnp.concatenate(
                    [lead_ref[0, s, :, lanes] * lead_mask[t], x_ref[0, s, :, lanes] * mask[t]],
                    axis=0,
                )
            )
        for t in range(1, tiles):
            pair = jnp.concatenate([parts[t - 1], parts[t]], axis=1)
            x = jnp.dot(pair, weights[s], preferred_element_type=F32)
            shade(
                s, x[8:], (t - 1) * rows, state,
                (frac_vertical, extinction, slice_total), rows,
            )
        return 0

    lax.fori_loop(0, slices, one, 0)
    swap = lax.axis_index("depth") % 2 == 1
    for t in range(tiles - 1):
        finish(state, gain[0], swap, out_keep, out_send, t)


def small_specs():
    return [pl.BlockSpec(memory_space=SMEM)] * 6


def interior(density, small, slice_total):
    _, slices, rows, cols = density.shape
    step = BLK
    width = cols - LANES
    return pl.pallas_call(
        functools.partial(interior_kernel, slice_total),
        grid=(rows // step,),
        in_specs=small_specs()
        + [
            pl.BlockSpec((1, slices, step, cols), lambda b: (0, 0, b, 0)),
            pl.BlockSpec(
                (1, slices, 16, cols), lambda b: (0, 0, jnp.maximum(b * (step // 16) - 1, 0), 0)
            ),
        ],
        out_specs=[pl.BlockSpec((2, step // 2, width), lambda b: (0, b, 0))] * 2,
        out_shape=[
            jax.ShapeDtypeStruct((2, rows // 2, width), F32),
            jax.ShapeDtypeStruct((2, rows // 2, width), F32),
        ],
        scratch_shapes=[
            pltpu.VMEM((slices, 2 * LANES, LANES), BF16),
            pltpu.VMEM((step * (cols // LANES - 1), LANES), F32),
            pltpu.VMEM((step * (cols // LANES - 1), LANES), F32),
        ],
        compiler_params=pltpu.CompilerParams(vmem_limit_bytes=40 * 2**20),
        name="interior",
    )(*small, density, density)


def border_kernel(
    chunk, slice_total, occ, offset, frac_lateral, frac_vertical, extinction, gain,
    first_ref, last_ref, first_lead, last_lead, right_ref, left_ref, right_lead, left_lead,
    out_keep, out_send, weights, through_ref, sum_ref,
):
    half = pl.program_id(0)
    block = 2 * chunk + half
    slices, rows = first_ref.shape[1], first_ref.shape[2]
    last_tile = occ.shape[2] - 1
    follows = jnp.where(lax.axis_index("lat") < lax.axis_size("lat") - 1, 1, 0)

    @pl.when(half == 0)
    def _():
        k = lax.broadcasted_iota(jnp.int32, (LANES, LANES), 0)
        n = lax.broadcasted_iota(jnp.int32, (LANES, LANES), 1)
        far = 1 << 20
        own = jnp.where(n >= HALF, n - k, far)
        before = jnp.where(n < HALF, LANES + n - k, far)
        swapped = jnp.where(k < HALF, k + HALF, k - HALF)

        def build(s, _):
            o, f = offset[0, s], frac_lateral[0, s]
            w_own = tap(own, o, f)
            w_before = tap(before, o, f)
            for v, kk in enumerate((k, swapped)):
                right = jnp.where((kk < HALF) & (n < HALF), n - kk, far)
                left = jnp.where((kk >= HALF) & (n >= HALF), LANES + n - kk, far)
                weights[v, s, 0:LANES] = w_own.astype(BF16)
                weights[v, s, LANES : 2 * LANES] = w_before.astype(BF16)
                weights[v, s, 2 * LANES : 3 * LANES] = tap(right, o, f).astype(BF16)
                weights[v, s, 3 * LANES :] = tap(left, o, f).astype(BF16)
            return 0

        lax.fori_loop(0, slices, build, 0)

    through_ref[...] = jnp.ones_like(through_ref)
    sum_ref[...] = jnp.zeros_like(sum_ref)
    inside = jnp.where(block > 0, 1, 0)
    above = jnp.maximum(block - 1, 0)

    def splat(value):
        return jnp.full((1, LANES), value, F32).astype(BF16)

    mask_first = splat(occ[0, block, 0])
    mask_last = splat(occ[0, block, last_tile] * follows)
    lead_first = splat(occ[0, above, 0] * inside)
    lead_last = splat(occ[0, above, last_tile] * follows * inside)
    lead_halo = splat(inside)
    state = (through_ref, sum_ref)

    def one(s, _):
        lead = jnp.concatenate(
            [
                first_lead[0, s] * lead_first,
                last_lead[0, s] * lead_last,
                right_lead[0, s] * lead_halo,
                left_lead[0, s] * lead_halo,
            ],
            axis=1,
        )
        main = jnp.concatenate(
            [first_ref[0, s] * mask_first, last_ref[0, s] * mask_last, right_ref[0, s], left_ref[0, s]],
            axis=1,
        )
        x_lead = jnp.dot(lead, weights[1 - half, s], preferred_element_type=F32)
        x_main = jnp.dot(main, weights[half, s], preferred_element_type=F32)
        x = jnp.concatenate([x_lead[8:], x_main], axis=0)
        shade(s, x, 0, state, (frac_vertical, extinction, slice_total), rows)
        return 0

    lax.fori_loop(0, slices, one, 0)
    swap = lax.axis_index("depth") % 2 == 1
    finish(state, gain[0], swap, out_keep, out_send, 0)


def border(density, small, halos, previous, chunk, chunks, slice_total):
    _, slices, rows, cols = density.shape
    step = BLK
    last = cols // LANES - 1
    first_block = 2 * chunk
    per = step // 16

    def body(column):
        return pl.BlockSpec((1, slices, step, LANES), lambda b: (0, 0, first_block + b, column))

    def lead(column):
        return pl.BlockSpec(
            (1, slices, 16, LANES),
            lambda b: (0, 0, jnp.maximum((first_block + b) * per - 1, 0), column),
        )

    halo = pl.BlockSpec((1, slices, step, LANES), lambda b: (0, 0, 0, 0))
    halo_lead = pl.BlockSpec((1, slices, 16, LANES), lambda b: (b, 0, 0, 0))
    right, left = halos
    leads = [
        jnp.concatenate([p[:, :, -16:], h[:, :, -16:]], axis=0) for p, h in zip(previous, halos)
    ]
    return pl.pallas_call(
        functools.partial(border_kernel, chunk, slice_total),
        grid=(2,),
        in_specs=small_specs()
        + [body(0), body(last), lead(0), lead(last), halo, halo, halo_lead, halo_lead],
        out_specs=[pl.BlockSpec((2, step // 2, LANES), lambda b: (0, b, 0))] * 2,
        out_shape=[
            jax.ShapeDtypeStruct((2, step, LANES), F32),
            jax.ShapeDtypeStruct((2, step, LANES), F32),
        ],
        scratch_shapes=[
            pltpu.VMEM((2, slices, 4 * LANES, LANES), BF16),
            pltpu.VMEM((step, LANES), F32),
            pltpu.VMEM((step, LANES), F32),
        ],
        compiler_params=pltpu.CompilerParams(vmem_limit_bytes=40 * 2**20),
        name=f"border{chunk}",
    )(*small, density, density, density, density, right, left, *leads)


def over(a, b, a_in_front):
    color = jnp.where(a_in_front, a[0], b[0]) + (
        1.0 - jnp.where(a_in_front, a[1], b[1])
    ) * jnp.where(a_in_front, b[0], a[0])
    return color, a[1] + (1.0 - a[1]) * b[1]


def load(ref, at):
    return ref[0, at].astype(F32), ref[1, at].astype(F32)


def merge_pair_kernel(rank, mine, other, own, *sends):
    me = lax.axis_index("depth")
    z = (me // 2) % 4
    front = rank[me] < rank[jnp.bitwise_xor(me, 1)]
    for k, out in enumerate((own,) + sends):
        target = jnp.bitwise_xor(z, k)
        for y in range(mine.shape[1] // (4 * PIECE)):
            at = pl.ds(pl.multiple_of((4 * y + target) * PIECE, PIECE), PIECE)
            color, alpha = over(load(mine, at), load(other, at), front)
            out[0, y * PIECE : (y + 1) * PIECE] = color.astype(out.dtype)
            out[1, y * PIECE : (y + 1) * PIECE] = alpha.astype(out.dtype)


def four(rank, stride, parts, at):
    me = lax.axis_index("depth")
    ranks = [rank[jnp.bitwise_xor(me, stride * k)] for k in range(4)]
    values = [load(ref, at) for ref in parts]
    low = over(values[0], values[1], ranks[0] < ranks[1])
    high = over(values[2], values[3], ranks[2] < ranks[3])
    return over(low, high, ranks[0] < ranks[2])


def merge_z_kernel(rank, p0, p1, p2, p3, own, *sends):
    y = lax.axis_index("depth") // 8
    for k, out in enumerate((own,) + sends):
        target = jnp.bitwise_xor(y, k)
        at = pl.ds(pl.multiple_of(target * PIECE, PIECE), PIECE)
        color, alpha = four(rank, 2, (p0, p1, p2, p3), at)
        out[0] = color.astype(out.dtype)
        out[1] = alpha.astype(out.dtype)


def vmem_call(kernel, outs, name, rank, *arrays):
    return pl.pallas_call(
        kernel,
        in_specs=[pl.BlockSpec(memory_space=SMEM)]
        + [pl.BlockSpec(memory_space=pltpu.VMEM)] * len(arrays),
        out_specs=[pl.BlockSpec(memory_space=pltpu.VMEM)] * len(outs),
        out_shape=outs,
        name=name,
    )(rank, *arrays)


def depth_swap(value, bits):
    count = lax.axis_size("depth")
    return lax.ppermute(value, "depth", [(i, i ^ bits) for i in range(count)])


def depth_and_lat(value, bits, step):
    depth, lat = lax.axis_size("depth"), lax.axis_size("lat")
    pairs = [
        (i * lat + x, (i ^ bits) * lat + (x + step) % lat) for i in range(depth) for x in range(lat)
    ]
    return lax.ppermute(value, ("depth", "lat"), pairs)


def over_depth(keep, send, rank, name):
    width = keep.shape[2]
    other = depth_swap(send, 1)
    part = (2, keep.shape[1] // 4, width)
    outs = [jax.ShapeDtypeStruct(part, F32)] + [jax.ShapeDtypeStruct(part, WIRE)] * 3
    own, *sends = vmem_call(merge_pair_kernel, outs, f"cores_{name}", rank, keep, other)
    received = [depth_swap(v, 2 * (k + 1)) for k, v in enumerate(sends)]
    part = (2, PIECE, width)
    outs = [jax.ShapeDtypeStruct(part, F32)] + [jax.ShapeDtypeStruct(part, WIRE)] * 3
    return vmem_call(merge_z_kernel, outs, f"chips_z_{name}", rank, own, *received)


def final_kernel(rank, *refs):
    inner, near, moved = refs[:4], refs[4:8], refs[8:12]
    out_color, out_alpha = refs[12:]
    everything = slice(None)
    color, alpha = four(rank, 8, inner, everything)
    out_color[:, LANES:] = color
    out_alpha[:, LANES:] = alpha
    here = four(rank, 8, near, everything)
    there = four(rank, 8, moved, everything)
    lane = lax.broadcasted_iota(jnp.int32, here[0].shape, 1)
    out_color[:, :LANES] = jnp.where(lane < HALF, there[0], here[0])
    out_alpha[:, :LANES] = jnp.where(lane < HALF, there[1], here[1])


def shards(
    density, occupancy, shear_offsets, frac_lateral, frac_vertical, extinction, slab_gain, view_rank
):
    _, slices, rows, cols = density.shape
    slice_total = lax.axis_size("depth") * slices
    lat = lax.axis_size("lat")
    small = (occupancy, shear_offsets, frac_lateral, frac_vertical, extinction, slab_gain)
    chunks = rows // (2 * BLK)
    to_left, to_right = edge_strips(density, occupancy, chunks)
    rightwards = [(x, x + 1) for x in range(lat - 1)]
    leftwards = [(x, (x - 1) % lat) for x in range(lat)]
    halos = []
    for c in range(chunks):
        from_right = lax.ppermute(to_left[c : c + 1], "lat", leftwards)
        from_left = lax.ppermute(to_right[c : c + 1], "lat", rightwards)
        halos.append((from_right, from_left))
    keep, send = interior(density, small, slice_total)
    inner = over_depth(keep, send, view_rank, "inner")
    inner = [inner[0]] + [depth_swap(v, 8 * (k + 1)) for k, v in enumerate(inner[1:])]
    keeps, sends = [], []
    for c in range(chunks):
        k, s = border(density, small, halos[c], halos[max(c - 1, 0)], c, chunks, slice_total)
        keeps.append(k)
        sends.append(s)
    keep = jnp.concatenate(keeps, axis=1)
    send = jnp.concatenate(sends, axis=1)
    edge = over_depth(keep, send, view_rank, "edge")
    near = [edge[0]] + [depth_swap(v, 8 * (k + 1)) for k, v in enumerate(edge[1:])]
    moved = [depth_and_lat(v.astype(WIRE), 8 * k, 1) for k, v in enumerate(edge)]
    out = jax.ShapeDtypeStruct((PIECE, cols), F32)
    return tuple(
        vmem_call(final_kernel, [out, out], "chips_y", view_rank, *inner, *near, *moved)
    )


def solution(mesh):
    placed = (
        P("depth", None, None, "lat"),
        P("depth", None, "lat"),
        P("depth", None),
        P("depth", None),
        P("depth", None),
        P("depth", None),
        P("depth"),
        P(),
    )
    return jax.shard_map(
        shards,
        mesh=mesh,
        in_specs=placed,
        out_specs=(P("depth", "lat"), P("depth", "lat")),
        check_vma=False,
    )
```

time: 190 us -> 113 us (0.59)
  waiting for transfers between devices: 69.5 us -> 14.7 us
  other arithmetic: 52 us -> 0.77 us
  Pallas kernels: 0 us -> 50.3 us
  matrix products: 24.5 us -> 0 us
  starting transfers between devices: 16.2 us -> 35.1 us
  local copies, waits for them, and re-layouts: 22 us -> 10.4 us
  between operations: 4.73 us -> 1.62 us
    ppermute x11 -> x22, waiting for transfers between devices: 69.5 us -> 14.7 us  [the longest x4 11.8 us: depth_and_lat(): return lax.ppermute(value, ('depth', 'lat'), pairs)]
    pallas_call x0 -> x9, Pallas kernels: none -> 50.3 us  [the longest x1 19.5 us: interior(): pl.pallas_call(functools.partial(interior_kernel, slice_total), grid=(row...]
    dot_general x2 -> x0, matrix products: 24.5 us -> none  [the longest x1 13.3 us: shards(): jnp.einsum('srw,swq->srq', masked, lateral_matrix, preferred_element_type...]
    reduce_sum x1 -> x0, other arithmetic: 23.7 us -> none  [shade_slices(): return (jnp.sum(emission * before, axis=0), 1.0 - through[-1])]
    ppermute x11 -> x22, starting transfers between devices: 16.2 us -> 35.1 us  [the longest x14 24.1 us: depth_swap(): return lax.ppermute(value, 'depth', [(i, i ^ bits) for i in range(count)])]
    add x5 -> x0, other arithmetic: 13.2 us -> none  [the longest x1 11.6 us: shards(): resampled[:, :, :col_count].astype(jnp.float32)]
    slice x2 -> x6, local copies, waits for them, and re-layouts: 15.4 us -> 2.58 us  [the longest x1 1.27 us: shards(): from_right = lax.ppermute(to_left[c:c + 1], 'lat', leftwards)]
    another operation x1 -> x0, other arithmetic: 10.8 us -> none  [shade_slices(): through = jnp.cumprod(1.0 - opacity, axis=0)]
  transfers between devices with their start and end apart: 11 -> 22, of which waited for: 10 -> 7; matrix products, arithmetic and copies ran while one was open for 19% -> 2% of each run, Pallas kernels for 0% -> 40%
where the time goes in v1:
time: 113 us
  Pallas kernels  50.3 us (45%)
  starting transfers between devices  35.1 us (31%)
  waiting for transfers between devices  14.7 us (13%)
  local copies, waits for them, and re-layouts  10.4 us (9%)
  between operations  1.62 us (1%)
    ppermute x14, starting transfers between devices, depth_swap(): return lax.ppermute(value, 'depth', [(i, i ^ bits) for i in range(count)])  24.1 us
    pallas_call x1, Pallas kernels, interior(): pl.pallas_call(functools.partial(interior_kernel, slice_total), grid=(row...  19.5 us
    pallas_call x2, Pallas kernels, border(): pl.pallas_call(functools.partial(border_kernel, chunk, slice_total), grid...  17.5 us
    ppermute x4, waiting for transfers between devices, depth_and_lat(): return lax.ppermute(value, ('depth', 'lat'), pairs)  11.8 us
    pallas_call x5, Pallas kernels, vmem_call(): pl.pallas_call(kernel, in_specs=[pl.BlockSpec(memory_space=SMEM)] + [pl.B...  9.31 us
    unnamed x50, local copies, waits for them, and re-layouts  7.86 us
    ppermute x2, starting transfers between devices, shards(): from_left = lax.ppermute(to_right[c:c + 1], 'lat', rightwards)  5.05 us
    pallas_call x1, Pallas kernels, edge_strips(): pl.pallas_call(strips_kernel, grid=(chunks,), in_specs=[pl.BlockSpec(memo...  3.9 us
  transfers between devices with their start and end apart: 22, of which 7 were waited for; matrix products, arithmetic and copies ran while one was open for 2% of the time, Pallas kernels for 40%

profile of v1, /device:TPU:0, one launch (start us, length us, event | category | flops | bytes accessed | tf_op | source)
XLA Modules:
  0.0 112.9 jit_solution(17258781204820888951)
XLA Ops:
  0.7 3.9 %edge_strips.1 = (bf16[2,16,128,128]{3,2,1,0:T(8,128)(2,1)}, bf16[2,16,128,128]{3,2,1,0:T(8,128)(2,1)}) custom-call(s32[1,4,4]{2,1,0:T(4,128)} %occ.7, bf16[1,16,512,512]{3,2,1,0:T(8,128)(2,1)} %last_lead.3, bf16[1,16,512,512]{3,2,1,0:T(8,128)(2,1)} %last_lead.3), custom_call_target="tpu_custom_call" | custom-call | tf_op jit(solution)/shard_map/edge_strips/pallas_call | solution.py:61
  4.6 1.3 %fusion.1 = (bf16[1,16,128,128]{3,2,1,0:T(8,128)(2,1)S(1)}, bf16[1,16,128,128]{3,2,1,0:T(8,128)(2,1)S(1)}) fusion(bf16[2,16,128,128]{3,2,1,0:T(8,128)(2,1)} %get-tuple-element.36), kind=kLoop, calls=%fused_computation.7 | loop fusion | bytes 2097152 | tf_op jit(solution)/shard_map/slice | solution.py:422
  5.9 2.9 %collective-permute-start.9 = (bf16[1,16,128,128]{3,2,1,0:T(8,128)(2,1)S(1)}, bf16[1,16,128,128]{3,2,1,0:T(8,128)(2,1)S(1)}, u32[]{:S(2)}, u32[]{:S(2)}) collective-permute-start(bf16[1,16,128,128]{3,2,1,0:T(8,128)(2,1)S(1)} %get-tuple-element.53), channel_id=1, source_target_pairs={{0,3},{1,0},{2,1},{3,2},{4,7},{5,4},{6,5},{7,6},{8,11},{9,8},{10,9... | collective-permute-start | bytes 1572872 | tf_op jit(solution)/shard_map/ppermute | solution.py:422
  8.7 0.8 collective-permute-start.7
  9.6 1.3 %fusion = (bf16[1,16,128,128]{3,2,1,0:T(8,128)(2,1)S(1)}, bf16[1,16,128,128]{3,2,1,0:T(8,128)(2,1)S(1)}) fusion(bf16[2,16,128,128]{3,2,1,0:T(8,128)(2,1)} %get-tuple-element.37), kind=kLoop, calls=%fused_computation.6 | loop fusion | bytes 2097152 | tf_op jit(solution)/shard_map/slice | solution.py:423
  10.8 3.1 %collective-permute-start.8 = (bf16[1,16,128,128]{3,2,1,0:T(8,128)(2,1)S(1)}, bf16[1,16,128,128]{3,2,1,0:T(8,128)(2,1)S(1)}, u32[]{:S(2)}, u32[]{:S(2)}) collective-permute-start(bf16[1,16,128,128]{3,2,1,0:T(8,128)(2,1)S(1)} %get-tuple-element.50), channel_id=1, source_target_pairs={{0,1},{1,2},{2,3},{4,5},{5,6},{6,7},{8,9},{9,10},{10,11},{12,13},{... | collective-permute-start | bytes 1572872 | tf_op jit(solution)/shard_map/ppermute | solution.py:423
  14.0 1.9 %collective-permute-start.10 = (bf16[1,16,128,128]{3,2,1,0:T(8,128)(2,1)S(1)}, bf16[1,16,128,128]{3,2,1,0:T(8,128)(2,1)S(1)}, u32[]{:S(2)}, u32[]{:S(2)}) collective-permute-start(bf16[1,16,128,128]{3,2,1,0:T(8,128)(2,1)S(1)} %get-tuple-element.51), channel_id=1, source_target_pairs={{0,1},{1,2},{2,3},{4,5},{5,6},{6,7},{8,9},{9,10},{10,11},{12,13},{... | collective-permute-start | bytes 1572872 | tf_op jit(solution)/shard_map/ppermute | solution.py:423
  16.6 3.4 %copy-done = bf16[1,16,512,512]{3,2,1,0:T(8,128)(2,1)S(1)} copy-done((bf16[1,16,512,512]{3,2,1,0:T(8,128)(2,1)S(1)}, bf16[1,16,512,512]{3,2,1,0:T(8,128)(2,1)}, u32[]{:S(2)}) %copy-start) | copy-done | bytes 8388632
  20.0 19.5 %interior.1 = (f32[2,256,384]{2,1,0:T(8,128)S(1)}, f32[2,256,384]{2,1,0:T(8,128)S(1)}) custom-call(s32[1,4,4]{2,1,0:T(4,128)S(1)} %copy-done.2, s32[1,16]{1,0:T(1,128)S(1)} %copy-done.3, f32[1,16]{1,0:T(1,128)S(1)} %copy-done.4, f32[1,16]{1,0:T(1,128)S(1)} %copy-done.5, f32[1,16]{1,0:T(1,128)S(1)} %copy-done.6, f32[1]{0:T(128)S(6)} %copy.10.gain, ...), custom_call_target="tpu_custom_call" | custom-call | tf_op jit(solution)/shard_map/interior/pallas_call | solution.py:174
  39.5 0.9 copy-done.1
  40.6 8.8 %border1.1 = (f32[2,128,128]{2,1,0:T(8,128)S(1)}, f32[2,128,128]{2,1,0:T(8,128)S(1)}) custom-call(s32[1,4,4]{2,1,0:T(4,128)S(1)} %copy-done.2, s32[1,16]{1,0:T(1,128)S(1)} %copy-done.3, f32[1,16]{1,0:T(1,128)S(1)} %copy-done.4, f32[1,16]{1,0:T(1,128)S(1)} %copy-done.5, f32[1,16]{1,0:T(1,128)S(1)} %copy-done.6, f32[1]{0:T(128)S(6)} %copy.10.gain, ...), custom_call_target="tpu_custom_call" | custom-call | tf_op jit(solution)/shard_map/border1/pallas_call | solution.py:296
  49.4 8.8 %border0.1 = (f32[2,128,128]{2,1,0:T(8,128)S(1)}, f32[2,128,128]{2,1,0:T(8,128)S(1)}) custom-call(s32[1,4,4]{2,1,0:T(4,128)S(1)} %copy-done.2, s32[1,16]{1,0:T(1,128)S(1)} %copy-done.3, f32[1,16]{1,0:T(1,128)S(1)} %copy-done.4, f32[1,16]{1,0:T(1,128)S(1)} %copy-done.5, f32[1,16]{1,0:T(1,128)S(1)} %copy-done.6, f32[1]{0:T(128)S(6)} %copy.10.gain, ...), custom_call_target="tpu_custom_call" | custom-call | tf_op jit(solution)/shard_map/border0/pallas_call | solution.py:296
  58.8 0.9 copy-done.7
  59.7 2.3 %cores_inner.1 = (f32[2,64,384]{2,1,0:T(8,128)}, f32[2,64,384]{2,1,0:T(8,128)}, f32[2,64,384]{2,1,0:T(8,128)}, f32[2,64,384]{2,1,0:T(8,128)}) custom-call(s32[32]{0:T(128)} %rank.9, f32[2,256,384]{2,1,0:T(8,128)} %copy-done.1, f32[2,256,384]{2,1,0:T(8,128)} %copy-done.7), custom_call_target="tpu_custom_call" | custom-call | tf_op jit(solution)/shard_map/cores_inner/pallas_call | solution.py:360
  62.0 2.0 %collective-permute-start.1 = (f32[2,64,384]{2,1,0:T(8,128)}, f32[2,64,384]{2,1,0:T(8,128)S(1)}, u32[]{:S(2)}, u32[]{:S(2)}) collective-permute-start(f32[2,64,384]{2,1,0:T(8,128)} %get-tuple-element.29), channel_id=1, source_target_pairs={{0,8},{4,12},{8,0},{12,4},{16,24},{20,28},{24,16},{28,20},{32,40},... | collective-permute-start | bytes 589832 | tf_op jit(solution)/shard_map/ppermute | solution.py:372
  64.0 3.5 %collective-permute-start.2 = (f32[2,64,384]{2,1,0:T(8,128)}, f32[2,64,384]{2,1,0:T(8,128)S(1)}, u32[]{:S(2)}, u32[]{:S(2)}) collective-permute-start(f32[2,64,384]{2,1,0:T(8,128)} %get-tuple-element.30), channel_id=1, source_target_pairs={{0,16},{4,20},{8,24},{12,28},{16,0},{20,4},{24,8},{28,12},{32,48},... | collective-permute-start | bytes 589832 | tf_op jit(solution)/shard_map/ppermute | solution.py:372
  67.5 0.7 pad_maximum_fusion.mine
  69.0 1.8 %cores_edge.1 = (f32[2,64,128]{2,1,0:T(8,128)}, f32[2,64,128]{2,1,0:T(8,128)}, f32[2,64,128]{2,1,0:T(8,128)}, f32[2,64,128]{2,1,0:T(8,128)}) custom-call(s32[32]{0:T(128)} %rank.9, f32[2,256,128]{2,1,0:T(8,128)} %pad_maximum_fusion.mine, f32[2,256,128]{2,1,0:T(8,128)} %copy-done.8), custom_call_target="tpu_custom_call" | custom-call | tf_op jit(solution)/shard_map/cores_edge/pallas_call | solution.py:360
  70.8 4.7 %collective-permute-start.13 = (f32[2,64,128]{2,1,0:T(8,128)}, f32[2,64,128]{2,1,0:T(8,128)S(1)}, u32[]{:S(2)}, u32[]{:S(2)}) collective-permute-start(f32[2,64,128]{2,1,0:T(8,128)} %get-tuple-element.44), channel_id=1, source_target_pairs={{0,16},{4,20},{8,24},{12,28},{16,0},{20,4},{24,8},{28,12},{32,48},... | collective-permute-start | bytes 196616 | tf_op jit(solution)/shard_map/ppermute | solution.py:372
  75.6 3.9 %collective-permute-start.14 = (f32[2,64,128]{2,1,0:T(8,128)}, f32[2,64,128]{2,1,0:T(8,128)S(1)}, u32[]{:S(2)}, u32[]{:S(2)}) collective-permute-start(f32[2,64,128]{2,1,0:T(8,128)} %get-tuple-element.45), channel_id=1, source_target_pairs={{0,24},{4,28},{8,16},{12,20},{16,8},{20,12},{24,0},{28,4},{32,56},... | collective-permute-start | bytes 196616 | tf_op jit(solution)/shard_map/ppermute | solution.py:372
  79.7 2.6 %collective-permute-done.14.p3 = f32[2,64,128]{2,1,0:T(8,128)S(1)} collective-permute-done((f32[2,64,128]{2,1,0:T(8,128)}, f32[2,64,128]{2,1,0:T(8,128)S(1)}, u32[]{:S(2)}, u32[]{:S(2)}) %collective-permute-start.14) | collective-permute-done | bytes 65568 | tf_op jit(solution)/shard_map/ppermute | solution.py:372
  82.9 1.6 %chips_z_edge.1 = (f32[2,16,128]{2,1,0:T(8,128)}, f32[2,16,128]{2,1,0:T(8,128)}, f32[2,16,128]{2,1,0:T(8,128)}, f32[2,16,128]{2,1,0:T(8,128)}) custom-call(s32[32]{0:T(128)} %rank.9, f32[2,64,128]{2,1,0:T(8,128)} %get-tuple-element.42.p0, f32[2,64,128]{2,1,0:T(8,128)} %copy-done.12, f32[2,64,128]{2,1,0:T(8,128)} %copy-done.13, f32[2,64,128]{2,1,0:T(8,128)} %copy-done.14), custom_call_target="tpu_custom_call" | custom-call | tf_op jit(solution)/shard_map/chips_z_edge/pallas_call | solution.py:360
  84.5 1.6 %collective-permute-start.15 = (f32[2,16,128]{2,1,0:T(8,128)}, f32[2,16,128]{2,1,0:T(8,128)S(1)}, u32[]{:S(2)}, u32[]{:S(2)}) collective-permute-start(f32[2,16,128]{2,1,0:T(8,128)} %get-tuple-element.47), channel_id=1, source_target_pairs={{0,32},{4,36},{8,40},{12,44},{16,48},{20,52},{24,56},{28,60},{32,0... | collective-permute-start | bytes 49160 | tf_op jit(solution)/shard_map/ppermute | solution.py:372
  86.1 2.8 %collective-permute-start.16 = (f32[2,16,128]{2,1,0:T(8,128)}, f32[2,16,128]{2,1,0:T(8,128)S(1)}, u32[]{:S(2)}, u32[]{:S(2)}) collective-permute-start(f32[2,16,128]{2,1,0:T(8,128)} %get-tuple-element.48), channel_id=1, source_target_pairs={{0,64},{4,68},{8,72},{12,76},{16,80},{20,84},{24,88},{28,92},{32,9... | collective-permute-start | bytes 49160 | tf_op jit(solution)/shard_map/ppermute | solution.py:372
  89.9 2.0 %chips_z_inner.1 = (f32[2,16,384]{2,1,0:T(8,128)}, f32[2,16,384]{2,1,0:T(8,128)}, f32[2,16,384]{2,1,0:T(8,128)}, f32[2,16,384]{2,1,0:T(8,128)}) custom-call(s32[32]{0:T(128)} %rank.9, f32[2,64,384]{2,1,0:T(8,128)} %get-tuple-element.28.p0, f32[2,64,384]{2,1,0:T(8,128)} %copy-done.9, f32[2,64,384]{2,1,0:T(8,128)} %copy-done.10, f32[2,64,384]{2,1,0:T(8,128)} %copy-done.11), custom_call_target="tpu_custom_call" | custom-call | tf_op jit(solution)/shard_map/chips_z_inner/pallas_call | solution.py:360
  92.3 4.1 %collective-permute-start.5 = (f32[2,16,384]{2,1,0:T(8,128)}, f32[2,16,384]{2,1,0:T(8,128)S(1)}, u32[]{:S(2)}, u32[]{:S(2)}) collective-permute-start(f32[2,16,384]{2,1,0:T(8,128)} %get-tuple-element.34), channel_id=1, source_target_pairs={{0,64},{4,68},{8,72},{12,76},{16,80},{20,84},{24,88},{28,92},{32,9... | collective-permute-start | bytes 147464 | tf_op jit(solution)/shard_map/ppermute | solution.py:372
  97.3 4.5 %collective-permute-done.18.refs_8_ = f32[2,16,128]{2,1,0:T(8,128)S(1)} collective-permute-done((f32[2,16,128]{2,1,0:T(8,128)}, f32[2,16,128]{2,1,0:T(8,128)S(1)}, u32[]{:S(2)}, u32[]{:S(2)}) %collective-permute-start.18) | collective-permute-done | bytes 16416 | tf_op jit(solution)/shard_map/ppermute | solution.py:380
  102.0 1.4 %collective-permute-done.19.refs_9_ = f32[2,16,128]{2,1,0:T(8,128)S(1)} collective-permute-done((f32[2,16,128]{2,1,0:T(8,128)}, f32[2,16,128]{2,1,0:T(8,128)S(1)}, u32[]{:S(2)}, u32[]{:S(2)}) %collective-permute-start.19) | collective-permute-done | bytes 16416 | tf_op jit(solution)/shard_map/ppermute | solution.py:380
  103.4 1.3 %collective-permute-start.21 = (f32[2,16,128]{2,1,0:T(8,128)}, f32[2,16,128]{2,1,0:T(8,128)S(1)}, u32[]{:S(2)}, u32[]{:S(2)}) collective-permute-start(f32[2,16,128]{2,1,0:T(8,128)} %get-tuple-element.49), channel_id=1, source_target_pairs={{0,97},{1,98},{2,99},{3,96},{4,101},{5,102},{6,103},{7,100},{8,105... | collective-permute-start | bytes 49160 | tf_op jit(solution)/shard_map/ppermute | solution.py:380
  104.7 4.6 %collective-permute-done.20.refs_10_ = f32[2,16,128]{2,1,0:T(8,128)S(1)} collective-permute-done((f32[2,16,128]{2,1,0:T(8,128)}, f32[2,16,128]{2,1,0:T(8,128)S(1)}, u32[]{:S(2)}, u32[]{:S(2)}) %collective-permute-start.20) | collective-permute-done | bytes 16416 | tf_op jit(solution)/shard_map/ppermute | solution.py:380
  109.3 1.3 %collective-permute-done.21.refs_11_ = f32[2,16,128]{2,1,0:T(8,128)S(1)} collective-permute-done((f32[2,16,128]{2,1,0:T(8,128)}, f32[2,16,128]{2,1,0:T(8,128)S(1)}, u32[]{:S(2)}, u32[]{:S(2)}) %collective-permute-start.21) | collective-permute-done | bytes 16416 | tf_op jit(solution)/shard_map/ppermute | solution.py:380
  111.3 1.6 %chips_y.1 = (f32[16,512]{1,0:T(8,128)}, f32[16,512]{1,0:T(8,128)}) custom-call(s32[32]{0:T(128)} %rank.9, f32[2,16,384]{2,1,0:T(8,128)} %get-tuple-element.32.refs_0_, f32[2,16,384]{2,1,0:T(8,128)} %copy-done.15, f32[2,16,384]{2,1,0:T(8,128)} %copy-done.16, f32[2,16,384]{2,1,0:T(8,128)} %copy-done.17, f32[2,16,128]{2,1,0:T(8,128)} %get-tuple-element.46.refs_4_, ...), custom_call_target="tpu_custom_call" | custom-call | tf_op jit(solution)/shard_map/chips_y/pallas_call | solution.py:360
  (81 shorter events, 5.6 us)
Async XLA Ops:
  0.6 15.9 %copy-start.2 = (s32[1,4,4]{2,1,0:T(4,128)S(1)}, s32[1,4,4]{2,1,0:T(4,128)}, u32[]{:S(2)}) copy-start(s32[1,4,4]{2,1,0:T(4,128)} %occ.7) | copy-start | bytes 196
  0.6 15.9 %copy-start.3 = (s32[1,16]{1,0:T(1,128)S(1)}, s32[1,16]{1,0:T(1,128)}, u32[]{:S(2)}) copy-start(s32[1,16]{1,0:T(1,128)} %offset.5) | copy-start | bytes 196
  0.7 15.9 %copy-start.4 = (f32[1,16]{1,0:T(1,128)S(1)}, f32[1,16]{1,0:T(1,128)}, u32[]{:S(2)}) copy-start(f32[1,16]{1,0:T(1,128)} %frac_lateral.5) | copy-start | bytes 196
  0.7 15.9 %copy-start.5 = (f32[1,16]{1,0:T(1,128)S(1)}, f32[1,16]{1,0:T(1,128)}, u32[]{:S(2)}) copy-start(f32[1,16]{1,0:T(1,128)} %frac_vertical.5) | copy-start | bytes 196
  0.7 15.9 %copy-start.6 = (f32[1,16]{1,0:T(1,128)S(1)}, f32[1,16]{1,0:T(1,128)}, u32[]{:S(2)}) copy-start(f32[1,16]{1,0:T(1,128)} %extinction.5) | copy-start | bytes 196
  5.9 34.6 %collective-permute-start.9 = (bf16[1,16,128,128]{3,2,1,0:T(8,128)(2,1)S(1)}, bf16[1,16,128,128]{3,2,1,0:T(8,128)(2,1)S(1)}, u32[]{:S(2)}, u32[]{:S(2)}) collective-permute-start(bf16[1,16,128,128]{3,2,1,0:T(8,128)(2,1)S(1)} %get-tuple-element.53), channel_id=1, source_target_pairs={{0,3},{1,0},{2,1},{3,2},{4,7},{5,4},{6,5},{7,6},{8,11},{9,8},{10,9... | collective-permute-start | bytes 1572872 | tf_op jit(solution)/shard_map/ppermute | solution.py:422
  8.7 31.7 %collective-permute-start.7 = (bf16[1,16,128,128]{3,2,1,0:T(8,128)(2,1)S(1)}, bf16[1,16,128,128]{3,2,1,0:T(8,128)(2,1)S(1)}, u32[]{:S(2)}, u32[]{:S(2)}) collective-permute-start(bf16[1,16,128,128]{3,2,1,0:T(8,128)(2,1)S(1)} %get-tuple-element.52), channel_id=1, source_target_pairs={{0,3},{1,0},{2,1},{3,2},{4,7},{5,4},{6,5},{7,6},{8,11},{9,8},{10,9... | collective-permute-start | bytes 1572872 | tf_op jit(solution)/shard_map/ppermute | solution.py:422
  10.8 29.7 %collective-permute-start.8 = (bf16[1,16,128,128]{3,2,1,0:T(8,128)(2,1)S(1)}, bf16[1,16,128,128]{3,2,1,0:T(8,128)(2,1)S(1)}, u32[]{:S(2)}, u32[]{:S(2)}) collective-permute-start(bf16[1,16,128,128]{3,2,1,0:T(8,128)(2,1)S(1)} %get-tuple-element.50), channel_id=1, source_target_pairs={{0,1},{1,2},{2,3},{4,5},{5,6},{6,7},{8,9},{9,10},{10,11},{12,13},{... | collective-permute-start | bytes 1572872 | tf_op jit(solution)/shard_map/ppermute | solution.py:423
  14.0 26.5 %collective-permute-start.10 = (bf16[1,16,128,128]{3,2,1,0:T(8,128)(2,1)S(1)}, bf16[1,16,128,128]{3,2,1,0:T(8,128)(2,1)S(1)}, u32[]{:S(2)}, u32[]{:S(2)}) collective-permute-start(bf16[1,16,128,128]{3,2,1,0:T(8,128)(2,1)S(1)} %get-tuple-element.51), channel_id=1, source_target_pairs={{0,1},{1,2},{2,3},{4,5},{5,6},{6,7},{8,9},{9,10},{10,11},{12,13},{... | collective-permute-start | bytes 1572872 | tf_op jit(solution)/shard_map/ppermute | solution.py:423
  40.4 18.3 %collective-permute-start = (f32[2,256,384]{2,1,0:T(8,128)S(1)}, f32[2,256,384]{2,1,0:T(8,128)S(1)}, u32[]{:S(2)}, u32[]{:S(2)}) collective-permute-start(f32[2,256,384]{2,1,0:T(8,128)S(1)} %get-tuple-element.27), channel_id=1, source_target_pairs={{0,4},{4,0},{8,12},{12,8},{16,20},{20,16},{24,28},{28,24},{32,36},... | collective-permute-start | bytes 2359304 | tf_op jit(solution)/shard_map/ppermute | solution.py:372
  58.2 10.1 %collective-permute-start.11 = (f32[2,256,128]{2,1,0:T(8,128)S(1)}, f32[2,256,128]{2,1,0:T(8,128)S(1)}, u32[]{:S(2)}, u32[]{:S(2)}) collective-permute-start(f32[2,256,128]{2,1,0:T(8,128)S(1)} %pad_maximum_fusion.1), channel_id=1, source_target_pairs={{0,4},{4,0},{8,12},{12,8},{16,20},{20,16},{24,28},{28,24},{32,36},... | collective-permute-start | bytes 786440 | tf_op jit(solution)/shard_map/ppermute | solution.py:372
  62.0 26.9 %collective-permute-start.1 = (f32[2,64,384]{2,1,0:T(8,128)}, f32[2,64,384]{2,1,0:T(8,128)S(1)}, u32[]{:S(2)}, u32[]{:S(2)}) collective-permute-start(f32[2,64,384]{2,1,0:T(8,128)} %get-tuple-element.29), channel_id=1, source_target_pairs={{0,8},{4,12},{8,0},{12,4},{16,24},{20,28},{24,16},{28,20},{32,40},... | collective-permute-start | bytes 589832 | tf_op jit(solution)/shard_map/ppermute | solution.py:372
  64.0 25.2 %collective-permute-start.2 = (f32[2,64,384]{2,1,0:T(8,128)}, f32[2,64,384]{2,1,0:T(8,128)S(1)}, u32[]{:S(2)}, u32[]{:S(2)}) collective-permute-start(f32[2,64,384]{2,1,0:T(8,128)} %get-tuple-element.30), channel_id=1, source_target_pairs={{0,16},{4,20},{8,24},{12,28},{16,0},{20,4},{24,8},{28,12},{32,48},... | collective-permute-start | bytes 589832 | tf_op jit(solution)/shard_map/ppermute | solution.py:372
  67.5 21.6 %collective-permute-start.3 = (f32[2,64,384]{2,1,0:T(8,128)}, f32[2,64,384]{2,1,0:T(8,128)S(1)}, u32[]{:S(2)}, u32[]{:S(2)}) collective-permute-start(f32[2,64,384]{2,1,0:T(8,128)} %get-tuple-element.31), channel_id=1, source_target_pairs={{0,24},{4,28},{8,16},{12,20},{16,8},{20,12},{24,0},{28,4},{32,56},... | collective-permute-start | bytes 589832 | tf_op jit(solution)/shard_map/ppermute | solution.py:372
  70.8 4.9 %collective-permute-start.12 = (f32[2,64,128]{2,1,0:T(8,128)}, f32[2,64,128]{2,1,0:T(8,128)S(1)}, u32[]{:S(2)}, u32[]{:S(2)}) collective-permute-start(f32[2,64,128]{2,1,0:T(8,128)} %get-tuple-element.43), channel_id=1, source_target_pairs={{0,8},{4,12},{8,0},{12,4},{16,24},{20,28},{24,16},{28,20},{32,40},... | collective-permute-start | bytes 196616 | tf_op jit(solution)/shard_map/ppermute | solution.py:372
  70.8 8.9 %collective-permute-start.13 = (f32[2,64,128]{2,1,0:T(8,128)}, f32[2,64,128]{2,1,0:T(8,128)S(1)}, u32[]{:S(2)}, u32[]{:S(2)}) collective-permute-start(f32[2,64,128]{2,1,0:T(8,128)} %get-tuple-element.44), channel_id=1, source_target_pairs={{0,16},{4,20},{8,24},{12,28},{16,0},{20,4},{24,8},{28,12},{32,48},... | collective-permute-start | bytes 196616 | tf_op jit(solution)/shard_map/ppermute | solution.py:372
  75.6 6.6 %collective-permute-start.14 = (f32[2,64,128]{2,1,0:T(8,128)}, f32[2,64,128]{2,1,0:T(8,128)S(1)}, u32[]{:S(2)}, u32[]{:S(2)}) collective-permute-start(f32[2,64,128]{2,1,0:T(8,128)} %get-tuple-element.45), channel_id=1, source_target_pairs={{0,24},{4,28},{8,16},{12,20},{16,8},{20,12},{24,0},{28,4},{32,56},... | collective-permute-start | bytes 196616 | tf_op jit(solution)/shard_map/ppermute | solution.py:372
  84.5 11.9 %collective-permute-start.15 = (f32[2,16,128]{2,1,0:T(8,128)}, f32[2,16,128]{2,1,0:T(8,128)S(1)}, u32[]{:S(2)}, u32[]{:S(2)}) collective-permute-start(f32[2,16,128]{2,1,0:T(8,128)} %get-tuple-element.47), channel_id=1, source_target_pairs={{0,32},{4,36},{8,40},{12,44},{16,48},{20,52},{24,56},{28,60},{32,0... | collective-permute-start | bytes 49160 | tf_op jit(solution)/shard_map/ppermute | solution.py:372
  86.1 10.5 %collective-permute-start.16 = (f32[2,16,128]{2,1,0:T(8,128)}, f32[2,16,128]{2,1,0:T(8,128)S(1)}, u32[]{:S(2)}, u32[]{:S(2)}) collective-permute-start(f32[2,16,128]{2,1,0:T(8,128)} %get-tuple-element.48), channel_id=1, source_target_pairs={{0,64},{4,68},{8,72},{12,76},{16,80},{20,84},{24,88},{28,92},{32,9... | collective-permute-start | bytes 49160 | tf_op jit(solution)/shard_map/ppermute | solution.py:372
  88.9 8.4 %collective-permute-start.17 = (f32[2,16,128]{2,1,0:T(8,128)}, f32[2,16,128]{2,1,0:T(8,128)S(1)}, u32[]{:S(2)}, u32[]{:S(2)}) collective-permute-start(f32[2,16,128]{2,1,0:T(8,128)} %get-tuple-element.49), channel_id=1, source_target_pairs={{0,96},{4,100},{8,104},{12,108},{16,112},{20,116},{24,120},{28,124... | collective-permute-start | bytes 49160 | tf_op jit(solution)/shard_map/ppermute | solution.py:372
  91.9 18.7 %collective-permute-start.4 = (f32[2,16,384]{2,1,0:T(8,128)}, f32[2,16,384]{2,1,0:T(8,128)S(1)}, u32[]{:S(2)}, u32[]{:S(2)}) collective-permute-start(f32[2,16,384]{2,1,0:T(8,128)} %get-tuple-element.33), channel_id=1, source_target_pairs={{0,32},{4,36},{8,40},{12,44},{16,48},{20,52},{24,56},{28,60},{32,0... | collective-permute-start | bytes 147464 | tf_op jit(solution)/shard_map/ppermute | solution.py:372
  92.3 18.4 %collective-permute-start.5 = (f32[2,16,384]{2,1,0:T(8,128)}, f32[2,16,384]{2,1,0:T(8,128)S(1)}, u32[]{:S(2)}, u32[]{:S(2)}) collective-permute-start(f32[2,16,384]{2,1,0:T(8,128)} %get-tuple-element.34), channel_id=1, source_target_pairs={{0,64},{4,68},{8,72},{12,76},{16,80},{20,84},{24,88},{28,92},{32,9... | collective-permute-start | bytes 147464 | tf_op jit(solution)/shard_map/ppermute | solution.py:372
  96.3 14.3 %copy-start.18 = (f32[2,16,128]{2,1,0:T(8,128)}, f32[2,16,128]{2,1,0:T(8,128)S(1)}, u32[]{:S(2)}) copy-start(f32[2,16,128]{2,1,0:T(8,128)S(1)} %collective-permute-done.15.refs_5_) | copy-start | bytes 49156
  96.3 14.3 %collective-permute-start.6 = (f32[2,16,384]{2,1,0:T(8,128)}, f32[2,16,384]{2,1,0:T(8,128)S(1)}, u32[]{:S(2)}, u32[]{:S(2)}) collective-permute-start(f32[2,16,384]{2,1,0:T(8,128)} %get-tuple-element.35), channel_id=1, source_target_pairs={{0,96},{4,100},{8,104},{12,108},{16,112},{20,116},{24,120},{28,124... | collective-permute-start | bytes 147464 | tf_op jit(solution)/shard_map/ppermute | solution.py:372
  96.6 14.1 %copy-start.19 = (f32[2,16,128]{2,1,0:T(8,128)}, f32[2,16,128]{2,1,0:T(8,128)S(1)}, u32[]{:S(2)}) copy-start(f32[2,16,128]{2,1,0:T(8,128)S(1)} %collective-permute-done.16.refs_6_) | copy-start | bytes 49156
  96.6 5.2 %collective-permute-start.18 = (f32[2,16,128]{2,1,0:T(8,128)}, f32[2,16,128]{2,1,0:T(8,128)S(1)}, u32[]{:S(2)}, u32[]{:S(2)}) collective-permute-start(f32[2,16,128]{2,1,0:T(8,128)} %get-tuple-element.46.refs_4_), channel_id=1, source_target_pairs={{0,1},{1,2},{2,3},{3,0},{4,5},{5,6},{6,7},{7,4},{8,9},{9,10},{10,1... | collective-permute-start | bytes 49160 | tf_op jit(solution)/shard_map/ppermute | solution.py:380
  97.3 13.4 %copy-start.20 = (f32[2,16,128]{2,1,0:T(8,128)}, f32[2,16,128]{2,1,0:T(8,128)S(1)}, u32[]{:S(2)}) copy-start(f32[2,16,128]{2,1,0:T(8,128)S(1)} %collective-permute-done.17.refs_7_) | copy-start | bytes 49156
  97.3 6.1 %collective-permute-start.19 = (f32[2,16,128]{2,1,0:T(8,128)}, f32[2,16,128]{2,1,0:T(8,128)S(1)}, u32[]{:S(2)}, u32[]{:S(2)}) collective-permute-start(f32[2,16,128]{2,1,0:T(8,128)} %get-tuple-element.47), channel_id=1, source_target_pairs={{0,33},{1,34},{2,35},{3,32},{4,37},{5,38},{6,39},{7,36},{8,41},{9,... | collective-permute-start | bytes 49160 | tf_op jit(solution)/shard_map/ppermute | solution.py:380
  101.8 8.9 %copy-start.21 = (f32[2,16,128]{2,1,0:T(8,128)}, f32[2,16,128]{2,1,0:T(8,128)S(1)}, u32[]{:S(2)}) copy-start(f32[2,16,128]{2,1,0:T(8,128)S(1)} %collective-permute-done.18.refs_8_) | copy-start | bytes 49156
  101.8 7.6 %collective-permute-start.20 = (f32[2,16,128]{2,1,0:T(8,128)}, f32[2,16,128]{2,1,0:T(8,128)S(1)}, u32[]{:S(2)}, u32[]{:S(2)}) collective-permute-start(f32[2,16,128]{2,1,0:T(8,128)} %get-tuple-element.48), channel_id=1, source_target_pairs={{0,65},{1,66},{2,67},{3,64},{4,69},{5,70},{6,71},{7,68},{8,73},{9,... | collective-permute-start | bytes 49160 | tf_op jit(solution)/shard_map/ppermute | solution.py:380
  103.4 7.4 %copy-start.22 = (f32[2,16,128]{2,1,0:T(8,128)}, f32[2,16,128]{2,1,0:T(8,128)S(1)}, u32[]{:S(2)}) copy-start(f32[2,16,128]{2,1,0:T(8,128)S(1)} %collective-permute-done.19.refs_9_) | copy-start | bytes 49156
  103.4 7.3 %collective-permute-start.21 = (f32[2,16,128]{2,1,0:T(8,128)}, f32[2,16,128]{2,1,0:T(8,128)S(1)}, u32[]{:S(2)}, u32[]{:S(2)}) collective-permute-start(f32[2,16,128]{2,1,0:T(8,128)} %get-tuple-element.49), channel_id=1, source_target_pairs={{0,97},{1,98},{2,99},{3,96},{4,101},{5,102},{6,103},{7,100},{8,105... | collective-permute-start | bytes 49160 | tf_op jit(solution)/shard_map/ppermute | solution.py:380
  (15 other events, 21.8 us)

commit v2 on v0

v2 whole, which is shorter than its diff:
```python
import functools
import math

import jax
import jax.numpy as jnp
from jax import lax
from jax.experimental import pallas as pl
from jax.experimental.pallas import tpu as pltpu
from jax.sharding import PartitionSpec as P

SHIFT = 128
BLK = 128
HALF = SHIFT // 2
LANES = 128
PIECE = 16
WIRE = jnp.float16
WIRE_SCALE = 4096.0
UNROLL = 4
LOG2E = math.log2(math.e)
SMEM = pltpu.SMEM
F32 = jnp.float32
BF16 = jnp.bfloat16


def rounded(scalar, shape):
    return jnp.full(shape, scalar, F32).astype(BF16).astype(F32)


def tap(distance, offset, fraction):
    second = jnp.where(distance == offset + 1, fraction, 0.0)
    return jnp.where(distance == offset, 1.0 - fraction, second)


def strips_kernel(chunk, occ, x_first, x_last, to_left, to_right):
    half = x_first.shape[2] // 2
    k = lax.broadcasted_iota(jnp.int32, (2 * LANES, LANES), 0)
    n = lax.broadcasted_iota(jnp.int32, (2 * LANES, LANES), 1)
    blocks = x_first.shape[2] // BLK
    first, last = 0, occ.shape[2] - 1
    for ref, out, column, source, near in (
        (x_first, to_left, first, jnp.where(n < HALF, n, n + HALF), n < HALF),
        (x_last, to_right, last, jnp.where(n < HALF, n + LANES + HALF, n), n >= HALF),
    ):
        low = occ[0, blocks * chunk, column].astype(F32)
        high = occ[0, blocks * chunk + 1, column].astype(F32)
        pick = jnp.where(k == source, jnp.where(near, low, high), 0.0).astype(BF16)
        for s in range(ref.shape[1]):
            rows = jnp.concatenate([ref[0, s, :half], ref[0, s, half:]], axis=1)
            out[s] = jnp.dot(rows, pick, preferred_element_type=F32).astype(BF16)


def edge_strips(density, occupancy, chunk):
    _, slices, _, cols = density.shape
    step = 2 * BLK
    shape = jax.ShapeDtypeStruct((slices, step // 2, LANES), BF16)
    last = cols // LANES - 1
    return pl.pallas_call(
        functools.partial(strips_kernel, chunk),
        grid=(1,),
        in_specs=[
            pl.BlockSpec(memory_space=SMEM),
            pl.BlockSpec((1, slices, step, LANES), lambda i: (0, 0, chunk, 0)),
            pl.BlockSpec((1, slices, step, LANES), lambda i: (0, 0, chunk, last)),
        ],
        out_specs=[pl.BlockSpec((slices, step // 2, LANES), lambda i: (0, 0, 0))] * 2,
        out_shape=[shape, shape],
        name=f"edge_strips{chunk}",
    )(occupancy, density, density)


def shade(s, x, base, state, refs):
    frac_vertical, extinction, slice_total = refs
    through_ref, sum_ref = state
    rows = x.shape[0] - 8
    v0 = 2.0 * rounded(1.0 - frac_vertical[0, s], (1, LANES))
    v1 = 2.0 * rounded(frac_vertical[0, s], (1, LANES))
    density = v0 * x + v1 * pltpu.roll(x, 1, 0)
    above = pltpu.roll(density, 1, 0)
    density, above = density[8:], above[8:]
    rate = extinction[0, s] * (-LOG2E / (2.0 * slice_total))
    kept = jnp.exp2(rate * density)
    slope = jnp.tanh(density - above)
    at = slice(base, base + rows)
    through = through_ref[at]
    after = through * kept
    through_ref[at] = after
    sum_ref[at] += (through - after) * slope


def finish(state, gain, swap, out_keep, out_send, tile):
    through_ref, sum_ref = state
    rows = out_keep.shape[1] * 2
    base = tile * rows
    alphas, colors = [], []
    for p in range(rows // PIECE):
        at = slice(base + p * PIECE, base + (p + 1) * PIECE)
        alpha = 1.0 - through_ref[at]
        alphas.append(alpha)
        colors.append(gain * (0.65 * alpha + 0.35 * sum_ref[at]))
    lanes = slice(tile * LANES, (tile + 1) * LANES)
    for q in range(rows // PIECE // 2):
        at = slice(q * PIECE, (q + 1) * PIECE)
        for i, values in enumerate((colors, alphas)):
            even, odd = values[2 * q], values[2 * q + 1]
            out_keep[i, at, lanes] = jnp.where(swap, odd, even)
            out_send[i, at, lanes] = jnp.where(swap, even, odd)


def splat(value):
    return jnp.full((1, LANES), value, F32).astype(BF16)


def over_slices(slices, one):
    lax.fori_loop(0, slices, one, 0, unroll=UNROLL)


def interior_kernel(
    slice_total, occ, offset, frac_lateral, frac_vertical, extinction, gain,
    x_ref, lead_ref, out_keep, out_send, weights, through_ref, sum_ref,
):
    block = pl.program_id(0)
    slices, rows = x_ref.shape[1], x_ref.shape[2]
    tiles = x_ref.shape[3] // LANES

    @pl.when(block == 0)
    def _():
        k = lax.broadcasted_iota(jnp.int32, (2 * LANES, LANES), 0)
        n = lax.broadcasted_iota(jnp.int32, (2 * LANES, LANES), 1)

        def build(s, _):
            weights[s] = tap(LANES + n - k, offset[0, s], frac_lateral[0, s]).astype(BF16)
            return 0

        lax.fori_loop(0, slices, build, 0)

    through_ref[...] = jnp.ones_like(through_ref)
    sum_ref[...] = jnp.zeros_like(sum_ref)
    inside = jnp.where(block > 0, 1, 0)
    above = jnp.maximum(block - 1, 0)
    mask = [splat(occ[0, block, t]) for t in range(tiles)]
    lead_mask = [splat(occ[0, above, t] * inside) for t in range(tiles)]
    state = (through_ref, sum_ref)
    refs = (frac_vertical, extinction, slice_total)

    def one(s, _):
        parts = []
        for t in range(tiles):
            lanes = slice(t * LANES, (t + 1) * LANES)
            lead = lead_ref[0, s, :, lanes] * lead_mask[t]
            parts.append(jnp.concatenate([lead, x_ref[0, s, :, lanes] * mask[t]], axis=0))
        for t in range(1, tiles):
            pair = jnp.concatenate([parts[t - 1], parts[t]], axis=1)
            x = jnp.dot(pair, weights[s], preferred_element_type=F32)
            shade(s, x[8:], (t - 1) * rows, state, refs)
        return 0

    over_slices(slices, one)
    swap = lax.axis_index("depth") % 2 == 1
    for t in range(tiles - 1):
        finish(state, gain[0], swap, out_keep, out_send, t)


def small_specs():
    return [pl.BlockSpec(memory_space=SMEM)] * 6


def interior(density, small, slice_total):
    _, slices, rows, cols = density.shape
    step = BLK
    width = cols - LANES
    image = jax.ShapeDtypeStruct((2, rows // 2, width), F32)
    return pl.pallas_call(
        functools.partial(interior_kernel, slice_total),
        grid=(rows // step,),
        in_specs=small_specs()
        + [
            pl.BlockSpec((1, slices, step, cols), lambda b: (0, 0, b, 0)),
            pl.BlockSpec(
                (1, slices, 16, cols), lambda b: (0, 0, jnp.maximum(b * (step // 16) - 1, 0), 0)
            ),
        ],
        out_specs=[pl.BlockSpec((2, step // 2, width), lambda b: (0, b, 0))] * 2
        + [pl.BlockSpec((slices, 2 * LANES, LANES), lambda b: (0, 0, 0))],
        out_shape=[image, image, jax.ShapeDtypeStruct((slices, 2 * LANES, LANES), BF16)],
        scratch_shapes=[pltpu.VMEM((step * (width // LANES), LANES), F32)] * 2,
        compiler_params=pltpu.CompilerParams(vmem_limit_bytes=32 * 2**20),
        name="interior",
    )(*small, density, density)


def border_kernel(
    chunk, slice_total, occ, offset, frac_lateral, frac_vertical, extinction, gain, weights,
    first_ref, last_ref, first_lead, last_lead, right_ref, left_ref, right_lead, left_lead,
    out_keep, out_send, through_ref, sum_ref,
):
    slices, rows = first_ref.shape[1], BLK
    last_tile = occ.shape[2] - 1
    follows = jnp.where(lax.axis_index("lat") < lax.axis_size("lat") - 1, 1, 0)
    own_lanes = lax.broadcasted_iota(jnp.int32, (1, LANES), 1) >= HALF
    refs = (frac_vertical, extinction, slice_total)
    state = (through_ref, sum_ref)
    through_ref[...] = jnp.ones_like(through_ref)
    sum_ref[...] = jnp.zeros_like(sum_ref)
    blocks = first_ref.shape[2] // BLK
    start = blocks * chunk
    masks = []
    for b in range(start - 1, start + blocks):
        inside = b >= 0
        masks.append(
            (
                splat(occ[0, b, 0] if inside else 0.0),
                splat(occ[0, b, last_tile] * follows if inside else 0.0),
            )
        )

    def one(s, _):
        before, own = weights[s, :LANES], weights[s, LANES:]
        turn = lambda w: jnp.concatenate([w[HALF:], w[:HALF]], axis=0)
        near = jnp.concatenate([before, own], axis=0)
        far = (
            jnp.concatenate([turn(before), own], axis=0),
            jnp.concatenate([before, turn(own)], axis=0),
        )

        def lateral(first, last, right, left, second_half):
            w_left, w_right = far if second_half else (near, near)
            here = jnp.dot(
                jnp.concatenate([left, first], axis=1), w_left, preferred_element_type=F32
            )
            there = jnp.dot(
                jnp.concatenate([last, right], axis=1), w_right, preferred_element_type=F32
            )
            return jnp.where(own_lanes, here, there)

        right, left = right_ref[s], left_ref[s]
        zero = jnp.zeros((16, LANES), BF16)
        lead = lateral(
            first_lead[0, s] * masks[0][0],
            last_lead[0, s] * masks[0][1],
            right_lead[s] if chunk else zero,
            left_lead[s] if chunk else zero,
            True,
        )[8:]
        for b in range(blocks):
            at = slice(b * rows, (b + 1) * rows)
            x = lateral(
                first_ref[0, s, at] * masks[b + 1][0],
                last_ref[0, s, at] * masks[b + 1][1],
                right,
                left,
                b == 1,
            )
            shade(s, jnp.concatenate([lead, x], axis=0), b * rows, state, refs)
            lead = x[rows - 8 :]
        return 0

    over_slices(slices, one)
    swap = lax.axis_index("depth") % 2 == 1
    finish(state, gain[0], swap, out_keep, out_send, 0)


def border(density, small, weights, halos, previous, chunk, slice_total):
    _, slices, _, cols = density.shape
    step = 2 * BLK
    last = cols // LANES - 1
    per = step // 16

    def body(column):
        return pl.BlockSpec((1, slices, step, LANES), lambda i: (0, 0, chunk, column))

    def lead(column):
        return pl.BlockSpec(
            (1, slices, 16, LANES), lambda i: (0, 0, max(chunk * per - 1, 0), column)
        )

    halo = pl.BlockSpec((slices, BLK, LANES), lambda i: (0, 0, 0))
    halo_lead = pl.BlockSpec((slices, 16, LANES), lambda i: (0, BLK // 16 - 1, 0))
    image = jax.ShapeDtypeStruct((2, step // 2, LANES), F32)
    return pl.pallas_call(
        functools.partial(border_kernel, chunk, slice_total),
        grid=(1,),
        in_specs=small_specs()
        + [pl.BlockSpec((slices, 2 * LANES, LANES), lambda i: (0, 0, 0))]
        + [body(0), body(last), lead(0), lead(last), halo, halo, halo_lead, halo_lead],
        out_specs=[pl.BlockSpec((2, step // 2, LANES), lambda i: (0, 0, 0))] * 2,
        out_shape=[image, image],
        scratch_shapes=[pltpu.VMEM((step, LANES), F32)] * 2,
        compiler_params=pltpu.CompilerParams(vmem_limit_bytes=32 * 2**20),
        name=f"border{chunk}",
    )(*small, weights, density, density, density, density, *halos, *previous)


def over(mine, other, in_front):
    color = jnp.where(in_front, mine[0], other[0]) + (
        1.0 - jnp.where(in_front, mine[1], other[1])
    ) * jnp.where(in_front, other[0], mine[0])
    return jnp.stack([color, mine[1] + (1.0 - mine[1]) * other[1]])


def depth_swap(value, bits):
    count = lax.axis_size("depth")
    return lax.ppermute(value, "depth", [(i, i ^ bits) for i in range(count)])


def wire(value):
    return (value * WIRE_SCALE).astype(WIRE)


def unwire(value):
    return value.astype(F32) * (1.0 / WIRE_SCALE)


def over_cores(keep, send, rank):
    me = lax.axis_index("depth")
    return over(keep, depth_swap(send, 1), rank[me] < rank[me ^ 1])


def over_level(image, level, axis, rank):
    me = lax.axis_index("depth")
    bit = me >> level & 1
    keep = lax.dynamic_index_in_dim(image, bit, axis, keepdims=False)
    send = lax.dynamic_index_in_dim(image, 1 - bit, axis, keepdims=False)
    other = unwire(depth_swap(wire(send), 1 << level))
    return over(keep, other, rank[me] < rank[me ^ (1 << level)])


def over_z(keep, send, rank):
    image = over_cores(keep, send, rank)
    width = image.shape[2]
    image = image.reshape(2, 4, 2, 2, PIECE, width)
    image = over_level(image, 1, 3, rank)
    return over_level(image, 2, 2, rank)


def over_y(image, rank):
    width = image.shape[3]
    image = image.reshape(2, 2, 2, PIECE, width)
    image = over_level(image, 3, 2, rank)
    return over_level(image, 4, 1, rank)


def shards(
    density, occupancy, shear_offsets, frac_lateral, frac_vertical, extinction, slab_gain, view_rank
):
    _, slices, rows, cols = density.shape
    slice_total = lax.axis_size("depth") * slices
    lat = lax.axis_size("lat")
    density = pltpu.with_memory_space_constraint(density, pltpu.HBM)
    small = (occupancy, shear_offsets, frac_lateral, frac_vertical, extinction, slab_gain)
    chunks = rows // (2 * BLK)
    rightwards = [(x, x + 1) for x in range(lat - 1)]
    leftwards = [(x, (x - 1) % lat) for x in range(lat)]
    halos = []
    for c in range(chunks):
        to_left, to_right = edge_strips(density, occupancy, c)
        from_right = lax.ppermute(to_left, "lat", leftwards)
        from_left = lax.ppermute(to_right, "lat", rightwards)
        halos.append((from_right, from_left))
    keep, send, weights = interior(density, small, slice_total)
    inner = over_z(keep, send, view_rank)
    pieces = [
        border(density, small, weights, halos[c], halos[max(c - 1, 0)], c, slice_total)
        for c in range(chunks)
    ]
    keep, send = (jnp.concatenate(p, axis=1) for p in zip(*pieces))
    edge = over_z(keep, send, view_rank)
    image = over_y(jnp.concatenate([edge, inner], axis=3), view_rank)
    moved = lax.ppermute(image[:, :, :LANES], "lat", [(x, (x + 1) % lat) for x in range(lat)])
    lane = jnp.arange(LANES, dtype=jnp.int32)
    first = jnp.where(lane < HALF, moved, image[:, :, :LANES])
    image = jnp.concatenate([first, image[:, :, LANES:]], axis=2)
    return image[0], image[1]


def solution(mesh):
    placed = (
        P("depth", None, None, "lat"),
        P("depth", None, "lat"),
        P("depth", None),
        P("depth", None),
        P("depth", None),
        P("depth", None),
        P("depth"),
        P(),
    )
    return jax.shard_map(
        shards,
        mesh=mesh,
        in_specs=placed,
        out_specs=(P("depth", "lat"), P("depth", "lat")),
        check_vma=False,
    )
```

time: 190 us -> 79.6 us (0.42)
  waiting for transfers between devices: 69.5 us -> 18.2 us
  other arithmetic: 52 us -> 0.77 us
  Pallas kernels: 0 us -> 27.9 us
  matrix products: 24.5 us -> 0 us
  local copies, waits for them, and re-layouts: 22 us -> 1.37 us
  starting transfers between devices: 16.2 us -> 23.1 us
  between operations: 4.73 us -> 7.94 us
    ppermute x11 -> x13, waiting for transfers between devices: 69.5 us -> 18.2 us  [the longest x8 14.6 us: depth_swap(): return lax.ppermute(value, 'depth', [(i, i ^ bits) for i in range(count)])]
    pallas_call x0 -> x5, Pallas kernels: none -> 27.9 us  [the longest x1 13.3 us: interior(): pl.pallas_call(functools.partial(interior_kernel, slice_total), grid=(row...]
    dot_general x2 -> x0, matrix products: 24.5 us -> none  [the longest x1 13.3 us: shards(): jnp.einsum('srw,swq->srq', masked, lateral_matrix, preferred_element_type...]
    reduce_sum x1 -> x0, other arithmetic: 23.7 us -> none  [shade_slices(): return (jnp.sum(emission * before, axis=0), 1.0 - through[-1])]
    slice x2, local copies, waits for them, and re-layouts: 15.4 us -> 0.04 us  [over(): mine[1]]
    add x5 -> x8, other arithmetic: 13.2 us -> 0.36 us  [the longest x5 0.3 us: over(): return jnp.stack([color, mine[1] + (1.0 - mine[1]) * other[1]])]
    another operation x1 -> x2, other arithmetic: 10.8 us -> 0.09 us  [over(): return jnp.stack([color, mine[1] + (1.0 - mine[1]) * other[1]])]
    ppermute x11 -> x13, starting transfers between devices: 16.2 us -> 23.1 us  [the longest x8 13.4 us: depth_swap(): return lax.ppermute(value, 'depth', [(i, i ^ bits) for i in range(count)])]
  transfers between devices with their start and end apart: 11 -> 13, of which waited for: 10 -> 7; matrix products, arithmetic and copies ran while one was open for 19% -> 1% of each run, Pallas kernels for 0% -> 26%
where the time goes in v2:
time: 79.6 us; the launch traced here: 79.2 us
  Pallas kernels  27.9 us (35%)
  starting transfers between devices  23.1 us (29%)
  waiting for transfers between devices  18.2 us (23%)
  between operations  7.94 us (10%)
  local copies, waits for them, and re-layouts  1.37 us (2%)
    ppermute x8, waiting for transfers between devices, depth_swap(): return lax.ppermute(value, 'depth', [(i, i ^ bits) for i in range(count)])  14.6 us
    ppermute x8, starting transfers between devices, depth_swap(): return lax.ppermute(value, 'depth', [(i, i ^ bits) for i in range(count)])  13.4 us
    pallas_call x1, Pallas kernels, interior(): pl.pallas_call(functools.partial(interior_kernel, slice_total), grid=(row...  13.3 us
    pallas_call x2, Pallas kernels, border(): pl.pallas_call(functools.partial(border_kernel, chunk, slice_total), grid...  8.25 us
    pallas_call x2, Pallas kernels, edge_strips(): pl.pallas_call(functools.partial(strips_kernel, chunk), grid=(1,), in_spe...  6.26 us
    ppermute x2, starting transfers between devices, shards(): from_left = lax.ppermute(to_right, 'lat', rightwards)  4.61 us
    ppermute x2, starting transfers between devices, shards(): from_right = lax.ppermute(to_left, 'lat', leftwards)  3.64 us
    ppermute x1, waiting for transfers between devices, shards(): lax.ppermute(image[:, :, :LANES], 'lat', [(x, (x + 1) % lat) for x in ran...  3.58 us
  transfers between devices with their start and end apart: 13, of which 7 were waited for; matrix products, arithmetic and copies ran while one was open for 1% of the time, Pallas kernels for 26%

profile of v2, /device:TPU:0, one launch (start us, length us, event | category | flops | bytes accessed | tf_op | source)
XLA Modules:
  0.0 79.2 jit_solution(15319253888671844583)
XLA Ops:
  0.6 3.1 %edge_strips0.1 = (bf16[16,128,128]{2,1,0:T(8,128)(2,1)}, bf16[16,128,128]{2,1,0:T(8,128)(2,1)}) custom-call(s32[1,4,4]{2,1,0:T(4,128)} %occ.9, bf16[1,16,512,512]{3,2,1,0:T(8,128)(2,1)} %last_lead.3, bf16[1,16,512,512]{3,2,1,0:T(8,128)(2,1)} %last_lead.3), custom_call_target="tpu_custom_call" | custom-call | tf_op jit(solution)/shard_map/edge_strips0/pallas_call | solution.py:57
  3.8 2.8 %collective-permute-start = (bf16[16,128,128]{2,1,0:T(8,128)(2,1)}, bf16[16,128,128]{2,1,0:T(8,128)(2,1)S(1)}, u32[]{:S(2)}, u32[]{:S(2)}) collective-permute-start(bf16[16,128,128]{2,1,0:T(8,128)(2,1)} %get-tuple-element.14), channel_id=1, source_target_pairs={{0,3},{1,0},{2,1},{3,2},{4,7},{5,4},{6,5},{7,6},{8,11},{9,8},{10,9... | collective-permute-start | bytes 1572872 | tf_op jit(solution)/shard_map/ppermute | solution.py:356
  6.6 0.0 copy-start.4
  6.6 1.5 %collective-permute-start.1 = (bf16[16,128,128]{2,1,0:T(8,128)(2,1)}, bf16[16,128,128]{2,1,0:T(8,128)(2,1)S(1)}, u32[]{:S(2)}, u32[]{:S(2)}) collective-permute-start(bf16[16,128,128]{2,1,0:T(8,128)(2,1)} %get-tuple-element.15), channel_id=1, source_target_pairs={{0,1},{1,2},{2,3},{4,5},{5,6},{6,7},{8,9},{9,10},{10,11},{12,13},{... | collective-permute-start | bytes 1572872 | tf_op jit(solution)/shard_map/ppermute | solution.py:357
  8.1 3.1 %edge_strips1.1 = (bf16[16,128,128]{2,1,0:T(8,128)(2,1)}, bf16[16,128,128]{2,1,0:T(8,128)(2,1)}) custom-call(s32[1,4,4]{2,1,0:T(4,128)} %occ.9, bf16[1,16,512,512]{3,2,1,0:T(8,128)(2,1)} %last_lead.3, bf16[1,16,512,512]{3,2,1,0:T(8,128)(2,1)} %last_lead.3), custom_call_target="tpu_custom_call" | custom-call | tf_op jit(solution)/shard_map/edge_strips1/pallas_call | solution.py:57
  11.2 0.8 %collective-permute-start.2 = (bf16[16,128,128]{2,1,0:T(8,128)(2,1)}, bf16[16,128,128]{2,1,0:T(8,128)(2,1)S(1)}, u32[]{:S(2)}, u32[]{:S(2)}) collective-permute-start(bf16[16,128,128]{2,1,0:T(8,128)(2,1)} %get-tuple-element.17), channel_id=1, source_target_pairs={{0,3},{1,0},{2,1},{3,2},{4,7},{5,4},{6,5},{7,6},{8,11},{9,8},{10,9... | collective-permute-start | bytes 1572872 | tf_op jit(solution)/shard_map/ppermute | solution.py:356
  12.0 3.2 %collective-permute-start.3 = (bf16[16,128,128]{2,1,0:T(8,128)(2,1)}, bf16[16,128,128]{2,1,0:T(8,128)(2,1)S(1)}, u32[]{:S(2)}, u32[]{:S(2)}) collective-permute-start(bf16[16,128,128]{2,1,0:T(8,128)(2,1)} %get-tuple-element.18), channel_id=1, source_target_pairs={{0,1},{1,2},{2,3},{4,5},{5,6},{6,7},{8,9},{9,10},{10,11},{12,13},{... | collective-permute-start | bytes 1572872 | tf_op jit(solution)/shard_map/ppermute | solution.py:357
  15.9 13.3 %interior.1 = (f32[2,256,384]{2,1,0:T(8,128)S(1)}, f32[2,256,384]{2,1,0:T(8,128)S(1)}, bf16[16,256,128]{2,1,0:T(8,128)(2,1)S(1)}) custom-call(s32[1,4,4]{2,1,0:T(4,128)S(1)} %copy-done, s32[1,16]{1,0:T(1,128)S(1)} %copy-done.1, f32[1,16]{1,0:T(1,128)S(1)} %copy-done.2, f32[1,16]{1,0:T(1,128)S(1)} %copy-done.3, f32[1,16]{1,0:T(1,128)S(1)} %copy-done.4, ...), custom_call_target="tpu_custom_call" | custom-call | tf_op jit(solution)/shard_map/interior/pallas_call | solution.py:172
  29.2 4.1 %border0.1 = (f32[2,128,128]{2,1,0:T(8,128)S(1)}, f32[2,128,128]{2,1,0:T(8,128)S(1)}) custom-call(s32[1,4,4]{2,1,0:T(4,128)S(1)} %copy-done, s32[1,16]{1,0:T(1,128)S(1)} %copy-done.1, f32[1,16]{1,0:T(1,128)S(1)} %copy-done.2, f32[1,16]{1,0:T(1,128)S(1)} %copy-done.3, f32[1,16]{1,0:T(1,128)S(1)} %copy-done.4, f32[1]{0:T(128)S(6)} %copy.59.gain, ...), custom_call_target="tpu_custom_call" | custom-call | tf_op jit(solution)/shard_map/border0/pallas_call | solution.py:279
  33.4 4.1 %border1.1 = (f32[2,128,128]{2,1,0:T(8,128)S(1)}, f32[2,128,128]{2,1,0:T(8,128)S(1)}) custom-call(s32[1,4,4]{2,1,0:T(4,128)S(1)} %copy-done, s32[1,16]{1,0:T(1,128)S(1)} %copy-done.1, f32[1,16]{1,0:T(1,128)S(1)} %copy-done.2, f32[1,16]{1,0:T(1,128)S(1)} %copy-done.3, f32[1,16]{1,0:T(1,128)S(1)} %copy-done.4, f32[1]{0:T(128)S(6)} %copy.59.gain, ...), custom_call_target="tpu_custom_call" | custom-call | tf_op jit(solution)/shard_map/border1/pallas_call | solution.py:279
  37.6 0.1 collective-permute-start.4
  37.7 0.5 collective-permute-start.7
  38.2 0.7 fusion.27
  42.6 0.1 multiply_add_fusion.4
  42.7 2.0 %collective-permute-start.5 = (f16[2,4,2,16,128]{4,3,1,2,0:T(8,128)(2,1)S(1)}, f16[2,4,2,16,128]{4,3,1,2,0:T(8,128)(2,1)S(1)}, u32[]{:S(2)}, u32[]{:S(2)}) collective-permute-start(f16[2,4,2,16,128]{4,3,1,2,0:T(8,128)(2,1)S(1)} %fusion.13), channel_id=1, source_target_pairs={{0,8},{4,12},{8,0},{12,4},{16,24},{20,28},{24,16},{28,20},{32,40},... | collective-permute-start | bytes 196616 | tf_op jit(solution)/shard_map/ppermute | solution.py:302
  44.8 0.1 multiply_add_fusion
  44.9 0.1 fusion
  45.0 2.1 %collective-permute-done.5 = f16[2,4,2,16,128]{4,3,1,2,0:T(8,128)(2,1)S(1)} collective-permute-done((f16[2,4,2,16,128]{4,3,1,2,0:T(8,128)(2,1)S(1)}, f16[2,4,2,16,128]{4,3,1,2,0:T(8,128)(2,1)S(1)}, u32[]{:S(2)}, u32[]{:S(2)}) %collective-permute-start.5) | collective-permute-done | bytes 65568 | tf_op jit(solution)/shard_map/ppermute | solution.py:302
  47.2 3.9 %collective-permute-start.6 = (f16[2,4,16,128]{3,2,1,0:T(8,128)(2,1)S(1)}, f16[2,4,16,128]{3,2,1,0:T(8,128)(2,1)S(1)}, u32[]{:S(2)}, u32[]{:S(2)}) collective-permute-start(f16[2,4,16,128]{3,2,1,0:T(8,128)(2,1)S(1)} %get-tuple-element.50), channel_id=1, source_target_pairs={{0,16},{4,20},{8,24},{12,28},{16,0},{20,4},{24,8},{28,12},{32,48},... | collective-permute-start | bytes 98312 | tf_op jit(solution)/shard_map/ppermute | solution.py:302
  51.2 1.1 %collective-permute-start.8 = (f16[2,4,2,16,384]{4,3,1,2,0:T(8,128)(2,1)S(1)}, f16[2,4,2,16,384]{4,3,1,2,0:T(8,128)(2,1)S(1)}, u32[]{:S(2)}, u32[]{:S(2)}) collective-permute-start(f16[2,4,2,16,384]{4,3,1,2,0:T(8,128)(2,1)S(1)} %fusion.3), channel_id=1, source_target_pairs={{0,8},{4,12},{8,0},{12,4},{16,24},{20,28},{24,16},{28,20},{32,40},... | collective-permute-start | bytes 589832 | tf_op jit(solution)/shard_map/ppermute | solution.py:302
  52.3 1.1 %collective-permute-done.6 = f16[2,4,16,128]{3,2,1,0:T(8,128)(2,1)S(1)} collective-permute-done((f16[2,4,16,128]{3,2,1,0:T(8,128)(2,1)S(1)}, f16[2,4,16,128]{3,2,1,0:T(8,128)(2,1)S(1)}, u32[]{:S(2)}, u32[]{:S(2)}) %collective-permute-start.6) | collective-permute-done | bytes 32800 | tf_op jit(solution)/shard_map/ppermute | solution.py:302
  53.4 3.7 %collective-permute-done.8 = f16[2,4,2,16,384]{4,3,1,2,0:T(8,128)(2,1)S(1)} collective-permute-done((f16[2,4,2,16,384]{4,3,1,2,0:T(8,128)(2,1)S(1)}, f16[2,4,2,16,384]{4,3,1,2,0:T(8,128)(2,1)S(1)}, u32[]{:S(2)}, u32[]{:S(2)}) %collective-permute-start.8) | collective-permute-done | bytes 196640 | tf_op jit(solution)/shard_map/ppermute | solution.py:302
  57.1 0.1 multiply_add_fusion.2
  57.2 0.8 collective-permute-start.9
  58.0 5.4 %collective-permute-done.9 = f16[2,4,16,384]{3,2,1,0:T(8,128)(2,1)S(1)} collective-permute-done((f16[2,4,16,384]{3,2,1,0:T(8,128)(2,1)S(1)}, f16[2,4,16,384]{3,2,1,0:T(8,128)(2,1)S(1)}, u32[]{:S(2)}, u32[]{:S(2)}) %collective-permute-start.9) | collective-permute-done | bytes 98336 | tf_op jit(solution)/shard_map/ppermute | solution.py:302
  63.6 1.7 %collective-permute-start.10 = (f16[2,2,16,512]{3,2,1,0:T(8,128)(2,1)S(1)}, f16[2,2,16,512]{3,2,1,0:T(8,128)(2,1)S(1)}, u32[]{:S(2)}, u32[]{:S(2)}) collective-permute-start(f16[2,2,16,512]{3,2,1,0:T(8,128)(2,1)S(1)} %fusion.12), channel_id=1, source_target_pairs={{0,32},{4,36},{8,40},{12,44},{16,48},{20,52},{24,56},{28,60},{32,0... | collective-permute-start | bytes 196616 | tf_op jit(solution)/shard_map/ppermute | solution.py:302
  66.5 1.4 %collective-permute-done.10 = f16[2,2,16,512]{3,2,1,0:T(8,128)(2,1)S(1)} collective-permute-done((f16[2,2,16,512]{3,2,1,0:T(8,128)(2,1)S(1)}, f16[2,2,16,512]{3,2,1,0:T(8,128)(2,1)S(1)}, u32[]{:S(2)}, u32[]{:S(2)}) %collective-permute-start.10) | collective-permute-done | bytes 65568 | tf_op jit(solution)/shard_map/ppermute | solution.py:302
  68.0 3.4 %collective-permute-start.11 = (f16[2,16,512]{2,1,0:T(8,128)(2,1)S(1)}, f16[2,16,512]{2,1,0:T(8,128)(2,1)S(1)}, u32[]{:S(2)}, u32[]{:S(2)}) collective-permute-start(f16[2,16,512]{2,1,0:T(8,128)(2,1)S(1)} %get-tuple-element.46), channel_id=1, source_target_pairs={{0,64},{4,68},{8,72},{12,76},{16,80},{20,84},{24,88},{28,92},{32,9... | collective-permute-start | bytes 98312 | tf_op jit(solution)/shard_map/ppermute | solution.py:302
  72.7 0.8 %collective-permute-done.11 = f16[2,16,512]{2,1,0:T(8,128)(2,1)S(1)} collective-permute-done((f16[2,16,512]{2,1,0:T(8,128)(2,1)S(1)}, f16[2,16,512]{2,1,0:T(8,128)(2,1)S(1)}, u32[]{:S(2)}, u32[]{:S(2)}) %collective-permute-start.11) | collective-permute-done | bytes 32800 | tf_op jit(solution)/shard_map/ppermute | solution.py:302
  73.5 1.4 %collective-permute-start.12 = (f32[2,16,128]{2,1,0:T(8,128)S(1)}, f32[2,16,128]{2,1,0:T(8,128)S(1)}, u32[]{:S(2)}, u32[]{:S(2)}) collective-permute-start(f32[2,16,128]{2,1,0:T(8,128)S(1)} %pad_maximum_fusion.1), channel_id=1, source_target_pairs={{0,1},{1,2},{2,3},{3,0},{4,5},{5,6},{6,7},{7,4},{8,9},{9,10},{10,1... | collective-permute-start | bytes 49160 | tf_op jit(solution)/shard_map/ppermute | solution.py:368
  75.0 3.6 %collective-permute-done.12 = f32[2,16,128]{2,1,0:T(8,128)S(1)} collective-permute-done((f32[2,16,128]{2,1,0:T(8,128)S(1)}, f32[2,16,128]{2,1,0:T(8,128)S(1)}, u32[]{:S(2)}, u32[]{:S(2)}) %collective-permute-start.12) | collective-permute-done | bytes 16416 | tf_op jit(solution)/shard_map/ppermute | solution.py:368
  78.6 0.6 slice_bitcast_fusion.2
  (45 shorter events, 0.6 us)
Async XLA Ops:
  3.8 25.5 %collective-permute-start = (bf16[16,128,128]{2,1,0:T(8,128)(2,1)}, bf16[16,128,128]{2,1,0:T(8,128)(2,1)S(1)}, u32[]{:S(2)}, u32[]{:S(2)}) collective-permute-start(bf16[16,128,128]{2,1,0:T(8,128)(2,1)} %get-tuple-element.14), channel_id=1, source_target_pairs={{0,3},{1,0},{2,1},{3,2},{4,7},{5,4},{6,5},{7,6},{8,11},{9,8},{10,9... | collective-permute-start | bytes 1572872 | tf_op jit(solution)/shard_map/ppermute | solution.py:356
  6.6 9.2 %copy-start = (s32[1,4,4]{2,1,0:T(4,128)S(1)}, s32[1,4,4]{2,1,0:T(4,128)}, u32[]{:S(2)}) copy-start(s32[1,4,4]{2,1,0:T(4,128)} %occ.9) | copy-start | bytes 196
  6.6 9.2 %copy-start.1 = (s32[1,16]{1,0:T(1,128)S(1)}, s32[1,16]{1,0:T(1,128)}, u32[]{:S(2)}) copy-start(s32[1,16]{1,0:T(1,128)} %offset.5) | copy-start | bytes 196
  6.6 9.2 %copy-start.2 = (f32[1,16]{1,0:T(1,128)S(1)}, f32[1,16]{1,0:T(1,128)}, u32[]{:S(2)}) copy-start(f32[1,16]{1,0:T(1,128)} %frac_lateral.5) | copy-start | bytes 196
  6.6 9.2 %copy-start.3 = (f32[1,16]{1,0:T(1,128)S(1)}, f32[1,16]{1,0:T(1,128)}, u32[]{:S(2)}) copy-start(f32[1,16]{1,0:T(1,128)} %frac_vertical.5) | copy-start | bytes 196
  6.6 9.3 %copy-start.4 = (f32[1,16]{1,0:T(1,128)S(1)}, f32[1,16]{1,0:T(1,128)}, u32[]{:S(2)}) copy-start(f32[1,16]{1,0:T(1,128)} %extinction.5) | copy-start | bytes 196
  6.6 22.6 %collective-permute-start.1 = (bf16[16,128,128]{2,1,0:T(8,128)(2,1)}, bf16[16,128,128]{2,1,0:T(8,128)(2,1)S(1)}, u32[]{:S(2)}, u32[]{:S(2)}) collective-permute-start(bf16[16,128,128]{2,1,0:T(8,128)(2,1)} %get-tuple-element.15), channel_id=1, source_target_pairs={{0,1},{1,2},{2,3},{4,5},{5,6},{6,7},{8,9},{9,10},{10,11},{12,13},{... | collective-permute-start | bytes 1572872 | tf_op jit(solution)/shard_map/ppermute | solution.py:357
  11.2 22.2 %collective-permute-start.2 = (bf16[16,128,128]{2,1,0:T(8,128)(2,1)}, bf16[16,128,128]{2,1,0:T(8,128)(2,1)S(1)}, u32[]{:S(2)}, u32[]{:S(2)}) collective-permute-start(bf16[16,128,128]{2,1,0:T(8,128)(2,1)} %get-tuple-element.17), channel_id=1, source_target_pairs={{0,3},{1,0},{2,1},{3,2},{4,7},{5,4},{6,5},{7,6},{8,11},{9,8},{10,9... | collective-permute-start | bytes 1572872 | tf_op jit(solution)/shard_map/ppermute | solution.py:356
  12.0 21.4 %collective-permute-start.3 = (bf16[16,128,128]{2,1,0:T(8,128)(2,1)}, bf16[16,128,128]{2,1,0:T(8,128)(2,1)S(1)}, u32[]{:S(2)}, u32[]{:S(2)}) collective-permute-start(bf16[16,128,128]{2,1,0:T(8,128)(2,1)} %get-tuple-element.18), channel_id=1, source_target_pairs={{0,1},{1,2},{2,3},{4,5},{5,6},{6,7},{8,9},{9,10},{10,11},{12,13},{... | collective-permute-start | bytes 1572872 | tf_op jit(solution)/shard_map/ppermute | solution.py:357
  33.4 4.8 %copy-start.5 = (s32[32]{0:T(128)S(1)}, s32[32]{0:T(128)}, u32[]{:S(2)}) copy-start(s32[32]{0:T(128)} %param.15) | copy-start | bytes 388
  37.6 5.1 %collective-permute-start.4 = (f32[2,256,128]{2,1,0:T(8,128)S(1)}, f32[2,256,128]{2,1,0:T(8,128)S(1)}, u32[]{:S(2)}, u32[]{:S(2)}) collective-permute-start(f32[2,256,128]{2,1,0:T(8,128)S(1)} %pad_maximum_fusion), channel_id=1, source_target_pairs={{0,4},{4,0},{8,12},{12,8},{16,20},{20,16},{24,28},{28,24},{32,36},... | collective-permute-start | bytes 786440 | tf_op jit(solution)/shard_map/ppermute | solution.py:302
  37.7 7.1 %collective-permute-start.7 = (f32[2,256,384]{2,1,0:T(8,128)S(1)}, f32[2,256,384]{2,1,0:T(8,128)S(1)}, u32[]{:S(2)}, u32[]{:S(2)}) collective-permute-start(f32[2,256,384]{2,1,0:T(8,128)S(1)} %get-tuple-element.23), channel_id=1, source_target_pairs={{0,4},{4,0},{8,12},{12,8},{16,20},{20,16},{24,28},{28,24},{32,36},... | collective-permute-start | bytes 2359304 | tf_op jit(solution)/shard_map/ppermute | solution.py:302
  42.7 4.4 %collective-permute-start.5 = (f16[2,4,2,16,128]{4,3,1,2,0:T(8,128)(2,1)S(1)}, f16[2,4,2,16,128]{4,3,1,2,0:T(8,128)(2,1)S(1)}, u32[]{:S(2)}, u32[]{:S(2)}) collective-permute-start(f16[2,4,2,16,128]{4,3,1,2,0:T(8,128)(2,1)S(1)} %fusion.13), channel_id=1, source_target_pairs={{0,8},{4,12},{8,0},{12,4},{16,24},{20,28},{24,16},{28,20},{32,40},... | collective-permute-start | bytes 196616 | tf_op jit(solution)/shard_map/ppermute | solution.py:302
  47.2 6.2 %collective-permute-start.6 = (f16[2,4,16,128]{3,2,1,0:T(8,128)(2,1)S(1)}, f16[2,4,16,128]{3,2,1,0:T(8,128)(2,1)S(1)}, u32[]{:S(2)}, u32[]{:S(2)}) collective-permute-start(f16[2,4,16,128]{3,2,1,0:T(8,128)(2,1)S(1)} %get-tuple-element.50), channel_id=1, source_target_pairs={{0,16},{4,20},{8,24},{12,28},{16,0},{20,4},{24,8},{28,12},{32,48},... | collective-permute-start | bytes 98312 | tf_op jit(solution)/shard_map/ppermute | solution.py:302
  51.2 5.9 %collective-permute-start.8 = (f16[2,4,2,16,384]{4,3,1,2,0:T(8,128)(2,1)S(1)}, f16[2,4,2,16,384]{4,3,1,2,0:T(8,128)(2,1)S(1)}, u32[]{:S(2)}, u32[]{:S(2)}) collective-permute-start(f16[2,4,2,16,384]{4,3,1,2,0:T(8,128)(2,1)S(1)} %fusion.3), channel_id=1, source_target_pairs={{0,8},{4,12},{8,0},{12,4},{16,24},{20,28},{24,16},{28,20},{32,40},... | collective-permute-start | bytes 589832 | tf_op jit(solution)/shard_map/ppermute | solution.py:302
  57.2 6.2 %collective-permute-start.9 = (f16[2,4,16,384]{3,2,1,0:T(8,128)(2,1)S(1)}, f16[2,4,16,384]{3,2,1,0:T(8,128)(2,1)S(1)}, u32[]{:S(2)}, u32[]{:S(2)}) collective-permute-start(f16[2,4,16,384]{3,2,1,0:T(8,128)(2,1)S(1)} %get-tuple-element.36), channel_id=1, source_target_pairs={{0,16},{4,20},{8,24},{12,28},{16,0},{20,4},{24,8},{28,12},{32,48},... | collective-permute-start | bytes 294920 | tf_op jit(solution)/shard_map/ppermute | solution.py:302
  63.6 4.3 %collective-permute-start.10 = (f16[2,2,16,512]{3,2,1,0:T(8,128)(2,1)S(1)}, f16[2,2,16,512]{3,2,1,0:T(8,128)(2,1)S(1)}, u32[]{:S(2)}, u32[]{:S(2)}) collective-permute-start(f16[2,2,16,512]{3,2,1,0:T(8,128)(2,1)S(1)} %fusion.12), channel_id=1, source_target_pairs={{0,32},{4,36},{8,40},{12,44},{16,48},{20,52},{24,56},{28,60},{32,0... | collective-permute-start | bytes 196616 | tf_op jit(solution)/shard_map/ppermute | solution.py:302
  68.0 5.5 %collective-permute-start.11 = (f16[2,16,512]{2,1,0:T(8,128)(2,1)S(1)}, f16[2,16,512]{2,1,0:T(8,128)(2,1)S(1)}, u32[]{:S(2)}, u32[]{:S(2)}) collective-permute-start(f16[2,16,512]{2,1,0:T(8,128)(2,1)S(1)} %get-tuple-element.46), channel_id=1, source_target_pairs={{0,64},{4,68},{8,72},{12,76},{16,80},{20,84},{24,88},{28,92},{32,9... | collective-permute-start | bytes 98312 | tf_op jit(solution)/shard_map/ppermute | solution.py:302
  73.5 5.0 %collective-permute-start.12 = (f32[2,16,128]{2,1,0:T(8,128)S(1)}, f32[2,16,128]{2,1,0:T(8,128)S(1)}, u32[]{:S(2)}, u32[]{:S(2)}) collective-permute-start(f32[2,16,128]{2,1,0:T(8,128)S(1)} %pad_maximum_fusion.1), channel_id=1, source_target_pairs={{0,1},{1,2},{2,3},{3,0},{4,5},{5,6},{6,7},{7,4},{8,9},{9,10},{10,1... | collective-permute-start | bytes 49160 | tf_op jit(solution)/shard_map/ppermute | solution.py:368

commit v3 on v2

--- a/solution.py
+++ b/solution.py
@@ -15,7 +15,8 @@
 PIECE = 16
 WIRE = jnp.float16
 WIRE_SCALE = 4096.0
-UNROLL = 4
+UNROLL = 16
+TAIL = 1
 LOG2E = math.log2(math.e)
 SMEM = pltpu.SMEM
 F32 = jnp.float32
@@ -31,40 +32,37 @@
     return jnp.where(distance == offset, 1.0 - fraction, second)
 
 
-def strips_kernel(chunk, occ, x_first, x_last, to_left, to_right):
+def strips_kernel(first_block, occ, x_first, x_last, to_left, to_right):
     half = x_first.shape[2] // 2
+    block = first_block + pl.program_id(0)
     k = lax.broadcasted_iota(jnp.int32, (2 * LANES, LANES), 0)
     n = lax.broadcasted_iota(jnp.int32, (2 * LANES, LANES), 1)
-    blocks = x_first.shape[2] // BLK
-    first, last = 0, occ.shape[2] - 1
-    for ref, out, column, source, near in (
-        (x_first, to_left, first, jnp.where(n < HALF, n, n + HALF), n < HALF),
-        (x_last, to_right, last, jnp.where(n < HALF, n + LANES + HALF, n), n >= HALF),
+    for ref, out, column, source in (
+        (x_first, to_left, 0, jnp.where(n < HALF, n, n + HALF)),
+        (x_last, to_right, occ.shape[2] - 1, jnp.where(n < HALF, n + LANES + HALF, n)),
     ):
-        low = occ[0, blocks * chunk, column].astype(F32)
-        high = occ[0, blocks * chunk + 1, column].astype(F32)
-        pick = jnp.where(k == source, jnp.where(near, low, high), 0.0).astype(BF16)
+        occupied = occ[0, block, column].astype(F32)
+        pick = jnp.where(k == source, occupied, 0.0).astype(BF16)
         for s in range(ref.shape[1]):
             rows = jnp.concatenate([ref[0, s, :half], ref[0, s, half:]], axis=1)
             out[s] = jnp.dot(rows, pick, preferred_element_type=F32).astype(BF16)
 
 
-def edge_strips(density, occupancy, chunk):
+def edge_strips(density, occupancy, first, blocks):
     _, slices, _, cols = density.shape
-    step = 2 * BLK
-    shape = jax.ShapeDtypeStruct((slices, step // 2, LANES), BF16)
+    shape = jax.ShapeDtypeStruct((slices, blocks * BLK // 2, LANES), BF16)
     last = cols // LANES - 1
     return pl.pallas_call(
-        functools.partial(strips_kernel, chunk),
-        grid=(1,),
+        functools.partial(strips_kernel, first),
+        grid=(blocks,),
         in_specs=[
             pl.BlockSpec(memory_space=SMEM),
-            pl.BlockSpec((1, slices, step, LANES), lambda i: (0, 0, chunk, 0)),
-            pl.BlockSpec((1, slices, step, LANES), lambda i: (0, 0, chunk, last)),
+            pl.BlockSpec((1, slices, BLK, LANES), lambda i: (0, 0, first + i, 0)),
+            pl.BlockSpec((1, slices, BLK, LANES), lambda i: (0, 0, first + i, last)),
         ],
-        out_specs=[pl.BlockSpec((slices, step // 2, LANES), lambda i: (0, 0, 0))] * 2,
+        out_specs=[pl.BlockSpec((slices, BLK // 2, LANES), lambda i: (0, i, 0))] * 2,
         out_shape=[shape, shape],
-        name=f"edge_strips{chunk}",
+        name=f"edge_strips{first}",
     )(occupancy, density, density)
 
 
@@ -189,11 +187,11 @@
 
 
 def border_kernel(
-    chunk, slice_total, occ, offset, frac_lateral, frac_vertical, extinction, gain, weights,
+    start, slice_total, occ, offset, frac_lateral, frac_vertical, extinction, gain, weights,
     first_ref, last_ref, first_lead, last_lead, right_ref, left_ref, right_lead, left_lead,
     out_keep, out_send, through_ref, sum_ref,
 ):
-    slices, rows = first_ref.shape[1], BLK
+    slices, half = first_ref.shape[1], BLK // 2
     last_tile = occ.shape[2] - 1
     follows = jnp.where(lax.axis_index("lat") < lax.axis_size("lat") - 1, 1, 0)
     own_lanes = lax.broadcasted_iota(jnp.int32, (1, LANES), 1) >= HALF
@@ -202,7 +200,6 @@
     through_ref[...] = jnp.ones_like(through_ref)
     sum_ref[...] = jnp.zeros_like(sum_ref)
     blocks = first_ref.shape[2] // BLK
-    start = blocks * chunk
     masks = []
     for b in range(start - 1, start + blocks):
         inside = b >= 0
@@ -212,18 +209,23 @@
                 splat(occ[0, b, last_tile] * follows if inside else 0.0),
             )
         )
+    zero = jnp.zeros((16, LANES), BF16)
 
     def one(s, _):
         before, own = weights[s, :LANES], weights[s, LANES:]
         turn = lambda w: jnp.concatenate([w[HALF:], w[:HALF]], axis=0)
         near = jnp.concatenate([before, own], axis=0)
-        far = (
-            jnp.concatenate([turn(before), own], axis=0),
-            jnp.concatenate([before, turn(own)], axis=0),
-        )
-
-        def lateral(first, last, right, left, second_half):
-            w_left, w_right = far if second_half else (near, near)
+        far_left = jnp.concatenate([turn(before), own], axis=0)
+        far_right = jnp.concatenate([before, turn(own)], axis=0)
+
+        def halves(ref, side, top, above):
+            parts = [above] if above is not None else []
+            for b in range(blocks):
+                at = slice(b * BLK + top, b * BLK + top + half)
+                parts.append(ref[0, s, at] * masks[b + 1][side])
+            return jnp.concatenate(parts, axis=0) if len(parts) > 1 else parts[0]
+
+        def lateral(first, last, right, left, w_left, w_right):
             here = jnp.dot(
                 jnp.concatenate([left, first], axis=1), w_left, preferred_element_type=F32
             )
@@ -233,25 +235,23 @@
             return jnp.where(own_lanes, here, there)
 
         right, left = right_ref[s], left_ref[s]
-        zero = jnp.zeros((16, LANES), BF16)
-        lead = lateral(
-            first_lead[0, s] * masks[0][0],
-            last_lead[0, s] * masks[0][1],
-            right_lead[s] if chunk else zero,
-            left_lead[s] if chunk else zero,
-            True,
-        )[8:]
+        x_near = lateral(
+            halves(first_ref, 0, 0, None), halves(last_ref, 1, 0, None), right, left, near, near
+        )
+        x_far = lateral(
+            halves(first_ref, 0, half, first_lead[0, s] * masks[0][0]),
+            halves(last_ref, 1, half, last_lead[0, s] * masks[0][1]),
+            jnp.concatenate([right_lead[s] if start else zero, right], axis=0),
+            jnp.concatenate([left_lead[s] if start else zero, left], axis=0),
+            far_left,
+            far_right,
+        )
         for b in range(blocks):
-            at = slice(b * rows, (b + 1) * rows)
-            x = lateral(
-                first_ref[0, s, at] * masks[b + 1][0],
-                last_ref[0, s, at] * masks[b + 1][1],
-                right,
-                left,
-                b == 1,
-            )
-            shade(s, jnp.concatenate([lead, x], axis=0), b * rows, state, refs)
-            lead = x[rows - 8 :]
+            rows = slice(b * half, (b + 1) * half)
+            far_rows = slice(b * half + 16, (b + 1) * half + 16)
+            lead = x_far[b * half + 8 : b * half + 16]
+            x = jnp.concatenate([lead, x_near[rows], x_far[far_rows]], axis=0)
+            shade(s, x, b * BLK, state, refs)
         return 0
 
     over_slices(slices, one)
@@ -259,25 +259,27 @@
     finish(state, gain[0], swap, out_keep, out_send, 0)
 
 
-def border(density, small, weights, halos, previous, chunk, slice_total):
+def border(density, small, weights, halos, previous, start, blocks, slice_total):
     _, slices, _, cols = density.shape
-    step = 2 * BLK
+    step = blocks * BLK
     last = cols // LANES - 1
-    per = step // 16
+    per = BLK // 16
 
     def body(column):
-        return pl.BlockSpec((1, slices, step, LANES), lambda i: (0, 0, chunk, column))
+        shape = tuple(pl.Element(n) for n in (1, slices, step, LANES))
+        return pl.BlockSpec(shape, lambda i: (0, 0, start * BLK, column * LANES))
 
     def lead(column):
         return pl.BlockSpec(
-            (1, slices, 16, LANES), lambda i: (0, 0, max(chunk * per - 1, 0), column)
+            (1, slices, 16, LANES), lambda i: (0, 0, max(start * per - 1, 0), column)
         )
 
-    halo = pl.BlockSpec((slices, BLK, LANES), lambda i: (0, 0, 0))
-    halo_lead = pl.BlockSpec((slices, 16, LANES), lambda i: (0, BLK // 16 - 1, 0))
+    halo = pl.BlockSpec((slices, step // 2, LANES), lambda i: (0, 0, 0))
+    end = previous[0].shape[1] // 16 - 1
+    halo_lead = pl.BlockSpec((slices, 16, LANES), lambda i: (0, end, 0))
     image = jax.ShapeDtypeStruct((2, step // 2, LANES), F32)
     return pl.pallas_call(
-        functools.partial(border_kernel, chunk, slice_total),
+        functools.partial(border_kernel, start, slice_total),
         grid=(1,),
         in_specs=small_specs()
         + [pl.BlockSpec((slices, 2 * LANES, LANES), lambda i: (0, 0, 0))]
@@ -286,7 +288,7 @@
         out_shape=[image, image],
         scratch_shapes=[pltpu.VMEM((step, LANES), F32)] * 2,
         compiler_params=pltpu.CompilerParams(vmem_limit_bytes=32 * 2**20),
-        name=f"border{chunk}",
+        name=f"border{start}",
     )(*small, weights, density, density, density, density, *halos, *previous)
 
 
@@ -324,12 +326,8 @@
     return over(keep, other, rank[me] < rank[me ^ (1 << level)])
 
 
-def over_z(keep, send, rank):
-    image = over_cores(keep, send, rank)
-    width = image.shape[2]
-    image = image.reshape(2, 4, 2, 2, PIECE, width)
-    image = over_level(image, 1, 3, rank)
-    return over_level(image, 2, 2, rank)
+def by_chip(image):
+    return image.reshape(2, 4, 2, 2, PIECE, image.shape[2])
 
 
 def over_y(image, rank):
@@ -347,23 +345,34 @@
     lat = lax.axis_size("lat")
     density = pltpu.with_memory_space_constraint(density, pltpu.HBM)
     small = (occupancy, shear_offsets, frac_lateral, frac_vertical, extinction, slab_gain)
-    chunks = rows // (2 * BLK)
+    blocks = rows // BLK
+    cuts = [(0, blocks - TAIL), (blocks - TAIL, TAIL)]
     rightwards = [(x, x + 1) for x in range(lat - 1)]
     leftwards = [(x, (x - 1) % lat) for x in range(lat)]
-    halos = []
-    for c in range(chunks):
-        to_left, to_right = edge_strips(density, occupancy, c)
+
+    def halo(cut):
+        to_left, to_right = edge_strips(density, occupancy, *cut)
         from_right = lax.ppermute(to_left, "lat", leftwards)
         from_left = lax.ppermute(to_right, "lat", rightwards)
-        halos.append((from_right, from_left))
-    keep, send, weights = interior(density, small, slice_total)
-    inner = over_z(keep, send, view_rank)
-    pieces = [
-        border(density, small, weights, halos[c], halos[max(c - 1, 0)], c, slice_total)
-        for c in range(chunks)
-    ]
+        return (to_left, to_right), (from_right, from_left)
+
+    strips, most = halo(cuts[0])
+    more_strips, rest = halo(cuts[1])
+    after_strips, _ = lax.optimization_barrier((occupancy, (strips, more_strips)))
+    small_first = (after_strips, *small[1:])
+    images = interior(density, small_first, slice_total)
+    (keep, send, weights), most = lax.optimization_barrier((images, most))
+    inner = over_cores(keep, send, view_rank)
+    pieces = [border(density, small, weights, most, most, *cuts[0], slice_total)]
+    inner, weights = lax.optimization_barrier((inner, weights))
+    inner = over_level(by_chip(inner), 1, 3, view_rank)
+    pieces.append(border(density, small, weights, rest, most, *cuts[1], slice_total))
     keep, send = (jnp.concatenate(p, axis=1) for p in zip(*pieces))
-    edge = over_z(keep, send, view_rank)
+    inner, keep, send = lax.optimization_barrier((inner, keep, send))
+    inner = over_level(inner, 2, 2, view_rank)
+    edge = by_chip(over_cores(keep, send, view_rank))
+    edge = over_level(edge, 1, 3, view_rank)
+    edge = over_level(edge, 2, 2, view_rank)
     image = over_y(jnp.concatenate([edge, inner], axis=3), view_rank)
     moved = lax.ppermute(image[:, :, :LANES], "lat", [(x, (x + 1) % lat) for x in range(lat)])
     lane = jnp.arange(LANES, dtype=jnp.int32)

time: 79.6 us -> 81.5 us (1.024)
  starting transfers between devices: 23.1 us -> 26.7 us
  waiting for transfers between devices: 18.2 us -> 16.4 us
  other arithmetic: 0.77 us -> 1.93 us
  Pallas kernels: 27.9 us -> 26.9 us
    ppermute x8, waiting for transfers between devices: 14.6 us -> 10.8 us  [depth_swap(): return lax.ppermute(value, 'depth', [(i, i ^ bits) for i in range(count)])]
    ppermute x8, starting transfers between devices: 13.4 us -> 16.2 us  [depth_swap(): return lax.ppermute(value, 'depth', [(i, i ^ bits) for i in range(count)])]
    ppermute x4, starting transfers between devices: 8.25 us -> 9.85 us  [the longest x2 6.39 us: halo(): from_right = lax.ppermute(to_left, 'lat', leftwards)]
    add x3 -> x5, other arithmetic: 0.07 us -> 1.37 us  [over(): jnp.where(in_front, mine[0], other[0])]
    ppermute x4, waiting for transfers between devices: 0.01 us -> 1.21 us  [the longest x2 1.21 us: halo(): from_left = lax.ppermute(to_right, 'lat', rightwards)]
    ppermute x1, waiting for transfers between devices: 3.58 us -> 4.4 us  [shards(): lax.ppermute(image[:, :, :LANES], 'lat', [(x, (x + 1) % lat) for x in ran...]
    ppermute x1, starting transfers between devices: 1.43 us -> 0.61 us  [shards(): lax.ppermute(image[:, :, :LANES], 'lat', [(x, (x + 1) % lat) for x in ran...]
  transfers between devices with their start and end apart: 13 -> 13, of which waited for: 7 -> 8; matrix products, arithmetic and copies ran while one was open for 1% -> 3% of each run, Pallas kernels for 26% -> 27%
where the time goes in v3:
time: 81.5 us; the launch traced here: 81 us
  Pallas kernels  26.9 us (33%)
  starting transfers between devices  26.7 us (33%)
  waiting for transfers between devices  16.4 us (20%)
  between operations  7.63 us (9%)
  other arithmetic  1.93 us (2%)
  local copies, waits for them, and re-layouts  1.37 us (2%)
    ppermute x8, starting transfers between devices, depth_swap(): return lax.ppermute(value, 'depth', [(i, i ^ bits) for i in range(count)])  16.2 us
    pallas_call x1, Pallas kernels, interior(): pl.pallas_call(functools.partial(interior_kernel, slice_total), grid=(row...  12.6 us
    ppermute x8, waiting for transfers between devices, depth_swap(): return lax.ppermute(value, 'depth', [(i, i ^ bits) for i in range(count)])  10.8 us
    pallas_call x2, Pallas kernels, edge_strips(): pl.pallas_call(functools.partial(strips_kernel, first), grid=(blocks,), i...  7.28 us
    pallas_call x2, Pallas kernels, border(): pl.pallas_call(functools.partial(border_kernel, start, slice_total), grid...  7.05 us
    ppermute x2, starting transfers between devices, halo(): from_right = lax.ppermute(to_left, 'lat', leftwards)  6.39 us
    ppermute x1, waiting for transfers between devices, shards(): lax.ppermute(image[:, :, :LANES], 'lat', [(x, (x + 1) % lat) for x in ran...  4.4 us
    ppermute x2, starting transfers between devices, halo(): from_left = lax.ppermute(to_right, 'lat', rightwards)  3.46 us
  transfers between devices with their start and end apart: 13, of which 8 were waited for; matrix products, arithmetic and copies ran while one was open for 3% of the time, Pallas kernels for 27%

profile of v3, /device:TPU:0, one launch (start us, length us, event | category | flops | bytes accessed | tf_op | source)
XLA Modules:
  0.0 81.0 jit_solution(4710837688981429275)
XLA Ops:
  0.6 4.7 %edge_strips0.1 = (bf16[16,192,128]{2,1,0:T(8,128)(2,1)}, bf16[16,192,128]{2,1,0:T(8,128)(2,1)}) custom-call(s32[1,4,4]{2,1,0:T(4,128)} %occ.8, bf16[1,16,512,512]{3,2,1,0:T(8,128)(2,1)} %last_lead.3, bf16[1,16,512,512]{3,2,1,0:T(8,128)(2,1)} %last_lead.3), custom_call_target="tpu_custom_call" | custom-call | tf_op jit(solution)/shard_map/edge_strips0/pallas_call | solution.py:55
  5.4 2.9 %collective-permute-start = (bf16[16,192,128]{2,1,0:T(8,128)(2,1)}, bf16[16,192,128]{2,1,0:T(8,128)(2,1)S(1)}, u32[]{:S(2)}, u32[]{:S(2)}) collective-permute-start(bf16[16,192,128]{2,1,0:T(8,128)(2,1)} %get-tuple-element.24), channel_id=1, source_target_pairs={{0,3},{1,0},{2,1},{3,2},{4,7},{5,4},{6,5},{7,6},{8,11},{9,8},{10,9... | collective-permute-start | bytes 2359304 | tf_op jit(solution)/shard_map/ppermute | solution.py:355
  8.2 0.0 copy-start.4
  8.2 1.5 %collective-permute-start.1 = (bf16[16,192,128]{2,1,0:T(8,128)(2,1)}, bf16[16,192,128]{2,1,0:T(8,128)(2,1)S(1)}, u32[]{:S(2)}, u32[]{:S(2)}) collective-permute-start(bf16[16,192,128]{2,1,0:T(8,128)(2,1)} %get-tuple-element.25), channel_id=1, source_target_pairs={{0,1},{1,2},{2,3},{4,5},{5,6},{6,7},{8,9},{9,10},{10,11},{12,13},{... | collective-permute-start | bytes 2359304 | tf_op jit(solution)/shard_map/ppermute | solution.py:356
  9.7 2.5 %edge_strips3.1 = (bf16[16,64,128]{2,1,0:T(8,128)(2,1)}, bf16[16,64,128]{2,1,0:T(8,128)(2,1)}) custom-call(s32[1,4,4]{2,1,0:T(4,128)} %occ.8, bf16[1,16,512,512]{3,2,1,0:T(8,128)(2,1)} %last_lead.3, bf16[1,16,512,512]{3,2,1,0:T(8,128)(2,1)} %last_lead.3), custom_call_target="tpu_custom_call" | custom-call | tf_op jit(solution)/shard_map/edge_strips3/pallas_call | solution.py:55
  13.0 0.0 copy-start.5
  13.0 12.6 %interior.1 = (f32[2,256,384]{2,1,0:T(8,128)S(1)}, f32[2,256,384]{2,1,0:T(8,128)}, bf16[16,256,128]{2,1,0:T(8,128)(2,1)S(1)}) custom-call(s32[1,4,4]{2,1,0:T(4,128)S(1)} %copy-done, s32[1,16]{1,0:T(1,128)S(1)} %copy-done.1, f32[1,16]{1,0:T(1,128)S(1)} %copy-done.2, f32[1,16]{1,0:T(1,128)S(1)} %copy-done.3, f32[1,16]{1,0:T(1,128)S(1)} %copy-done.4, ...), custom_call_target="tpu_custom_call" | custom-call | tf_op jit(solution)/shard_map/interior/pallas_call | solution.py:170
  25.6 0.0 collective-permute-done.right_ref.right_lead
  25.6 1.2 %collective-permute-done.1.left_ref.left_lead = bf16[16,192,128]{2,1,0:T(8,128)(2,1)S(1)} collective-permute-done((bf16[16,192,128]{2,1,0:T(8,128)(2,1)}, bf16[16,192,128]{2,1,0:T(8,128)(2,1)S(1)}, u32[]{:S(2)}, u32[]{:S(2)}) %collective-permute-start.1) | collective-permute-done | bytes 786464 | tf_op jit(solution)/shard_map/ppermute | solution.py:356
  26.8 3.5 %collective-permute-start.4 = (bf16[16,64,128]{2,1,0:T(8,128)(2,1)}, bf16[16,64,128]{2,1,0:T(8,128)(2,1)}, u32[]{:S(2)}, u32[]{:S(2)}) collective-permute-start(bf16[16,64,128]{2,1,0:T(8,128)(2,1)} %get-tuple-element.26), channel_id=1, source_target_pairs={{0,3},{1,0},{2,1},{3,2},{4,7},{5,4},{6,5},{7,6},{8,11},{9,8},{10,9... | collective-permute-start | bytes 786440 | tf_op jit(solution)/shard_map/ppermute | solution.py:355
  30.3 2.0 %collective-permute-start.5 = (bf16[16,64,128]{2,1,0:T(8,128)(2,1)}, bf16[16,64,128]{2,1,0:T(8,128)(2,1)}, u32[]{:S(2)}, u32[]{:S(2)}) collective-permute-start(bf16[16,64,128]{2,1,0:T(8,128)(2,1)} %get-tuple-element.27), channel_id=1, source_target_pairs={{0,1},{1,2},{2,3},{4,5},{5,6},{6,7},{8,9},{9,10},{10,11},{12,13},{... | collective-permute-start | bytes 786440 | tf_op jit(solution)/shard_map/ppermute | solution.py:356
  32.3 0.7 fusion.20
  35.3 4.6 %border0.1 = (f32[2,192,128]{2,1,0:T(8,128)S(1)}, f32[2,192,128]{2,1,0:T(8,128)S(1)}) custom-call(s32[1,4,4]{2,1,0:T(4,128)S(1)} %copy-done, s32[1,16]{1,0:T(1,128)S(1)} %copy-done.1, f32[1,16]{1,0:T(1,128)S(1)} %copy-done.2, f32[1,16]{1,0:T(1,128)S(1)} %copy-done.3, f32[1,16]{1,0:T(1,128)S(1)} %copy-done.4, f32[1]{0:T(128)S(6)} %copy.57.gain, ...), custom_call_target="tpu_custom_call" | custom-call | tf_op jit(solution)/shard_map/border0/pallas_call | solution.py:281
  39.9 1.2 %multiply_add_fusion.1 = (f32[1,256,384]{2,1,0:T(8,128)S(1)}, f32[1,256,384]{2,1,0:T(8,128)S(1)}) fusion(f32[2,256,384]{2,1,0:T(8,128)} %collective-permute-done.2, f32[2,256,384]{2,1,0:T(8,128)S(1)} %get-tuple-element.32, pred[]{:T(512)} %bitcast.4), kind=kLoop, calls=%fused_computation.6 | loop fusion | flops 884736 | bytes 2359297 | tf_op jit(solution)/shard_map/add | solution.py:296
  41.2 0.1 pad_maximum_fusion
  41.3 2.0 %collective-permute-start.3 = (f16[2,4,2,16,384]{4,3,1,2,0:T(8,128)(2,1)S(1)}, f16[2,4,2,16,384]{4,3,1,2,0:T(8,128)(2,1)S(1)}, u32[]{:S(2)}, u32[]{:S(2)}) collective-permute-start(f16[2,4,2,16,384]{4,3,1,2,0:T(8,128)(2,1)S(1)} %fusion.1), channel_id=1, source_target_pairs={{0,8},{4,12},{8,0},{12,4},{16,24},{20,28},{24,16},{28,20},{32,40},... | collective-permute-start | bytes 589832 | tf_op jit(solution)/shard_map/ppermute | solution.py:304
  43.3 2.4 %border3.1 = (f32[2,64,128]{2,1,0:T(8,128)S(1)}, f32[2,64,128]{2,1,0:T(8,128)S(1)}) custom-call(s32[1,4,4]{2,1,0:T(4,128)S(1)} %copy-done, s32[1,16]{1,0:T(1,128)S(1)} %copy-done.1, f32[1,16]{1,0:T(1,128)S(1)} %copy-done.2, f32[1,16]{1,0:T(1,128)S(1)} %copy-done.3, f32[1,16]{1,0:T(1,128)S(1)} %copy-done.4, f32[1]{0:T(128)S(6)} %copy.57.gain, ...), custom_call_target="tpu_custom_call" | custom-call | tf_op jit(solution)/shard_map/border3/pallas_call | solution.py:281
  45.8 2.8 %collective-permute-done.3 = f16[2,4,2,16,384]{4,3,1,2,0:T(8,128)(2,1)S(1)} collective-permute-done((f16[2,4,2,16,384]{4,3,1,2,0:T(8,128)(2,1)S(1)}, f16[2,4,2,16,384]{4,3,1,2,0:T(8,128)(2,1)S(1)}, u32[]{:S(2)}, u32[]{:S(2)}) %collective-permute-start.3) | collective-permute-done | bytes 196640 | tf_op jit(solution)/shard_map/ppermute | solution.py:304
  48.6 0.1 multiply_add_fusion.3
  48.8 3.8 %collective-permute-start.9 = (f16[2,4,16,384]{3,2,1,0:T(8,128)(2,1)S(1)}, f16[2,4,16,384]{3,2,1,0:T(8,128)(2,1)S(1)}, u32[]{:S(2)}, u32[]{:S(2)}) collective-permute-start(f16[2,4,16,384]{3,2,1,0:T(8,128)(2,1)S(1)} %fusion.5), channel_id=1, source_target_pairs={{0,16},{4,20},{8,24},{12,28},{16,0},{20,4},{24,8},{28,12},{32,48},... | collective-permute-start | bytes 294920 | tf_op jit(solution)/shard_map/ppermute | solution.py:304
  53.8 1.4 %collective-permute-done.9 = f16[2,4,16,384]{3,2,1,0:T(8,128)(2,1)S(1)} collective-permute-done((f16[2,4,16,384]{3,2,1,0:T(8,128)(2,1)S(1)}, f16[2,4,16,384]{3,2,1,0:T(8,128)(2,1)S(1)}, u32[]{:S(2)}, u32[]{:S(2)}) %collective-permute-start.9) | collective-permute-done | bytes 98336 | tf_op jit(solution)/shard_map/ppermute | solution.py:304
  55.3 1.7 %collective-permute-start.7 = (f16[2,4,2,16,128]{4,3,1,2,0:T(8,128)(2,1)S(1)}, f16[2,4,2,16,128]{4,3,1,2,0:T(8,128)(2,1)S(1)}, u32[]{:S(2)}, u32[]{:S(2)}) collective-permute-start(f16[2,4,2,16,128]{4,3,1,2,0:T(8,128)(2,1)S(1)} %fusion.7), channel_id=1, source_target_pairs={{0,8},{4,12},{8,0},{12,4},{16,24},{20,28},{24,16},{28,20},{32,40},... | collective-permute-start | bytes 196616 | tf_op jit(solution)/shard_map/ppermute | solution.py:304
  57.0 2.7 %collective-permute-done.7 = f16[2,4,2,16,128]{4,3,1,2,0:T(8,128)(2,1)S(1)} collective-permute-done((f16[2,4,2,16,128]{4,3,1,2,0:T(8,128)(2,1)S(1)}, f16[2,4,2,16,128]{4,3,1,2,0:T(8,128)(2,1)S(1)}, u32[]{:S(2)}, u32[]{:S(2)}) %collective-permute-start.7) | collective-permute-done | bytes 65568 | tf_op jit(solution)/shard_map/ppermute | solution.py:304
  59.7 3.6 %collective-permute-start.8 = (f16[2,4,16,128]{3,2,1,0:T(8,128)(2,1)S(1)}, f16[2,4,16,128]{3,2,1,0:T(8,128)(2,1)S(1)}, u32[]{:S(2)}, u32[]{:S(2)}) collective-permute-start(f16[2,4,16,128]{3,2,1,0:T(8,128)(2,1)S(1)} %get-tuple-element.68), channel_id=1, source_target_pairs={{0,16},{4,20},{8,24},{12,28},{16,0},{20,4},{24,8},{28,12},{32,48},... | collective-permute-start | bytes 98312 | tf_op jit(solution)/shard_map/ppermute | solution.py:304
  63.4 1.9 %collective-permute-done.8 = f16[2,4,16,128]{3,2,1,0:T(8,128)(2,1)S(1)} collective-permute-done((f16[2,4,16,128]{3,2,1,0:T(8,128)(2,1)S(1)}, f16[2,4,16,128]{3,2,1,0:T(8,128)(2,1)S(1)}, u32[]{:S(2)}, u32[]{:S(2)}) %collective-permute-start.8) | collective-permute-done | bytes 32800 | tf_op jit(solution)/shard_map/ppermute | solution.py:304
  65.3 1.7 %collective-permute-start.10 = (f16[2,2,16,512]{3,2,1,0:T(8,128)(2,1)S(1)}, f16[2,2,16,512]{3,2,1,0:T(8,128)(2,1)S(1)}, u32[]{:S(2)}, u32[]{:S(2)}) collective-permute-start(f16[2,2,16,512]{3,2,1,0:T(8,128)(2,1)S(1)} %fusion.6), channel_id=1, source_target_pairs={{0,32},{4,36},{8,40},{12,44},{16,48},{20,52},{24,56},{28,60},{32,0... | collective-permute-start | bytes 196616 | tf_op jit(solution)/shard_map/ppermute | solution.py:304
  68.2 1.4 %collective-permute-done.10 = f16[2,2,16,512]{3,2,1,0:T(8,128)(2,1)S(1)} collective-permute-done((f16[2,2,16,512]{3,2,1,0:T(8,128)(2,1)S(1)}, f16[2,2,16,512]{3,2,1,0:T(8,128)(2,1)S(1)}, u32[]{:S(2)}, u32[]{:S(2)}) %collective-permute-start.10) | collective-permute-done | bytes 65568 | tf_op jit(solution)/shard_map/ppermute | solution.py:304
  69.8 3.5 %collective-permute-start.11 = (f16[2,16,512]{2,1,0:T(8,128)(2,1)S(1)}, f16[2,16,512]{2,1,0:T(8,128)(2,1)S(1)}, u32[]{:S(2)}, u32[]{:S(2)}) collective-permute-start(f16[2,16,512]{2,1,0:T(8,128)(2,1)S(1)} %get-tuple-element.64), channel_id=1, source_target_pairs={{0,64},{4,68},{8,72},{12,76},{16,80},{20,84},{24,88},{28,92},{32,9... | collective-permute-start | bytes 98312 | tf_op jit(solution)/shard_map/ppermute | solution.py:304
  74.5 0.8 collective-permute-done.11
  75.3 0.6 collective-permute-start.12
  75.9 4.4 %collective-permute-done.12 = f32[2,16,128]{2,1,0:T(8,128)S(1)} collective-permute-done((f32[2,16,128]{2,1,0:T(8,128)S(1)}, f32[2,16,128]{2,1,0:T(8,128)S(1)}, u32[]{:S(2)}, u32[]{:S(2)}) %collective-permute-start.12) | collective-permute-done | bytes 16416 | tf_op jit(solution)/shard_map/ppermute | solution.py:377
  80.3 0.6 slice_bitcast_fusion
  (44 shorter events, 0.6 us)
Async XLA Ops:
  5.4 20.2 %collective-permute-start = (bf16[16,192,128]{2,1,0:T(8,128)(2,1)}, bf16[16,192,128]{2,1,0:T(8,128)(2,1)S(1)}, u32[]{:S(2)}, u32[]{:S(2)}) collective-permute-start(bf16[16,192,128]{2,1,0:T(8,128)(2,1)} %get-tuple-element.24), channel_id=1, source_target_pairs={{0,3},{1,0},{2,1},{3,2},{4,7},{5,4},{6,5},{7,6},{8,11},{9,8},{10,9... | collective-permute-start | bytes 2359304 | tf_op jit(solution)/shard_map/ppermute | solution.py:355
  8.2 4.7 %copy-start = (s32[1,4,4]{2,1,0:T(4,128)S(1)}, s32[1,4,4]{2,1,0:T(4,128)}, u32[]{:S(2)}) copy-start(s32[1,4,4]{2,1,0:T(4,128)} %occ.8) | copy-start | bytes 196
  8.2 4.7 %copy-start.1 = (s32[1,16]{1,0:T(1,128)S(1)}, s32[1,16]{1,0:T(1,128)}, u32[]{:S(2)}) copy-start(s32[1,16]{1,0:T(1,128)} %offset.5) | copy-start | bytes 196
  8.2 4.7 %copy-start.2 = (f32[1,16]{1,0:T(1,128)S(1)}, f32[1,16]{1,0:T(1,128)}, u32[]{:S(2)}) copy-start(f32[1,16]{1,0:T(1,128)} %frac_lateral.5) | copy-start | bytes 196
  8.2 4.7 %copy-start.3 = (f32[1,16]{1,0:T(1,128)S(1)}, f32[1,16]{1,0:T(1,128)}, u32[]{:S(2)}) copy-start(f32[1,16]{1,0:T(1,128)} %frac_vertical.5) | copy-start | bytes 196
  8.2 4.7 %copy-start.4 = (f32[1,16]{1,0:T(1,128)S(1)}, f32[1,16]{1,0:T(1,128)}, u32[]{:S(2)}) copy-start(f32[1,16]{1,0:T(1,128)} %extinction.5) | copy-start | bytes 196
  8.2 18.5 %collective-permute-start.1 = (bf16[16,192,128]{2,1,0:T(8,128)(2,1)}, bf16[16,192,128]{2,1,0:T(8,128)(2,1)S(1)}, u32[]{:S(2)}, u32[]{:S(2)}) collective-permute-start(bf16[16,192,128]{2,1,0:T(8,128)(2,1)} %get-tuple-element.25), channel_id=1, source_target_pairs={{0,1},{1,2},{2,3},{4,5},{5,6},{6,7},{8,9},{9,10},{10,11},{12,13},{... | collective-permute-start | bytes 2359304 | tf_op jit(solution)/shard_map/ppermute | solution.py:356
  13.0 19.3 %copy-start.5 = (s32[32]{0:T(128)S(1)}, s32[32]{0:T(128)}, u32[]{:S(2)}) copy-start(s32[32]{0:T(128)} %param.15) | copy-start | bytes 388
  26.8 13.2 %collective-permute-start.2 = (f32[2,256,384]{2,1,0:T(8,128)}, f32[2,256,384]{2,1,0:T(8,128)}, u32[]{:S(2)}, u32[]{:S(2)}) collective-permute-start(f32[2,256,384]{2,1,0:T(8,128)} %get-tuple-element.33), channel_id=1, source_target_pairs={{0,4},{4,0},{8,12},{12,8},{16,20},{20,16},{24,28},{28,24},{32,36},... | collective-permute-start | bytes 2359304 | tf_op jit(solution)/shard_map/ppermute | solution.py:304
  26.8 16.5 %collective-permute-start.4 = (bf16[16,64,128]{2,1,0:T(8,128)(2,1)}, bf16[16,64,128]{2,1,0:T(8,128)(2,1)}, u32[]{:S(2)}, u32[]{:S(2)}) collective-permute-start(bf16[16,64,128]{2,1,0:T(8,128)(2,1)} %get-tuple-element.26), channel_id=1, source_target_pairs={{0,3},{1,0},{2,1},{3,2},{4,7},{5,4},{6,5},{7,6},{8,11},{9,8},{10,9... | collective-permute-start | bytes 786440 | tf_op jit(solution)/shard_map/ppermute | solution.py:355
  30.3 13.0 %collective-permute-start.5 = (bf16[16,64,128]{2,1,0:T(8,128)(2,1)}, bf16[16,64,128]{2,1,0:T(8,128)(2,1)}, u32[]{:S(2)}, u32[]{:S(2)}) collective-permute-start(bf16[16,64,128]{2,1,0:T(8,128)(2,1)} %get-tuple-element.27), channel_id=1, source_target_pairs={{0,1},{1,2},{2,3},{4,5},{5,6},{6,7},{8,9},{9,10},{10,11},{12,13},{... | collective-permute-start | bytes 786440 | tf_op jit(solution)/shard_map/ppermute | solution.py:356
  41.3 7.3 %collective-permute-start.3 = (f16[2,4,2,16,384]{4,3,1,2,0:T(8,128)(2,1)S(1)}, f16[2,4,2,16,384]{4,3,1,2,0:T(8,128)(2,1)S(1)}, u32[]{:S(2)}, u32[]{:S(2)}) collective-permute-start(f16[2,4,2,16,384]{4,3,1,2,0:T(8,128)(2,1)S(1)} %fusion.1), channel_id=1, source_target_pairs={{0,8},{4,12},{8,0},{12,4},{16,24},{20,28},{24,16},{28,20},{32,40},... | collective-permute-start | bytes 589832 | tf_op jit(solution)/shard_map/ppermute | solution.py:304
  48.8 6.4 %collective-permute-start.9 = (f16[2,4,16,384]{3,2,1,0:T(8,128)(2,1)S(1)}, f16[2,4,16,384]{3,2,1,0:T(8,128)(2,1)S(1)}, u32[]{:S(2)}, u32[]{:S(2)}) collective-permute-start(f16[2,4,16,384]{3,2,1,0:T(8,128)(2,1)S(1)} %fusion.5), channel_id=1, source_target_pairs={{0,16},{4,20},{8,24},{12,28},{16,0},{20,4},{24,8},{28,12},{32,48},... | collective-permute-start | bytes 294920 | tf_op jit(solution)/shard_map/ppermute | solution.py:304
  52.6 2.6 %collective-permute-start.6 = (f32[2,256,128]{2,1,0:T(8,128)S(1)}, f32[2,256,128]{2,1,0:T(8,128)S(1)}, u32[]{:S(2)}, u32[]{:S(2)}) collective-permute-start(f32[2,256,128]{2,1,0:T(8,128)S(1)} %get-tuple-element.44), channel_id=1, source_target_pairs={{0,4},{4,0},{8,12},{12,8},{16,20},{20,16},{24,28},{28,24},{32,36},... | collective-permute-start | bytes 786440 | tf_op jit(solution)/shard_map/ppermute | solution.py:304
  55.3 4.3 %collective-permute-start.7 = (f16[2,4,2,16,128]{4,3,1,2,0:T(8,128)(2,1)S(1)}, f16[2,4,2,16,128]{4,3,1,2,0:T(8,128)(2,1)S(1)}, u32[]{:S(2)}, u32[]{:S(2)}) collective-permute-start(f16[2,4,2,16,128]{4,3,1,2,0:T(8,128)(2,1)S(1)} %fusion.7), channel_id=1, source_target_pairs={{0,8},{4,12},{8,0},{12,4},{16,24},{20,28},{24,16},{28,20},{32,40},... | collective-permute-start | bytes 196616 | tf_op jit(solution)/shard_map/ppermute | solution.py:304
  59.7 5.5 %collective-permute-start.8 = (f16[2,4,16,128]{3,2,1,0:T(8,128)(2,1)S(1)}, f16[2,4,16,128]{3,2,1,0:T(8,128)(2,1)S(1)}, u32[]{:S(2)}, u32[]{:S(2)}) collective-permute-start(f16[2,4,16,128]{3,2,1,0:T(8,128)(2,1)S(1)} %get-tuple-element.68), channel_id=1, source_target_pairs={{0,16},{4,20},{8,24},{12,28},{16,0},{20,4},{24,8},{28,12},{32,48},... | collective-permute-start | bytes 98312 | tf_op jit(solution)/shard_map/ppermute | solution.py:304
  65.3 4.3 %collective-permute-start.10 = (f16[2,2,16,512]{3,2,1,0:T(8,128)(2,1)S(1)}, f16[2,2,16,512]{3,2,1,0:T(8,128)(2,1)S(1)}, u32[]{:S(2)}, u32[]{:S(2)}) collective-permute-start(f16[2,2,16,512]{3,2,1,0:T(8,128)(2,1)S(1)} %fusion.6), channel_id=1, source_target_pairs={{0,32},{4,36},{8,40},{12,44},{16,48},{20,52},{24,56},{28,60},{32,0... | collective-permute-start | bytes 196616 | tf_op jit(solution)/shard_map/ppermute | solution.py:304
  69.8 5.5 %collective-permute-start.11 = (f16[2,16,512]{2,1,0:T(8,128)(2,1)S(1)}, f16[2,16,512]{2,1,0:T(8,128)(2,1)S(1)}, u32[]{:S(2)}, u32[]{:S(2)}) collective-permute-start(f16[2,16,512]{2,1,0:T(8,128)(2,1)S(1)} %get-tuple-element.64), channel_id=1, source_target_pairs={{0,64},{4,68},{8,72},{12,76},{16,80},{20,84},{24,88},{28,92},{32,9... | collective-permute-start | bytes 98312 | tf_op jit(solution)/shard_map/ppermute | solution.py:304
  75.3 5.0 %collective-permute-start.12 = (f32[2,16,128]{2,1,0:T(8,128)S(1)}, f32[2,16,128]{2,1,0:T(8,128)S(1)}, u32[]{:S(2)}, u32[]{:S(2)}) collective-permute-start(f32[2,16,128]{2,1,0:T(8,128)S(1)} %pad_maximum_fusion.4), channel_id=1, source_target_pairs={{0,1},{1,2},{2,3},{3,0},{4,5},{5,6},{6,7},{7,4},{8,9},{9,10},{10,1... | collective-permute-start | bytes 49160 | tf_op jit(solution)/shard_map/ppermute | solution.py:377

commit v4 on v3

--- a/solution.py
+++ b/solution.py
@@ -13,10 +13,10 @@
 HALF = SHIFT // 2
 LANES = 128
 PIECE = 16
+PARTNERS = (1, 2, 6, 8, 24)
 WIRE = jnp.float16
 WIRE_SCALE = 4096.0
 UNROLL = 16
-TAIL = 1
 LOG2E = math.log2(math.e)
 SMEM = pltpu.SMEM
 F32 = jnp.float32
@@ -85,7 +85,11 @@
     sum_ref[at] += (through - after) * slope
 
 
-def finish(state, gain, swap, out_keep, out_send, tile):
+def gray(index):
+    return index ^ (index >> 1)
+
+
+def finish(state, gain, swap, out_keep, out_send, tile, first=0):
     through_ref, sum_ref = state
     rows = out_keep.shape[1] * 2
     base = tile * rows
@@ -97,7 +101,8 @@
         colors.append(gain * (0.65 * alpha + 0.35 * sum_ref[at]))
     lanes = slice(tile * LANES, (tile + 1) * LANES)
     for q in range(rows // PIECE // 2):
-        at = slice(q * PIECE, (q + 1) * PIECE)
+        place = 4 * (gray(first + q // 4) - first) + gray(q % 4)
+        at = slice(place * PIECE, (place + 1) * PIECE)
         for i, values in enumerate((colors, alphas)):
             even, odd = values[2 * q], values[2 * q + 1]
             out_keep[i, at, lanes] = jnp.where(swap, odd, even)
@@ -113,8 +118,8 @@
 
 
 def interior_kernel(
-    slice_total, occ, offset, frac_lateral, frac_vertical, extinction, gain,
-    x_ref, lead_ref, out_keep, out_send, weights, through_ref, sum_ref,
+    slice_total, occ, offset, frac_lateral, frac_vertical, extinction, gain, rank,
+    x_ref, lead_ref, out_keep, out_send, weights, flags, through_ref, sum_ref,
 ):
     block = pl.program_id(0)
     slices, rows = x_ref.shape[1], x_ref.shape[2]
@@ -130,6 +135,13 @@
             return 0
 
         lax.fori_loop(0, slices, build, 0)
+        me = lax.axis_index("depth")
+        rows_of_flags = [rank[me] < rank[jnp.bitwise_xor(me, partner)] for partner in PARTNERS]
+        z, y = (me // 2) % 4, me // 8
+        for place in (jnp.bitwise_xor(z, z // 2), jnp.bitwise_xor(y, y // 2)):
+            rows_of_flags += [place % 2 == 1, place // 2 == 1]
+        for i, flag in enumerate(rows_of_flags):
+            flags[i : i + 1] = jnp.full((1, LANES), jnp.where(flag, 1.0, 0.0), F32)
 
     through_ref[...] = jnp.ones_like(through_ref)
     sum_ref[...] = jnp.zeros_like(sum_ref)
@@ -162,7 +174,7 @@
     return [pl.BlockSpec(memory_space=SMEM)] * 6
 
 
-def interior(density, small, slice_total):
+def interior(density, small, rank, slice_total):
     _, slices, rows, cols = density.shape
     step = BLK
     width = cols - LANES
@@ -171,19 +183,31 @@
         functools.partial(interior_kernel, slice_total),
         grid=(rows // step,),
         in_specs=small_specs()
+        + [pl.BlockSpec(memory_space=SMEM)]
         + [
             pl.BlockSpec((1, slices, step, cols), lambda b: (0, 0, b, 0)),
             pl.BlockSpec(
                 (1, slices, 16, cols), lambda b: (0, 0, jnp.maximum(b * (step // 16) - 1, 0), 0)
             ),
         ],
-        out_specs=[pl.BlockSpec((2, step // 2, width), lambda b: (0, b, 0))] * 2
-        + [pl.BlockSpec((slices, 2 * LANES, LANES), lambda b: (0, 0, 0))],
-        out_shape=[image, image, jax.ShapeDtypeStruct((slices, 2 * LANES, LANES), BF16)],
+        out_specs=[
+            pl.BlockSpec((2, step // 2, width), lambda b: (0, jnp.bitwise_xor(b, b // 2), 0))
+        ]
+        * 2
+        + [
+            pl.BlockSpec((slices, 2 * LANES, LANES), lambda b: (0, 0, 0)),
+            pl.BlockSpec((16, LANES), lambda b: (0, 0)),
+        ],
+        out_shape=[
+            image,
+            image,
+            jax.ShapeDtypeStruct((slices, 2 * LANES, LANES), BF16),
+            jax.ShapeDtypeStruct((16, LANES), F32),
+        ],
         scratch_shapes=[pltpu.VMEM((step * (width // LANES), LANES), F32)] * 2,
         compiler_params=pltpu.CompilerParams(vmem_limit_bytes=32 * 2**20),
         name="interior",
-    )(*small, density, density)
+    )(*small, rank, density, density)
 
 
 def border_kernel(
@@ -256,10 +280,10 @@
 
     over_slices(slices, one)
     swap = lax.axis_index("depth") % 2 == 1
-    finish(state, gain[0], swap, out_keep, out_send, 0)
-
-
-def border(density, small, weights, halos, previous, start, blocks, slice_total):
+    finish(state, gain[0], swap, out_keep, out_send, 0, start)
+
+
+def border(density, small, weights, halos, start, blocks, slice_total):
     _, slices, _, cols = density.shape
     step = blocks * BLK
     last = cols // LANES - 1
@@ -274,9 +298,9 @@
             (1, slices, 16, LANES), lambda i: (0, 0, max(start * per - 1, 0), column)
         )
 
-    halo = pl.BlockSpec((slices, step // 2, LANES), lambda i: (0, 0, 0))
-    end = previous[0].shape[1] // 16 - 1
-    halo_lead = pl.BlockSpec((slices, 16, LANES), lambda i: (0, end, 0))
+    halo = pl.BlockSpec((slices, step // 2, LANES), lambda i: (0, start // blocks, 0))
+    above = max(start * per // 2 - 1, 0)
+    halo_lead = pl.BlockSpec((slices, 16, LANES), lambda i: (0, above, 0))
     image = jax.ShapeDtypeStruct((2, step // 2, LANES), F32)
     return pl.pallas_call(
         functools.partial(border_kernel, start, slice_total),
@@ -289,7 +313,7 @@
         scratch_shapes=[pltpu.VMEM((step, LANES), F32)] * 2,
         compiler_params=pltpu.CompilerParams(vmem_limit_bytes=32 * 2**20),
         name=f"border{start}",
-    )(*small, weights, density, density, density, density, *halos, *previous)
+    )(*small, weights, density, density, density, density, *halos, *halos)
 
 
 def over(mine, other, in_front):
@@ -312,29 +336,22 @@
     return value.astype(F32) * (1.0 / WIRE_SCALE)
 
 
-def over_cores(keep, send, rank):
-    me = lax.axis_index("depth")
-    return over(keep, depth_swap(send, 1), rank[me] < rank[me ^ 1])
-
-
-def over_level(image, level, axis, rank):
-    me = lax.axis_index("depth")
-    bit = me >> level & 1
-    keep = lax.dynamic_index_in_dim(image, bit, axis, keepdims=False)
-    send = lax.dynamic_index_in_dim(image, 1 - bit, axis, keepdims=False)
-    other = unwire(depth_swap(wire(send), 1 << level))
-    return over(keep, other, rank[me] < rank[me ^ (1 << level)])
+def over_cores(keep, send, flags):
+    return over(keep, depth_swap(send, PARTNERS[0]), flags[0, 0] > 0.0)
+
+
+def over_level(image, level, flags):
+    axis = 5 - level
+    second = flags[4 + level, 0] > 0.0
+    low = lax.index_in_dim(image, 0, axis, keepdims=False)
+    high = lax.index_in_dim(image, 1, axis, keepdims=False)
+    send = wire(jnp.where(second, low, high))
+    other = unwire(depth_swap(send, PARTNERS[level]))
+    return over(jnp.where(second, high, low), other, flags[level, 0] > 0.0)
 
 
 def by_chip(image):
-    return image.reshape(2, 4, 2, 2, PIECE, image.shape[2])
-
-
-def over_y(image, rank):
-    width = image.shape[3]
-    image = image.reshape(2, 2, 2, PIECE, width)
-    image = over_level(image, 3, 2, rank)
-    return over_level(image, 4, 1, rank)
+    return image.reshape(2, 2, 2, 2, 2, PIECE, image.shape[2])
 
 
 def shards(
@@ -346,34 +363,29 @@
     density = pltpu.with_memory_space_constraint(density, pltpu.HBM)
     small = (occupancy, shear_offsets, frac_lateral, frac_vertical, extinction, slab_gain)
     blocks = rows // BLK
-    cuts = [(0, blocks - TAIL), (blocks - TAIL, TAIL)]
     rightwards = [(x, x + 1) for x in range(lat - 1)]
     leftwards = [(x, (x - 1) % lat) for x in range(lat)]
-
-    def halo(cut):
-        to_left, to_right = edge_strips(density, occupancy, *cut)
-        from_right = lax.ppermute(to_left, "lat", leftwards)
-        from_left = lax.ppermute(to_right, "lat", rightwards)
-        return (to_left, to_right), (from_right, from_left)
-
-    strips, most = halo(cuts[0])
-    more_strips, rest = halo(cuts[1])
-    after_strips, _ = lax.optimization_barrier((occupancy, (strips, more_strips)))
-    small_first = (after_strips, *small[1:])
-    images = interior(density, small_first, slice_total)
-    (keep, send, weights), most = lax.optimization_barrier((images, most))
-    inner = over_cores(keep, send, view_rank)
-    pieces = [border(density, small, weights, most, most, *cuts[0], slice_total)]
+    to_left, to_right = edge_strips(density, occupancy, 0, blocks)
+    halos = (
+        lax.ppermute(to_left, "lat", leftwards),
+        lax.ppermute(to_right, "lat", rightwards),
+    )
+    images = interior(density, small, view_rank, slice_total)
+    (keep, send, weights, flags), halos = lax.optimization_barrier((images, halos))
+    inner = over_cores(keep, send, flags)
+    half = blocks // 2
+    top = border(density, small, weights, halos, 0, half, slice_total)
     inner, weights = lax.optimization_barrier((inner, weights))
-    inner = over_level(by_chip(inner), 1, 3, view_rank)
-    pieces.append(border(density, small, weights, rest, most, *cuts[1], slice_total))
-    keep, send = (jnp.concatenate(p, axis=1) for p in zip(*pieces))
-    inner, keep, send = lax.optimization_barrier((inner, keep, send))
-    inner = over_level(inner, 2, 2, view_rank)
-    edge = by_chip(over_cores(keep, send, view_rank))
-    edge = over_level(edge, 1, 3, view_rank)
-    edge = over_level(edge, 2, 2, view_rank)
-    image = over_y(jnp.concatenate([edge, inner], axis=3), view_rank)
+    inner = over_level(by_chip(inner), 1, flags)
+    bottom = border(density, small, weights, halos, half, blocks - half, slice_total)
+    keep, send = (jnp.concatenate(p, axis=1) for p in zip(top, bottom))
+    edge = by_chip(over_cores(keep, send, flags))
+    edge = over_level(edge, 1, flags)
+    edge = over_level(edge, 2, flags)
+    inner = over_level(inner, 2, flags)
+    image = jnp.concatenate([edge, inner], axis=4)
+    image = over_level(image, 3, flags)
+    image = over_level(image, 4, flags)
     moved = lax.ppermute(image[:, :, :LANES], "lat", [(x, (x + 1) % lat) for x in range(lat)])
     lane = jnp.arange(LANES, dtype=jnp.int32)
     first = jnp.where(lane < HALF, moved, image[:, :, :LANES])

time: 81.5 us -> 82.1 us (level)
  waiting for transfers between devices: 16.4 us -> 28.7 us
  starting transfers between devices: 26.7 us -> 19.2 us
  Pallas kernels: 26.9 us -> 24.6 us
  other arithmetic: 1.93 us -> 0.82 us
    ppermute x4 -> x2, waiting for transfers between devices: 1.21 us -> 9.72 us  [the longest x1 8.46 us: shards(): lax.ppermute(to_left, 'lat', leftwards)]
    ppermute x4 -> x2, starting transfers between devices: 9.85 us -> 4.19 us  [the longest x1 2.84 us: shards(): lax.ppermute(to_left, 'lat', leftwards)]
    ppermute x8, waiting for transfers between devices: 10.8 us -> 16.1 us  [depth_swap(): return lax.ppermute(value, 'depth', [(i, i ^ bits) for i in range(count)])]
    ppermute x8, starting transfers between devices: 16.2 us -> 12.6 us  [depth_swap(): return lax.ppermute(value, 'depth', [(i, i ^ bits) for i in range(count)])]
    pallas_call x2 -> x1, Pallas kernels: 7.28 us -> 5.43 us  [edge_strips(): pl.pallas_call(functools.partial(strips_kernel, first), grid=(blocks,), i...]
    ppermute x1, starting transfers between devices: 0.61 us -> 2.45 us  [shards(): lax.ppermute(image[:, :, :LANES], 'lat', [(x, (x + 1) % lat) for x in ran...]
    ppermute x1, waiting for transfers between devices: 4.4 us -> 2.89 us  [shards(): lax.ppermute(image[:, :, :LANES], 'lat', [(x, (x + 1) % lat) for x in ran...]
    add x5 -> x8, other arithmetic: 1.37 us -> 0.39 us  [over(): jnp.where(in_front, mine[0], other[0])]
  transfers between devices with their start and end apart: 13 -> 11, of which waited for: 8 -> 9; matrix products, arithmetic and copies ran while one was open for 3% -> 1% of each run, Pallas kernels for 27% -> 19%
where the time goes in v4:
time: 82.1 us; the launch traced here: 81.8 us
  waiting for transfers between devices  28.7 us (35%)
  Pallas kernels  24.6 us (30%)
  starting transfers between devices  19.2 us (23%)
  between operations  7.12 us (9%)
  local copies, waits for them, and re-layouts  1.34 us (2%)
    ppermute x8, waiting for transfers between devices, depth_swap(): return lax.ppermute(value, 'depth', [(i, i ^ bits) for i in range(count)])  16.1 us
    ppermute x8, starting transfers between devices, depth_swap(): return lax.ppermute(value, 'depth', [(i, i ^ bits) for i in range(count)])  12.6 us
    pallas_call x1, Pallas kernels, interior(): pl.pallas_call(functools.partial(interior_kernel, slice_total), grid=(row...  12.2 us
    ppermute x1, waiting for transfers between devices, shards(): lax.ppermute(to_left, 'lat', leftwards)  8.46 us
    pallas_call x2, Pallas kernels, border(): pl.pallas_call(functools.partial(border_kernel, start, slice_total), grid...  6.96 us
    pallas_call x1, Pallas kernels, edge_strips(): pl.pallas_call(functools.partial(strips_kernel, first), grid=(blocks,), i...  5.43 us
    ppermute x1, waiting for transfers between devices, shards(): lax.ppermute(image[:, :, :LANES], 'lat', [(x, (x + 1) % lat) for x in ran...  2.89 us
    ppermute x1, starting transfers between devices, shards(): lax.ppermute(to_left, 'lat', leftwards)  2.84 us
  transfers between devices with their start and end apart: 11, of which 9 were waited for; matrix products, arithmetic and copies ran while one was open for 1% of the time, Pallas kernels for 19%

profile of v4, /device:TPU:0, one launch (start us, length us, event | category | flops | bytes accessed | tf_op | source)
XLA Modules:
  0.0 81.8 jit_solution(11706850543604538023)
XLA Ops:
  0.7 5.4 %edge_strips0.1 = (bf16[16,256,128]{2,1,0:T(8,128)(2,1)}, bf16[16,256,128]{2,1,0:T(8,128)(2,1)}) custom-call(s32[1,4,4]{2,1,0:T(4,128)} %occ.7, bf16[1,16,512,512]{3,2,1,0:T(8,128)(2,1)} %last_lead.3, bf16[1,16,512,512]{3,2,1,0:T(8,128)(2,1)} %last_lead.3), custom_call_target="tpu_custom_call" | custom-call | tf_op jit(solution)/shard_map/edge_strips0/pallas_call | solution.py:55
  6.1 2.8 %collective-permute-start = (bf16[16,256,128]{2,1,0:T(8,128)(2,1)}, bf16[16,256,128]{2,1,0:T(8,128)(2,1)S(1)}, u32[]{:S(2)}, u32[]{:S(2)}) collective-permute-start(bf16[16,256,128]{2,1,0:T(8,128)(2,1)} %get-tuple-element.24), channel_id=1, source_target_pairs={{0,3},{1,0},{2,1},{3,2},{4,7},{5,4},{6,5},{7,6},{8,11},{9,8},{10,9... | collective-permute-start | bytes 3145736 | tf_op jit(solution)/shard_map/ppermute | solution.py:370
  9.0 1.3 %collective-permute-start.1 = (bf16[16,256,128]{2,1,0:T(8,128)(2,1)}, bf16[16,256,128]{2,1,0:T(8,128)(2,1)S(1)}, u32[]{:S(2)}, u32[]{:S(2)}) collective-permute-start(bf16[16,256,128]{2,1,0:T(8,128)(2,1)} %get-tuple-element.25), channel_id=1, source_target_pairs={{0,1},{1,2},{2,3},{4,5},{5,6},{6,7},{8,9},{9,10},{10,11},{12,13},{... | collective-permute-start | bytes 3145736 | tf_op jit(solution)/shard_map/ppermute | solution.py:371
  11.0 12.2 %interior.1 = (f32[2,256,384]{2,1,0:T(8,128)S(1)}, f32[2,256,384]{2,1,0:T(8,128)S(1)}, bf16[16,256,128]{2,1,0:T(8,128)(2,1)S(1)}, f32[16,128]{1,0:T(8,128)S(1)}) custom-call(s32[1,4,4]{2,1,0:T(4,128)S(1)} %copy-done, s32[1,16]{1,0:T(1,128)S(1)} %copy-done.1, f32[1,16]{1,0:T(1,128)S(1)} %copy-done.2, f32[1,16]{1,0:T(1,128)S(1)} %copy-done.3, ...), custom_call_target="tpu_custom_call" | custom-call | tf_op jit(solution)/shard_map/interior/pallas_call | solution.py:182
  23.3 8.5 %collective-permute-done.right_ref.right_lead = bf16[16,256,128]{2,1,0:T(8,128)(2,1)S(1)} collective-permute-done((bf16[16,256,128]{2,1,0:T(8,128)(2,1)}, bf16[16,256,128]{2,1,0:T(8,128)(2,1)S(1)}, u32[]{:S(2)}, u32[]{:S(2)}) %collective-permute-start) | collective-permute-done | bytes 1048608 | tf_op jit(solution)/shard_map/ppermute | solution.py:370
  31.7 1.3 %collective-permute-done.1.left_ref.left_lead = bf16[16,256,128]{2,1,0:T(8,128)(2,1)S(1)} collective-permute-done((bf16[16,256,128]{2,1,0:T(8,128)(2,1)}, bf16[16,256,128]{2,1,0:T(8,128)(2,1)S(1)}, u32[]{:S(2)}, u32[]{:S(2)}) %collective-permute-start.1) | collective-permute-done | bytes 1048608 | tf_op jit(solution)/shard_map/ppermute | solution.py:371
  33.0 0.0 collective-permute-start.2
  33.0 0.6 fusion.12
  37.2 3.5 %border0.1 = (f32[2,128,128]{2,1,0:T(8,128)S(1)}, f32[2,128,128]{2,1,0:T(8,128)S(1)}) custom-call(s32[1,4,4]{2,1,0:T(4,128)S(1)} %copy-done, s32[1,16]{1,0:T(1,128)S(1)} %copy-done.1, f32[1,16]{1,0:T(1,128)S(1)} %copy-done.2, f32[1,16]{1,0:T(1,128)S(1)} %copy-done.3, f32[1,16]{1,0:T(1,128)S(1)} %copy-done.4, f32[1]{0:T(128)S(6)} %copy.36.gain, ...), custom_call_target="tpu_custom_call" | custom-call | tf_op jit(solution)/shard_map/border0/pallas_call | solution.py:305
  40.8 0.2 multiply_add_fusion.1
  40.9 0.1 pad_maximum_fusion
  41.0 3.5 %border2.1 = (f32[2,128,128]{2,1,0:T(8,128)S(1)}, f32[2,128,128]{2,1,0:T(8,128)S(1)}) custom-call(s32[1,4,4]{2,1,0:T(4,128)S(1)} %copy-done, s32[1,16]{1,0:T(1,128)S(1)} %copy-done.1, f32[1,16]{1,0:T(1,128)S(1)} %copy-done.2, f32[1,16]{1,0:T(1,128)S(1)} %copy-done.3, f32[1,16]{1,0:T(1,128)S(1)} %copy-done.4, f32[1]{0:T(128)S(6)} %copy.36.gain, ...), custom_call_target="tpu_custom_call" | custom-call | tf_op jit(solution)/shard_map/border2/pallas_call | solution.py:305
  44.5 0.1 fusion.11
  44.5 0.1 fusion
  44.6 2.0 %collective-permute-start.6 = (f16[2,2,2,2,16,384]{5,4,1,2,3,0:T(8,128)(2,1)S(1)}, f16[2,2,2,2,16,384]{5,4,1,2,3,0:T(8,128)(2,1)S(1)}, u32[]{:S(2)}, u32[]{:S(2)}) collective-permute-start(f16[2,2,2,2,16,384]{5,4,1,2,3,0:T(8,128)(2,1)S(1)} %get-tuple-element.42), channel_id=1, source_target_pairs={{0,8},{4,12},{8,0},{12,4},{16,24},{20,28},{24,16},{28,20},{32,40},... | collective-permute-start | bytes 589832 | tf_op jit(solution)/shard_map/ppermute | solution.py:328
  46.6 0.3 collective-permute-start.3
  46.9 5.2 %collective-permute-done.6 = f16[2,2,2,2,16,384]{5,4,1,2,3,0:T(8,128)(2,1)S(1)} collective-permute-done((f16[2,2,2,2,16,384]{5,4,1,2,3,0:T(8,128)(2,1)S(1)}, f16[2,2,2,2,16,384]{5,4,1,2,3,0:T(8,128)(2,1)S(1)}, u32[]{:S(2)}, u32[]{:S(2)}) %collective-permute-start.6) | collective-permute-done | bytes 196640 | tf_op jit(solution)/shard_map/ppermute | solution.py:328
  52.2 0.1 multiply_add_fusion.3
  52.3 3.9 %collective-permute-start.7 = (f16[2,2,2,16,384]{4,3,1,2,0:T(8,128)(2,1)S(1)}, f16[2,2,2,16,384]{4,3,1,2,0:T(8,128)(2,1)S(1)}, u32[]{:S(2)}, u32[]{:S(2)}) collective-permute-start(f16[2,2,2,16,384]{4,3,1,2,0:T(8,128)(2,1)S(1)} %get-tuple-element.50), channel_id=1, source_target_pairs={{0,24},{4,28},{8,16},{12,20},{16,8},{20,12},{24,0},{28,4},{32,56},... | collective-permute-start | bytes 294920 | tf_op jit(solution)/shard_map/ppermute | solution.py:328
  56.3 0.1 multiply_add_fusion.5
  56.4 0.1 collective-permute-start.4
  56.5 2.5 %collective-permute-done.7 = f16[2,2,2,16,384]{4,3,1,2,0:T(8,128)(2,1)S(1)} collective-permute-done((f16[2,2,2,16,384]{4,3,1,2,0:T(8,128)(2,1)S(1)}, f16[2,2,2,16,384]{4,3,1,2,0:T(8,128)(2,1)S(1)}, u32[]{:S(2)}, u32[]{:S(2)}) %collective-permute-start.7) | collective-permute-done | bytes 98336 | tf_op jit(solution)/shard_map/ppermute | solution.py:328
  59.0 1.8 %collective-permute-done.4 = f16[2,2,2,2,16,128]{5,4,1,2,3,0:T(8,128)(2,1)S(1)} collective-permute-done((f16[2,2,2,2,16,128]{5,4,1,2,3,0:T(8,128)(2,1)S(1)}, f16[2,2,2,2,16,128]{5,4,1,2,3,0:T(8,128)(2,1)S(1)}, u32[]{:S(2)}, u32[]{:S(2)}) %collective-permute-start.4) | collective-permute-done | bytes 65568 | tf_op jit(solution)/shard_map/ppermute | solution.py:328
  60.8 1.5 %collective-permute-start.5 = (f16[2,2,2,16,128]{4,3,1,2,0:T(8,128)(2,1)S(1)}, f16[2,2,2,16,128]{4,3,1,2,0:T(8,128)(2,1)S(1)}, u32[]{:S(2)}, u32[]{:S(2)}) collective-permute-start(f16[2,2,2,16,128]{4,3,1,2,0:T(8,128)(2,1)S(1)} %get-tuple-element.68), channel_id=1, source_target_pairs={{0,24},{4,28},{8,16},{12,20},{16,8},{20,12},{24,0},{28,4},{32,56},... | collective-permute-start | bytes 98312 | tf_op jit(solution)/shard_map/ppermute | solution.py:328
  62.3 3.7 %collective-permute-done.5 = f16[2,2,2,16,128]{4,3,1,2,0:T(8,128)(2,1)S(1)} collective-permute-done((f16[2,2,2,16,128]{4,3,1,2,0:T(8,128)(2,1)S(1)}, f16[2,2,2,16,128]{4,3,1,2,0:T(8,128)(2,1)S(1)}, u32[]{:S(2)}, u32[]{:S(2)}) %collective-permute-start.5) | collective-permute-done | bytes 32800 | tf_op jit(solution)/shard_map/ppermute | solution.py:328
  66.1 1.7 %collective-permute-start.8 = (f16[2,2,16,512]{3,2,1,0:T(8,128)(2,1)S(1)}, f16[2,2,16,512]{3,2,1,0:T(8,128)(2,1)S(1)}, u32[]{:S(2)}, u32[]{:S(2)}) collective-permute-start(f16[2,2,16,512]{3,2,1,0:T(8,128)(2,1)S(1)} %get-tuple-element.54), channel_id=1, source_target_pairs={{0,32},{4,36},{8,40},{12,44},{16,48},{20,52},{24,56},{28,60},{32,0... | collective-permute-start | bytes 196616 | tf_op jit(solution)/shard_map/ppermute | solution.py:328
  69.0 1.5 %collective-permute-done.8 = f16[2,2,16,512]{3,2,1,0:T(8,128)(2,1)S(1)} collective-permute-done((f16[2,2,16,512]{3,2,1,0:T(8,128)(2,1)S(1)}, f16[2,2,16,512]{3,2,1,0:T(8,128)(2,1)S(1)}, u32[]{:S(2)}, u32[]{:S(2)}) %collective-permute-start.8) | collective-permute-done | bytes 65568 | tf_op jit(solution)/shard_map/ppermute | solution.py:328
  70.5 3.1 %collective-permute-start.9 = (f16[2,16,512]{2,1,0:T(8,128)(2,1)S(1)}, f16[2,16,512]{2,1,0:T(8,128)(2,1)S(1)}, u32[]{:S(2)}, u32[]{:S(2)}) collective-permute-start(f16[2,16,512]{2,1,0:T(8,128)(2,1)S(1)} %get-tuple-element.64), channel_id=1, source_target_pairs={{0,96},{4,100},{8,104},{12,108},{16,112},{20,116},{24,120},{28,124... | collective-permute-start | bytes 98312 | tf_op jit(solution)/shard_map/ppermute | solution.py:328
  74.3 1.4 %collective-permute-done.9 = f16[2,16,512]{2,1,0:T(8,128)(2,1)S(1)} collective-permute-done((f16[2,16,512]{2,1,0:T(8,128)(2,1)S(1)}, f16[2,16,512]{2,1,0:T(8,128)(2,1)S(1)}, u32[]{:S(2)}, u32[]{:S(2)}) %collective-permute-start.9) | collective-permute-done | bytes 32800 | tf_op jit(solution)/shard_map/ppermute | solution.py:328
  75.8 2.4 %collective-permute-start.10 = (f32[2,16,128]{2,1,0:T(8,128)S(1)}, f32[2,16,128]{2,1,0:T(8,128)S(1)}, u32[]{:S(2)}, u32[]{:S(2)}) collective-permute-start(f32[2,16,128]{2,1,0:T(8,128)S(1)} %pad_maximum_fusion.6), channel_id=1, source_target_pairs={{0,1},{1,2},{2,3},{3,0},{4,5},{5,6},{6,7},{7,4},{8,9},{9,10},{10,1... | collective-permute-start | bytes 49160 | tf_op jit(solution)/shard_map/ppermute | solution.py:389
  78.3 2.9 %collective-permute-done.10 = f32[2,16,128]{2,1,0:T(8,128)S(1)} collective-permute-done((f32[2,16,128]{2,1,0:T(8,128)S(1)}, f32[2,16,128]{2,1,0:T(8,128)S(1)}, u32[]{:S(2)}, u32[]{:S(2)}) %collective-permute-start.10) | collective-permute-done | bytes 16416 | tf_op jit(solution)/shard_map/ppermute | solution.py:389
  81.2 0.6 slice_bitcast_fusion.8
  (39 shorter events, 0.5 us)
Async XLA Ops:
  0.6 10.3 %copy-start = (s32[1,4,4]{2,1,0:T(4,128)S(1)}, s32[1,4,4]{2,1,0:T(4,128)}, u32[]{:S(2)}) copy-start(s32[1,4,4]{2,1,0:T(4,128)} %occ.7) | copy-start | bytes 196
  0.6 10.3 %copy-start.1 = (s32[1,16]{1,0:T(1,128)S(1)}, s32[1,16]{1,0:T(1,128)}, u32[]{:S(2)}) copy-start(s32[1,16]{1,0:T(1,128)} %offset.5) | copy-start | bytes 196
  0.7 10.3 %copy-start.2 = (f32[1,16]{1,0:T(1,128)S(1)}, f32[1,16]{1,0:T(1,128)}, u32[]{:S(2)}) copy-start(f32[1,16]{1,0:T(1,128)} %frac_lateral.5) | copy-start | bytes 196
  0.7 10.3 %copy-start.3 = (f32[1,16]{1,0:T(1,128)S(1)}, f32[1,16]{1,0:T(1,128)}, u32[]{:S(2)}) copy-start(f32[1,16]{1,0:T(1,128)} %frac_vertical.5) | copy-start | bytes 196
  0.7 10.3 %copy-start.4 = (f32[1,16]{1,0:T(1,128)S(1)}, f32[1,16]{1,0:T(1,128)}, u32[]{:S(2)}) copy-start(f32[1,16]{1,0:T(1,128)} %extinction.5) | copy-start | bytes 196
  0.7 10.3 %copy-start.5 = (s32[32]{0:T(128)S(1)}, s32[32]{0:T(128)}, u32[]{:S(2)}) copy-start(s32[32]{0:T(128)} %rank.1) | copy-start | bytes 388
  6.1 25.6 %collective-permute-start = (bf16[16,256,128]{2,1,0:T(8,128)(2,1)}, bf16[16,256,128]{2,1,0:T(8,128)(2,1)S(1)}, u32[]{:S(2)}, u32[]{:S(2)}) collective-permute-start(bf16[16,256,128]{2,1,0:T(8,128)(2,1)} %get-tuple-element.24), channel_id=1, source_target_pairs={{0,3},{1,0},{2,1},{3,2},{4,7},{5,4},{6,5},{7,6},{8,11},{9,8},{10,9... | collective-permute-start | bytes 3145736 | tf_op jit(solution)/shard_map/ppermute | solution.py:370
  9.0 24.0 %collective-permute-start.1 = (bf16[16,256,128]{2,1,0:T(8,128)(2,1)}, bf16[16,256,128]{2,1,0:T(8,128)(2,1)S(1)}, u32[]{:S(2)}, u32[]{:S(2)}) collective-permute-start(bf16[16,256,128]{2,1,0:T(8,128)(2,1)} %get-tuple-element.25), channel_id=1, source_target_pairs={{0,1},{1,2},{2,3},{4,5},{5,6},{6,7},{8,9},{9,10},{10,11},{12,13},{... | collective-permute-start | bytes 3145736 | tf_op jit(solution)/shard_map/ppermute | solution.py:371
  33.0 7.8 %collective-permute-start.2 = (f32[2,256,384]{2,1,0:T(8,128)S(1)}, f32[2,256,384]{2,1,0:T(8,128)S(1)}, u32[]{:S(2)}, u32[]{:S(2)}) collective-permute-start(f32[2,256,384]{2,1,0:T(8,128)S(1)} %get-tuple-element.32), channel_id=1, source_target_pairs={{0,4},{4,0},{8,12},{12,8},{16,20},{20,16},{24,28},{28,24},{32,36},... | collective-permute-start | bytes 2359304 | tf_op jit(solution)/shard_map/ppermute | solution.py:328
  44.6 7.6 %collective-permute-start.6 = (f16[2,2,2,2,16,384]{5,4,1,2,3,0:T(8,128)(2,1)S(1)}, f16[2,2,2,2,16,384]{5,4,1,2,3,0:T(8,128)(2,1)S(1)}, u32[]{:S(2)}, u32[]{:S(2)}) collective-permute-start(f16[2,2,2,2,16,384]{5,4,1,2,3,0:T(8,128)(2,1)S(1)} %get-tuple-element.42), channel_id=1, source_target_pairs={{0,8},{4,12},{8,0},{12,4},{16,24},{20,28},{24,16},{28,20},{32,40},... | collective-permute-start | bytes 589832 | tf_op jit(solution)/shard_map/ppermute | solution.py:328
  46.6 9.7 %collective-permute-start.3 = (f32[2,256,128]{2,1,0:T(8,128)S(1)}, f32[2,256,128]{2,1,0:T(8,128)S(1)}, u32[]{:S(2)}, u32[]{:S(2)}) collective-permute-start(f32[2,256,128]{2,1,0:T(8,128)S(1)} %pad_maximum_fusion.1), channel_id=1, source_target_pairs={{0,4},{4,0},{8,12},{12,8},{16,20},{20,16},{24,28},{28,24},{32,36},... | collective-permute-start | bytes 786440 | tf_op jit(solution)/shard_map/ppermute | solution.py:328
  52.3 6.6 %collective-permute-start.7 = (f16[2,2,2,16,384]{4,3,1,2,0:T(8,128)(2,1)S(1)}, f16[2,2,2,16,384]{4,3,1,2,0:T(8,128)(2,1)S(1)}, u32[]{:S(2)}, u32[]{:S(2)}) collective-permute-start(f16[2,2,2,16,384]{4,3,1,2,0:T(8,128)(2,1)S(1)} %get-tuple-element.50), channel_id=1, source_target_pairs={{0,24},{4,28},{8,16},{12,20},{16,8},{20,12},{24,0},{28,4},{32,56},... | collective-permute-start | bytes 294920 | tf_op jit(solution)/shard_map/ppermute | solution.py:328
  56.4 4.3 %collective-permute-start.4 = (f16[2,2,2,2,16,128]{5,4,1,2,3,0:T(8,128)(2,1)S(1)}, f16[2,2,2,2,16,128]{5,4,1,2,3,0:T(8,128)(2,1)S(1)}, u32[]{:S(2)}, u32[]{:S(2)}) collective-permute-start(f16[2,2,2,2,16,128]{5,4,1,2,3,0:T(8,128)(2,1)S(1)} %get-tuple-element.58), channel_id=1, source_target_pairs={{0,8},{4,12},{8,0},{12,4},{16,24},{20,28},{24,16},{28,20},{32,40},... | collective-permute-start | bytes 196616 | tf_op jit(solution)/shard_map/ppermute | solution.py:328
  60.8 5.2 %collective-permute-start.5 = (f16[2,2,2,16,128]{4,3,1,2,0:T(8,128)(2,1)S(1)}, f16[2,2,2,16,128]{4,3,1,2,0:T(8,128)(2,1)S(1)}, u32[]{:S(2)}, u32[]{:S(2)}) collective-permute-start(f16[2,2,2,16,128]{4,3,1,2,0:T(8,128)(2,1)S(1)} %get-tuple-element.68), channel_id=1, source_target_pairs={{0,24},{4,28},{8,16},{12,20},{16,8},{20,12},{24,0},{28,4},{32,56},... | collective-permute-start | bytes 98312 | tf_op jit(solution)/shard_map/ppermute | solution.py:328
  66.1 4.3 %collective-permute-start.8 = (f16[2,2,16,512]{3,2,1,0:T(8,128)(2,1)S(1)}, f16[2,2,16,512]{3,2,1,0:T(8,128)(2,1)S(1)}, u32[]{:S(2)}, u32[]{:S(2)}) collective-permute-start(f16[2,2,16,512]{3,2,1,0:T(8,128)(2,1)S(1)} %get-tuple-element.54), channel_id=1, source_target_pairs={{0,32},{4,36},{8,40},{12,44},{16,48},{20,52},{24,56},{28,60},{32,0... | collective-permute-start | bytes 196616 | tf_op jit(solution)/shard_map/ppermute | solution.py:328
  70.5 5.2 %collective-permute-start.9 = (f16[2,16,512]{2,1,0:T(8,128)(2,1)S(1)}, f16[2,16,512]{2,1,0:T(8,128)(2,1)S(1)}, u32[]{:S(2)}, u32[]{:S(2)}) collective-permute-start(f16[2,16,512]{2,1,0:T(8,128)(2,1)S(1)} %get-tuple-element.64), channel_id=1, source_target_pairs={{0,96},{4,100},{8,104},{12,108},{16,112},{20,116},{24,120},{28,124... | collective-permute-start | bytes 98312 | tf_op jit(solution)/shard_map/ppermute | solution.py:328
  75.8 5.3 %collective-permute-start.10 = (f32[2,16,128]{2,1,0:T(8,128)S(1)}, f32[2,16,128]{2,1,0:T(8,128)S(1)}, u32[]{:S(2)}, u32[]{:S(2)}) collective-permute-start(f32[2,16,128]{2,1,0:T(8,128)S(1)} %pad_maximum_fusion.6), channel_id=1, source_target_pairs={{0,1},{1,2},{2,3},{3,0},{4,5},{5,6},{6,7},{7,4},{8,9},{9,10},{10,1... | collective-permute-start | bytes 49160 | tf_op jit(solution)/shard_map/ppermute | solution.py:389

commit v5 on v4

--- a/solution.py
+++ b/solution.py
@@ -13,7 +13,6 @@
 HALF = SHIFT // 2
 LANES = 128
 PIECE = 16
-PARTNERS = (1, 2, 6, 8, 24)
 WIRE = jnp.float16
 WIRE_SCALE = 4096.0
 UNROLL = 16
@@ -85,11 +84,7 @@
     sum_ref[at] += (through - after) * slope
 
 
-def gray(index):
-    return index ^ (index >> 1)
-
-
-def finish(state, gain, swap, out_keep, out_send, tile, first=0):
+def finish(state, gain, swap, out_keep, out_send, tile):
     through_ref, sum_ref = state
     rows = out_keep.shape[1] * 2
     base = tile * rows
@@ -101,8 +96,7 @@
         colors.append(gain * (0.65 * alpha + 0.35 * sum_ref[at]))
     lanes = slice(tile * LANES, (tile + 1) * LANES)
     for q in range(rows // PIECE // 2):
-        place = 4 * (gray(first + q // 4) - first) + gray(q % 4)
-        at = slice(place * PIECE, (place + 1) * PIECE)
+        at = slice(q * PIECE, (q + 1) * PIECE)
         for i, values in enumerate((colors, alphas)):
             even, odd = values[2 * q], values[2 * q + 1]
             out_keep[i, at, lanes] = jnp.where(swap, odd, even)
@@ -136,12 +130,11 @@
 
         lax.fori_loop(0, slices, build, 0)
         me = lax.axis_index("depth")
-        rows_of_flags = [rank[me] < rank[jnp.bitwise_xor(me, partner)] for partner in PARTNERS]
-        z, y = (me // 2) % 4, me // 8
-        for place in (jnp.bitwise_xor(z, z // 2), jnp.bitwise_xor(y, y // 2)):
-            rows_of_flags += [place % 2 == 1, place // 2 == 1]
-        for i, flag in enumerate(rows_of_flags):
-            flags[i : i + 1] = jnp.full((1, LANES), jnp.where(flag, 1.0, 0.0), F32)
+        in_front = [rank[me] < rank[jnp.bitwise_xor(me, 1)]]
+        for span in (2, 4, 8, 16):
+            in_front += [rank[a] < rank[a + span] for a in range(0, rank.shape[0], 2 * span)]
+        for i, flag in enumerate(in_front):
+            flags[i : i + 1] = jnp.full((1, flags.shape[1]), jnp.where(flag, 1.0, 0.0), F32)
 
     through_ref[...] = jnp.ones_like(through_ref)
     sum_ref[...] = jnp.zeros_like(sum_ref)
@@ -191,18 +184,18 @@
             ),
         ],
         out_specs=[
-            pl.BlockSpec((2, step // 2, width), lambda b: (0, jnp.bitwise_xor(b, b // 2), 0))
+            pl.BlockSpec((2, step // 2, width), lambda b: (0, b, 0))
         ]
         * 2
         + [
             pl.BlockSpec((slices, 2 * LANES, LANES), lambda b: (0, 0, 0)),
-            pl.BlockSpec((16, LANES), lambda b: (0, 0)),
+            pl.BlockSpec((16, cols), lambda b: (0, 0)),
         ],
         out_shape=[
             image,
             image,
             jax.ShapeDtypeStruct((slices, 2 * LANES, LANES), BF16),
-            jax.ShapeDtypeStruct((16, LANES), F32),
+            jax.ShapeDtypeStruct((16, cols), F32),
         ],
         scratch_shapes=[pltpu.VMEM((step * (width // LANES), LANES), F32)] * 2,
         compiler_params=pltpu.CompilerParams(vmem_limit_bytes=32 * 2**20),
@@ -280,10 +273,10 @@
 
     over_slices(slices, one)
     swap = lax.axis_index("depth") % 2 == 1
-    finish(state, gain[0], swap, out_keep, out_send, 0, start)
-
-
-def border(density, small, weights, halos, start, blocks, slice_total):
+    finish(state, gain[0], swap, out_keep, out_send, 0)
+
+
+def border(density, small, weights, halos, above, start, blocks, slice_total):
     _, slices, _, cols = density.shape
     step = blocks * BLK
     last = cols // LANES - 1
@@ -298,9 +291,9 @@
             (1, slices, 16, LANES), lambda i: (0, 0, max(start * per - 1, 0), column)
         )
 
-    halo = pl.BlockSpec((slices, step // 2, LANES), lambda i: (0, start // blocks, 0))
-    above = max(start * per // 2 - 1, 0)
-    halo_lead = pl.BlockSpec((slices, 16, LANES), lambda i: (0, above, 0))
+    halo = pl.BlockSpec((slices, step // 2, LANES), lambda i: (0, 0, 0))
+    last_rows = above[0].shape[1] // 16 - 1
+    halo_lead = pl.BlockSpec((slices, 16, LANES), lambda i: (0, last_rows, 0))
     image = jax.ShapeDtypeStruct((2, step // 2, LANES), F32)
     return pl.pallas_call(
         functools.partial(border_kernel, start, slice_total),
@@ -313,45 +306,38 @@
         scratch_shapes=[pltpu.VMEM((step, LANES), F32)] * 2,
         compiler_params=pltpu.CompilerParams(vmem_limit_bytes=32 * 2**20),
         name=f"border{start}",
-    )(*small, weights, density, density, density, density, *halos, *halos)
+    )(*small, weights, density, density, density, density, *halos, *above)
 
 
 def over(mine, other, in_front):
-    color = jnp.where(in_front, mine[0], other[0]) + (
-        1.0 - jnp.where(in_front, mine[1], other[1])
-    ) * jnp.where(in_front, other[0], mine[0])
-    return jnp.stack([color, mine[1] + (1.0 - mine[1]) * other[1]])
-
-
-def depth_swap(value, bits):
+    color = mine[0] * (1.0 - (1.0 - in_front) * other[1]) + other[0] * (1.0 - in_front * mine[1])
+    return color, mine[1] + (1.0 - mine[1]) * other[1]
+
+
+def over_cores(keep, send, flags):
     count = lax.axis_size("depth")
-    return lax.ppermute(value, "depth", [(i, i ^ bits) for i in range(count)])
-
-
-def wire(value):
-    return (value * WIRE_SCALE).astype(WIRE)
-
-
-def unwire(value):
-    return value.astype(F32) * (1.0 / WIRE_SCALE)
-
-
-def over_cores(keep, send, flags):
-    return over(keep, depth_swap(send, PARTNERS[0]), flags[0, 0] > 0.0)
-
-
-def over_level(image, level, flags):
-    axis = 5 - level
-    second = flags[4 + level, 0] > 0.0
-    low = lax.index_in_dim(image, 0, axis, keepdims=False)
-    high = lax.index_in_dim(image, 1, axis, keepdims=False)
-    send = wire(jnp.where(second, low, high))
-    other = unwire(depth_swap(send, PARTNERS[level]))
-    return over(jnp.where(second, high, low), other, flags[level, 0] > 0.0)
-
-
-def by_chip(image):
-    return image.reshape(2, 2, 2, 2, 2, PIECE, image.shape[2])
+    other = lax.ppermute(send, "depth", [(i, i ^ 1) for i in range(count)])
+    return jnp.stack(over(keep, other, flags[0, : keep.shape[2]]))
+
+
+def over_chips(image, flags):
+    count = lax.axis_size("depth")
+    chips = count // 2
+    width = image.shape[2]
+    pieces = image.reshape(2, chips, PIECE, width).transpose(1, 0, 2, 3)
+    pieces = (pieces * WIRE_SCALE).astype(WIRE)
+    groups = [[2 * i + core for i in range(chips)] for core in range(2)]
+    pieces = lax.all_to_all(
+        pieces, "depth", 0, 0, axis_index_groups=groups, tiled=True
+    )
+    pieces = pieces.astype(F32) * (1.0 / WIRE_SCALE)
+    level = [(pieces[i, 0], pieces[i, 1]) for i in range(chips)]
+    row = 1
+    while len(level) > 1:
+        half = len(level) // 2
+        level = [over(level[2 * i], level[2 * i + 1], flags[row + i]) for i in range(half)]
+        row += half
+    return level[0]
 
 
 def shards(
@@ -363,34 +349,28 @@
     density = pltpu.with_memory_space_constraint(density, pltpu.HBM)
     small = (occupancy, shear_offsets, frac_lateral, frac_vertical, extinction, slab_gain)
     blocks = rows // BLK
+    half = blocks // 2
     rightwards = [(x, x + 1) for x in range(lat - 1)]
     leftwards = [(x, (x - 1) % lat) for x in range(lat)]
-    to_left, to_right = edge_strips(density, occupancy, 0, blocks)
-    halos = (
-        lax.ppermute(to_left, "lat", leftwards),
-        lax.ppermute(to_right, "lat", rightwards),
-    )
-    images = interior(density, small, view_rank, slice_total)
-    (keep, send, weights, flags), halos = lax.optimization_barrier((images, halos))
+    halos = []
+    for first, count in ((0, half), (half, blocks - half)):
+        to_left, to_right = edge_strips(density, occupancy, first, count)
+        halos.append(
+            (lax.ppermute(to_left, "lat", leftwards), lax.ppermute(to_right, "lat", rightwards))
+        )
+    keep, send, weights, flags = interior(density, small, view_rank, slice_total)
+    top = border(density, small, weights, halos[0], halos[0], 0, half, slice_total)
+    send, top = lax.optimization_barrier((send, top))
     inner = over_cores(keep, send, flags)
-    half = blocks // 2
-    top = border(density, small, weights, halos, 0, half, slice_total)
-    inner, weights = lax.optimization_barrier((inner, weights))
-    inner = over_level(by_chip(inner), 1, flags)
-    bottom = border(density, small, weights, halos, half, blocks - half, slice_total)
+    bottom = border(density, small, weights, halos[1], halos[0], half, blocks - half, slice_total)
     keep, send = (jnp.concatenate(p, axis=1) for p in zip(top, bottom))
-    edge = by_chip(over_cores(keep, send, flags))
-    edge = over_level(edge, 1, flags)
-    edge = over_level(edge, 2, flags)
-    inner = over_level(inner, 2, flags)
-    image = jnp.concatenate([edge, inner], axis=4)
-    image = over_level(image, 3, flags)
-    image = over_level(image, 4, flags)
+    edge = over_cores(keep, send, flags)
+    color, alpha = over_chips(jnp.concatenate([edge, inner], axis=2), flags)
+    image = jnp.stack([color, alpha])
     moved = lax.ppermute(image[:, :, :LANES], "lat", [(x, (x + 1) % lat) for x in range(lat)])
     lane = jnp.arange(LANES, dtype=jnp.int32)
     first = jnp.where(lane < HALF, moved, image[:, :, :LANES])
-    image = jnp.concatenate([first, image[:, :, LANES:]], axis=2)
-    return image[0], image[1]
+    return tuple(jnp.concatenate([first[i], image[i, :, LANES:]], axis=1) for i in range(2))
 
 
 def solution(mesh):

time: 82.1 us -> 65.1 us (0.79)
  waiting for transfers between devices: 28.7 us -> 16.7 us
  between operations: 7.12 us -> 1.54 us
  Pallas kernels: 24.6 us -> 25.7 us
  starting transfers between devices: 19.2 us -> 18.3 us
    ppermute x8 -> x2, waiting for transfers between devices: 16.1 us -> 1.11 us  [over_cores(): other = lax.ppermute(send, 'depth', [(i, i ^ 1) for i in range(count)])]
    all_to_all x0 -> x1, waiting for transfers between devices: none -> 11.9 us  [over_chips(): lax.all_to_all(pieces, 'depth', 0, 0, axis_index_groups=groups, tiled=True)]
    ppermute x8 -> x2, starting transfers between devices: 12.6 us -> 0.64 us  [over_cores(): other = lax.ppermute(send, 'depth', [(i, i ^ 1) for i in range(count)])]
    ppermute x1 -> x2, waiting for transfers between devices: 8.46 us -> 0.01 us  [shards(): lax.ppermute(to_left, 'lat', leftwards)]
    all_to_all x0 -> x1, starting transfers between devices: none -> 8.06 us  [over_chips(): lax.all_to_all(pieces, 'depth', 0, 0, axis_index_groups=groups, tiled=True)]
    ppermute x1 -> x2, starting transfers between devices: 1.34 us -> 4.64 us  [shards(): lax.ppermute(to_right, 'lat', rightwards)]
    ppermute x1 -> x2, waiting for transfers between devices: 1.27 us -> 0.01 us  [shards(): lax.ppermute(to_right, 'lat', rightwards)]
    pallas_call x1 -> x2, Pallas kernels: 5.43 us -> 6.58 us  [edge_strips(): pl.pallas_call(functools.partial(strips_kernel, first), grid=(blocks,), i...]
  transfers between devices with their start and end apart: 11 -> 8, of which waited for: 9 -> 3; matrix products, arithmetic and copies ran while one was open for 1% -> 0% of each run, Pallas kernels for 19% -> 35%
where the time goes in v5:
time: 65.1 us; the launch traced here: 64.7 us
  Pallas kernels  25.7 us (39%)
  starting transfers between devices  18.3 us (28%)
  waiting for transfers between devices  16.7 us (26%)
  between operations  1.54 us (2%)
  other arithmetic  1.45 us (2%)
  local copies, waits for them, and re-layouts  1 us (2%)
    pallas_call x1, Pallas kernels, interior(): pl.pallas_call(functools.partial(interior_kernel, slice_total), grid=(row...  12.1 us
    all_to_all x1, waiting for transfers between devices, over_chips(): lax.all_to_all(pieces, 'depth', 0, 0, axis_index_groups=groups, tiled=True)  11.9 us
    all_to_all x1, starting transfers between devices, over_chips(): lax.all_to_all(pieces, 'depth', 0, 0, axis_index_groups=groups, tiled=True)  8.06 us
    pallas_call x2, Pallas kernels, border(): pl.pallas_call(functools.partial(border_kernel, start, slice_total), grid...  7.04 us
    pallas_call x2, Pallas kernels, edge_strips(): pl.pallas_call(functools.partial(strips_kernel, first), grid=(blocks,), i...  6.58 us
    ppermute x2, starting transfers between devices, shards(): lax.ppermute(to_right, 'lat', rightwards)  4.64 us
    ppermute x1, waiting for transfers between devices, shards(): lax.ppermute(image[:, :, :LANES], 'lat', [(x, (x + 1) % lat) for x in ran...  3.65 us
    ppermute x2, starting transfers between devices, shards(): lax.ppermute(to_left, 'lat', leftwards)  3.62 us
  transfers between devices with their start and end apart: 8, of which 3 were waited for; matrix products, arithmetic and copies ran while one was open for 0% of the time, Pallas kernels for 35%

profile of v5, /device:TPU:0, one launch (start us, length us, event | category | flops | bytes accessed | tf_op | source)
XLA Modules:
  0.0 64.7 jit_solution(5280214228203606885)
XLA Ops:
  0.6 3.3 %edge_strips0.1 = (bf16[16,128,128]{2,1,0:T(8,128)(2,1)}, bf16[16,128,128]{2,1,0:T(8,128)(2,1)}) custom-call(s32[1,4,4]{2,1,0:T(4,128)} %occ.9, bf16[1,16,512,512]{3,2,1,0:T(8,128)(2,1)} %last_lead.3, bf16[1,16,512,512]{3,2,1,0:T(8,128)(2,1)} %last_lead.3), custom_call_target="tpu_custom_call" | custom-call | tf_op jit(solution)/shard_map/edge_strips0/pallas_call | solution.py:54
  3.9 2.9 %collective-permute-start = (bf16[16,128,128]{2,1,0:T(8,128)(2,1)}, bf16[16,128,128]{2,1,0:T(8,128)(2,1)S(1)}, u32[]{:S(2)}, u32[]{:S(2)}) collective-permute-start(bf16[16,128,128]{2,1,0:T(8,128)(2,1)} %get-tuple-element.19), channel_id=1, source_target_pairs={{0,3},{1,0},{2,1},{3,2},{4,7},{5,4},{6,5},{7,6},{8,11},{9,8},{10,9... | collective-permute-start | bytes 1572872 | tf_op jit(solution)/shard_map/ppermute | solution.py:359
  6.8 0.0 copy-start.4
  6.8 0.0 copy-start.5
  6.8 1.5 %collective-permute-start.1 = (bf16[16,128,128]{2,1,0:T(8,128)(2,1)}, bf16[16,128,128]{2,1,0:T(8,128)(2,1)S(1)}, u32[]{:S(2)}, u32[]{:S(2)}) collective-permute-start(bf16[16,128,128]{2,1,0:T(8,128)(2,1)} %get-tuple-element.20), channel_id=1, source_target_pairs={{0,1},{1,2},{2,3},{4,5},{5,6},{6,7},{8,9},{9,10},{10,11},{12,13},{... | collective-permute-start | bytes 1572872 | tf_op jit(solution)/shard_map/ppermute | solution.py:359
  8.3 3.3 %edge_strips2.1 = (bf16[16,128,128]{2,1,0:T(8,128)(2,1)}, bf16[16,128,128]{2,1,0:T(8,128)(2,1)}) custom-call(s32[1,4,4]{2,1,0:T(4,128)} %occ.9, bf16[1,16,512,512]{3,2,1,0:T(8,128)(2,1)} %last_lead.3, bf16[1,16,512,512]{3,2,1,0:T(8,128)(2,1)} %last_lead.3), custom_call_target="tpu_custom_call" | custom-call | tf_op jit(solution)/shard_map/edge_strips2/pallas_call | solution.py:54
  11.6 0.8 %collective-permute-start.2 = (bf16[16,128,128]{2,1,0:T(8,128)(2,1)}, bf16[16,128,128]{2,1,0:T(8,128)(2,1)S(1)}, u32[]{:S(2)}, u32[]{:S(2)}) collective-permute-start(bf16[16,128,128]{2,1,0:T(8,128)(2,1)} %get-tuple-element.24), channel_id=1, source_target_pairs={{0,3},{1,0},{2,1},{3,2},{4,7},{5,4},{6,5},{7,6},{8,11},{9,8},{10,9... | collective-permute-start | bytes 1572872 | tf_op jit(solution)/shard_map/ppermute | solution.py:359
  12.3 3.2 %collective-permute-start.3 = (bf16[16,128,128]{2,1,0:T(8,128)(2,1)}, bf16[16,128,128]{2,1,0:T(8,128)(2,1)S(1)}, u32[]{:S(2)}, u32[]{:S(2)}) collective-permute-start(bf16[16,128,128]{2,1,0:T(8,128)(2,1)} %get-tuple-element.25), channel_id=1, source_target_pairs={{0,1},{1,2},{2,3},{4,5},{5,6},{6,7},{8,9},{9,10},{10,11},{12,13},{... | collective-permute-start | bytes 1572872 | tf_op jit(solution)/shard_map/ppermute | solution.py:359
  16.2 0.0 copy-done
  16.2 0.0 copy-done.1
  16.2 12.1 %interior.1 = (f32[2,256,384]{2,1,0:T(8,128)S(1)}, f32[2,256,384]{2,1,0:T(8,128)S(1)}, bf16[16,256,128]{2,1,0:T(8,128)(2,1)S(1)}, f32[16,512]{1,0:T(8,128)S(1)}) custom-call(s32[1,4,4]{2,1,0:T(4,128)S(1)} %copy-done, s32[1,16]{1,0:T(1,128)S(1)} %copy-done.1, f32[1,16]{1,0:T(1,128)S(1)} %copy-done.2, f32[1,16]{1,0:T(1,128)S(1)} %copy-done.3, ...), custom_call_target="tpu_custom_call" | custom-call | tf_op jit(solution)/shard_map/interior/pallas_call | solution.py:175
  28.3 0.0 collective-permute-done.right_ref.right_lead
  28.3 0.0 collective-permute-done.1.left_ref.left_lead
  28.3 3.5 %border0.1 = (f32[2,128,128]{2,1,0:T(8,128)S(1)}, f32[2,128,128]{2,1,0:T(8,128)S(1)}) custom-call(s32[1,4,4]{2,1,0:T(4,128)S(1)} %copy-done, s32[1,16]{1,0:T(1,128)S(1)} %copy-done.1, f32[1,16]{1,0:T(1,128)S(1)} %copy-done.2, f32[1,16]{1,0:T(1,128)S(1)} %copy-done.3, f32[1,16]{1,0:T(1,128)S(1)} %copy-done.4, f32[1]{0:T(128)S(6)} %copy.14.gain, ...), custom_call_target="tpu_custom_call" | custom-call | tf_op jit(solution)/shard_map/border0/pallas_call | solution.py:298
  31.8 0.1 collective-permute-start.5
  31.9 0.0 collective-permute-done.2.right_ref
  31.9 0.0 collective-permute-done.3.left_ref
  31.9 3.5 %border2.1 = (f32[2,128,128]{2,1,0:T(8,128)S(1)}, f32[2,128,128]{2,1,0:T(8,128)S(1)}) custom-call(s32[1,4,4]{2,1,0:T(4,128)S(1)} %copy-done, s32[1,16]{1,0:T(1,128)S(1)} %copy-done.1, f32[1,16]{1,0:T(1,128)S(1)} %copy-done.2, f32[1,16]{1,0:T(1,128)S(1)} %copy-done.3, f32[1,16]{1,0:T(1,128)S(1)} %copy-done.4, f32[1]{0:T(128)S(6)} %copy.14.gain, ...), custom_call_target="tpu_custom_call" | custom-call | tf_op jit(solution)/shard_map/border2/pallas_call | solution.py:298
  35.5 0.6 collective-permute-start.4
  36.1 1.1 %collective-permute-done.4 = f32[2,256,128]{2,1,0:T(8,128)S(1)} collective-permute-done((f32[2,256,128]{2,1,0:T(8,128)S(1)}, f32[2,256,128]{2,1,0:T(8,128)S(1)}, u32[]{:S(2)}, u32[]{:S(2)}) %collective-permute-start.4) | collective-permute-done | bytes 262176 | tf_op jit(solution)/shard_map/ppermute | solution.py:319
  37.3 0.0 collective-permute-done.5
  37.3 0.2 fusion.1
  37.5 0.1 fusion
  37.6 0.9 %copy.12 = f16[2,16,16,512]{3,2,0,1:T(8,128)(2,1)} copy(f16[2,16,16,512]{3,2,1,0:T(8,128)(2,1)S(1)} %bitcast.318) | data formatting | bytes 1048576 | tf_op jit(solution)/shard_map/convert_element_type | solution.py:328
  38.5 8.1 %all-to-all-start = ((f16[16,2,16,512]{3,2,1,0:T(8,128)(2,1)}), f16[16,2,16,512]{3,2,1,0:T(8,128)(2,1)S(1)}, u32[]{:S(2)}, u32[]{:S(2)}) async-start(f16[16,2,16,512]{3,2,1,0:T(8,128)(2,1)} %bitcast.317), calls=%async_computation | async-start | bytes 1048576 | tf_op jit(solution)/shard_map/all_to_all | solution.py:330
  46.7 11.9 %all-to-all-done = f16[16,2,16,512]{3,2,1,0:T(8,128)(2,1)S(1)} async-done(((f16[16,2,16,512]{3,2,1,0:T(8,128)(2,1)}), f16[16,2,16,512]{3,2,1,0:T(8,128)(2,1)S(1)}, u32[]{:S(2)}, u32[]{:S(2)}) %all-to-all-start) | async-done | bytes 524320 | tf_op jit(solution)/shard_map/all_to_all | solution.py:330
  58.6 0.2 convert_multiply_fusion
  58.7 0.1 multiply_add_fusion.2
  58.8 0.2 fusion.10
  59.0 1.4 %collective-permute-start.6 = (f32[2,16,128]{2,1,0:T(8,128)S(1)}, f32[2,16,128]{2,1,0:T(8,128)S(1)}, u32[]{:S(2)}, u32[]{:S(2)}) collective-permute-start(f32[2,16,128]{2,1,0:T(8,128)S(1)} %pad_maximum_fusion.3), channel_id=1, source_target_pairs={{0,1},{1,2},{2,3},{3,0},{4,5},{5,6},{6,7},{7,4},{8,9},{9,10},{10,1... | collective-permute-start | bytes 49160 | tf_op jit(solution)/shard_map/ppermute | solution.py:370
  60.4 3.7 %collective-permute-done.6 = f32[2,16,128]{2,1,0:T(8,128)S(1)} collective-permute-done((f32[2,16,128]{2,1,0:T(8,128)S(1)}, f32[2,16,128]{2,1,0:T(8,128)S(1)}, u32[]{:S(2)}, u32[]{:S(2)}) %collective-permute-start.6) | collective-permute-done | bytes 16416 | tf_op jit(solution)/shard_map/ppermute | solution.py:370
  64.1 0.6 pad_maximum_fusion.1
  (22 shorter events, 0.2 us)
Async XLA Ops:
  3.9 24.4 %collective-permute-start = (bf16[16,128,128]{2,1,0:T(8,128)(2,1)}, bf16[16,128,128]{2,1,0:T(8,128)(2,1)S(1)}, u32[]{:S(2)}, u32[]{:S(2)}) collective-permute-start(bf16[16,128,128]{2,1,0:T(8,128)(2,1)} %get-tuple-element.19), channel_id=1, source_target_pairs={{0,3},{1,0},{2,1},{3,2},{4,7},{5,4},{6,5},{7,6},{8,11},{9,8},{10,9... | collective-permute-start | bytes 1572872 | tf_op jit(solution)/shard_map/ppermute | solution.py:359
  6.8 9.4 %copy-start = (s32[1,4,4]{2,1,0:T(4,128)S(1)}, s32[1,4,4]{2,1,0:T(4,128)}, u32[]{:S(2)}) copy-start(s32[1,4,4]{2,1,0:T(4,128)} %occ.9) | copy-start | bytes 196
  6.8 9.4 %copy-start.1 = (s32[1,16]{1,0:T(1,128)S(1)}, s32[1,16]{1,0:T(1,128)}, u32[]{:S(2)}) copy-start(s32[1,16]{1,0:T(1,128)} %offset.5) | copy-start | bytes 196
  6.8 9.4 %copy-start.2 = (f32[1,16]{1,0:T(1,128)S(1)}, f32[1,16]{1,0:T(1,128)}, u32[]{:S(2)}) copy-start(f32[1,16]{1,0:T(1,128)} %frac_lateral.5) | copy-start | bytes 196
  6.8 9.4 %copy-start.3 = (f32[1,16]{1,0:T(1,128)S(1)}, f32[1,16]{1,0:T(1,128)}, u32[]{:S(2)}) copy-start(f32[1,16]{1,0:T(1,128)} %frac_vertical.5) | copy-start | bytes 196
  6.8 9.4 %copy-start.4 = (f32[1,16]{1,0:T(1,128)S(1)}, f32[1,16]{1,0:T(1,128)}, u32[]{:S(2)}) copy-start(f32[1,16]{1,0:T(1,128)} %extinction.5) | copy-start | bytes 196
  6.8 9.4 %copy-start.5 = (s32[32]{0:T(128)S(1)}, s32[32]{0:T(128)}, u32[]{:S(2)}) copy-start(s32[32]{0:T(128)} %rank.1) | copy-start | bytes 388
  6.8 21.5 %collective-permute-start.1 = (bf16[16,128,128]{2,1,0:T(8,128)(2,1)}, bf16[16,128,128]{2,1,0:T(8,128)(2,1)S(1)}, u32[]{:S(2)}, u32[]{:S(2)}) collective-permute-start(bf16[16,128,128]{2,1,0:T(8,128)(2,1)} %get-tuple-element.20), channel_id=1, source_target_pairs={{0,1},{1,2},{2,3},{4,5},{5,6},{6,7},{8,9},{9,10},{10,11},{12,13},{... | collective-permute-start | bytes 1572872 | tf_op jit(solution)/shard_map/ppermute | solution.py:359
  11.6 20.4 %collective-permute-start.2 = (bf16[16,128,128]{2,1,0:T(8,128)(2,1)}, bf16[16,128,128]{2,1,0:T(8,128)(2,1)S(1)}, u32[]{:S(2)}, u32[]{:S(2)}) collective-permute-start(bf16[16,128,128]{2,1,0:T(8,128)(2,1)} %get-tuple-element.24), channel_id=1, source_target_pairs={{0,3},{1,0},{2,1},{3,2},{4,7},{5,4},{6,5},{7,6},{8,11},{9,8},{10,9... | collective-permute-start | bytes 1572872 | tf_op jit(solution)/shard_map/ppermute | solution.py:359
  12.3 19.6 %collective-permute-start.3 = (bf16[16,128,128]{2,1,0:T(8,128)(2,1)}, bf16[16,128,128]{2,1,0:T(8,128)(2,1)S(1)}, u32[]{:S(2)}, u32[]{:S(2)}) collective-permute-start(bf16[16,128,128]{2,1,0:T(8,128)(2,1)} %get-tuple-element.25), channel_id=1, source_target_pairs={{0,1},{1,2},{2,3},{4,5},{5,6},{6,7},{8,9},{9,10},{10,11},{12,13},{... | collective-permute-start | bytes 1572872 | tf_op jit(solution)/shard_map/ppermute | solution.py:359
  31.8 5.5 %collective-permute-start.5 = (f32[2,256,384]{2,1,0:T(8,128)S(1)}, f32[2,256,384]{2,1,0:T(8,128)S(1)}, u32[]{:S(2)}, u32[]{:S(2)}) collective-permute-start(f32[2,256,384]{2,1,0:T(8,128)S(1)} %get-tuple-element.31), channel_id=1, source_target_pairs={{0,4},{4,0},{8,12},{12,8},{16,20},{20,16},{24,28},{28,24},{32,36},... | collective-permute-start | bytes 2359304 | tf_op jit(solution)/shard_map/ppermute | solution.py:319
  35.5 1.7 %collective-permute-start.4 = (f32[2,256,128]{2,1,0:T(8,128)S(1)}, f32[2,256,128]{2,1,0:T(8,128)S(1)}, u32[]{:S(2)}, u32[]{:S(2)}) collective-permute-start(f32[2,256,128]{2,1,0:T(8,128)S(1)} %pad_maximum_fusion), channel_id=1, source_target_pairs={{0,4},{4,0},{8,12},{12,8},{16,20},{20,16},{24,28},{28,24},{32,36},... | collective-permute-start | bytes 786440 | tf_op jit(solution)/shard_map/ppermute | solution.py:319
  38.5 20.1 %all-to-all-start = ((f16[16,2,16,512]{3,2,1,0:T(8,128)(2,1)}), f16[16,2,16,512]{3,2,1,0:T(8,128)(2,1)S(1)}, u32[]{:S(2)}, u32[]{:S(2)}) async-start(f16[16,2,16,512]{3,2,1,0:T(8,128)(2,1)} %bitcast.317), calls=%async_computation | async-start | bytes 1048576 | tf_op jit(solution)/shard_map/all_to_all | solution.py:330
  59.0 5.0 %collective-permute-start.6 = (f32[2,16,128]{2,1,0:T(8,128)S(1)}, f32[2,16,128]{2,1,0:T(8,128)S(1)}, u32[]{:S(2)}, u32[]{:S(2)}) collective-permute-start(f32[2,16,128]{2,1,0:T(8,128)S(1)} %pad_maximum_fusion.3), channel_id=1, source_target_pairs={{0,1},{1,2},{2,3},{3,0},{4,5},{5,6},{6,7},{7,4},{8,9},{9,10},{10,1... | collective-permute-start | bytes 49160 | tf_op jit(solution)/shard_map/ppermute | solution.py:370

commit v6 on v5

--- a/solution.py
+++ b/solution.py
@@ -15,7 +15,8 @@
 PIECE = 16
 WIRE = jnp.float16
 WIRE_SCALE = 4096.0
-UNROLL = 16
+STEPS = 4
+TAIL = 1
 LOG2E = math.log2(math.e)
 SMEM = pltpu.SMEM
 F32 = jnp.float32
@@ -32,19 +33,33 @@
 
 
 def strips_kernel(first_block, occ, x_first, x_last, to_left, to_right):
-    half = x_first.shape[2] // 2
-    block = first_block + pl.program_id(0)
+    half = BLK // 2
+    count = x_first.shape[1]
     k = lax.broadcasted_iota(jnp.int32, (2 * LANES, LANES), 0)
     n = lax.broadcasted_iota(jnp.int32, (2 * LANES, LANES), 1)
     for ref, out, column, source in (
         (x_first, to_left, 0, jnp.where(n < HALF, n, n + HALF)),
         (x_last, to_right, occ.shape[2] - 1, jnp.where(n < HALF, n + LANES + HALF, n)),
     ):
-        occupied = occ[0, block, column].astype(F32)
-        pick = jnp.where(k == source, occupied, 0.0).astype(BF16)
-        for s in range(ref.shape[1]):
-            rows = jnp.concatenate([ref[0, s, :half], ref[0, s, half:]], axis=1)
-            out[s] = jnp.dot(rows, pick, preferred_element_type=F32).astype(BF16)
+        for b in range(x_first.shape[2] // BLK):
+            occupied = occ[0, first_block + b, column].astype(F32)
+            pick = jnp.where(k == source, occupied, 0.0).astype(BF16)
+            top, bottom = slice(b * BLK, b * BLK + half), slice(b * BLK + half, (b + 1) * BLK)
+            for u in range(count):
+                rows = jnp.concatenate([ref[0, u, top], ref[0, u, bottom]], axis=1)
+                moved = jnp.dot(rows, pick, preferred_element_type=F32)
+                out[u, b * half : (b + 1) * half] = moved.astype(BF16)
+
+
+def column_tile(slices, first, blocks, column):
+    shape = tuple(pl.Element(n) for n in (1, slices // STEPS, blocks * BLK, LANES))
+    return pl.BlockSpec(
+        shape, lambda i: (0, i * (slices // STEPS), first * BLK, column * LANES)
+    )
+
+
+def whole():
+    return pl.BlockSpec(memory_space=pltpu.VMEM)
 
 
 def edge_strips(density, occupancy, first, blocks):
@@ -53,13 +68,16 @@
     last = cols // LANES - 1
     return pl.pallas_call(
         functools.partial(strips_kernel, first),
-        grid=(blocks,),
+        grid=(STEPS,),
         in_specs=[
             pl.BlockSpec(memory_space=SMEM),
-            pl.BlockSpec((1, slices, BLK, LANES), lambda i: (0, 0, first + i, 0)),
-            pl.BlockSpec((1, slices, BLK, LANES), lambda i: (0, 0, first + i, last)),
+            column_tile(slices, first, blocks, 0),
+            column_tile(slices, first, blocks, last),
         ],
-        out_specs=[pl.BlockSpec((slices, BLK // 2, LANES), lambda i: (0, i, 0))] * 2,
+        out_specs=[
+            pl.BlockSpec((slices // STEPS, blocks * BLK // 2, LANES), lambda i: (i, 0, 0))
+        ]
+        * 2,
         out_shape=[shape, shape],
         name=f"edge_strips{first}",
     )(occupancy, density, density)
@@ -86,7 +104,7 @@
 
 def finish(state, gain, swap, out_keep, out_send, tile):
     through_ref, sum_ref = state
-    rows = out_keep.shape[1] * 2
+    rows = out_keep.shape[0] * 2 * PIECE
     base = tile * rows
     alphas, colors = [], []
     for p in range(rows // PIECE):
@@ -96,11 +114,10 @@
         colors.append(gain * (0.65 * alpha + 0.35 * sum_ref[at]))
     lanes = slice(tile * LANES, (tile + 1) * LANES)
     for q in range(rows // PIECE // 2):
-        at = slice(q * PIECE, (q + 1) * PIECE)
         for i, values in enumerate((colors, alphas)):
             even, odd = values[2 * q], values[2 * q + 1]
-            out_keep[i, at, lanes] = jnp.where(swap, odd, even)
-            out_send[i, at, lanes] = jnp.where(swap, even, odd)
+            out_keep[q, i, :, lanes] = jnp.where(swap, odd, even)
+            out_send[q, i, :, lanes] = jnp.where(swap, even, odd)
 
 
 def splat(value):
@@ -108,7 +125,8 @@
 
 
 def over_slices(slices, one):
-    lax.fori_loop(0, slices, one, 0, unroll=UNROLL)
+    for s in range(slices):
+        one(s, 0)
 
 
 def interior_kernel(
@@ -171,7 +189,8 @@
     _, slices, rows, cols = density.shape
     step = BLK
     width = cols - LANES
-    image = jax.ShapeDtypeStruct((2, rows // 2, width), F32)
+    pieces = step // (2 * PIECE)
+    image = jax.ShapeDtypeStruct((rows // (2 * PIECE), 2, PIECE, width), F32)
     return pl.pallas_call(
         functools.partial(interior_kernel, slice_total),
         grid=(rows // step,),
@@ -184,7 +203,7 @@
             ),
         ],
         out_specs=[
-            pl.BlockSpec((2, step // 2, width), lambda b: (0, b, 0))
+            pl.BlockSpec((pieces, 2, PIECE, width), lambda b: (b, 0, 0, 0))
         ]
         * 2
         + [
@@ -208,14 +227,19 @@
     first_ref, last_ref, first_lead, last_lead, right_ref, left_ref, right_lead, left_lead,
     out_keep, out_send, through_ref, sum_ref,
 ):
-    slices, half = first_ref.shape[1], BLK // 2
+    count, half = first_ref.shape[1], BLK // 2
+    step = pl.program_id(0)
     last_tile = occ.shape[2] - 1
     follows = jnp.where(lax.axis_index("lat") < lax.axis_size("lat") - 1, 1, 0)
     own_lanes = lax.broadcasted_iota(jnp.int32, (1, LANES), 1) >= HALF
     refs = (frac_vertical, extinction, slice_total)
     state = (through_ref, sum_ref)
-    through_ref[...] = jnp.ones_like(through_ref)
-    sum_ref[...] = jnp.zeros_like(sum_ref)
+
+    @pl.when(step == 0)
+    def _():
+        through_ref[...] = jnp.ones_like(through_ref)
+        sum_ref[...] = jnp.zeros_like(sum_ref)
+
     blocks = first_ref.shape[2] // BLK
     masks = []
     for b in range(start - 1, start + blocks):
@@ -228,7 +252,8 @@
         )
     zero = jnp.zeros((16, LANES), BF16)
 
-    def one(s, _):
+    def one(u, _):
+        s = step * count + u
         before, own = weights[s, :LANES], weights[s, LANES:]
         turn = lambda w: jnp.concatenate([w[HALF:], w[:HALF]], axis=0)
         near = jnp.concatenate([before, own], axis=0)
@@ -239,7 +264,7 @@
             parts = [above] if above is not None else []
             for b in range(blocks):
                 at = slice(b * BLK + top, b * BLK + top + half)
-                parts.append(ref[0, s, at] * masks[b + 1][side])
+                parts.append(ref[0, u, at] * masks[b + 1][side])
             return jnp.concatenate(parts, axis=0) if len(parts) > 1 else parts[0]
 
         def lateral(first, last, right, left, w_left, w_right):
@@ -256,10 +281,10 @@
             halves(first_ref, 0, 0, None), halves(last_ref, 1, 0, None), right, left, near, near
         )
         x_far = lateral(
-            halves(first_ref, 0, half, first_lead[0, s] * masks[0][0]),
-            halves(last_ref, 1, half, last_lead[0, s] * masks[0][1]),
-            jnp.concatenate([right_lead[s] if start else zero, right], axis=0),
-            jnp.concatenate([left_lead[s] if start else zero, left], axis=0),
+            halves(first_ref, 0, half, first_lead[0, u] * masks[0][0]),
+            halves(last_ref, 1, half, last_lead[0, u] * masks[0][1]),
+            jnp.concatenate([right_lead[s, -16:] if start else zero, right], axis=0),
+            jnp.concatenate([left_lead[s, -16:] if start else zero, left], axis=0),
             far_left,
             far_right,
         )
@@ -271,37 +296,33 @@
             shade(s, x, b * BLK, state, refs)
         return 0
 
-    over_slices(slices, one)
-    swap = lax.axis_index("depth") % 2 == 1
-    finish(state, gain[0], swap, out_keep, out_send, 0)
+    over_slices(count, one)
+
+    @pl.when(step == pl.num_programs(0) - 1)
+    def _():
+        swap = lax.axis_index("depth") % 2 == 1
+        finish(state, gain[0], swap, out_keep, out_send, 0)
 
 
 def border(density, small, weights, halos, above, start, blocks, slice_total):
     _, slices, _, cols = density.shape
     step = blocks * BLK
     last = cols // LANES - 1
-    per = BLK // 16
-
-    def body(column):
-        shape = tuple(pl.Element(n) for n in (1, slices, step, LANES))
-        return pl.BlockSpec(shape, lambda i: (0, 0, start * BLK, column * LANES))
+    lead_rows = max(start * BLK // 16 - 1, 0)
 
     def lead(column):
-        return pl.BlockSpec(
-            (1, slices, 16, LANES), lambda i: (0, 0, max(start * per - 1, 0), column)
-        )
-
-    halo = pl.BlockSpec((slices, step // 2, LANES), lambda i: (0, 0, 0))
-    last_rows = above[0].shape[1] // 16 - 1
-    halo_lead = pl.BlockSpec((slices, 16, LANES), lambda i: (0, last_rows, 0))
-    image = jax.ShapeDtypeStruct((2, step // 2, LANES), F32)
+        return pl.BlockSpec((1, slices // STEPS, 16, LANES), lambda i: (0, i, lead_rows, column))
+
+    image = jax.ShapeDtypeStruct((step // (2 * PIECE), 2, PIECE, LANES), F32)
     return pl.pallas_call(
         functools.partial(border_kernel, start, slice_total),
-        grid=(1,),
+        grid=(STEPS,),
         in_specs=small_specs()
-        + [pl.BlockSpec((slices, 2 * LANES, LANES), lambda i: (0, 0, 0))]
-        + [body(0), body(last), lead(0), lead(last), halo, halo, halo_lead, halo_lead],
-        out_specs=[pl.BlockSpec((2, step // 2, LANES), lambda i: (0, 0, 0))] * 2,
+        + [whole()]
+        + [column_tile(slices, start, blocks, column) for column in (0, last)]
+        + [lead(0), lead(last)]
+        + [whole()] * 4,
+        out_specs=[whole()] * 2,
         out_shape=[image, image],
         scratch_shapes=[pltpu.VMEM((step, LANES), F32)] * 2,
         compiler_params=pltpu.CompilerParams(vmem_limit_bytes=32 * 2**20),
@@ -317,14 +338,13 @@
 def over_cores(keep, send, flags):
     count = lax.axis_size("depth")
     other = lax.ppermute(send, "depth", [(i, i ^ 1) for i in range(count)])
-    return jnp.stack(over(keep, other, flags[0, : keep.shape[2]]))
-
-
-def over_chips(image, flags):
+    front = flags[0, : keep.shape[3]]
+    return jnp.stack(over((keep[:, 0], keep[:, 1]), (other[:, 0], other[:, 1]), front), axis=1)
+
+
+def over_chips(pieces, flags):
     count = lax.axis_size("depth")
     chips = count // 2
-    width = image.shape[2]
-    pieces = image.reshape(2, chips, PIECE, width).transpose(1, 0, 2, 3)
     pieces = (pieces * WIRE_SCALE).astype(WIRE)
     groups = [[2 * i + core for i in range(chips)] for core in range(2)]
     pieces = lax.all_to_all(
@@ -349,7 +369,7 @@
     density = pltpu.with_memory_space_constraint(density, pltpu.HBM)
     small = (occupancy, shear_offsets, frac_lateral, frac_vertical, extinction, slab_gain)
     blocks = rows // BLK
-    half = blocks // 2
+    half = blocks - TAIL
     rightwards = [(x, x + 1) for x in range(lat - 1)]
     leftwards = [(x, (x - 1) % lat) for x in range(lat)]
     halos = []
@@ -363,9 +383,9 @@
     send, top = lax.optimization_barrier((send, top))
     inner = over_cores(keep, send, flags)
     bottom = border(density, small, weights, halos[1], halos[0], half, blocks - half, slice_total)
-    keep, send = (jnp.concatenate(p, axis=1) for p in zip(top, bottom))
+    keep, send = (jnp.concatenate(p, axis=0) for p in zip(top, bottom))
     edge = over_cores(keep, send, flags)
-    color, alpha = over_chips(jnp.concatenate([edge, inner], axis=2), flags)
+    color, alpha = over_chips(jnp.concatenate([edge, inner], axis=3), flags)
     image = jnp.stack([color, alpha])
     moved = lax.ppermute(image[:, :, :LANES], "lat", [(x, (x + 1) % lat) for x in range(lat)])
     lane = jnp.arange(LANES, dtype=jnp.int32)

time: 65.1 us -> 68 us (1.045)
  Pallas kernels: 25.7 us -> 28.6 us
  local copies, waits for them, and re-layouts: 1 us -> 0.1 us
  other arithmetic: 1.45 us -> 2.21 us
    pallas_call x2, Pallas kernels: 6.58 us -> 8.44 us  [edge_strips(): pl.pallas_call(functools.partial(strips_kernel, first), grid=(STEPS,), in...]
    pallas_call x2, Pallas kernels: 7.04 us -> 8.21 us  [border(): pl.pallas_call(functools.partial(border_kernel, start, slice_total), grid...]
    convert_element_type x1 -> x0, local copies, waits for them, and re-layouts: 0.92 us -> none  [over_chips(): pieces = (pieces * WIRE_SCALE).astype(WIRE)]
    convert_element_type x1, other arithmetic: 0.09 us -> 0.9 us  [over_chips(): pieces = (pieces * WIRE_SCALE).astype(WIRE)]
where the time goes in v6:
time: 68 us; the launch traced here: 67.5 us
  Pallas kernels  28.6 us (42%)
  starting transfers between devices  18.3 us (27%)
  waiting for transfers between devices  16.7 us (25%)
  other arithmetic  2.21 us (3%)
  between operations  1.53 us (2%)
    pallas_call x1, Pallas kernels, interior(): pl.pallas_call(functools.partial(interior_kernel, slice_total), grid=(row...  11.9 us
    all_to_all x1, waiting for transfers between devices, over_chips(): lax.all_to_all(pieces, 'depth', 0, 0, axis_index_groups=groups, tiled=True)  11.9 us
    pallas_call x2, Pallas kernels, edge_strips(): pl.pallas_call(functools.partial(strips_kernel, first), grid=(STEPS,), in...  8.44 us
    pallas_call x2, Pallas kernels, border(): pl.pallas_call(functools.partial(border_kernel, start, slice_total), grid...  8.21 us
    all_to_all x1, starting transfers between devices, over_chips(): lax.all_to_all(pieces, 'depth', 0, 0, axis_index_groups=groups, tiled=True)  8.06 us
    ppermute x2, starting transfers between devices, shards(): lax.ppermute(to_right, 'lat', rightwards)  4.62 us
    ppermute x1, waiting for transfers between devices, shards(): lax.ppermute(image[:, :, :LANES], 'lat', [(x, (x + 1) % lat) for x in ran...  3.63 us
    ppermute x2, starting transfers between devices, shards(): lax.ppermute(to_left, 'lat', leftwards)  3.63 us
  transfers between devices with their start and end apart: 8, of which 3 were waited for; matrix products, arithmetic and copies ran while one was open for 0% of the time, Pallas kernels for 35%

profile of v6, /device:TPU:0, one launch (start us, length us, event | category | flops | bytes accessed | tf_op | source)
XLA Modules:
  0.0 67.5 jit_solution(11229496500797131393)
XLA Ops:
  0.6 4.7 %edge_strips0.1 = (bf16[16,192,128]{2,1,0:T(8,128)(2,1)}, bf16[16,192,128]{2,1,0:T(8,128)(2,1)}) custom-call(s32[1,4,4]{2,1,0:T(4,128)} %occ.9, bf16[1,16,512,512]{3,2,1,0:T(8,128)(2,1)} %last_lead.3, bf16[1,16,512,512]{3,2,1,0:T(8,128)(2,1)} %last_lead.3), custom_call_target="tpu_custom_call" | custom-call | tf_op jit(solution)/shard_map/edge_strips0/pallas_call | solution.py:69
  5.3 2.8 %collective-permute-start = (bf16[16,192,128]{2,1,0:T(8,128)(2,1)}, bf16[16,192,128]{2,1,0:T(8,128)(2,1)S(1)}, u32[]{:S(2)}, u32[]{:S(2)}) collective-permute-start(bf16[16,192,128]{2,1,0:T(8,128)(2,1)} %get-tuple-element.19), channel_id=1, source_target_pairs={{0,3},{1,0},{2,1},{3,2},{4,7},{5,4},{6,5},{7,6},{8,11},{9,8},{10,9... | collective-permute-start | bytes 2359304 | tf_op jit(solution)/shard_map/ppermute | solution.py:379
  8.2 0.0 copy-start.4
  8.2 0.0 copy-start.5
  8.2 1.5 %collective-permute-start.1 = (bf16[16,192,128]{2,1,0:T(8,128)(2,1)}, bf16[16,192,128]{2,1,0:T(8,128)(2,1)S(1)}, u32[]{:S(2)}, u32[]{:S(2)}) collective-permute-start(bf16[16,192,128]{2,1,0:T(8,128)(2,1)} %get-tuple-element.20), channel_id=1, source_target_pairs={{0,1},{1,2},{2,3},{4,5},{5,6},{6,7},{8,9},{9,10},{10,11},{12,13},{... | collective-permute-start | bytes 2359304 | tf_op jit(solution)/shard_map/ppermute | solution.py:379
  9.7 3.8 %edge_strips3.1 = (bf16[16,64,128]{2,1,0:T(8,128)(2,1)}, bf16[16,64,128]{2,1,0:T(8,128)(2,1)}) custom-call(s32[1,4,4]{2,1,0:T(4,128)} %occ.9, bf16[1,16,512,512]{3,2,1,0:T(8,128)(2,1)} %last_lead.3, bf16[1,16,512,512]{3,2,1,0:T(8,128)(2,1)} %last_lead.3), custom_call_target="tpu_custom_call" | custom-call | tf_op jit(solution)/shard_map/edge_strips3/pallas_call | solution.py:69
  13.4 0.8 %collective-permute-start.2 = (bf16[16,64,128]{2,1,0:T(8,128)(2,1)}, bf16[16,64,128]{2,1,0:T(8,128)(2,1)S(1)}, u32[]{:S(2)}, u32[]{:S(2)}) collective-permute-start(bf16[16,64,128]{2,1,0:T(8,128)(2,1)} %get-tuple-element.24), channel_id=1, source_target_pairs={{0,3},{1,0},{2,1},{3,2},{4,7},{5,4},{6,5},{7,6},{8,11},{9,8},{10,9... | collective-permute-start | bytes 786440 | tf_op jit(solution)/shard_map/ppermute | solution.py:379
  14.2 3.2 %collective-permute-start.3 = (bf16[16,64,128]{2,1,0:T(8,128)(2,1)}, bf16[16,64,128]{2,1,0:T(8,128)(2,1)S(1)}, u32[]{:S(2)}, u32[]{:S(2)}) collective-permute-start(bf16[16,64,128]{2,1,0:T(8,128)(2,1)} %get-tuple-element.25), channel_id=1, source_target_pairs={{0,1},{1,2},{2,3},{4,5},{5,6},{6,7},{8,9},{9,10},{10,11},{12,13},{... | collective-permute-start | bytes 786440 | tf_op jit(solution)/shard_map/ppermute | solution.py:379
  18.0 0.0 copy-done
  18.0 0.0 copy-done.1
  18.0 0.0 copy-done.2
  18.1 11.9 %interior.1 = (f32[16,2,16,384]{3,2,1,0:T(8,128)S(1)}, f32[16,2,16,384]{3,2,1,0:T(8,128)S(1)}, bf16[16,256,128]{2,1,0:T(8,128)(2,1)S(1)}, f32[16,512]{1,0:T(8,128)S(1)}) custom-call(s32[1,4,4]{2,1,0:T(4,128)S(1)} %copy-done, s32[1,16]{1,0:T(1,128)S(1)} %copy-done.1, f32[1,16]{1,0:T(1,128)S(1)} %copy-done.2, f32[1,16]{1,0:T(1,128)S(1)} %copy-done.3, ...), custom_call_target="tpu_custom_call" | custom-call | tf_op jit(solution)/shard_map/interior/pallas_call | solution.py:194
  30.1 0.0 collective-permute-done.right_ref.right_lead
  30.1 0.0 collective-permute-done.1.left_ref.left_lead
  30.1 4.9 %border0.1 = (f32[12,2,16,128]{3,2,1,0:T(8,128)S(1)}, f32[12,2,16,128]{3,2,1,0:T(8,128)S(1)}) custom-call(s32[1,4,4]{2,1,0:T(4,128)S(1)} %copy-done, s32[1,16]{1,0:T(1,128)S(1)} %copy-done.1, f32[1,16]{1,0:T(1,128)S(1)} %copy-done.2, f32[1,16]{1,0:T(1,128)S(1)} %copy-done.3, f32[1,16]{1,0:T(1,128)S(1)} %copy-done.4, f32[1]{0:T(128)S(6)} %copy.11.gain, ...), custom_call_target="tpu_custom_call" | custom-call | tf_op jit(solution)/shard_map/border0/pallas_call | solution.py:317
  35.0 0.1 collective-permute-start.5
  35.1 0.0 collective-permute-done.2.right_ref
  35.1 0.0 collective-permute-done.3.left_ref
  35.2 3.3 %border3.1 = (f32[4,2,16,128]{3,2,1,0:T(8,128)S(1)}, f32[4,2,16,128]{3,2,1,0:T(8,128)S(1)}) custom-call(s32[1,4,4]{2,1,0:T(4,128)S(1)} %copy-done, s32[1,16]{1,0:T(1,128)S(1)} %copy-done.1, f32[1,16]{1,0:T(1,128)S(1)} %copy-done.2, f32[1,16]{1,0:T(1,128)S(1)} %copy-done.3, f32[1,16]{1,0:T(1,128)S(1)} %copy-done.4, f32[1]{0:T(128)S(6)} %copy.11.gain, ...), custom_call_target="tpu_custom_call" | custom-call | tf_op jit(solution)/shard_map/border3/pallas_call | solution.py:317
  38.5 0.5 collective-permute-start.4
  39.0 1.1 %collective-permute-done.4 = f32[16,2,16,128]{3,2,1,0:T(8,128)S(1)} collective-permute-done((f32[16,2,16,128]{3,2,1,0:T(8,128)S(1)}, f32[16,2,16,128]{3,2,1,0:T(8,128)S(1)}, u32[]{:S(2)}, u32[]{:S(2)}) %collective-permute-start.4) | collective-permute-done | bytes 262176 | tf_op jit(solution)/shard_map/ppermute | solution.py:340
  40.2 0.0 collective-permute-done.5
  40.2 0.1 fusion.1
  40.4 0.9 %fusion = f16[16,2,16,512]{3,2,1,0:T(8,128)(2,1)} fusion(f32[16,1,16,384]{3,2,1,0:T(8,128)S(1)} %get-tuple-element.36, f32[16,1,16,384]{3,2,1,0:T(8,128)S(1)} %get-tuple-element.35, f32[16,1,16,128]{3,2,1,0:T(8,128)S(1)} %get-tuple-element.38, f32[16,1,16,128]{3,2,1,0:T(8,128)S(1)} %get-tuple-element.37), kind=kLoop, calls=%fused_computation.1 | loop fusion | flops 1310720 | bytes 1572864 | tf_op jit(solution)/shard_map/convert_element_type | solution.py:348
  41.3 8.1 %all-to-all-start = ((f16[16,2,16,512]{3,2,1,0:T(8,128)(2,1)}), f16[16,2,16,512]{3,2,1,0:T(8,128)(2,1)S(1)}, u32[]{:S(2)}, u32[]{:S(2)}) async-start(f16[16,2,16,512]{3,2,1,0:T(8,128)(2,1)} %fusion), calls=%async_computation | async-start | bytes 1048576 | tf_op jit(solution)/shard_map/all_to_all | solution.py:350
  49.4 11.9 %all-to-all-done = f16[16,2,16,512]{3,2,1,0:T(8,128)(2,1)S(1)} async-done(((f16[16,2,16,512]{3,2,1,0:T(8,128)(2,1)}), f16[16,2,16,512]{3,2,1,0:T(8,128)(2,1)S(1)}, u32[]{:S(2)}, u32[]{:S(2)}) %all-to-all-start) | async-done | bytes 524320 | tf_op jit(solution)/shard_map/all_to_all | solution.py:350
  61.3 0.2 convert_multiply_fusion
  61.5 0.1 multiply_add_fusion.2
  61.6 0.2 fusion.10
  61.8 1.4 %collective-permute-start.6 = (f32[2,16,128]{2,1,0:T(8,128)S(1)}, f32[2,16,128]{2,1,0:T(8,128)S(1)}, u32[]{:S(2)}, u32[]{:S(2)}) collective-permute-start(f32[2,16,128]{2,1,0:T(8,128)S(1)} %pad_maximum_fusion.3), channel_id=1, source_target_pairs={{0,1},{1,2},{2,3},{3,0},{4,5},{5,6},{6,7},{7,4},{8,9},{9,10},{10,1... | collective-permute-start | bytes 49160 | tf_op jit(solution)/shard_map/ppermute | solution.py:390
  63.2 3.6 %collective-permute-done.6 = f32[2,16,128]{2,1,0:T(8,128)S(1)} collective-permute-done((f32[2,16,128]{2,1,0:T(8,128)S(1)}, f32[2,16,128]{2,1,0:T(8,128)S(1)}, u32[]{:S(2)}, u32[]{:S(2)}) %collective-permute-start.6) | collective-permute-done | bytes 16416 | tf_op jit(solution)/shard_map/ppermute | solution.py:390
  66.8 0.6 pad_maximum_fusion.1
  (23 shorter events, 0.2 us)
Async XLA Ops:
  5.3 24.8 %collective-permute-start = (bf16[16,192,128]{2,1,0:T(8,128)(2,1)}, bf16[16,192,128]{2,1,0:T(8,128)(2,1)S(1)}, u32[]{:S(2)}, u32[]{:S(2)}) collective-permute-start(bf16[16,192,128]{2,1,0:T(8,128)(2,1)} %get-tuple-element.19), channel_id=1, source_target_pairs={{0,3},{1,0},{2,1},{3,2},{4,7},{5,4},{6,5},{7,6},{8,11},{9,8},{10,9... | collective-permute-start | bytes 2359304 | tf_op jit(solution)/shard_map/ppermute | solution.py:379
  8.2 9.9 %copy-start = (s32[1,4,4]{2,1,0:T(4,128)S(1)}, s32[1,4,4]{2,1,0:T(4,128)}, u32[]{:S(2)}) copy-start(s32[1,4,4]{2,1,0:T(4,128)} %occ.9) | copy-start | bytes 196
  8.2 9.9 %copy-start.1 = (s32[1,16]{1,0:T(1,128)S(1)}, s32[1,16]{1,0:T(1,128)}, u32[]{:S(2)}) copy-start(s32[1,16]{1,0:T(1,128)} %offset.5) | copy-start | bytes 196
  8.2 9.9 %copy-start.2 = (f32[1,16]{1,0:T(1,128)S(1)}, f32[1,16]{1,0:T(1,128)}, u32[]{:S(2)}) copy-start(f32[1,16]{1,0:T(1,128)} %frac_lateral.5) | copy-start | bytes 196
  8.2 9.9 %copy-start.3 = (f32[1,16]{1,0:T(1,128)S(1)}, f32[1,16]{1,0:T(1,128)}, u32[]{:S(2)}) copy-start(f32[1,16]{1,0:T(1,128)} %frac_vertical.5) | copy-start | bytes 196
  8.2 9.9 %copy-start.4 = (f32[1,16]{1,0:T(1,128)S(1)}, f32[1,16]{1,0:T(1,128)}, u32[]{:S(2)}) copy-start(f32[1,16]{1,0:T(1,128)} %extinction.5) | copy-start | bytes 196
  8.2 9.9 %copy-start.5 = (s32[32]{0:T(128)S(1)}, s32[32]{0:T(128)}, u32[]{:S(2)}) copy-start(s32[32]{0:T(128)} %rank.1) | copy-start | bytes 388
  8.2 21.9 %collective-permute-start.1 = (bf16[16,192,128]{2,1,0:T(8,128)(2,1)}, bf16[16,192,128]{2,1,0:T(8,128)(2,1)S(1)}, u32[]{:S(2)}, u32[]{:S(2)}) collective-permute-start(bf16[16,192,128]{2,1,0:T(8,128)(2,1)} %get-tuple-element.20), channel_id=1, source_target_pairs={{0,1},{1,2},{2,3},{4,5},{5,6},{6,7},{8,9},{9,10},{10,11},{12,13},{... | collective-permute-start | bytes 2359304 | tf_op jit(solution)/shard_map/ppermute | solution.py:379
  13.4 21.7 %collective-permute-start.2 = (bf16[16,64,128]{2,1,0:T(8,128)(2,1)}, bf16[16,64,128]{2,1,0:T(8,128)(2,1)S(1)}, u32[]{:S(2)}, u32[]{:S(2)}) collective-permute-start(bf16[16,64,128]{2,1,0:T(8,128)(2,1)} %get-tuple-element.24), channel_id=1, source_target_pairs={{0,3},{1,0},{2,1},{3,2},{4,7},{5,4},{6,5},{7,6},{8,11},{9,8},{10,9... | collective-permute-start | bytes 786440 | tf_op jit(solution)/shard_map/ppermute | solution.py:379
  14.2 20.9 %collective-permute-start.3 = (bf16[16,64,128]{2,1,0:T(8,128)(2,1)}, bf16[16,64,128]{2,1,0:T(8,128)(2,1)S(1)}, u32[]{:S(2)}, u32[]{:S(2)}) collective-permute-start(bf16[16,64,128]{2,1,0:T(8,128)(2,1)} %get-tuple-element.25), channel_id=1, source_target_pairs={{0,1},{1,2},{2,3},{4,5},{5,6},{6,7},{8,9},{9,10},{10,11},{12,13},{... | collective-permute-start | bytes 786440 | tf_op jit(solution)/shard_map/ppermute | solution.py:379
  35.0 5.2 %collective-permute-start.5 = (f32[16,2,16,384]{3,2,1,0:T(8,128)S(1)}, f32[16,2,16,384]{3,2,1,0:T(8,128)S(1)}, u32[]{:S(2)}, u32[]{:S(2)}) collective-permute-start(f32[16,2,16,384]{3,2,1,0:T(8,128)S(1)} %get-tuple-element.31), channel_id=1, source_target_pairs={{0,4},{4,0},{8,12},{12,8},{16,20},{20,16},{24,28},{28,24},{32,36},... | collective-permute-start | bytes 2359304 | tf_op jit(solution)/shard_map/ppermute | solution.py:340
  38.5 1.7 %collective-permute-start.4 = (f32[16,2,16,128]{3,2,1,0:T(8,128)S(1)}, f32[16,2,16,128]{3,2,1,0:T(8,128)S(1)}, u32[]{:S(2)}, u32[]{:S(2)}) collective-permute-start(f32[16,2,16,128]{3,2,1,0:T(8,128)S(1)} %pad_maximum_fusion), channel_id=1, source_target_pairs={{0,4},{4,0},{8,12},{12,8},{16,20},{20,16},{24,28},{28,24},{32,36},... | collective-permute-start | bytes 786440 | tf_op jit(solution)/shard_map/ppermute | solution.py:340
  41.3 20.1 %all-to-all-start = ((f16[16,2,16,512]{3,2,1,0:T(8,128)(2,1)}), f16[16,2,16,512]{3,2,1,0:T(8,128)(2,1)S(1)}, u32[]{:S(2)}, u32[]{:S(2)}) async-start(f16[16,2,16,512]{3,2,1,0:T(8,128)(2,1)} %fusion), calls=%async_computation | async-start | bytes 1048576 | tf_op jit(solution)/shard_map/all_to_all | solution.py:350
  61.8 5.0 %collective-permute-start.6 = (f32[2,16,128]{2,1,0:T(8,128)S(1)}, f32[2,16,128]{2,1,0:T(8,128)S(1)}, u32[]{:S(2)}, u32[]{:S(2)}) collective-permute-start(f32[2,16,128]{2,1,0:T(8,128)S(1)} %pad_maximum_fusion.3), channel_id=1, source_target_pairs={{0,1},{1,2},{2,3},{3,0},{4,5},{5,6},{6,7},{7,4},{8,9},{9,10},{10,1... | collective-permute-start | bytes 49160 | tf_op jit(solution)/shard_map/ppermute | solution.py:390

commit v7 on v5

v7 whole, which is shorter than its diff:
```python
import functools
import math

import jax
import jax.numpy as jnp
from jax import lax
from jax.experimental import pallas as pl
from jax.experimental.pallas import tpu as pltpu
from jax.sharding import PartitionSpec as P

SHIFT = 128
BLK = 128
LANES = 128
PIECE = 16
WIRE = jnp.float16
WIRE_SCALE = 4096.0
PACKED = 4 * LANES
LOG2E = math.log2(math.e)
SMEM = pltpu.SMEM
F32 = jnp.float32
BF16 = jnp.bfloat16


def rounded(scalar, shape):
    return jnp.full(shape, scalar, F32).astype(BF16).astype(F32)


def tap(distance, offset, fraction):
    second = jnp.where(distance == offset + 1, fraction, 0.0)
    return jnp.where(distance == offset, 1.0 - fraction, second)


class Packing:
    def __init__(self, offset):
        slices = offset.shape[1]
        lane = lax.broadcasted_iota(jnp.int32, (8, LANES), 1)
        right, left = jnp.zeros_like(lane), jnp.zeros_like(lane)
        for s in range(slices):
            right = right + jnp.maximum(lane - offset[0, s], 0)
            left = left + jnp.maximum(offset[0, s] + 1 - lane, 0)
        fits = (right <= PACKED) & (left <= PACKED)
        self.border = jnp.min(jnp.where(fits, lane.astype(F32), 127.0)).astype(jnp.int32)
        self.from_left, self.count, self.tile, self.first = [], [], [], []
        used = [0, 0]
        for s in range(slices):
            o = offset[0, s]
            from_left = o >= self.border
            count = jnp.where(from_left, o + 1 - self.border, self.border - o)
            first = jnp.where(from_left, used[1], used[0])
            used[1] = used[1] + jnp.where(from_left, count, 0)
            used[0] = used[0] + jnp.where(from_left, 0, count)
            tile = jnp.minimum(jnp.right_shift(first, 7), PACKED // LANES - 2)
            self.from_left.append(from_left)
            self.count.append(count)
            self.tile.append(tile)
            self.first.append(first - LANES * tile)


def pack_kernel(occ, offset, x_first, x_last, to_left, to_right, picks, packed):
    block = pl.program_id(0)
    slices, cols = x_first.shape[1], LANES
    packing = Packing(offset)

    @pl.when(block == 0)
    def _():
        k = lax.broadcasted_iota(jnp.int32, (LANES, 2 * LANES), 0)
        p = lax.broadcasted_iota(jnp.int32, (LANES, 2 * LANES), 1)
        for s in range(slices):
            skip = jnp.where(packing.from_left[s], cols - packing.count[s], 0)
            inside = (k >= skip) & (k < skip + packing.count[s])
            same = k - skip == p - packing.first[s]
            picks[s] = jnp.where(inside & same, 1.0, 0.0).astype(BF16)

    packed[...] = jnp.zeros_like(packed)
    first_occ = occ[0, block, 0].astype(F32)
    last_occ = occ[0, block, occ.shape[2] - 1].astype(F32)
    for s in range(slices):
        from_left = packing.from_left[s]
        columns = x_first[0, s] * splat(jnp.where(from_left, 0.0, first_occ)) + x_last[
            0, s
        ] * splat(jnp.where(from_left, last_occ, 0.0))
        moved = jnp.dot(columns, picks[s], preferred_element_type=F32).astype(BF16)
        way = jnp.where(from_left, 1, 0)
        tile = packing.tile[s]
        packed[way, tile] += moved[:, :LANES]
        packed[way, tile + 1] += moved[:, LANES:]
    to_left[...] = packed[0]
    to_right[...] = packed[1]


def pack_halo(density, occupancy, offsets):
    _, slices, rows, cols = density.shape
    tiles = PACKED // LANES
    shape = jax.ShapeDtypeStruct((tiles, rows, LANES), BF16)
    last = cols // LANES - 1
    return pl.pallas_call(
        pack_kernel,
        grid=(rows // BLK,),
        in_specs=[
            pl.BlockSpec(memory_space=SMEM),
            pl.BlockSpec(memory_space=SMEM),
            pl.BlockSpec((1, slices, BLK, LANES), lambda b: (0, 0, b, 0)),
            pl.BlockSpec((1, slices, BLK, LANES), lambda b: (0, 0, b, last)),
        ],
        out_specs=[pl.BlockSpec((tiles, BLK, LANES), lambda b: (0, b, 0))] * 2,
        out_shape=[shape, shape],
        scratch_shapes=[
            pltpu.VMEM((slices, LANES, 2 * LANES), BF16),
            pltpu.VMEM((2, tiles, BLK, LANES), BF16),
        ],
        name="pack_halo",
    )(occupancy, offsets, density, density)


def whole():
    return pl.BlockSpec(memory_space=pltpu.VMEM)


def border_weights(s, offset, frac_lateral, packing, weights, out):
    n = lax.broadcasted_iota(jnp.int32, (2 * LANES, LANES), 1)
    p = lax.broadcasted_iota(jnp.int32, (2 * LANES, LANES), 0)
    own = jnp.where(n[:1] >= packing.border, 1.0, 0.0)
    out[s, :LANES] = weights[s, LANES:] * own.astype(BF16)
    out[s, LANES : 2 * LANES] = weights[s, :LANES] * (1.0 - own).astype(BF16)
    from_left, count = packing.from_left[s], packing.count[s]
    index = p - packing.first[s]
    reach = n + jnp.where(from_left, count, 0) - index
    weight = tap(reach, offset[0, s], frac_lateral[0, s])
    weight = jnp.where((index >= 0) & (index < count), weight, 0.0)
    mine = jnp.where(from_left, own, 1.0 - own)
    out[s, 2 * LANES :] = (weight * mine).astype(BF16)


def shade(s, x, base, state, refs):
    frac_vertical, extinction, slice_total = refs
    through_ref, sum_ref = state
    rows = x.shape[0] - 8
    v0 = 2.0 * rounded(1.0 - frac_vertical[0, s], (1, LANES))
    v1 = 2.0 * rounded(frac_vertical[0, s], (1, LANES))
    density = v0 * x + v1 * pltpu.roll(x, 1, 0)
    above = pltpu.roll(density, 1, 0)
    density, above = density[8:], above[8:]
    rate = extinction[0, s] * (-LOG2E / (2.0 * slice_total))
    kept = jnp.exp2(rate * density)
    slope = jnp.tanh(density - above)
    at = slice(base, base + rows)
    through = through_ref[at]
    after = through * kept
    through_ref[at] = after
    sum_ref[at] += (through - after) * slope


def finish(state, gain, swap, out_keep, out_send, tile):
    through_ref, sum_ref = state
    rows = out_keep.shape[0] * 2 * PIECE
    base = tile * rows
    alphas, colors = [], []
    for p in range(rows // PIECE):
        at = slice(base + p * PIECE, base + (p + 1) * PIECE)
        alpha = 1.0 - through_ref[at]
        alphas.append(alpha)
        colors.append(gain * (0.65 * alpha + 0.35 * sum_ref[at]))
    lanes = slice(tile * LANES, (tile + 1) * LANES)
    for q in range(rows // PIECE // 2):
        for i, values in enumerate((colors, alphas)):
            even, odd = values[2 * q], values[2 * q + 1]
            out_keep[q, i, :, lanes] = jnp.where(swap, odd, even)
            out_send[q, i, :, lanes] = jnp.where(swap, even, odd)


def splat(value):
    return jnp.full((1, LANES), value, F32).astype(BF16)


def over_slices(slices, one):
    for s in range(slices):
        one(s, 0)


def interior_kernel(
    slice_total, occ, offset, frac_lateral, frac_vertical, extinction, gain, rank,
    x_ref, lead_ref, out_keep, out_send, out_weights, flags, weights, through_ref, sum_ref,
):
    block = pl.program_id(0)
    slices, rows = x_ref.shape[1], x_ref.shape[2]
    tiles = x_ref.shape[3] // LANES

    @pl.when(block == 0)
    def _():
        k = lax.broadcasted_iota(jnp.int32, (2 * LANES, LANES), 0)
        n = lax.broadcasted_iota(jnp.int32, (2 * LANES, LANES), 1)

        def build(s, _):
            weights[s] = tap(LANES + n - k, offset[0, s], frac_lateral[0, s]).astype(BF16)
            return 0

        lax.fori_loop(0, slices, build, 0)
        packing = Packing(offset)
        for s in range(slices):
            border_weights(s, offset, frac_lateral, packing, weights, out_weights)
        lane = lax.broadcasted_iota(jnp.int32, (1, flags.shape[1]), 1)
        flags[16:17] = jnp.where(lane < packing.border, 1.0, 0.0)
        me = lax.axis_index("depth")
        in_front = [rank[me] < rank[jnp.bitwise_xor(me, 1)]]
        for span in (2, 4, 8, 16):
            in_front += [rank[a] < rank[a + span] for a in range(0, rank.shape[0], 2 * span)]
        for i, flag in enumerate(in_front):
            flags[i : i + 1] = jnp.full((1, flags.shape[1]), jnp.where(flag, 1.0, 0.0), F32)

    through_ref[...] = jnp.ones_like(through_ref)
    sum_ref[...] = jnp.zeros_like(sum_ref)
    inside = jnp.where(block > 0, 1, 0)
    above = jnp.maximum(block - 1, 0)
    mask = [splat(occ[0, block, t]) for t in range(tiles)]
    lead_mask = [splat(occ[0, above, t] * inside) for t in range(tiles)]
    state = (through_ref, sum_ref)
    refs = (frac_vertical, extinction, slice_total)

    def one(s, _):
        parts = []
        for t in range(tiles):
            lanes = slice(t * LANES, (t + 1) * LANES)
            lead = lead_ref[0, s, :, lanes] * lead_mask[t]
            parts.append(jnp.concatenate([lead, x_ref[0, s, :, lanes] * mask[t]], axis=0))
        for t in range(1, tiles):
            pair = jnp.concatenate([parts[t - 1], parts[t]], axis=1)
            x = jnp.dot(pair, weights[s], preferred_element_type=F32)
            shade(s, x[8:], (t - 1) * rows, state, refs)
        return 0

    over_slices(slices, one)
    swap = lax.axis_index("depth") % 2 == 1
    for t in range(tiles - 1):
        finish(state, gain[0], swap, out_keep, out_send, t)


def small_specs():
    return [pl.BlockSpec(memory_space=SMEM)] * 6


def interior(density, small, rank, slice_total):
    _, slices, rows, cols = density.shape
    step = BLK
    width = cols - LANES
    pieces = step // (2 * PIECE)
    image = jax.ShapeDtypeStruct((rows // (2 * PIECE), 2, PIECE, width), F32)
    return pl.pallas_call(
        functools.partial(interior_kernel, slice_total),
        grid=(rows // step,),
        in_specs=small_specs()
        + [pl.BlockSpec(memory_space=SMEM)]
        + [
            pl.BlockSpec((1, slices, step, cols), lambda b: (0, 0, b, 0)),
            pl.BlockSpec(
                (1, slices, 16, cols), lambda b: (0, 0, jnp.maximum(b * (step // 16) - 1, 0), 0)
            ),
        ],
        out_specs=[
            pl.BlockSpec((pieces, 2, PIECE, width), lambda b: (b, 0, 0, 0))
        ]
        * 2
        + [
            pl.BlockSpec((slices, 4 * LANES, LANES), lambda b: (0, 0, 0)),
            pl.BlockSpec((24, cols), lambda b: (0, 0)),
        ],
        out_shape=[
            image,
            image,
            jax.ShapeDtypeStruct((slices, 4 * LANES, LANES), BF16),
            jax.ShapeDtypeStruct((24, cols), F32),
        ],
        scratch_shapes=[pltpu.VMEM((slices, 2 * LANES, LANES), BF16)]
        + [pltpu.VMEM((step * (width // LANES), LANES), F32)] * 2,
        compiler_params=pltpu.CompilerParams(vmem_limit_bytes=32 * 2**20),
        name="interior",
    )(*small, rank, density, density)


def border_kernel(
    start, slice_total, occ, offset, frac_lateral, frac_vertical, extinction, gain, weights,
    first_ref, last_ref, first_lead, last_lead, right_ref, left_ref,
    out_keep, out_send, through_ref, sum_ref,
):
    slices = first_ref.shape[1]
    blocks = first_ref.shape[2] // BLK
    last_tile = occ.shape[2] - 1
    follows = jnp.where(lax.axis_index("lat") < lax.axis_size("lat") - 1, 1, 0)
    refs = (frac_vertical, extinction, slice_total)
    state = (through_ref, sum_ref)
    through_ref[...] = jnp.ones_like(through_ref)
    sum_ref[...] = jnp.zeros_like(sum_ref)
    packing = Packing(offset)
    masks = []
    for b in range(start - 1, start + blocks):
        inside = b >= 0
        masks.append(
            (
                splat(occ[0, b, 0] if inside else 0.0),
                splat(occ[0, b, last_tile] * follows if inside else 0.0),
            )
        )
    top = start * BLK

    def tiles(ref, lead, s, side):
        parts = [lead[0, s] * masks[0][side]]
        for b in range(blocks):
            parts.append(ref[0, s, b * BLK : (b + 1) * BLK] * masks[b + 1][side])
        return jnp.concatenate(parts, axis=0)

    def one(s, _):
        is_left = splat(jnp.where(packing.from_left[s], 1.0, 0.0))
        is_right = splat(jnp.where(packing.from_left[s], 0.0, 1.0))

        def halo(tile):
            rows = slice(top - 16 if start else top, top + blocks * BLK)
            columns = left_ref[tile, rows] * is_left + right_ref[tile, rows] * is_right
            if start == 0:
                columns = jnp.concatenate([jnp.zeros((16, LANES), BF16), columns], axis=0)
            return columns

        tile = packing.tile[s]
        operand = jnp.concatenate(
            [
                tiles(first_ref, first_lead, s, 0),
                tiles(last_ref, last_lead, s, 1),
                halo(tile),
                halo(tile + 1),
            ],
            axis=1,
        )
        x = jnp.dot(operand, weights[s], preferred_element_type=F32)
        for b in range(blocks):
            shade(s, x[b * BLK + 8 : (b + 1) * BLK + 16], b * BLK, state, refs)
        return 0

    over_slices(slices, one)
    swap = lax.axis_index("depth") % 2 == 1
    finish(state, gain[0], swap, out_keep, out_send, 0)


def border(density, small, weights, halos, start, blocks, slice_total):
    _, slices, _, cols = density.shape
    step = blocks * BLK
    last = cols // LANES - 1
    lead_rows = max(start * BLK // 16 - 1, 0)

    def tile(column):
        shape = tuple(pl.Element(n) for n in (1, slices, step, LANES))
        return pl.BlockSpec(shape, lambda i: (0, 0, start * BLK, column * LANES))

    def lead(column):
        return pl.BlockSpec((1, slices, 16, LANES), lambda i: (0, 0, lead_rows, column))

    image = jax.ShapeDtypeStruct((step // (2 * PIECE), 2, PIECE, LANES), F32)
    return pl.pallas_call(
        functools.partial(border_kernel, start, slice_total),
        grid=(1,),
        in_specs=small_specs()
        + [whole(), tile(0), tile(last), lead(0), lead(last), whole(), whole()],
        out_specs=[whole()] * 2,
        out_shape=[image, image],
        scratch_shapes=[pltpu.VMEM((step, LANES), F32)] * 2,
        compiler_params=pltpu.CompilerParams(vmem_limit_bytes=32 * 2**20),
        name=f"border{start}",
    )(*small, weights, density, density, density, density, *halos)


def over(mine, other, in_front):
    color = mine[0] * (1.0 - (1.0 - in_front) * other[1]) + other[0] * (1.0 - in_front * mine[1])
    return color, mine[1] + (1.0 - mine[1]) * other[1]


def over_cores(keep, send, flags):
    count = lax.axis_size("depth")
    other = lax.ppermute(send, "depth", [(i, i ^ 1) for i in range(count)])
    front = flags[0, : keep.shape[3]]
    return jnp.stack(over((keep[:, 0], keep[:, 1]), (other[:, 0], other[:, 1]), front), axis=1)


def over_chips(pieces, flags):
    count = lax.axis_size("depth")
    chips = count // 2
    pieces = (pieces * WIRE_SCALE).astype(WIRE)
    groups = [[2 * i + core for i in range(chips)] for core in range(2)]
    pieces = lax.all_to_all(
        pieces, "depth", 0, 0, axis_index_groups=groups, tiled=True
    )
    pieces = pieces.astype(F32) * (1.0 / WIRE_SCALE)
    level = [(pieces[i, 0], pieces[i, 1]) for i in range(chips)]
    row = 1
    while len(level) > 1:
        half = len(level) // 2
        level = [over(level[2 * i], level[2 * i + 1], flags[row + i]) for i in range(half)]
        row += half
    return level[0]


def shards(
    density, occupancy, shear_offsets, frac_lateral, frac_vertical, extinction, slab_gain, view_rank
):
    _, slices, rows, cols = density.shape
    slice_total = lax.axis_size("depth") * slices
    lat = lax.axis_size("lat")
    density = pltpu.with_memory_space_constraint(density, pltpu.HBM)
    small = (occupancy, shear_offsets, frac_lateral, frac_vertical, extinction, slab_gain)
    blocks = rows // BLK
    rightwards = [(x, x + 1) for x in range(lat - 1)]
    leftwards = [(x, (x - 1) % lat) for x in range(lat)]
    around = [(x, (x + 1) % lat) for x in range(lat)]
    to_left, to_right = pack_halo(density, occupancy, shear_offsets)
    halos = (
        lax.ppermute(to_left, "lat", leftwards),
        lax.ppermute(to_right, "lat", rightwards),
    )
    images = interior(density, small, view_rank, slice_total)
    (keep, send, weights, flags), halos = lax.optimization_barrier((images, halos))
    inner = over_cores(keep, send, flags)

    def edge_rows(first, count, weights):
        image = jnp.stack(border(density, small, weights, halos, first, count, slice_total))
        moved = lax.ppermute((image * WIRE_SCALE).astype(WIRE), "lat", around)
        below = flags[16, :LANES]
        return image, image * (1.0 - below) + moved.astype(F32) * (below / WIRE_SCALE)

    half = blocks // 2
    top, moved_top = edge_rows(0, half, weights)
    weights, _ = lax.optimization_barrier((weights, top))
    _, moved_bottom = edge_rows(half, blocks - half, weights)
    keep, send = jnp.concatenate([moved_top, moved_bottom], axis=1)
    edge = over_cores(keep, send, flags)
    return tuple(over_chips(jnp.concatenate([edge, inner], axis=3), flags))


def solution(mesh):
    placed = (
        P("depth", None, None, "lat"),
        P("depth", None, "lat"),
        P("depth", None),
        P("depth", None),
        P("depth", None),
        P("depth", None),
        P("depth"),
        P(),
    )
    return jax.shard_map(
        shards,
        mesh=mesh,
        in_specs=placed,
        out_specs=(P("depth", "lat"), P("depth", "lat")),
        check_vma=False,
    )
```

time: 65.1 us -> 66.1 us (1.015)
  starting transfers between devices: 18.3 us -> 15.3 us
  waiting for transfers between devices: 16.7 us -> 19.2 us
  other arithmetic: 1.45 us -> 2.91 us
  Pallas kernels: 25.7 us -> 26.7 us
  local copies, waits for them, and re-layouts: 1 us -> 0.07 us
    ppermute x2 -> x1, starting transfers between devices: 4.64 us -> 1.31 us  [shards(): lax.ppermute(to_right, 'lat', rightwards)]
    ppermute x1 -> x2, waiting for transfers between devices: 3.65 us -> 6 us  [edge_rows(): moved = lax.ppermute((image * WIRE_SCALE).astype(WIRE), 'lat', around)]
    ppermute x1 -> x2, starting transfers between devices: 1.36 us -> 2.97 us  [edge_rows(): moved = lax.ppermute((image * WIRE_SCALE).astype(WIRE), 'lat', around)]
    convert_element_type x1 -> x0, local copies, waits for them, and re-layouts: 0.92 us -> none  [over_chips(): pieces = (pieces * WIRE_SCALE).astype(WIRE)]
    pallas_call x1, Pallas kernels: 12.1 us -> 13 us  [interior(): pl.pallas_call(functools.partial(interior_kernel, slice_total), grid=(row...]
    convert_element_type x1, other arithmetic: 0.09 us -> 0.9 us  [over_chips(): pieces = (pieces * WIRE_SCALE).astype(WIRE)]
    ppermute x2 -> x1, starting transfers between devices: 3.62 us -> 2.84 us  [shards(): lax.ppermute(to_left, 'lat', leftwards)]
    pallas_call x2, Pallas kernels: 7.04 us -> 7.76 us  [border(): pl.pallas_call(functools.partial(border_kernel, start, slice_total), grid...]
  transfers between devices with their start and end apart: 8 -> 7, of which waited for: 3 -> 4; matrix products, arithmetic and copies ran while one was open for 0% -> 0% of each run, Pallas kernels for 35% -> 20%
where the time goes in v7:
time: 66.1 us; the launch traced here: 65.7 us
  Pallas kernels  26.7 us (40%)
  waiting for transfers between devices  19.2 us (29%)
  starting transfers between devices  15.3 us (23%)
  other arithmetic  2.91 us (4%)
  between operations  1.53 us (2%)
    pallas_call x1, Pallas kernels, interior(): pl.pallas_call(functools.partial(interior_kernel, slice_total), grid=(row...  13 us
    all_to_all x1, waiting for transfers between devices, over_chips(): lax.all_to_all(pieces, 'depth', 0, 0, axis_index_groups=groups, tiled=True)  11.7 us
    all_to_all x1, starting transfers between devices, over_chips(): lax.all_to_all(pieces, 'depth', 0, 0, axis_index_groups=groups, tiled=True)  8.05 us
    pallas_call x2, Pallas kernels, border(): pl.pallas_call(functools.partial(border_kernel, start, slice_total), grid...  7.76 us
    pallas_call x1, Pallas kernels, pack_halo(): pl.pallas_call(pack_kernel, grid=(rows // BLK,), in_specs=[pl.BlockSpec(m...  6.01 us
    ppermute x2, waiting for transfers between devices, edge_rows(): moved = lax.ppermute((image * WIRE_SCALE).astype(WIRE), 'lat', around)  6 us
    ppermute x2, starting transfers between devices, edge_rows(): moved = lax.ppermute((image * WIRE_SCALE).astype(WIRE), 'lat', around)  2.97 us
    ppermute x1, starting transfers between devices, shards(): lax.ppermute(to_left, 'lat', leftwards)  2.84 us
  transfers between devices with their start and end apart: 7, of which 4 were waited for; matrix products, arithmetic and copies ran while one was open for 0% of the time, Pallas kernels for 20%

profile of v7, /device:TPU:0, one launch (start us, length us, event | category | flops | bytes accessed | tf_op | source)
XLA Modules:
  0.0 65.7 jit_solution(9789108770237798244)
XLA Ops:
  0.6 0.0 copy-start.1
  0.6 0.0 copy-start
  0.7 6.0 %pack_halo.1 = (bf16[4,512,128]{2,1,0:T(8,128)(2,1)}, bf16[4,512,128]{2,1,0:T(8,128)(2,1)}) custom-call(s32[1,4,4]{2,1,0:T(4,128)} %occ.7, s32[1,16]{1,0:T(1,128)} %offset.7, bf16[1,16,512,512]{3,2,1,0:T(8,128)(2,1)} %last_lead.3, bf16[1,16,512,512]{3,2,1,0:T(8,128)(2,1)} %last_lead.3), custom_call_target="tpu_custom_call" | custom-call | tf_op jit(solution)/shard_map/pack_halo/pallas_call | solution.py:96
  6.7 2.8 %collective-permute-start = (bf16[4,512,128]{2,1,0:T(8,128)(2,1)}, bf16[4,512,128]{2,1,0:T(8,128)(2,1)S(1)}, u32[]{:S(2)}, u32[]{:S(2)}) collective-permute-start(bf16[4,512,128]{2,1,0:T(8,128)(2,1)} %get-tuple-element.23), channel_id=1, source_target_pairs={{0,3},{1,0},{2,1},{3,2},{4,7},{5,4},{6,5},{7,6},{8,11},{9,8},{10,9... | collective-permute-start | bytes 1572872 | tf_op jit(solution)/shard_map/ppermute | solution.py:412
  9.5 1.3 %collective-permute-start.1 = (bf16[4,512,128]{2,1,0:T(8,128)(2,1)}, bf16[4,512,128]{2,1,0:T(8,128)(2,1)S(1)}, u32[]{:S(2)}, u32[]{:S(2)}) collective-permute-start(bf16[4,512,128]{2,1,0:T(8,128)(2,1)} %get-tuple-element.24), channel_id=1, source_target_pairs={{0,1},{1,2},{2,3},{4,5},{5,6},{6,7},{8,9},{9,10},{10,11},{12,13},{... | collective-permute-start | bytes 1572872 | tf_op jit(solution)/shard_map/ppermute | solution.py:413
  11.5 0.0 copy-done.1
  11.5 0.0 copy-done
  11.5 0.0 copy-done.4
  11.5 0.0 copy-done.3
  11.5 0.0 copy-done.2
  11.6 0.0 copy-done.5
  11.6 13.0 %interior.1 = (f32[16,2,16,384]{3,2,1,0:T(8,128)S(1)}, f32[16,2,16,384]{3,2,1,0:T(8,128)S(1)}, bf16[16,512,128]{2,1,0:T(8,128)(2,1)S(1)}, f32[24,512]{1,0:T(8,128)S(1)}) custom-call(s32[1,4,4]{2,1,0:T(4,128)S(1)} %copy-done, s32[1,16]{1,0:T(1,128)S(1)} %copy-done.1, f32[1,16]{1,0:T(1,128)S(1)} %copy-done.2, f32[1,16]{1,0:T(1,128)S(1)} %copy-done.3, ...), custom_call_target="tpu_custom_call" | custom-call | tf_op jit(solution)/shard_map/interior/pallas_call | solution.py:247
  24.6 0.0 collective-permute-done.right_ref
  24.6 0.0 collective-permute-done.1.left_ref
  24.6 3.9 %border0.1 = (f32[8,2,16,128]{3,2,1,0:T(8,128)S(1)}, f32[8,2,16,128]{3,2,1,0:T(8,128)S(1)}) custom-call(s32[1,4,4]{2,1,0:T(4,128)S(1)} %copy-done, s32[1,16]{1,0:T(1,128)S(1)} %copy-done.1, f32[1,16]{1,0:T(1,128)S(1)} %copy-done.2, f32[1,16]{1,0:T(1,128)S(1)} %copy-done.3, f32[1,16]{1,0:T(1,128)S(1)} %copy-done.4, f32[1]{0:T(128)S(6)} %copy.10.gain, ...), custom_call_target="tpu_custom_call" | custom-call | tf_op jit(solution)/shard_map/border0/pallas_call | solution.py:355
  28.4 3.9 %border2.1 = (f32[8,2,16,128]{3,2,1,0:T(8,128)S(1)}, f32[8,2,16,128]{3,2,1,0:T(8,128)S(1)}) custom-call(s32[1,4,4]{2,1,0:T(4,128)S(1)} %copy-done, s32[1,16]{1,0:T(1,128)S(1)} %copy-done.1, f32[1,16]{1,0:T(1,128)S(1)} %copy-done.2, f32[1,16]{1,0:T(1,128)S(1)} %copy-done.3, f32[1,16]{1,0:T(1,128)S(1)} %copy-done.4, f32[1]{0:T(128)S(6)} %copy.10.gain, ...), custom_call_target="tpu_custom_call" | custom-call | tf_op jit(solution)/shard_map/border2/pallas_call | solution.py:355
  32.4 1.4 %collective-permute-start.2 = (f16[2,8,2,16,128]{4,3,2,1,0:T(8,128)(2,1)S(1)}, f16[2,8,2,16,128]{4,3,2,1,0:T(8,128)(2,1)S(1)}, u32[]{:S(2)}, u32[]{:S(2)}) collective-permute-start(f16[2,8,2,16,128]{4,3,2,1,0:T(8,128)(2,1)S(1)} %multiply_convert_fusion.1), channel_id=1, source_target_pairs={{0,1},{1,2},{2,3},{3,0},{4,5},{5,6},{6,7},{7,4},{8,9},{9,10},{10,1... | collective-permute-start | bytes 393224 | tf_op jit(solution)/shard_map/ppermute | solution.py:421
  33.8 1.6 %collective-permute-start.3 = (f16[2,8,2,16,128]{4,3,2,1,0:T(8,128)(2,1)S(1)}, f16[2,8,2,16,128]{4,3,2,1,0:T(8,128)(2,1)S(1)}, u32[]{:S(2)}, u32[]{:S(2)}) collective-permute-start(f16[2,8,2,16,128]{4,3,2,1,0:T(8,128)(2,1)S(1)} %multiply_convert_fusion), channel_id=1, source_target_pairs={{0,1},{1,2},{2,3},{3,0},{4,5},{5,6},{6,7},{7,4},{8,9},{9,10},{10,1... | collective-permute-start | bytes 393224 | tf_op jit(solution)/shard_map/ppermute | solution.py:421
  35.4 0.0 collective-permute-start.5
  35.4 4.6 %collective-permute-done.2 = f16[2,8,2,16,128]{4,3,2,1,0:T(8,128)(2,1)S(1)} collective-permute-done((f16[2,8,2,16,128]{4,3,2,1,0:T(8,128)(2,1)S(1)}, f16[2,8,2,16,128]{4,3,2,1,0:T(8,128)(2,1)S(1)}, u32[]{:S(2)}, u32[]{:S(2)}) %collective-permute-start.2) | collective-permute-done | bytes 131104 | tf_op jit(solution)/shard_map/ppermute | solution.py:421
  40.0 1.4 %collective-permute-done.3 = f16[2,8,2,16,128]{4,3,2,1,0:T(8,128)(2,1)S(1)} collective-permute-done((f16[2,8,2,16,128]{4,3,2,1,0:T(8,128)(2,1)S(1)}, f16[2,8,2,16,128]{4,3,2,1,0:T(8,128)(2,1)S(1)}, u32[]{:S(2)}, u32[]{:S(2)}) %collective-permute-start.3) | collective-permute-done | bytes 131104 | tf_op jit(solution)/shard_map/ppermute | solution.py:421
  41.4 0.1 multiply_add_fusion.1
  41.6 0.1 collective-permute-start.4
  41.7 1.5 %collective-permute-done.4 = f32[16,2,16,128]{3,2,1,0:T(8,128)S(1)} collective-permute-done((f32[16,2,16,128]{3,2,1,0:T(8,128)S(1)}, f32[16,2,16,128]{3,2,1,0:T(8,128)S(1)}, u32[]{:S(2)}, u32[]{:S(2)}) %collective-permute-start.4) | collective-permute-done | bytes 262176 | tf_op jit(solution)/shard_map/ppermute | solution.py:375
  43.2 0.0 collective-permute-done.5
  43.2 0.1 fusion.1
  43.4 0.9 %fusion = f16[16,2,16,512]{3,2,1,0:T(8,128)(2,1)} fusion(f32[16,1,16,384]{3,2,1,0:T(8,128)S(1)} %get-tuple-element.40, f32[16,1,16,384]{3,2,1,0:T(8,128)S(1)} %get-tuple-element.39, f32[16,1,16,128]{3,2,1,0:T(8,128)S(1)} %get-tuple-element.42, f32[16,1,16,128]{3,2,1,0:T(8,128)S(1)} %get-tuple-element.41), kind=kLoop, calls=%fused_computation.1 | loop fusion | flops 1310720 | bytes 1572864 | tf_op jit(solution)/shard_map/convert_element_type | solution.py:383
  44.3 8.0 %all-to-all-start = ((f16[16,2,16,512]{3,2,1,0:T(8,128)(2,1)}), f16[16,2,16,512]{3,2,1,0:T(8,128)(2,1)S(1)}, u32[]{:S(2)}, u32[]{:S(2)}) async-start(f16[16,2,16,512]{3,2,1,0:T(8,128)(2,1)} %fusion), calls=%async_computation | async-start | bytes 1048576 | tf_op jit(solution)/shard_map/all_to_all | solution.py:385
  52.4 11.7 %all-to-all-done = f16[16,2,16,512]{3,2,1,0:T(8,128)(2,1)S(1)} async-done(((f16[16,2,16,512]{3,2,1,0:T(8,128)(2,1)}), f16[16,2,16,512]{3,2,1,0:T(8,128)(2,1)S(1)}, u32[]{:S(2)}, u32[]{:S(2)}) %all-to-all-start) | async-done | bytes 524320 | tf_op jit(solution)/shard_map/all_to_all | solution.py:385
  64.1 0.1 convert_multiply_fusion
  64.3 0.7 %multiply_add_fusion.4 = (f32[16,512]{1,0:T(8,128)}, f32[16,512]{1,0:T(8,128)S(1)}, f32[16,512]{1,0:T(8,128)S(1)}) fusion(f32[16,2,16,512]{3,2,1,0:T(8,128)S(1)} %convert_multiply_fusion), kind=kLoop, calls=%fused_computation.99 | loop fusion | flops 368640 | bytes 622592 | tf_op jit(solution)/shard_map/add | solution.py:370
  64.9 0.8 %fusion.13 = f32[16,512]{1,0:T(8,128)} fusion(f32[16,2,16,512]{3,2,1,0:T(8,128)S(1)} %convert_multiply_fusion, f32[16,512]{1,0:T(8,128)S(1)} %get-tuple-element.38, f32[16,512]{1,0:T(8,128)S(1)} %get-tuple-element.37, f32[512]{0:T(512)S(1)} %bitcast.330, f32[512]{0:T(512)S(1)} %bitcast.355, f32[512]{0:T(512)S(1)} %bitcast.353, f32[512]{0:T(512)S(1)} %bitcast.352, ...), kind=kLoop, calls=%fused_computation.30 | loop fusion | flops 1155072 | bytes 1208320 | tf_op jit(solution)/shard_map/add | solution.py:369
  (14 shorter events, 0.2 us)
Async XLA Ops:
  0.6 10.9 %copy-start.1 = (s32[1,16]{1,0:T(1,128)S(1)}, s32[1,16]{1,0:T(1,128)}, u32[]{:S(2)}) copy-start(s32[1,16]{1,0:T(1,128)} %offset.7) | copy-start | bytes 196
  0.6 10.9 %copy-start = (s32[1,4,4]{2,1,0:T(4,128)S(1)}, s32[1,4,4]{2,1,0:T(4,128)}, u32[]{:S(2)}) copy-start(s32[1,4,4]{2,1,0:T(4,128)} %occ.7) | copy-start | bytes 196
  0.7 10.9 %copy-start.4 = (f32[1,16]{1,0:T(1,128)S(1)}, f32[1,16]{1,0:T(1,128)}, u32[]{:S(2)}) copy-start(f32[1,16]{1,0:T(1,128)} %extinction.5) | copy-start | bytes 196
  0.7 10.9 %copy-start.3 = (f32[1,16]{1,0:T(1,128)S(1)}, f32[1,16]{1,0:T(1,128)}, u32[]{:S(2)}) copy-start(f32[1,16]{1,0:T(1,128)} %frac_vertical.5) | copy-start | bytes 196
  0.7 10.9 %copy-start.2 = (f32[1,16]{1,0:T(1,128)S(1)}, f32[1,16]{1,0:T(1,128)}, u32[]{:S(2)}) copy-start(f32[1,16]{1,0:T(1,128)} %frac_lateral.5) | copy-start | bytes 196
  0.7 10.9 %copy-start.5 = (s32[32]{0:T(128)S(1)}, s32[32]{0:T(128)}, u32[]{:S(2)}) copy-start(s32[32]{0:T(128)} %rank.1) | copy-start | bytes 388
  6.7 17.8 %collective-permute-start = (bf16[4,512,128]{2,1,0:T(8,128)(2,1)}, bf16[4,512,128]{2,1,0:T(8,128)(2,1)S(1)}, u32[]{:S(2)}, u32[]{:S(2)}) collective-permute-start(bf16[4,512,128]{2,1,0:T(8,128)(2,1)} %get-tuple-element.23), channel_id=1, source_target_pairs={{0,3},{1,0},{2,1},{3,2},{4,7},{5,4},{6,5},{7,6},{8,11},{9,8},{10,9... | collective-permute-start | bytes 1572872 | tf_op jit(solution)/shard_map/ppermute | solution.py:412
  9.5 15.0 %collective-permute-start.1 = (bf16[4,512,128]{2,1,0:T(8,128)(2,1)}, bf16[4,512,128]{2,1,0:T(8,128)(2,1)S(1)}, u32[]{:S(2)}, u32[]{:S(2)}) collective-permute-start(bf16[4,512,128]{2,1,0:T(8,128)(2,1)} %get-tuple-element.24), channel_id=1, source_target_pairs={{0,1},{1,2},{2,3},{4,5},{5,6},{6,7},{8,9},{9,10},{10,11},{12,13},{... | collective-permute-start | bytes 1572872 | tf_op jit(solution)/shard_map/ppermute | solution.py:413
  32.4 7.6 %collective-permute-start.2 = (f16[2,8,2,16,128]{4,3,2,1,0:T(8,128)(2,1)S(1)}, f16[2,8,2,16,128]{4,3,2,1,0:T(8,128)(2,1)S(1)}, u32[]{:S(2)}, u32[]{:S(2)}) collective-permute-start(f16[2,8,2,16,128]{4,3,2,1,0:T(8,128)(2,1)S(1)} %multiply_convert_fusion.1), channel_id=1, source_target_pairs={{0,1},{1,2},{2,3},{3,0},{4,5},{5,6},{6,7},{7,4},{8,9},{9,10},{10,1... | collective-permute-start | bytes 393224 | tf_op jit(solution)/shard_map/ppermute | solution.py:421
  33.8 7.6 %collective-permute-start.3 = (f16[2,8,2,16,128]{4,3,2,1,0:T(8,128)(2,1)S(1)}, f16[2,8,2,16,128]{4,3,2,1,0:T(8,128)(2,1)S(1)}, u32[]{:S(2)}, u32[]{:S(2)}) collective-permute-start(f16[2,8,2,16,128]{4,3,2,1,0:T(8,128)(2,1)S(1)} %multiply_convert_fusion), channel_id=1, source_target_pairs={{0,1},{1,2},{2,3},{3,0},{4,5},{5,6},{6,7},{7,4},{8,9},{9,10},{10,1... | collective-permute-start | bytes 393224 | tf_op jit(solution)/shard_map/ppermute | solution.py:421
  35.4 7.8 %collective-permute-start.5 = (f32[16,2,16,384]{3,2,1,0:T(8,128)S(1)}, f32[16,2,16,384]{3,2,1,0:T(8,128)S(1)}, u32[]{:S(2)}, u32[]{:S(2)}) collective-permute-start(f32[16,2,16,384]{3,2,1,0:T(8,128)S(1)} %get-tuple-element.35), channel_id=1, source_target_pairs={{0,4},{4,0},{8,12},{12,8},{16,20},{20,16},{24,28},{28,24},{32,36},... | collective-permute-start | bytes 2359304 | tf_op jit(solution)/shard_map/ppermute | solution.py:375
  41.6 1.6 %collective-permute-start.4 = (f32[16,2,16,128]{3,2,1,0:T(8,128)S(1)}, f32[16,2,16,128]{3,2,1,0:T(8,128)S(1)}, u32[]{:S(2)}, u32[]{:S(2)}) collective-permute-start(f32[16,2,16,128]{3,2,1,0:T(8,128)S(1)} %get-tuple-element.43), channel_id=1, source_target_pairs={{0,4},{4,0},{8,12},{12,8},{16,20},{20,16},{24,28},{28,24},{32,36},... | collective-permute-start | bytes 786440 | tf_op jit(solution)/shard_map/ppermute | solution.py:375
  44.3 19.8 %all-to-all-start = ((f16[16,2,16,512]{3,2,1,0:T(8,128)(2,1)}), f16[16,2,16,512]{3,2,1,0:T(8,128)(2,1)S(1)}, u32[]{:S(2)}, u32[]{:S(2)}) async-start(f16[16,2,16,512]{3,2,1,0:T(8,128)(2,1)} %fusion), calls=%async_computation | async-start | bytes 1048576 | tf_op jit(solution)/shard_map/all_to_all | solution.py:385

commit v8 on v7

--- a/solution.py
+++ b/solution.py
@@ -56,60 +56,65 @@
             self.first.append(first - LANES * tile)
 
 
-def pack_kernel(occ, offset, x_first, x_last, to_left, to_right, picks, packed):
-    block = pl.program_id(0)
-    slices, cols = x_first.shape[1], LANES
+def pack_kernel(occ, offset, density, to_left, to_right, columns, picks, packed, arrived):
+    slices, rows, cols = density.shape[1:]
     packing = Packing(offset)
-
-    @pl.when(block == 0)
-    def _():
-        k = lax.broadcasted_iota(jnp.int32, (LANES, 2 * LANES), 0)
-        p = lax.broadcasted_iota(jnp.int32, (LANES, 2 * LANES), 1)
-        for s in range(slices):
-            skip = jnp.where(packing.from_left[s], cols - packing.count[s], 0)
-            inside = (k >= skip) & (k < skip + packing.count[s])
-            same = k - skip == p - packing.first[s]
-            picks[s] = jnp.where(inside & same, 1.0, 0.0).astype(BF16)
-
+    copies = []
+    for s in range(slices):
+        column = pl.multiple_of(jnp.where(packing.from_left[s], cols - LANES, 0), LANES)
+        copy = pltpu.make_async_copy(
+            density.at[0, s, :, pl.ds(column, LANES)], columns.at[s], arrived.at[s]
+        )
+        copy.start()
+        copies.append(copy)
+    k = lax.broadcasted_iota(jnp.int32, (LANES, 2 * LANES), 0)
+    p = lax.broadcasted_iota(jnp.int32, (LANES, 2 * LANES), 1)
+    for s in range(slices):
+        skip = jnp.where(packing.from_left[s], LANES - packing.count[s], 0)
+        inside = (k >= skip) & (k < skip + packing.count[s])
+        same = k - skip == p - packing.first[s]
+        picks[s] = jnp.where(inside & same, 1.0, 0.0).astype(BF16)
     packed[...] = jnp.zeros_like(packed)
-    first_occ = occ[0, block, 0].astype(F32)
-    last_occ = occ[0, block, occ.shape[2] - 1].astype(F32)
+    last = occ.shape[2] - 1
     for s in range(slices):
+        copies[s].wait()
         from_left = packing.from_left[s]
-        columns = x_first[0, s] * splat(jnp.where(from_left, 0.0, first_occ)) + x_last[
-            0, s
-        ] * splat(jnp.where(from_left, last_occ, 0.0))
-        moved = jnp.dot(columns, picks[s], preferred_element_type=F32).astype(BF16)
         way = jnp.where(from_left, 1, 0)
         tile = packing.tile[s]
-        packed[way, tile] += moved[:, :LANES]
-        packed[way, tile + 1] += moved[:, LANES:]
+        for b in range(rows // BLK):
+            at = slice(b * BLK, (b + 1) * BLK)
+            occupied = jnp.where(from_left, occ[0, b, last], occ[0, b, 0])
+            moved = jnp.dot(
+                columns[s, at] * splat(occupied), picks[s], preferred_element_type=F32
+            ).astype(BF16)
+            packed[way, tile, at] += moved[:, :LANES]
+            packed[way, tile + 1, at] += moved[:, LANES:]
     to_left[...] = packed[0]
     to_right[...] = packed[1]
 
 
 def pack_halo(density, occupancy, offsets):
-    _, slices, rows, cols = density.shape
+    _, slices, rows, _ = density.shape
     tiles = PACKED // LANES
     shape = jax.ShapeDtypeStruct((tiles, rows, LANES), BF16)
-    last = cols // LANES - 1
     return pl.pallas_call(
         pack_kernel,
-        grid=(rows // BLK,),
         in_specs=[
             pl.BlockSpec(memory_space=SMEM),
             pl.BlockSpec(memory_space=SMEM),
-            pl.BlockSpec((1, slices, BLK, LANES), lambda b: (0, 0, b, 0)),
-            pl.BlockSpec((1, slices, BLK, LANES), lambda b: (0, 0, b, last)),
+            pl.BlockSpec(memory_space=pl.ANY),
         ],
-        out_specs=[pl.BlockSpec((tiles, BLK, LANES), lambda b: (0, b, 0))] * 2,
+        out_specs=[whole()] * 2,
         out_shape=[shape, shape],
         scratch_shapes=[
+            pltpu.VMEM((slices, rows, LANES), BF16),
             pltpu.VMEM((slices, LANES, 2 * LANES), BF16),
-            pltpu.VMEM((2, tiles, BLK, LANES), BF16),
+            pltpu.VMEM((2, tiles, rows, LANES), BF16),
+            pltpu.SemaphoreType.DMA((slices,)),
         ],
+        compiler_params=pltpu.CompilerParams(vmem_limit_bytes=32 * 2**20),
         name="pack_halo",
-    )(occupancy, offsets, density, density)
+    )(occupancy, offsets, density)
 
 
 def whole():
@@ -377,10 +382,14 @@
     return jnp.stack(over((keep[:, 0], keep[:, 1]), (other[:, 0], other[:, 1]), front), axis=1)
 
 
+def wire(image):
+    return (image * WIRE_SCALE).astype(WIRE)
+
+
 def over_chips(pieces, flags):
     count = lax.axis_size("depth")
     chips = count // 2
-    pieces = (pieces * WIRE_SCALE).astype(WIRE)
+    pieces = wire(pieces)
     groups = [[2 * i + core for i in range(chips)] for core in range(2)]
     pieces = lax.all_to_all(
         pieces, "depth", 0, 0, axis_index_groups=groups, tiled=True
@@ -416,17 +425,17 @@
     (keep, send, weights, flags), halos = lax.optimization_barrier((images, halos))
     inner = over_cores(keep, send, flags)
 
-    def edge_rows(first, count, weights):
-        image = jnp.stack(border(density, small, weights, halos, first, count, slice_total))
-        moved = lax.ppermute((image * WIRE_SCALE).astype(WIRE), "lat", around)
-        below = flags[16, :LANES]
-        return image, image * (1.0 - below) + moved.astype(F32) * (below / WIRE_SCALE)
-
     half = blocks // 2
-    top, moved_top = edge_rows(0, half, weights)
-    weights, _ = lax.optimization_barrier((weights, top))
-    _, moved_bottom = edge_rows(half, blocks - half, weights)
-    keep, send = jnp.concatenate([moved_top, moved_bottom], axis=1)
+    tops = jnp.stack(border(density, small, weights, halos, 0, half, slice_total))
+    moved_tops = lax.ppermute(wire(tops), "lat", around)
+    weights, tops = lax.optimization_barrier((weights, tops))
+    ends = jnp.stack(border(density, small, weights, halos, half, blocks - half, slice_total))
+    ends, moved_tops = lax.optimization_barrier((ends, moved_tops))
+    moved_ends = lax.ppermute(wire(ends), "lat", around)
+    images = jnp.concatenate([tops, ends], axis=1)
+    moved = jnp.concatenate([moved_tops, moved_ends], axis=1)
+    below = flags[16, :LANES]
+    keep, send = images * (1.0 - below) + moved.astype(F32) * (below / WIRE_SCALE)
     edge = over_cores(keep, send, flags)
     return tuple(over_chips(jnp.concatenate([edge, inner], axis=3), flags))
 

time: 66.1 us -> 66.6 us (level)
  local copies, waits for them, and re-layouts: 0.07 us -> 1.42 us
  starting transfers between devices: 15.3 us -> 14.6 us
    unnamed x12, local copies, waits for them, and re-layouts: 0.03 us -> 1.34 us
    ppermute x2, starting transfers between devices: 2.97 us -> 2.23 us  [the longest x1 1.59 us: shards(): moved_tops = lax.ppermute(wire(tops), 'lat', around)]
    pallas_call x1, Pallas kernels: 6.01 us -> 5.34 us  [pack_halo(): pl.pallas_call(pack_kernel, in_specs=[pl.BlockSpec(memory_space=SMEM), pl...]
  transfers between devices with their start and end apart: 7 -> 7, of which waited for: 4 -> 4; matrix products, arithmetic and copies ran while one was open for 0% -> 0% of each run, Pallas kernels for 20% -> 25%
where the time goes in v8:
time: 66.6 us; the launch traced here: 66.2 us
  Pallas kernels  26.1 us (39%)
  waiting for transfers between devices  19.7 us (30%)
  starting transfers between devices  14.6 us (22%)
  other arithmetic  2.97 us (4%)
  between operations  1.49 us (2%)
  local copies, waits for them, and re-layouts  1.42 us (2%)
    pallas_call x1, Pallas kernels, interior(): pl.pallas_call(functools.partial(interior_kernel, slice_total), grid=(row...  13 us
    all_to_all x1, waiting for transfers between devices, over_chips(): lax.all_to_all(pieces, 'depth', 0, 0, axis_index_groups=groups, tiled=True)  11.7 us
    all_to_all x1, starting transfers between devices, over_chips(): lax.all_to_all(pieces, 'depth', 0, 0, axis_index_groups=groups, tiled=True)  8.05 us
    pallas_call x2, Pallas kernels, border(): pl.pallas_call(functools.partial(border_kernel, start, slice_total), grid...  7.74 us
    ppermute x1, waiting for transfers between devices, shards(): moved_ends = lax.ppermute(wire(ends), 'lat', around)  5.58 us
    pallas_call x1, Pallas kernels, pack_halo(): pl.pallas_call(pack_kernel, in_specs=[pl.BlockSpec(memory_space=SMEM), pl...  5.34 us
    ppermute x1, starting transfers between devices, shards(): lax.ppermute(to_left, 'lat', leftwards)  2.91 us
    ppermute x1, starting transfers between devices, shards(): moved_tops = lax.ppermute(wire(tops), 'lat', around)  1.59 us
  transfers between devices with their start and end apart: 7, of which 4 were waited for; matrix products, arithmetic and copies ran while one was open for 0% of the time, Pallas kernels for 25%

profile of v8, /device:TPU:0, one launch (start us, length us, event | category | flops | bytes accessed | tf_op | source)
XLA Modules:
  0.0 66.2 jit_solution(4333972656317382553)
XLA Ops:
  0.6 0.0 copy-start
  0.6 0.7 %copy-done = s32[1,4,4]{2,1,0:T(4,128)S(1)} copy-done((s32[1,4,4]{2,1,0:T(4,128)S(1)}, s32[1,4,4]{2,1,0:T(4,128)}, u32[]{:S(2)}) %copy-start) | copy-done | bytes 88
  1.3 0.0 copy-start.1
  1.3 0.7 copy-done.1
  2.0 5.3 %pack_halo.1 = (bf16[4,512,128]{2,1,0:T(8,128)(2,1)S(1)}, bf16[4,512,128]{2,1,0:T(8,128)(2,1)S(1)}) custom-call(s32[1,4,4]{2,1,0:T(4,128)S(1)} %copy-done, s32[1,16]{1,0:T(1,128)S(1)} %copy-done.1, bf16[1,16,512,512]{3,2,1,0:T(8,128)(2,1)} %last_lead.3), custom_call_target="tpu_custom_call" | custom-call | tf_op jit(solution)/shard_map/pack_halo/pallas_call | solution.py:100
  7.3 2.9 %collective-permute-start = (bf16[4,512,128]{2,1,0:T(8,128)(2,1)S(1)}, bf16[4,512,128]{2,1,0:T(8,128)(2,1)S(1)}, u32[]{:S(2)}, u32[]{:S(2)}) collective-permute-start(bf16[4,512,128]{2,1,0:T(8,128)(2,1)S(1)} %get-tuple-element.26), channel_id=1, source_target_pairs={{0,3},{1,0},{2,1},{3,2},{4,7},{5,4},{6,5},{7,6},{8,11},{9,8},{10,9... | collective-permute-start | bytes 1572872 | tf_op jit(solution)/shard_map/ppermute | solution.py:421
  10.2 1.3 %collective-permute-start.1 = (bf16[4,512,128]{2,1,0:T(8,128)(2,1)S(1)}, bf16[4,512,128]{2,1,0:T(8,128)(2,1)S(1)}, u32[]{:S(2)}, u32[]{:S(2)}) collective-permute-start(bf16[4,512,128]{2,1,0:T(8,128)(2,1)S(1)} %get-tuple-element.27), channel_id=1, source_target_pairs={{0,1},{1,2},{2,3},{4,5},{5,6},{6,7},{8,9},{9,10},{10,11},{12,13},{... | collective-permute-start | bytes 1572872 | tf_op jit(solution)/shard_map/ppermute | solution.py:422
  12.2 0.0 copy-done.2
  12.2 0.0 copy-done.3
  12.2 0.0 copy-done.4
  12.2 0.0 copy-done.5
  12.2 13.0 %interior.1 = (f32[16,2,16,384]{3,2,1,0:T(8,128)S(1)}, f32[16,2,16,384]{3,2,1,0:T(8,128)S(1)}, bf16[16,512,128]{2,1,0:T(8,128)(2,1)S(1)}, f32[24,512]{1,0:T(8,128)S(1)}) custom-call(s32[1,4,4]{2,1,0:T(4,128)S(1)} %copy-done, s32[1,16]{1,0:T(1,128)S(1)} %copy-done.1, f32[1,16]{1,0:T(1,128)S(1)} %copy-done.2, f32[1,16]{1,0:T(1,128)S(1)} %copy-done.3, ...), custom_call_target="tpu_custom_call" | custom-call | tf_op jit(solution)/shard_map/interior/pallas_call | solution.py:252
  25.2 0.0 collective-permute-done.right_ref
  25.2 0.0 collective-permute-done.1.left_ref
  25.3 3.9 %border0.1 = (f32[8,2,16,128]{3,2,1,0:T(8,128)S(1)}, f32[8,2,16,128]{3,2,1,0:T(8,128)S(1)}) custom-call(s32[1,4,4]{2,1,0:T(4,128)S(1)} %copy-done, s32[1,16]{1,0:T(1,128)S(1)} %copy-done.1, f32[1,16]{1,0:T(1,128)S(1)} %copy-done.2, f32[1,16]{1,0:T(1,128)S(1)} %copy-done.3, f32[1,16]{1,0:T(1,128)S(1)} %copy-done.4, f32[1]{0:T(128)S(6)} %copy.10.gain, ...), custom_call_target="tpu_custom_call" | custom-call | tf_op jit(solution)/shard_map/border0/pallas_call | solution.py:360
  29.2 1.6 %collective-permute-start.2 = (f16[2,8,2,16,128]{4,3,2,1,0:T(8,128)(2,1)S(1)}, f16[2,8,2,16,128]{4,3,2,1,0:T(8,128)(2,1)S(1)}, u32[]{:S(2)}, u32[]{:S(2)}) collective-permute-start(f16[2,8,2,16,128]{4,3,2,1,0:T(8,128)(2,1)S(1)} %get-tuple-element.51), channel_id=1, source_target_pairs={{0,1},{1,2},{2,3},{3,0},{4,5},{5,6},{6,7},{7,4},{8,9},{9,10},{10,1... | collective-permute-start | bytes 393224 | tf_op jit(solution)/shard_map/ppermute | solution.py:430
  30.8 3.9 %border2.1 = (f32[8,2,16,128]{3,2,1,0:T(8,128)S(1)}, f32[8,2,16,128]{3,2,1,0:T(8,128)S(1)}) custom-call(s32[1,4,4]{2,1,0:T(4,128)S(1)} %copy-done, s32[1,16]{1,0:T(1,128)S(1)} %copy-done.1, f32[1,16]{1,0:T(1,128)S(1)} %copy-done.2, f32[1,16]{1,0:T(1,128)S(1)} %copy-done.3, f32[1,16]{1,0:T(1,128)S(1)} %copy-done.4, f32[1]{0:T(128)S(6)} %copy.10.gain, ...), custom_call_target="tpu_custom_call" | custom-call | tf_op jit(solution)/shard_map/border2/pallas_call | solution.py:360
  34.7 0.9 %collective-permute-done.2 = f16[2,8,2,16,128]{4,3,2,1,0:T(8,128)(2,1)S(1)} collective-permute-done((f16[2,8,2,16,128]{4,3,2,1,0:T(8,128)(2,1)S(1)}, f16[2,8,2,16,128]{4,3,2,1,0:T(8,128)(2,1)S(1)}, u32[]{:S(2)}, u32[]{:S(2)}) %collective-permute-start.2) | collective-permute-done | bytes 131104 | tf_op jit(solution)/shard_map/ppermute | solution.py:430
  35.6 0.6 collective-permute-start.3
  36.3 0.0 collective-permute-start.5
  36.3 5.6 %collective-permute-done.3 = f16[2,8,2,16,128]{4,3,2,1,0:T(8,128)(2,1)S(1)} collective-permute-done((f16[2,8,2,16,128]{4,3,2,1,0:T(8,128)(2,1)S(1)}, f16[2,8,2,16,128]{4,3,2,1,0:T(8,128)(2,1)S(1)}, u32[]{:S(2)}, u32[]{:S(2)}) %collective-permute-start.3) | collective-permute-done | bytes 131104 | tf_op jit(solution)/shard_map/ppermute | solution.py:434
  41.9 0.1 fusion.1
  42.0 0.1 collective-permute-start.4
  42.2 1.5 %collective-permute-done.4 = f32[16,2,16,128]{3,2,1,0:T(8,128)S(1)} collective-permute-done((f32[16,2,16,128]{3,2,1,0:T(8,128)S(1)}, f32[16,2,16,128]{3,2,1,0:T(8,128)S(1)}, u32[]{:S(2)}, u32[]{:S(2)}) %collective-permute-start.4) | collective-permute-done | bytes 262176 | tf_op jit(solution)/shard_map/ppermute | solution.py:380
  43.7 0.0 collective-permute-done.5
  43.7 0.2 fusion.2
  43.9 0.9 %fusion = f16[16,2,16,512]{3,2,1,0:T(8,128)(2,1)} fusion(f32[16,1,16,384]{3,2,1,0:T(8,128)S(1)} %get-tuple-element.46, f32[16,1,16,384]{3,2,1,0:T(8,128)S(1)} %get-tuple-element.45, f32[16,1,16,128]{3,2,1,0:T(8,128)S(1)} %get-tuple-element.48, f32[16,1,16,128]{3,2,1,0:T(8,128)S(1)} %get-tuple-element.47), kind=kLoop, calls=%fused_computation.1 | loop fusion | flops 1310720 | bytes 1572864 | tf_op jit(solution)/shard_map/convert_element_type | solution.py:386
  44.8 8.0 %all-to-all-start = ((f16[16,2,16,512]{3,2,1,0:T(8,128)(2,1)}), f16[16,2,16,512]{3,2,1,0:T(8,128)(2,1)S(1)}, u32[]{:S(2)}, u32[]{:S(2)}) async-start(f16[16,2,16,512]{3,2,1,0:T(8,128)(2,1)} %fusion), calls=%async_computation | async-start | bytes 1048576 | tf_op jit(solution)/shard_map/all_to_all | solution.py:394
  52.9 11.7 %all-to-all-done = f16[16,2,16,512]{3,2,1,0:T(8,128)(2,1)S(1)} async-done(((f16[16,2,16,512]{3,2,1,0:T(8,128)(2,1)}), f16[16,2,16,512]{3,2,1,0:T(8,128)(2,1)S(1)}, u32[]{:S(2)}, u32[]{:S(2)}) %all-to-all-start) | async-done | bytes 524320 | tf_op jit(solution)/shard_map/all_to_all | solution.py:394
  64.6 0.1 convert_multiply_fusion
  64.8 0.7 %multiply_add_fusion.2 = (f32[16,512]{1,0:T(8,128)}, f32[16,512]{1,0:T(8,128)S(1)}, f32[16,512]{1,0:T(8,128)S(1)}) fusion(f32[16,2,16,512]{3,2,1,0:T(8,128)S(1)} %convert_multiply_fusion), kind=kLoop, calls=%fused_computation.95 | loop fusion | flops 368640 | bytes 622592 | tf_op jit(solution)/shard_map/add | solution.py:375
  65.5 0.8 %fusion.11 = f32[16,512]{1,0:T(8,128)} fusion(f32[16,2,16,512]{3,2,1,0:T(8,128)S(1)} %convert_multiply_fusion, f32[16,512]{1,0:T(8,128)S(1)} %get-tuple-element.44, f32[16,512]{1,0:T(8,128)S(1)} %get-tuple-element.43, f32[512]{0:T(512)S(1)} %bitcast.326, f32[512]{0:T(512)S(1)} %bitcast.351, f32[512]{0:T(512)S(1)} %bitcast.349, f32[512]{0:T(512)S(1)} %bitcast.348, ...), kind=kLoop, calls=%fused_computation.26 | loop fusion | flops 1155072 | bytes 1208320 | tf_op jit(solution)/shard_map/add | solution.py:374
  (15 shorter events, 0.3 us)
Async XLA Ops:
  0.6 0.7 %copy-start = (s32[1,4,4]{2,1,0:T(4,128)S(1)}, s32[1,4,4]{2,1,0:T(4,128)}, u32[]{:S(2)}) copy-start(s32[1,4,4]{2,1,0:T(4,128)} %occ.7) | copy-start | bytes 196
  1.3 0.7 copy-start.1
  2.0 10.2 %copy-start.2 = (f32[1,16]{1,0:T(1,128)S(1)}, f32[1,16]{1,0:T(1,128)}, u32[]{:S(2)}) copy-start(f32[1,16]{1,0:T(1,128)} %frac_lateral.5) | copy-start | bytes 196
  2.0 10.2 %copy-start.3 = (f32[1,16]{1,0:T(1,128)S(1)}, f32[1,16]{1,0:T(1,128)}, u32[]{:S(2)}) copy-start(f32[1,16]{1,0:T(1,128)} %frac_vertical.5) | copy-start | bytes 196
  2.0 10.3 %copy-start.4 = (f32[1,16]{1,0:T(1,128)S(1)}, f32[1,16]{1,0:T(1,128)}, u32[]{:S(2)}) copy-start(f32[1,16]{1,0:T(1,128)} %extinction.5) | copy-start | bytes 196
  2.0 10.3 %copy-start.5 = (s32[32]{0:T(128)S(1)}, s32[32]{0:T(128)}, u32[]{:S(2)}) copy-start(s32[32]{0:T(128)} %rank.1) | copy-start | bytes 388
  7.3 17.9 %collective-permute-start = (bf16[4,512,128]{2,1,0:T(8,128)(2,1)S(1)}, bf16[4,512,128]{2,1,0:T(8,128)(2,1)S(1)}, u32[]{:S(2)}, u32[]{:S(2)}) collective-permute-start(bf16[4,512,128]{2,1,0:T(8,128)(2,1)S(1)} %get-tuple-element.26), channel_id=1, source_target_pairs={{0,3},{1,0},{2,1},{3,2},{4,7},{5,4},{6,5},{7,6},{8,11},{9,8},{10,9... | collective-permute-start | bytes 1572872 | tf_op jit(solution)/shard_map/ppermute | solution.py:421
  10.2 15.0 %collective-permute-start.1 = (bf16[4,512,128]{2,1,0:T(8,128)(2,1)S(1)}, bf16[4,512,128]{2,1,0:T(8,128)(2,1)S(1)}, u32[]{:S(2)}, u32[]{:S(2)}) collective-permute-start(bf16[4,512,128]{2,1,0:T(8,128)(2,1)S(1)} %get-tuple-element.27), channel_id=1, source_target_pairs={{0,1},{1,2},{2,3},{4,5},{5,6},{6,7},{8,9},{9,10},{10,11},{12,13},{... | collective-permute-start | bytes 1572872 | tf_op jit(solution)/shard_map/ppermute | solution.py:422
  29.2 6.4 %collective-permute-start.2 = (f16[2,8,2,16,128]{4,3,2,1,0:T(8,128)(2,1)S(1)}, f16[2,8,2,16,128]{4,3,2,1,0:T(8,128)(2,1)S(1)}, u32[]{:S(2)}, u32[]{:S(2)}) collective-permute-start(f16[2,8,2,16,128]{4,3,2,1,0:T(8,128)(2,1)S(1)} %get-tuple-element.51), channel_id=1, source_target_pairs={{0,1},{1,2},{2,3},{3,0},{4,5},{5,6},{6,7},{7,4},{8,9},{9,10},{10,1... | collective-permute-start | bytes 393224 | tf_op jit(solution)/shard_map/ppermute | solution.py:430
  35.6 6.2 %collective-permute-start.3 = (f16[2,8,2,16,128]{4,3,2,1,0:T(8,128)(2,1)S(1)}, f16[2,8,2,16,128]{4,3,2,1,0:T(8,128)(2,1)S(1)}, u32[]{:S(2)}, u32[]{:S(2)}) collective-permute-start(f16[2,8,2,16,128]{4,3,2,1,0:T(8,128)(2,1)S(1)} %multiply_convert_fusion), channel_id=1, source_target_pairs={{0,1},{1,2},{2,3},{3,0},{4,5},{5,6},{6,7},{7,4},{8,9},{9,10},{10,1... | collective-permute-start | bytes 393224 | tf_op jit(solution)/shard_map/ppermute | solution.py:434
  36.3 7.4 %collective-permute-start.5 = (f32[16,2,16,384]{3,2,1,0:T(8,128)S(1)}, f32[16,2,16,384]{3,2,1,0:T(8,128)S(1)}, u32[]{:S(2)}, u32[]{:S(2)}) collective-permute-start(f32[16,2,16,384]{3,2,1,0:T(8,128)S(1)} %get-tuple-element.41), channel_id=1, source_target_pairs={{0,4},{4,0},{8,12},{12,8},{16,20},{20,16},{24,28},{28,24},{32,36},... | collective-permute-start | bytes 2359304 | tf_op jit(solution)/shard_map/ppermute | solution.py:380
  42.0 1.6 %collective-permute-start.4 = (f32[16,2,16,128]{3,2,1,0:T(8,128)S(1)}, f32[16,2,16,128]{3,2,1,0:T(8,128)S(1)}, u32[]{:S(2)}, u32[]{:S(2)}) collective-permute-start(f32[16,2,16,128]{3,2,1,0:T(8,128)S(1)} %get-tuple-element.49), channel_id=1, source_target_pairs={{0,4},{4,0},{8,12},{12,8},{16,20},{20,16},{24,28},{28,24},{32,36},... | collective-permute-start | bytes 786440 | tf_op jit(solution)/shard_map/ppermute | solution.py:380
  44.8 19.8 %all-to-all-start = ((f16[16,2,16,512]{3,2,1,0:T(8,128)(2,1)}), f16[16,2,16,512]{3,2,1,0:T(8,128)(2,1)S(1)}, u32[]{:S(2)}, u32[]{:S(2)}) async-start(f16[16,2,16,512]{3,2,1,0:T(8,128)(2,1)} %fusion), calls=%async_computation | async-start | bytes 1048576 | tf_op jit(solution)/shard_map/all_to_all | solution.py:394

commit v9 on v7

--- a/solution.py
+++ b/solution.py
@@ -14,7 +14,8 @@
 PIECE = 16
 WIRE = jnp.float16
 WIRE_SCALE = 4096.0
-PACKED = 4 * LANES
+PACKED = 5 * LANES
+HALF = SHIFT // 2
 LOG2E = math.log2(math.e)
 SMEM = pltpu.SMEM
 F32 = jnp.float32
@@ -33,13 +34,7 @@
 class Packing:
     def __init__(self, offset):
         slices = offset.shape[1]
-        lane = lax.broadcasted_iota(jnp.int32, (8, LANES), 1)
-        right, left = jnp.zeros_like(lane), jnp.zeros_like(lane)
-        for s in range(slices):
-            right = right + jnp.maximum(lane - offset[0, s], 0)
-            left = left + jnp.maximum(offset[0, s] + 1 - lane, 0)
-        fits = (right <= PACKED) & (left <= PACKED)
-        self.border = jnp.min(jnp.where(fits, lane.astype(F32), 127.0)).astype(jnp.int32)
+        self.border = HALF
         self.from_left, self.count, self.tile, self.first = [], [], [], []
         used = [0, 0]
         for s in range(slices):
@@ -54,6 +49,7 @@
             self.count.append(count)
             self.tile.append(tile)
             self.first.append(first - LANES * tile)
+        self.overflow = jnp.maximum(used[0], used[1]) > PACKED
 
 
 def pack_kernel(occ, offset, x_first, x_last, to_left, to_right, picks, packed):
@@ -179,7 +175,7 @@
 
 def interior_kernel(
     slice_total, occ, offset, frac_lateral, frac_vertical, extinction, gain, rank,
-    x_ref, lead_ref, out_keep, out_send, out_weights, flags, weights, through_ref, sum_ref,
+    x_ref, lead_ref, out_keep, out_send, out_weights, weights, flags, overflow, through_ref, sum_ref,
 ):
     block = pl.program_id(0)
     slices, rows = x_ref.shape[1], x_ref.shape[2]
@@ -198,8 +194,7 @@
         packing = Packing(offset)
         for s in range(slices):
             border_weights(s, offset, frac_lateral, packing, weights, out_weights)
-        lane = lax.broadcasted_iota(jnp.int32, (1, flags.shape[1]), 1)
-        flags[16:17] = jnp.where(lane < packing.border, 1.0, 0.0)
+        overflow[0] = jnp.where(packing.overflow, 1, 0)
         me = lax.axis_index("depth")
         in_front = [rank[me] < rank[jnp.bitwise_xor(me, 1)]]
         for span in (2, 4, 8, 16):
@@ -261,16 +256,19 @@
         * 2
         + [
             pl.BlockSpec((slices, 4 * LANES, LANES), lambda b: (0, 0, 0)),
-            pl.BlockSpec((24, cols), lambda b: (0, 0)),
+            pl.BlockSpec((slices, 2 * LANES, LANES), lambda b: (0, 0, 0)),
+            pl.BlockSpec((16, cols), lambda b: (0, 0)),
+            pl.BlockSpec(memory_space=SMEM),
         ],
         out_shape=[
             image,
             image,
             jax.ShapeDtypeStruct((slices, 4 * LANES, LANES), BF16),
-            jax.ShapeDtypeStruct((24, cols), F32),
+            jax.ShapeDtypeStruct((slices, 2 * LANES, LANES), BF16),
+            jax.ShapeDtypeStruct((16, cols), F32),
+            jax.ShapeDtypeStruct((1,), jnp.int32),
         ],
-        scratch_shapes=[pltpu.VMEM((slices, 2 * LANES, LANES), BF16)]
-        + [pltpu.VMEM((step * (width // LANES), LANES), F32)] * 2,
+        scratch_shapes=[pltpu.VMEM((step * (width // LANES), LANES), F32)] * 2,
         compiler_params=pltpu.CompilerParams(vmem_limit_bytes=32 * 2**20),
         name="interior",
     )(*small, rank, density, density)
@@ -365,6 +363,155 @@
     )(*small, weights, density, density, density, density, *halos)
 
 
+def column_tile(slices, first, blocks, column):
+    shape = tuple(pl.Element(n) for n in (1, slices, blocks * BLK, LANES))
+    return pl.BlockSpec(
+        shape, lambda i: (0, i * (slices), first * BLK, column * LANES)
+    )
+
+
+def strips_kernel(first_block, occ, x_first, x_last, to_left, to_right):
+    half = x_first.shape[2] // 2
+    block = first_block + pl.program_id(0)
+    k = lax.broadcasted_iota(jnp.int32, (2 * LANES, LANES), 0)
+    n = lax.broadcasted_iota(jnp.int32, (2 * LANES, LANES), 1)
+    for ref, out, column, source in (
+        (x_first, to_left, 0, jnp.where(n < HALF, n, n + HALF)),
+        (x_last, to_right, occ.shape[2] - 1, jnp.where(n < HALF, n + LANES + HALF, n)),
+    ):
+        occupied = occ[0, block, column].astype(F32)
+        pick = jnp.where(k == source, occupied, 0.0).astype(BF16)
+        for s in range(ref.shape[1]):
+            rows = jnp.concatenate([ref[0, s, :half], ref[0, s, half:]], axis=1)
+            out[s] = jnp.dot(rows, pick, preferred_element_type=F32).astype(BF16)
+
+
+def edge_strips(density, occupancy, first, blocks):
+    _, slices, _, cols = density.shape
+    shape = jax.ShapeDtypeStruct((slices, blocks * BLK // 2, LANES), BF16)
+    last = cols // LANES - 1
+    return pl.pallas_call(
+        functools.partial(strips_kernel, first),
+        grid=(blocks,),
+        in_specs=[
+            pl.BlockSpec(memory_space=SMEM),
+            pl.BlockSpec((1, slices, BLK, LANES), lambda i: (0, 0, first + i, 0)),
+            pl.BlockSpec((1, slices, BLK, LANES), lambda i: (0, 0, first + i, last)),
+        ],
+        out_specs=[pl.BlockSpec((slices, BLK // 2, LANES), lambda i: (0, i, 0))] * 2,
+        out_shape=[shape, shape],
+        name=f"edge_strips{first}",
+    )(occupancy, density, density)
+
+
+def full_border_kernel(
+    start, slice_total, occ, offset, frac_lateral, frac_vertical, extinction, gain, weights,
+    first_ref, last_ref, first_lead, last_lead, right_ref, left_ref, right_lead, left_lead,
+    out_keep, out_send, through_ref, sum_ref,
+):
+    count, half = first_ref.shape[1], BLK // 2
+    step = pl.program_id(0)
+    last_tile = occ.shape[2] - 1
+    follows = jnp.where(lax.axis_index("lat") < lax.axis_size("lat") - 1, 1, 0)
+    own_lanes = lax.broadcasted_iota(jnp.int32, (1, LANES), 1) >= HALF
+    refs = (frac_vertical, extinction, slice_total)
+    state = (through_ref, sum_ref)
+
+    @pl.when(step == 0)
+    def _():
+        through_ref[...] = jnp.ones_like(through_ref)
+        sum_ref[...] = jnp.zeros_like(sum_ref)
+
+    blocks = first_ref.shape[2] // BLK
+    masks = []
+    for b in range(start - 1, start + blocks):
+        inside = b >= 0
+        masks.append(
+            (
+                splat(occ[0, b, 0] if inside else 0.0),
+                splat(occ[0, b, last_tile] * follows if inside else 0.0),
+            )
+        )
+    zero = jnp.zeros((16, LANES), BF16)
+
+    def one(u, _):
+        s = step * count + u
+        before, own = weights[s, :LANES], weights[s, LANES:]
+        turn = lambda w: jnp.concatenate([w[HALF:], w[:HALF]], axis=0)
+        near = jnp.concatenate([before, own], axis=0)
+        far_left = jnp.concatenate([turn(before), own], axis=0)
+        far_right = jnp.concatenate([before, turn(own)], axis=0)
+
+        def halves(ref, side, top, above):
+            parts = [above] if above is not None else []
+            for b in range(blocks):
+                at = slice(b * BLK + top, b * BLK + top + half)
+                parts.append(ref[0, u, at] * masks[b + 1][side])
+            return jnp.concatenate(parts, axis=0) if len(parts) > 1 else parts[0]
+
+        def lateral(first, last, right, left, w_left, w_right):
+            here = jnp.dot(
+                jnp.concatenate([left, first], axis=1), w_left, preferred_element_type=F32
+            )
+            there = jnp.dot(
+                jnp.concatenate([last, right], axis=1), w_right, preferred_element_type=F32
+            )
+            return jnp.where(own_lanes, here, there)
+
+        right, left = right_ref[s], left_ref[s]
+        x_near = lateral(
+            halves(first_ref, 0, 0, None), halves(last_ref, 1, 0, None), right, left, near, near
+        )
+        x_far = lateral(
+            halves(first_ref, 0, half, first_lead[0, u] * masks[0][0]),
+            halves(last_ref, 1, half, last_lead[0, u] * masks[0][1]),
+            jnp.concatenate([right_lead[s, -16:] if start else zero, right], axis=0),
+            jnp.concatenate([left_lead[s, -16:] if start else zero, left], axis=0),
+            far_left,
+            far_right,
+        )
+        for b in range(blocks):
+            rows = slice(b * half, (b + 1) * half)
+            far_rows = slice(b * half + 16, (b + 1) * half + 16)
+            lead = x_far[b * half + 8 : b * half + 16]
+            x = jnp.concatenate([lead, x_near[rows], x_far[far_rows]], axis=0)
+            shade(s, x, b * BLK, state, refs)
+        return 0
+
+    over_slices(count, one)
+
+    @pl.when(step == pl.num_programs(0) - 1)
+    def _():
+        swap = lax.axis_index("depth") % 2 == 1
+        finish(state, gain[0], swap, out_keep, out_send, 0)
+
+
+def full_border(density, small, weights, halos, above, start, blocks, slice_total):
+    _, slices, _, cols = density.shape
+    step = blocks * BLK
+    last = cols // LANES - 1
+    lead_rows = max(start * BLK // 16 - 1, 0)
+
+    def lead(column):
+        return pl.BlockSpec((1, slices, 16, LANES), lambda i: (0, i, lead_rows, column))
+
+    image = jax.ShapeDtypeStruct((step // (2 * PIECE), 2, PIECE, LANES), F32)
+    return pl.pallas_call(
+        functools.partial(full_border_kernel, start, slice_total),
+        grid=(1,),
+        in_specs=small_specs()
+        + [whole()]
+        + [column_tile(slices, start, blocks, column) for column in (0, last)]
+        + [lead(0), lead(last)]
+        + [whole()] * 4,
+        out_specs=[whole()] * 2,
+        out_shape=[image, image],
+        scratch_shapes=[pltpu.VMEM((step, LANES), F32)] * 2,
+        compiler_params=pltpu.CompilerParams(vmem_limit_bytes=32 * 2**20),
+        name=f"full_border{start}",
+    )(*small, weights, density, density, density, density, *halos, *above)
+
+
 def over(mine, other, in_front):
     color = mine[0] * (1.0 - (1.0 - in_front) * other[1]) + other[0] * (1.0 - in_front * mine[1])
     return color, mine[1] + (1.0 - mine[1]) * other[1]
@@ -406,29 +553,42 @@
     blocks = rows // BLK
     rightwards = [(x, x + 1) for x in range(lat - 1)]
     leftwards = [(x, (x - 1) % lat) for x in range(lat)]
-    around = [(x, (x + 1) % lat) for x in range(lat)]
-    to_left, to_right = pack_halo(density, occupancy, shear_offsets)
-    halos = (
-        lax.ppermute(to_left, "lat", leftwards),
-        lax.ppermute(to_right, "lat", rightwards),
-    )
+
+    def travel(to_left, to_right):
+        return lax.ppermute(to_left, "lat", leftwards), lax.ppermute(to_right, "lat", rightwards)
+
+    halos = travel(*pack_halo(density, occupancy, shear_offsets))
     images = interior(density, small, view_rank, slice_total)
-    (keep, send, weights, flags), halos = lax.optimization_barrier((images, halos))
+    images, halos = lax.optimization_barrier((images, halos))
+    keep, send, packed_weights, weights, flags, overflow = images
+    half = blocks // 2
+    cuts = ((0, half), (half, blocks - half))
+
+    def packed_border():
+        parts = [
+            border(density, small, packed_weights, halos, *cut, slice_total) for cut in cuts
+        ]
+        return tuple(jnp.concatenate(p, axis=0) for p in zip(*parts))
+
+    def full_exchange():
+        parts, above = [], None
+        for cut in cuts:
+            strips = travel(*edge_strips(density, occupancy, *cut))
+            above = strips if above is None else above
+            parts.append(
+                full_border(density, small, weights, strips, above, *cut, slice_total)
+            )
+        return tuple(jnp.concatenate(p, axis=0) for p in zip(*parts))
+
     inner = over_cores(keep, send, flags)
-
-    def edge_rows(first, count, weights):
-        image = jnp.stack(border(density, small, weights, halos, first, count, slice_total))
-        moved = lax.ppermute((image * WIRE_SCALE).astype(WIRE), "lat", around)
-        below = flags[16, :LANES]
-        return image, image * (1.0 - below) + moved.astype(F32) * (below / WIRE_SCALE)
-
-    half = blocks // 2
-    top, moved_top = edge_rows(0, half, weights)
-    weights, _ = lax.optimization_barrier((weights, top))
-    _, moved_bottom = edge_rows(half, blocks - half, weights)
-    keep, send = jnp.concatenate([moved_top, moved_bottom], axis=1)
+    keep, send = lax.cond(overflow[0] > 0, full_exchange, packed_border)
     edge = over_cores(keep, send, flags)
-    return tuple(over_chips(jnp.concatenate([edge, inner], axis=3), flags))
+    color, alpha = over_chips(jnp.concatenate([edge, inner], axis=3), flags)
+    image = jnp.stack([color, alpha])
+    moved = lax.ppermute(image[:, :, :LANES], "lat", [(x, (x + 1) % lat) for x in range(lat)])
+    lane = jnp.arange(LANES, dtype=jnp.int32)
+    first = jnp.where(lane < HALF, moved, image[:, :, :LANES])
+    return tuple(jnp.concatenate([first[i], image[i, :, LANES:]], axis=1) for i in range(2))
 
 
 def solution(mesh):

time: 66.1 us -> 67.1 us (1.015)
  waiting for transfers between devices: 19.2 us -> 16 us
  Pallas kernels: 26.7 us -> 28.3 us
  other arithmetic: 2.91 us -> 4.05 us
  local copies, waits for them, and re-layouts: 0.07 us -> 1.03 us
    ppermute x4 -> x3, waiting for transfers between devices: 6 us -> 2.91 us  [the longest x1 2.9 us: shards(): lax.ppermute(image[:, :, :LANES], 'lat', [(x, (x + 1) % lat) for x in ran...]
    concatenate x0 -> x2, other arithmetic: none -> 1.38 us  [the longest x1 0.75 us: packed_border(): return tuple((jnp.concatenate(p, axis=0) for p in zip(*parts)))]
    pallas_call x2, Pallas kernels: 7.76 us -> 9.06 us  [border(): pl.pallas_call(functools.partial(border_kernel, start, slice_total), grid...]
    cond x0 -> x1, local copies, waits for them, and re-layouts: none -> 0.95 us
    ppermute x4 -> x3, starting transfers between devices: 7.12 us -> 6.5 us  [the longest x1 2.84 us: travel(): lax.ppermute(to_left, 'lat', leftwards)]
  transfers between devices with their start and end apart: 7 -> 6, of which waited for: 4 -> 3; matrix products, arithmetic and copies ran while one was open for 0% -> 3% of each run, Pallas kernels for 20% -> 34%
where the time goes in v9:
time: 67.1 us; the launch traced here: 66.6 us
  Pallas kernels  28.3 us (42%)
  waiting for transfers between devices  16 us (24%)
  starting transfers between devices  15.1 us (23%)
  other arithmetic  4.05 us (6%)
  between operations  2.15 us (3%)
  local copies, waits for them, and re-layouts  1.03 us (2%)
    pallas_call x1, Pallas kernels, interior(): pl.pallas_call(functools.partial(interior_kernel, slice_total), grid=(row...  13.5 us
    all_to_all x1, waiting for transfers between devices, over_chips(): lax.all_to_all(pieces, 'depth', 0, 0, axis_index_groups=groups, tiled=True)  11.9 us
    pallas_call x2, Pallas kernels, border(): pl.pallas_call(functools.partial(border_kernel, start, slice_total), grid...  9.06 us
    all_to_all x1, starting transfers between devices, over_chips(): lax.all_to_all(pieces, 'depth', 0, 0, axis_index_groups=groups, tiled=True)  8.06 us
    pallas_call x1, Pallas kernels, pack_halo(): pl.pallas_call(pack_kernel, grid=(rows // BLK,), in_specs=[pl.BlockSpec(m...  5.69 us
    ppermute x1, waiting for transfers between devices, shards(): lax.ppermute(image[:, :, :LANES], 'lat', [(x, (x + 1) % lat) for x in ran...  2.9 us
    ppermute x1, starting transfers between devices, travel(): lax.ppermute(to_left, 'lat', leftwards)  2.84 us
    ppermute x1, starting transfers between devices, shards(): lax.ppermute(image[:, :, :LANES], 'lat', [(x, (x + 1) % lat) for x in ran...  2.34 us
  transfers between devices with their start and end apart: 6, of which 3 were waited for; matrix products, arithmetic and copies ran while one was open for 3% of the time, Pallas kernels for 34%

profile of v9, /device:TPU:0, one launch (start us, length us, event | category | flops | bytes accessed | tf_op | source)
XLA Modules:
  0.0 66.6 jit_solution(11437921386697723958)
XLA Ops:
  0.6 0.0 copy-start.2
  0.7 5.7 %pack_halo.1 = (bf16[5,512,128]{2,1,0:T(8,128)(2,1)}, bf16[5,512,128]{2,1,0:T(8,128)(2,1)}) custom-call(s32[1,4,4]{2,1,0:T(4,128)} %occ.3, s32[1,16]{1,0:T(1,128)} %offset.3, bf16[1,16,512,512]{3,2,1,0:T(8,128)(2,1)} %x_last.1, bf16[1,16,512,512]{3,2,1,0:T(8,128)(2,1)} %x_last.1), custom_call_target="tpu_custom_call" | custom-call | tf_op jit(solution)/shard_map/pack_halo/pallas_call | solution.py:92
  6.4 2.8 %collective-permute-start.4 = (bf16[5,512,128]{2,1,0:T(8,128)(2,1)}, bf16[5,512,128]{2,1,0:T(8,128)(2,1)S(1)}, u32[]{:S(2)}, u32[]{:S(2)}) collective-permute-start(bf16[5,512,128]{2,1,0:T(8,128)(2,1)} %get-tuple-element.102), channel_id=1, source_target_pairs={{0,3},{1,0},{2,1},{3,2},{4,7},{5,4},{6,5},{7,6},{8,11},{9,8},{10,9... | collective-permute-start | bytes 1966088 | tf_op jit(solution)/shard_map/ppermute | solution.py:558
  9.2 1.3 %collective-permute-start.5 = (bf16[5,512,128]{2,1,0:T(8,128)(2,1)}, bf16[5,512,128]{2,1,0:T(8,128)(2,1)S(1)}, u32[]{:S(2)}, u32[]{:S(2)}) collective-permute-start(bf16[5,512,128]{2,1,0:T(8,128)(2,1)} %get-tuple-element.103), channel_id=1, source_target_pairs={{0,1},{1,2},{2,3},{4,5},{5,6},{6,7},{8,9},{9,10},{10,11},{12,13},{... | collective-permute-start | bytes 1966088 | tf_op jit(solution)/shard_map/ppermute | solution.py:558
  11.2 0.0 copy-done.2
  11.2 0.0 copy-done.3
  11.2 0.0 copy-done.4
  11.2 0.0 copy-done.5
  11.2 0.0 copy-done.6
  11.2 0.0 copy-done
  11.3 13.5 %interior.1 = (f32[16,2,16,384]{3,2,1,0:T(8,128)S(1)}, f32[16,2,16,384]{3,2,1,0:T(8,128)S(1)}, bf16[16,512,128]{2,1,0:T(8,128)(2,1)S(1)}, bf16[16,256,128]{2,1,0...) custom-call(s32[1,4,4]{2,1,0:T(4,128)S(1)} %copy-done.2, s32[1,16]{1,0:T(1,128)S(1)} %copy-done.3, ...), custom_call_target="tpu_custom_call" | custom-call | tf_op jit(solution)/shard_map/interior/pallas_call | solution.py:242
  24.8 0.0 collective-permute-done.4
  24.8 0.0 collective-permute-done.5
  24.8 0.1 collective-permute-start.7
  25.6 10.8 %conditional.1 = (f32[16,2,16,128]{3,2,1,0:T(8,128)}, f32[16,2,16,128]{3,2,1,0:T(8,128)S(1)}, f32[16,2,16,128]{3,2,1,0:T(8,128)S(1)}) conditional(s32[]{:T(128)} %bitcast, (s32[1,4,4]{2,1,0:T(4,128)S(1)}, s32[1,16]{1,0:T(1,128)S(1)}, f32[1,16]{1,0:T(1,128)S(1)}, f32[1,16]{1,0:T(1,128)S(1)}, f32[1,16]{1,0:T(1,128)S(1)}, /*index=5*/f32[1]{0:T(128)}, ...), branch_computations={%region_0.0_spmd, %region_1.0_spmd} | conditional | flops 131072 | bytes 14155988 | solution.py:584
  25.6 4.5 %border2.1 = (f32[8,2,16,128]{3,2,1,0:T(8,128)S(1)}, f32[8,2,16,128]{3,2,1,0:T(8,128)S(1)}) custom-call(s32[1,4,4]{2,1,0:T(4,128)S(1)} %get-tuple-element.46.occ, s32[1,16]{1,0:T(1,128)S(1)} %get-tuple-element.47.offset, f32[1,16]{1,0:T(1,128)S(1)} %get-tuple-element.48.frac_lateral, f32[1,16]{1,0:T(1,128)S(1)} %get-tuple-element.49.frac_vertical, ...), custom_call_target="tpu_custom_call" | custom-call | tf_op jit(solution)/shard_map/cond/branch_0_fun/border2/pallas_call | solution.py:353
  30.1 4.5 %border0.1 = (f32[8,2,16,128]{3,2,1,0:T(8,128)S(1)}, f32[8,2,16,128]{3,2,1,0:T(8,128)S(1)}) custom-call(s32[1,4,4]{2,1,0:T(4,128)S(1)} %get-tuple-element.46.occ, s32[1,16]{1,0:T(1,128)S(1)} %get-tuple-element.47.offset, f32[1,16]{1,0:T(1,128)S(1)} %get-tuple-element.48.frac_lateral, f32[1,16]{1,0:T(1,128)S(1)} %get-tuple-element.49.frac_vertical, ...), custom_call_target="tpu_custom_call" | custom-call | tf_op jit(solution)/shard_map/cond/branch_0_fun/border0/pallas_call | solution.py:353
  34.6 0.7 %pad_maximum_fusion = (f32[16,2,16,128]{3,2,1,0:T(8,128)}, f32[16,2,16,128]{3,2,1,0:T(8,128)S(1)}) fusion(f32[8,2,16,128]{3,2,1,0:T(8,128)S(1)} %get-tuple-element.57, f32[8,2,16,128]{3,2,1,0:T(8,128)S(1)} %get-tuple-element.56, f32[8,2,16,128]{3,2,1,0:T(8,128)S(1)} %get-tuple-element.59, f32[8,2,16,128]{3,2,1,0:T(8,128)S(1)} %get-tuple-element.58), kind=kLoop, calls=%fused_computation | loop fusion | flops 131072 | bytes 1048576 | tf_op jit(solution)/shard_map/cond/branch_0_fun/concatenate | solution.py:571
  35.4 0.9 %copy.19 = f32[16,2,16,128]{3,2,1,0:T(8,128)S(1)} copy(f32[16,2,16,128]{3,2,1,0:T(8,128)} %get-tuple-element.177) | data formatting | bytes 524288 | tf_op jit(solution)/shard_map/cond
  36.3 0.5 collective-permute-start.6
  36.9 1.1 %collective-permute-done.6 = f32[16,2,16,128]{3,2,1,0:T(8,128)S(1)} collective-permute-done((f32[16,2,16,128]{3,2,1,0:T(8,128)S(1)}, f32[16,2,16,128]{3,2,1,0:T(8,128)S(1)}, u32[]{:S(2)}, u32[]{:S(2)}) %collective-permute-start.6) | collective-permute-done | bytes 262176 | tf_op jit(solution)/shard_map/ppermute | solution.py:522
  38.0 0.0 collective-permute-done.7
  38.0 1.3 %fusion.1 = (f32[16,1,16,384]{3,2,1,0:T(8,128)S(1)}, f32[16,1,16,384]{3,2,1,0:T(8,128)S(1)}) fusion(f32[16,2,16,384]{3,2,1,0:T(8,128)} %collective-permute-done.7, f32[16,2,16,384]{3,2,1,0:T(8,128)S(1)} %get-tuple-element.112, f32[384]{0:T(512)S(1)} %slice_reduce_fusion, f32[384]{0:T(512)S(1)} %broadcast_subtract_fusion.15), kind=kLoop, calls=%fused_computation.8 | loop fusion | flops 983040 | bytes 2362368 | tf_op jit(solution)/shard_map/add | solution.py:516
  39.3 0.9 %fusion = f16[16,2,16,512]{3,2,1,0:T(8,128)(2,1)} fusion(f32[16,1,16,384]{3,2,1,0:T(8,128)S(1)} %get-tuple-element.127, f32[16,1,16,384]{3,2,1,0:T(8,128)S(1)} %get-tuple-element.126, f32[16,1,16,128]{3,2,1,0:T(8,128)S(1)} %get-tuple-element.129, f32[16,1,16,128]{3,2,1,0:T(8,128)S(1)} %get-tuple-element.128), kind=kLoop, calls=%fused_computation.5 | loop fusion | flops 1310720 | bytes 1572864 | tf_op jit(solution)/shard_map/convert_element_type | solution.py:530
  40.2 8.1 %all-to-all-start = ((f16[16,2,16,512]{3,2,1,0:T(8,128)(2,1)}), f16[16,2,16,512]{3,2,1,0:T(8,128)(2,1)S(1)}, u32[]{:S(2)}, u32[]{:S(2)}) async-start(f16[16,2,16,512]{3,2,1,0:T(8,128)(2,1)} %fusion), calls=%async_computation | async-start | bytes 1048576 | tf_op jit(solution)/shard_map/all_to_all | solution.py:532
  48.4 11.9 %all-to-all-done = f16[16,2,16,512]{3,2,1,0:T(8,128)(2,1)S(1)} async-done(((f16[16,2,16,512]{3,2,1,0:T(8,128)(2,1)}), f16[16,2,16,512]{3,2,1,0:T(8,128)(2,1)S(1)}, u32[]{:S(2)}, u32[]{:S(2)}) %all-to-all-start) | async-done | bytes 524320 | tf_op jit(solution)/shard_map/all_to_all | solution.py:532
  60.3 0.2 convert_multiply_fusion
  60.4 0.1 multiply_add_fusion.2
  60.5 0.2 fusion.10
  60.7 2.3 %collective-permute-start.8 = (f32[2,16,128]{2,1,0:T(8,128)S(1)}, f32[2,16,128]{2,1,0:T(8,128)S(1)}, u32[]{:S(2)}, u32[]{:S(2)}) collective-permute-start(f32[2,16,128]{2,1,0:T(8,128)S(1)} %pad_maximum_fusion.6), channel_id=1, source_target_pairs={{0,1},{1,2},{2,3},{3,0},{4,5},{5,6},{6,7},{7,4},{8,9},{9,10},{10,1... | collective-permute-start | bytes 49160 | tf_op jit(solution)/shard_map/ppermute | solution.py:588
  63.1 2.9 %collective-permute-done.8 = f32[2,16,128]{2,1,0:T(8,128)S(1)} collective-permute-done((f32[2,16,128]{2,1,0:T(8,128)S(1)}, f32[2,16,128]{2,1,0:T(8,128)S(1)}, u32[]{:S(2)}, u32[]{:S(2)}) %collective-permute-start.8) | collective-permute-done | bytes 16416 | tf_op jit(solution)/shard_map/ppermute | solution.py:588
  66.0 0.6 pad_maximum_fusion.4
  (18 shorter events, 0.2 us)
Async XLA Ops:
  0.6 10.6 %copy-start.2 = (s32[1,4,4]{2,1,0:T(4,128)S(1)}, s32[1,4,4]{2,1,0:T(4,128)}, u32[]{:S(2)}) copy-start(s32[1,4,4]{2,1,0:T(4,128)} %occ.3) | copy-start | bytes 196
  0.6 10.6 %copy-start.3 = (s32[1,16]{1,0:T(1,128)S(1)}, s32[1,16]{1,0:T(1,128)}, u32[]{:S(2)}) copy-start(s32[1,16]{1,0:T(1,128)} %offset.3) | copy-start | bytes 196
  0.7 10.6 %copy-start.4 = (f32[1,16]{1,0:T(1,128)S(1)}, f32[1,16]{1,0:T(1,128)}, u32[]{:S(2)}) copy-start(f32[1,16]{1,0:T(1,128)} %frac_lateral.1) | copy-start | bytes 196
  0.7 10.6 %copy-start.5 = (f32[1,16]{1,0:T(1,128)S(1)}, f32[1,16]{1,0:T(1,128)}, u32[]{:S(2)}) copy-start(f32[1,16]{1,0:T(1,128)} %frac_vertical.1) | copy-start | bytes 196
  0.7 10.6 %copy-start.6 = (f32[1,16]{1,0:T(1,128)S(1)}, f32[1,16]{1,0:T(1,128)}, u32[]{:S(2)}) copy-start(f32[1,16]{1,0:T(1,128)} %extinction.1) | copy-start | bytes 196
  0.7 10.6 %copy-start = (s32[32]{0:T(128)S(1)}, s32[32]{0:T(128)}, u32[]{:S(2)}) copy-start(s32[32]{0:T(128)} %rank.1) | copy-start | bytes 388
  6.4 18.4 %collective-permute-start.4 = (bf16[5,512,128]{2,1,0:T(8,128)(2,1)}, bf16[5,512,128]{2,1,0:T(8,128)(2,1)S(1)}, u32[]{:S(2)}, u32[]{:S(2)}) collective-permute-start(bf16[5,512,128]{2,1,0:T(8,128)(2,1)} %get-tuple-element.102), channel_id=1, source_target_pairs={{0,3},{1,0},{2,1},{3,2},{4,7},{5,4},{6,5},{7,6},{8,11},{9,8},{10,9... | collective-permute-start | bytes 1966088 | tf_op jit(solution)/shard_map/ppermute | solution.py:558
  9.2 15.6 %collective-permute-start.5 = (bf16[5,512,128]{2,1,0:T(8,128)(2,1)}, bf16[5,512,128]{2,1,0:T(8,128)(2,1)S(1)}, u32[]{:S(2)}, u32[]{:S(2)}) collective-permute-start(bf16[5,512,128]{2,1,0:T(8,128)(2,1)} %get-tuple-element.103), channel_id=1, source_target_pairs={{0,1},{1,2},{2,3},{4,5},{5,6},{6,7},{8,9},{9,10},{10,11},{12,13},{... | collective-permute-start | bytes 1966088 | tf_op jit(solution)/shard_map/ppermute | solution.py:558
  24.8 13.2 %collective-permute-start.7 = (f32[16,2,16,384]{3,2,1,0:T(8,128)S(1)}, f32[16,2,16,384]{3,2,1,0:T(8,128)}, u32[]{:S(2)}, u32[]{:S(2)}) collective-permute-start(f32[16,2,16,384]{3,2,1,0:T(8,128)S(1)} %get-tuple-element.113), channel_id=1, source_target_pairs={{0,4},{4,0},{8,12},{12,8},{16,20},{20,16},{24,28},{28,24},{32,36},... | collective-permute-start | bytes 2359304 | tf_op jit(solution)/shard_map/ppermute | solution.py:522
  36.3 1.6 %collective-permute-start.6 = (f32[16,2,16,128]{3,2,1,0:T(8,128)S(1)}, f32[16,2,16,128]{3,2,1,0:T(8,128)S(1)}, u32[]{:S(2)}, u32[]{:S(2)}) collective-permute-start(f32[16,2,16,128]{3,2,1,0:T(8,128)S(1)} %get-tuple-element.118), channel_id=1, source_target_pairs={{0,4},{4,0},{8,12},{12,8},{16,20},{20,16},{24,28},{28,24},{32,36},... | collective-permute-start | bytes 786440 | tf_op jit(solution)/shard_map/ppermute | solution.py:522
  40.2 20.1 %all-to-all-start = ((f16[16,2,16,512]{3,2,1,0:T(8,128)(2,1)}), f16[16,2,16,512]{3,2,1,0:T(8,128)(2,1)S(1)}, u32[]{:S(2)}, u32[]{:S(2)}) async-start(f16[16,2,16,512]{3,2,1,0:T(8,128)(2,1)} %fusion), calls=%async_computation | async-start | bytes 1048576 | tf_op jit(solution)/shard_map/all_to_all | solution.py:532
  60.7 5.2 %collective-permute-start.8 = (f32[2,16,128]{2,1,0:T(8,128)S(1)}, f32[2,16,128]{2,1,0:T(8,128)S(1)}, u32[]{:S(2)}, u32[]{:S(2)}) collective-permute-start(f32[2,16,128]{2,1,0:T(8,128)S(1)} %pad_maximum_fusion.6), channel_id=1, source_target_pairs={{0,1},{1,2},{2,3},{3,0},{4,5},{5,6},{6,7},{7,4},{8,9},{9,10},{10,1... | collective-permute-start | bytes 49160 | tf_op jit(solution)/shard_map/ppermute | solution.py:588

commit v10 on v5

--- a/solution.py
+++ b/solution.py
@@ -15,7 +15,7 @@
 PIECE = 16
 WIRE = jnp.float16
 WIRE_SCALE = 4096.0
-UNROLL = 16
+TAIL = 2
 LOG2E = math.log2(math.e)
 SMEM = pltpu.SMEM
 F32 = jnp.float32
@@ -31,38 +31,64 @@
     return jnp.where(distance == offset, 1.0 - fraction, second)
 
 
-def strips_kernel(first_block, occ, x_first, x_last, to_left, to_right):
-    half = x_first.shape[2] // 2
-    block = first_block + pl.program_id(0)
+def whole():
+    return pl.BlockSpec(memory_space=pltpu.VMEM)
+
+
+def strips_kernel(
+    first_block, occ, density, to_left, to_right, first_tile, last_tile, first_here, last_here
+):
+    slices, cols = density.shape[1], density.shape[3]
+    rows, half = first_tile.shape[1], BLK // 2
+    copies = []
+    for s in range(slices):
+        pair = []
+        for buffer, arrived, column in (
+            (first_tile, first_here, 0),
+            (last_tile, last_here, cols - LANES),
+        ):
+            copy = pltpu.make_async_copy(
+                density.at[0, s, pl.ds(first_block * BLK, rows), pl.ds(column, LANES)],
+                buffer.at[s],
+                arrived.at[s],
+            )
+            copy.start()
+            pair.append(copy)
+        copies.append(pair)
     k = lax.broadcasted_iota(jnp.int32, (2 * LANES, LANES), 0)
     n = lax.broadcasted_iota(jnp.int32, (2 * LANES, LANES), 1)
-    for ref, out, column, source in (
-        (x_first, to_left, 0, jnp.where(n < HALF, n, n + HALF)),
-        (x_last, to_right, occ.shape[2] - 1, jnp.where(n < HALF, n + LANES + HALF, n)),
-    ):
-        occupied = occ[0, block, column].astype(F32)
-        pick = jnp.where(k == source, occupied, 0.0).astype(BF16)
-        for s in range(ref.shape[1]):
-            rows = jnp.concatenate([ref[0, s, :half], ref[0, s, half:]], axis=1)
-            out[s] = jnp.dot(rows, pick, preferred_element_type=F32).astype(BF16)
+    left = jnp.where(k == jnp.where(n < HALF, n, n + HALF), 1.0, 0.0).astype(BF16)
+    right = jnp.where(k == jnp.where(n < HALF, n + LANES + HALF, n), 1.0, 0.0).astype(BF16)
+    for s in range(slices):
+        for copy in copies[s]:
+            copy.wait()
+        for buffer, out, pick, column in (
+            (first_tile, to_left, left, 0),
+            (last_tile, to_right, right, occ.shape[2] - 1),
+        ):
+            parts = []
+            for b in range(rows // BLK):
+                top, middle, end = b * BLK, b * BLK + half, (b + 1) * BLK
+                pair = jnp.concatenate([buffer[s, top:middle], buffer[s, middle:end]], axis=1)
+                parts.append(pair * jnp.full((1, 2 * LANES), occ[0, first_block + b, column], F32).astype(BF16))
+            moved = jnp.dot(jnp.concatenate(parts, axis=0), pick, preferred_element_type=F32)
+            out[s] = moved.astype(BF16)
 
 
 def edge_strips(density, occupancy, first, blocks):
-    _, slices, _, cols = density.shape
-    shape = jax.ShapeDtypeStruct((slices, blocks * BLK // 2, LANES), BF16)
-    last = cols // LANES - 1
+    slices = density.shape[1]
+    rows = blocks * BLK
+    shape = jax.ShapeDtypeStruct((slices, rows // 2, LANES), BF16)
     return pl.pallas_call(
         functools.partial(strips_kernel, first),
-        grid=(blocks,),
-        in_specs=[
-            pl.BlockSpec(memory_space=SMEM),
-            pl.BlockSpec((1, slices, BLK, LANES), lambda i: (0, 0, first + i, 0)),
-            pl.BlockSpec((1, slices, BLK, LANES), lambda i: (0, 0, first + i, last)),
-        ],
-        out_specs=[pl.BlockSpec((slices, BLK // 2, LANES), lambda i: (0, i, 0))] * 2,
+        in_specs=[pl.BlockSpec(memory_space=SMEM), pl.BlockSpec(memory_space=pl.ANY)],
+        out_specs=[whole()] * 2,
         out_shape=[shape, shape],
+        scratch_shapes=[pltpu.VMEM((slices, rows, LANES), BF16)] * 2
+        + [pltpu.SemaphoreType.DMA((slices,))] * 2,
+        compiler_params=pltpu.CompilerParams(vmem_limit_bytes=32 * 2**20),
         name=f"edge_strips{first}",
-    )(occupancy, density, density)
+    )(occupancy, density)
 
 
 def shade(s, x, base, state, refs):
@@ -86,7 +112,7 @@
 
 def finish(state, gain, swap, out_keep, out_send, tile):
     through_ref, sum_ref = state
-    rows = out_keep.shape[1] * 2
+    rows = out_keep.shape[0] * 2 * PIECE
     base = tile * rows
     alphas, colors = [], []
     for p in range(rows // PIECE):
@@ -96,11 +122,10 @@
         colors.append(gain * (0.65 * alpha + 0.35 * sum_ref[at]))
     lanes = slice(tile * LANES, (tile + 1) * LANES)
     for q in range(rows // PIECE // 2):
-        at = slice(q * PIECE, (q + 1) * PIECE)
         for i, values in enumerate((colors, alphas)):
             even, odd = values[2 * q], values[2 * q + 1]
-            out_keep[i, at, lanes] = jnp.where(swap, odd, even)
-            out_send[i, at, lanes] = jnp.where(swap, even, odd)
+            out_keep[q, i, :, lanes] = jnp.where(swap, odd, even)
+            out_send[q, i, :, lanes] = jnp.where(swap, even, odd)
 
 
 def splat(value):
@@ -108,7 +133,8 @@
 
 
 def over_slices(slices, one):
-    lax.fori_loop(0, slices, one, 0, unroll=UNROLL)
+    for s in range(slices):
+        one(s, 0)
 
 
 def interior_kernel(
@@ -160,7 +186,7 @@
     over_slices(slices, one)
     swap = lax.axis_index("depth") % 2 == 1
     for t in range(tiles - 1):
-        finish(state, gain[0], swap, out_keep, out_send, t)
+        finish(state, gain[0, 0], swap, out_keep, out_send, t)
 
 
 def small_specs():
@@ -171,7 +197,8 @@
     _, slices, rows, cols = density.shape
     step = BLK
     width = cols - LANES
-    image = jax.ShapeDtypeStruct((2, rows // 2, width), F32)
+    pieces = step // (2 * PIECE)
+    image = jax.ShapeDtypeStruct((rows // (2 * PIECE), 2, PIECE, width), F32)
     return pl.pallas_call(
         functools.partial(interior_kernel, slice_total),
         grid=(rows // step,),
@@ -184,7 +211,7 @@
             ),
         ],
         out_specs=[
-            pl.BlockSpec((2, step // 2, width), lambda b: (0, b, 0))
+            pl.BlockSpec((pieces, 2, PIECE, width), lambda b: (b, 0, 0, 0))
         ]
         * 2
         + [
@@ -273,7 +300,7 @@
 
     over_slices(slices, one)
     swap = lax.axis_index("depth") % 2 == 1
-    finish(state, gain[0], swap, out_keep, out_send, 0)
+    finish(state, gain[0, 0], swap, out_keep, out_send, 0)
 
 
 def border(density, small, weights, halos, above, start, blocks, slice_total):
@@ -294,14 +321,15 @@
     halo = pl.BlockSpec((slices, step // 2, LANES), lambda i: (0, 0, 0))
     last_rows = above[0].shape[1] // 16 - 1
     halo_lead = pl.BlockSpec((slices, 16, LANES), lambda i: (0, last_rows, 0))
-    image = jax.ShapeDtypeStruct((2, step // 2, LANES), F32)
+    shape = (step // (2 * PIECE), 2, PIECE, LANES)
+    image = jax.ShapeDtypeStruct(shape, F32)
     return pl.pallas_call(
         functools.partial(border_kernel, start, slice_total),
         grid=(1,),
         in_specs=small_specs()
         + [pl.BlockSpec((slices, 2 * LANES, LANES), lambda i: (0, 0, 0))]
         + [body(0), body(last), lead(0), lead(last), halo, halo, halo_lead, halo_lead],
-        out_specs=[pl.BlockSpec((2, step // 2, LANES), lambda i: (0, 0, 0))] * 2,
+        out_specs=[pl.BlockSpec(shape, lambda i: (0, 0, 0, 0))] * 2,
         out_shape=[image, image],
         scratch_shapes=[pltpu.VMEM((step, LANES), F32)] * 2,
         compiler_params=pltpu.CompilerParams(vmem_limit_bytes=32 * 2**20),
@@ -317,14 +345,13 @@
 def over_cores(keep, send, flags):
     count = lax.axis_size("depth")
     other = lax.ppermute(send, "depth", [(i, i ^ 1) for i in range(count)])
-    return jnp.stack(over(keep, other, flags[0, : keep.shape[2]]))
-
-
-def over_chips(image, flags):
+    front = flags[0, : keep.shape[3]]
+    return jnp.stack(over((keep[:, 0], keep[:, 1]), (other[:, 0], other[:, 1]), front), axis=1)
+
+
+def over_chips(pieces, flags):
     count = lax.axis_size("depth")
     chips = count // 2
-    width = image.shape[2]
-    pieces = image.reshape(2, chips, PIECE, width).transpose(1, 0, 2, 3)
     pieces = (pieces * WIRE_SCALE).astype(WIRE)
     groups = [[2 * i + core for i in range(chips)] for core in range(2)]
     pieces = lax.all_to_all(
@@ -347,9 +374,9 @@
     slice_total = lax.axis_size("depth") * slices
     lat = lax.axis_size("lat")
     density = pltpu.with_memory_space_constraint(density, pltpu.HBM)
-    small = (occupancy, shear_offsets, frac_lateral, frac_vertical, extinction, slab_gain)
+    small = (occupancy, shear_offsets, frac_lateral, frac_vertical, extinction, slab_gain[None])
     blocks = rows // BLK
-    half = blocks // 2
+    half = blocks - TAIL
     rightwards = [(x, x + 1) for x in range(lat - 1)]
     leftwards = [(x, (x - 1) % lat) for x in range(lat)]
     halos = []
@@ -363,9 +390,9 @@
     send, top = lax.optimization_barrier((send, top))
     inner = over_cores(keep, send, flags)
     bottom = border(density, small, weights, halos[1], halos[0], half, blocks - half, slice_total)
-    keep, send = (jnp.concatenate(p, axis=1) for p in zip(top, bottom))
+    keep, send = (jnp.concatenate(p, axis=0) for p in zip(top, bottom))
     edge = over_cores(keep, send, flags)
-    color, alpha = over_chips(jnp.concatenate([edge, inner], axis=2), flags)
+    color, alpha = over_chips(jnp.concatenate([edge, inner], axis=3), flags)
     image = jnp.stack([color, alpha])
     moved = lax.ppermute(image[:, :, :LANES], "lat", [(x, (x + 1) % lat) for x in range(lat)])
     lane = jnp.arange(LANES, dtype=jnp.int32)

time: 65.1 us -> 68.4 us (1.051)
  Pallas kernels: 25.7 us -> 28.4 us
  other arithmetic: 1.45 us -> 2.21 us
    pallas_call x2, Pallas kernels: 6.58 us -> 9.32 us  [edge_strips(): pl.pallas_call(functools.partial(strips_kernel, first), in_specs=[pl.Bloc...]
    convert_element_type x1 -> x0, local copies, waits for them, and re-layouts: 0.92 us -> none  [over_chips(): pieces = (pieces * WIRE_SCALE).astype(WIRE)]
    convert_element_type x1, other arithmetic: 0.09 us -> 0.9 us  [over_chips(): pieces = (pieces * WIRE_SCALE).astype(WIRE)]
where the time goes in v10:
time: 68.4 us; the launch traced here: 67.9 us
  Pallas kernels  28.4 us (42%)
  starting transfers between devices  18.3 us (27%)
  waiting for transfers between devices  16.7 us (24%)
  other arithmetic  2.21 us (3%)
  between operations  1.54 us (2%)
  local copies, waits for them, and re-layouts  0.77 us (1%)
    pallas_call x1, Pallas kernels, interior(): pl.pallas_call(functools.partial(interior_kernel, slice_total), grid=(row...  11.9 us
    all_to_all x1, waiting for transfers between devices, over_chips(): lax.all_to_all(pieces, 'depth', 0, 0, axis_index_groups=groups, tiled=True)  11.9 us
    pallas_call x2, Pallas kernels, edge_strips(): pl.pallas_call(functools.partial(strips_kernel, first), in_specs=[pl.Bloc...  9.32 us
    all_to_all x1, starting transfers between devices, over_chips(): lax.all_to_all(pieces, 'depth', 0, 0, axis_index_groups=groups, tiled=True)  8.06 us
    pallas_call x2, Pallas kernels, border(): pl.pallas_call(functools.partial(border_kernel, start, slice_total), grid...  7.11 us
    ppermute x2, starting transfers between devices, shards(): lax.ppermute(to_right, 'lat', rightwards)  4.46 us
    ppermute x2, starting transfers between devices, shards(): lax.ppermute(to_left, 'lat', leftwards)  3.78 us
    ppermute x1, waiting for transfers between devices, shards(): lax.ppermute(image[:, :, :LANES], 'lat', [(x, (x + 1) % lat) for x in ran...  3.63 us
  transfers between devices with their start and end apart: 8, of which 3 were waited for; matrix products, arithmetic and copies ran while one was open for 0% of the time, Pallas kernels for 35%

profile of v10, /device:TPU:0, one launch (start us, length us, event | category | flops | bytes accessed | tf_op | source)
XLA Modules:
  0.0 67.9 jit_solution(2812731283878765908)
XLA Ops:
  0.6 0.0 copy-start
  0.6 0.7 copy-done
  1.3 0.0 copy-start.5
  1.3 4.7 %edge_strips0.1 = (bf16[16,128,128]{2,1,0:T(8,128)(2,1)S(1)}, bf16[16,128,128]{2,1,0:T(8,128)(2,1)S(1)}) custom-call(s32[1,4,4]{2,1,0:T(4,128)S(1)} %copy-done, bf16[1,16,512,512]{3,2,1,0:T(8,128)(2,1)} %last_lead.3), custom_call_target="tpu_custom_call" | custom-call | tf_op jit(solution)/shard_map/edge_strips0/pallas_call | solution.py:82
  6.0 2.9 %collective-permute-start = (bf16[16,128,128]{2,1,0:T(8,128)(2,1)S(1)}, bf16[16,128,128]{2,1,0:T(8,128)(2,1)S(1)}, u32[]{:S(2)}, u32[]{:S(2)}) collective-permute-start(bf16[16,128,128]{2,1,0:T(8,128)(2,1)S(1)} %get-tuple-element.19), channel_id=1, source_target_pairs={{0,3},{1,0},{2,1},{3,2},{4,7},{5,4},{6,5},{7,6},{8,11},{9,8},{10,9... | collective-permute-start | bytes 1572872 | tf_op jit(solution)/shard_map/ppermute | solution.py:386
  8.9 1.3 %collective-permute-start.1 = (bf16[16,128,128]{2,1,0:T(8,128)(2,1)S(1)}, bf16[16,128,128]{2,1,0:T(8,128)(2,1)S(1)}, u32[]{:S(2)}, u32[]{:S(2)}) collective-permute-start(bf16[16,128,128]{2,1,0:T(8,128)(2,1)S(1)} %get-tuple-element.20), channel_id=1, source_target_pairs={{0,1},{1,2},{2,3},{4,5},{5,6},{6,7},{8,9},{9,10},{10,11},{12,13},{... | collective-permute-start | bytes 1572872 | tf_op jit(solution)/shard_map/ppermute | solution.py:386
  10.2 4.7 %edge_strips2.1 = (bf16[16,128,128]{2,1,0:T(8,128)(2,1)S(1)}, bf16[16,128,128]{2,1,0:T(8,128)(2,1)S(1)}) custom-call(s32[1,4,4]{2,1,0:T(4,128)S(1)} %copy-done, bf16[1,16,512,512]{3,2,1,0:T(8,128)(2,1)} %last_lead.3), custom_call_target="tpu_custom_call" | custom-call | tf_op jit(solution)/shard_map/edge_strips2/pallas_call | solution.py:82
  14.9 0.9 %collective-permute-start.2 = (bf16[16,128,128]{2,1,0:T(8,128)(2,1)S(1)}, bf16[16,128,128]{2,1,0:T(8,128)(2,1)S(1)}, u32[]{:S(2)}, u32[]{:S(2)}) collective-permute-start(bf16[16,128,128]{2,1,0:T(8,128)(2,1)S(1)} %get-tuple-element.24), channel_id=1, source_target_pairs={{0,3},{1,0},{2,1},{3,2},{4,7},{5,4},{6,5},{7,6},{8,11},{9,8},{10,9... | collective-permute-start | bytes 1572872 | tf_op jit(solution)/shard_map/ppermute | solution.py:386
  15.8 3.2 %collective-permute-start.3 = (bf16[16,128,128]{2,1,0:T(8,128)(2,1)S(1)}, bf16[16,128,128]{2,1,0:T(8,128)(2,1)S(1)}, u32[]{:S(2)}, u32[]{:S(2)}) collective-permute-start(bf16[16,128,128]{2,1,0:T(8,128)(2,1)S(1)} %get-tuple-element.25), channel_id=1, source_target_pairs={{0,1},{1,2},{2,3},{4,5},{5,6},{6,7},{8,9},{9,10},{10,11},{12,13},{... | collective-permute-start | bytes 1572872 | tf_op jit(solution)/shard_map/ppermute | solution.py:386
  19.6 0.0 copy-done.1
  19.6 0.0 copy-done.2
  19.6 11.9 %interior.1 = (f32[16,2,16,384]{3,2,1,0:T(8,128)S(1)}, f32[16,2,16,384]{3,2,1,0:T(8,128)S(1)}, bf16[16,256,128]{2,1,0:T(8,128)(2,1)S(1)}, f32[16,512]{1,0:T(8,128)S(1)}) custom-call(s32[1,4,4]{2,1,0:T(4,128)S(1)} %copy-done, s32[1,16]{1,0:T(1,128)S(1)} %copy-done.1, f32[1,16]{1,0:T(1,128)S(1)} %copy-done.2, f32[1,16]{1,0:T(1,128)S(1)} %copy-done.3, ...), custom_call_target="tpu_custom_call" | custom-call | tf_op jit(solution)/shard_map/interior/pallas_call | solution.py:202
  31.6 0.0 collective-permute-done.right_ref.right_lead
  31.6 0.0 collective-permute-done.1.left_ref.left_lead
  31.6 3.6 %border0.1 = (f32[8,2,16,128]{3,2,1,0:T(8,128)S(1)}, f32[8,2,16,128]{3,2,1,0:T(8,128)S(1)}) custom-call(s32[1,4,4]{2,1,0:T(4,128)S(1)} %copy-done, s32[1,16]{1,0:T(1,128)S(1)} %copy-done.1, f32[1,16]{1,0:T(1,128)S(1)} %copy-done.2, f32[1,16]{1,0:T(1,128)S(1)} %copy-done.3, f32[1,16]{1,0:T(1,128)S(1)} %copy-done.4, f32[1,1]{1,0:T(1,128)} %bitcast.316.gain, ...), custom_call_target="tpu_custom_call" | custom-call | tf_op jit(solution)/shard_map/border0/pallas_call | solution.py:326
  35.2 0.1 collective-permute-start.5
  35.3 0.0 collective-permute-done.2.right_ref
  35.3 0.0 collective-permute-done.3.left_ref
  35.3 3.5 %border2.1 = (f32[8,2,16,128]{3,2,1,0:T(8,128)S(1)}, f32[8,2,16,128]{3,2,1,0:T(8,128)S(1)}) custom-call(s32[1,4,4]{2,1,0:T(4,128)S(1)} %copy-done, s32[1,16]{1,0:T(1,128)S(1)} %copy-done.1, f32[1,16]{1,0:T(1,128)S(1)} %copy-done.2, f32[1,16]{1,0:T(1,128)S(1)} %copy-done.3, f32[1,16]{1,0:T(1,128)S(1)} %copy-done.4, f32[1,1]{1,0:T(1,128)} %bitcast.317.gain, ...), custom_call_target="tpu_custom_call" | custom-call | tf_op jit(solution)/shard_map/border2/pallas_call | solution.py:326
  38.9 0.5 collective-permute-start.4
  39.5 1.1 %collective-permute-done.4 = f32[16,2,16,128]{3,2,1,0:T(8,128)S(1)} collective-permute-done((f32[16,2,16,128]{3,2,1,0:T(8,128)S(1)}, f32[16,2,16,128]{3,2,1,0:T(8,128)S(1)}, u32[]{:S(2)}, u32[]{:S(2)}) %collective-permute-start.4) | collective-permute-done | bytes 262176 | tf_op jit(solution)/shard_map/ppermute | solution.py:347
  40.7 0.0 collective-permute-done.5
  40.7 0.1 fusion.1
  40.8 0.9 %fusion = f16[16,2,16,512]{3,2,1,0:T(8,128)(2,1)} fusion(f32[16,1,16,384]{3,2,1,0:T(8,128)S(1)} %get-tuple-element.36, f32[16,1,16,384]{3,2,1,0:T(8,128)S(1)} %get-tuple-element.35, f32[16,1,16,128]{3,2,1,0:T(8,128)S(1)} %get-tuple-element.38, f32[16,1,16,128]{3,2,1,0:T(8,128)S(1)} %get-tuple-element.37), kind=kLoop, calls=%fused_computation.1 | loop fusion | flops 1310720 | bytes 1572864 | tf_op jit(solution)/shard_map/convert_element_type | solution.py:355
  41.7 8.1 %all-to-all-start = ((f16[16,2,16,512]{3,2,1,0:T(8,128)(2,1)}), f16[16,2,16,512]{3,2,1,0:T(8,128)(2,1)S(1)}, u32[]{:S(2)}, u32[]{:S(2)}) async-start(f16[16,2,16,512]{3,2,1,0:T(8,128)(2,1)} %fusion), calls=%async_computation | async-start | bytes 1048576 | tf_op jit(solution)/shard_map/all_to_all | solution.py:357
  49.9 11.9 %all-to-all-done = f16[16,2,16,512]{3,2,1,0:T(8,128)(2,1)S(1)} async-done(((f16[16,2,16,512]{3,2,1,0:T(8,128)(2,1)}), f16[16,2,16,512]{3,2,1,0:T(8,128)(2,1)S(1)}, u32[]{:S(2)}, u32[]{:S(2)}) %all-to-all-start) | async-done | bytes 524320 | tf_op jit(solution)/shard_map/all_to_all | solution.py:357
  61.8 0.2 convert_multiply_fusion
  62.0 0.1 multiply_add_fusion.2
  62.0 0.2 fusion.10
  62.2 1.4 %collective-permute-start.6 = (f32[2,16,128]{2,1,0:T(8,128)S(1)}, f32[2,16,128]{2,1,0:T(8,128)S(1)}, u32[]{:S(2)}, u32[]{:S(2)}) collective-permute-start(f32[2,16,128]{2,1,0:T(8,128)S(1)} %pad_maximum_fusion.3), channel_id=1, source_target_pairs={{0,1},{1,2},{2,3},{3,0},{4,5},{5,6},{6,7},{7,4},{8,9},{9,10},{10,1... | collective-permute-start | bytes 49160 | tf_op jit(solution)/shard_map/ppermute | solution.py:397
  63.6 3.6 %collective-permute-done.6 = f32[2,16,128]{2,1,0:T(8,128)S(1)} collective-permute-done((f32[2,16,128]{2,1,0:T(8,128)S(1)}, f32[2,16,128]{2,1,0:T(8,128)S(1)}, u32[]{:S(2)}, u32[]{:S(2)}) %collective-permute-start.6) | collective-permute-done | bytes 16416 | tf_op jit(solution)/shard_map/ppermute | solution.py:397
  67.3 0.6 pad_maximum_fusion.1
  (23 shorter events, 0.2 us)
Async XLA Ops:
  0.6 0.7 %copy-start = (s32[1,4,4]{2,1,0:T(4,128)S(1)}, s32[1,4,4]{2,1,0:T(4,128)}, u32[]{:S(2)}) copy-start(s32[1,4,4]{2,1,0:T(4,128)} %occ.9) | copy-start | bytes 196
  1.3 18.3 %copy-start.1 = (s32[1,16]{1,0:T(1,128)S(1)}, s32[1,16]{1,0:T(1,128)}, u32[]{:S(2)}) copy-start(s32[1,16]{1,0:T(1,128)} %offset.5) | copy-start | bytes 196
  1.3 18.3 %copy-start.2 = (f32[1,16]{1,0:T(1,128)S(1)}, f32[1,16]{1,0:T(1,128)}, u32[]{:S(2)}) copy-start(f32[1,16]{1,0:T(1,128)} %frac_lateral.5) | copy-start | bytes 196
  1.3 18.3 %copy-start.3 = (f32[1,16]{1,0:T(1,128)S(1)}, f32[1,16]{1,0:T(1,128)}, u32[]{:S(2)}) copy-start(f32[1,16]{1,0:T(1,128)} %frac_vertical.5) | copy-start | bytes 196
  1.3 18.3 %copy-start.4 = (f32[1,16]{1,0:T(1,128)S(1)}, f32[1,16]{1,0:T(1,128)}, u32[]{:S(2)}) copy-start(f32[1,16]{1,0:T(1,128)} %extinction.5) | copy-start | bytes 196
  1.3 18.3 %copy-start.5 = (s32[32]{0:T(128)S(1)}, s32[32]{0:T(128)}, u32[]{:S(2)}) copy-start(s32[32]{0:T(128)} %rank.1) | copy-start | bytes 388
  6.0 25.6 %collective-permute-start = (bf16[16,128,128]{2,1,0:T(8,128)(2,1)S(1)}, bf16[16,128,128]{2,1,0:T(8,128)(2,1)S(1)}, u32[]{:S(2)}, u32[]{:S(2)}) collective-permute-start(bf16[16,128,128]{2,1,0:T(8,128)(2,1)S(1)} %get-tuple-element.19), channel_id=1, source_target_pairs={{0,3},{1,0},{2,1},{3,2},{4,7},{5,4},{6,5},{7,6},{8,11},{9,8},{10,9... | collective-permute-start | bytes 1572872 | tf_op jit(solution)/shard_map/ppermute | solution.py:386
  8.9 22.7 %collective-permute-start.1 = (bf16[16,128,128]{2,1,0:T(8,128)(2,1)S(1)}, bf16[16,128,128]{2,1,0:T(8,128)(2,1)S(1)}, u32[]{:S(2)}, u32[]{:S(2)}) collective-permute-start(bf16[16,128,128]{2,1,0:T(8,128)(2,1)S(1)} %get-tuple-element.20), channel_id=1, source_target_pairs={{0,1},{1,2},{2,3},{4,5},{5,6},{6,7},{8,9},{9,10},{10,11},{12,13},{... | collective-permute-start | bytes 1572872 | tf_op jit(solution)/shard_map/ppermute | solution.py:386
  14.9 20.4 %collective-permute-start.2 = (bf16[16,128,128]{2,1,0:T(8,128)(2,1)S(1)}, bf16[16,128,128]{2,1,0:T(8,128)(2,1)S(1)}, u32[]{:S(2)}, u32[]{:S(2)}) collective-permute-start(bf16[16,128,128]{2,1,0:T(8,128)(2,1)S(1)} %get-tuple-element.24), channel_id=1, source_target_pairs={{0,3},{1,0},{2,1},{3,2},{4,7},{5,4},{6,5},{7,6},{8,11},{9,8},{10,9... | collective-permute-start | bytes 1572872 | tf_op jit(solution)/shard_map/ppermute | solution.py:386
  15.8 19.5 %collective-permute-start.3 = (bf16[16,128,128]{2,1,0:T(8,128)(2,1)S(1)}, bf16[16,128,128]{2,1,0:T(8,128)(2,1)S(1)}, u32[]{:S(2)}, u32[]{:S(2)}) collective-permute-start(bf16[16,128,128]{2,1,0:T(8,128)(2,1)S(1)} %get-tuple-element.25), channel_id=1, source_target_pairs={{0,1},{1,2},{2,3},{4,5},{5,6},{6,7},{8,9},{9,10},{10,11},{12,13},{... | collective-permute-start | bytes 1572872 | tf_op jit(solution)/shard_map/ppermute | solution.py:386
  35.2 5.5 %collective-permute-start.5 = (f32[16,2,16,384]{3,2,1,0:T(8,128)S(1)}, f32[16,2,16,384]{3,2,1,0:T(8,128)S(1)}, u32[]{:S(2)}, u32[]{:S(2)}) collective-permute-start(f32[16,2,16,384]{3,2,1,0:T(8,128)S(1)} %get-tuple-element.31), channel_id=1, source_target_pairs={{0,4},{4,0},{8,12},{12,8},{16,20},{20,16},{24,28},{28,24},{32,36},... | collective-permute-start | bytes 2359304 | tf_op jit(solution)/shard_map/ppermute | solution.py:347
  38.9 1.7 %collective-permute-start.4 = (f32[16,2,16,128]{3,2,1,0:T(8,128)S(1)}, f32[16,2,16,128]{3,2,1,0:T(8,128)S(1)}, u32[]{:S(2)}, u32[]{:S(2)}) collective-permute-start(f32[16,2,16,128]{3,2,1,0:T(8,128)S(1)} %pad_maximum_fusion), channel_id=1, source_target_pairs={{0,4},{4,0},{8,12},{12,8},{16,20},{20,16},{24,28},{28,24},{32,36},... | collective-permute-start | bytes 786440 | tf_op jit(solution)/shard_map/ppermute | solution.py:347
  41.7 20.1 %all-to-all-start = ((f16[16,2,16,512]{3,2,1,0:T(8,128)(2,1)}), f16[16,2,16,512]{3,2,1,0:T(8,128)(2,1)S(1)}, u32[]{:S(2)}, u32[]{:S(2)}) async-start(f16[16,2,16,512]{3,2,1,0:T(8,128)(2,1)} %fusion), calls=%async_computation | async-start | bytes 1048576 | tf_op jit(solution)/shard_map/all_to_all | solution.py:357
  62.2 5.0 %collective-permute-start.6 = (f32[2,16,128]{2,1,0:T(8,128)S(1)}, f32[2,16,128]{2,1,0:T(8,128)S(1)}, u32[]{:S(2)}, u32[]{:S(2)}) collective-permute-start(f32[2,16,128]{2,1,0:T(8,128)S(1)} %pad_maximum_fusion.3), channel_id=1, source_target_pairs={{0,1},{1,2},{2,3},{3,0},{4,5},{5,6},{6,7},{7,4},{8,9},{9,10},{10,1... | collective-permute-start | bytes 49160 | tf_op jit(solution)/shard_map/ppermute | solution.py:397

commit v11 on v5

--- a/solution.py
+++ b/solution.py
@@ -15,7 +15,7 @@
 PIECE = 16
 WIRE = jnp.float16
 WIRE_SCALE = 4096.0
-UNROLL = 16
+TAIL = 2
 LOG2E = math.log2(math.e)
 SMEM = pltpu.SMEM
 F32 = jnp.float32
@@ -29,6 +29,10 @@
 def tap(distance, offset, fraction):
     second = jnp.where(distance == offset + 1, fraction, 0.0)
     return jnp.where(distance == offset, 1.0 - fraction, second)
+
+
+def whole():
+    return pl.BlockSpec(memory_space=pltpu.VMEM)
 
 
 def strips_kernel(first_block, occ, x_first, x_last, to_left, to_right):
@@ -86,7 +90,7 @@
 
 def finish(state, gain, swap, out_keep, out_send, tile):
     through_ref, sum_ref = state
-    rows = out_keep.shape[1] * 2
+    rows = out_keep.shape[0] * 2 * PIECE
     base = tile * rows
     alphas, colors = [], []
     for p in range(rows // PIECE):
@@ -96,11 +100,10 @@
         colors.append(gain * (0.65 * alpha + 0.35 * sum_ref[at]))
     lanes = slice(tile * LANES, (tile + 1) * LANES)
     for q in range(rows // PIECE // 2):
-        at = slice(q * PIECE, (q + 1) * PIECE)
         for i, values in enumerate((colors, alphas)):
             even, odd = values[2 * q], values[2 * q + 1]
-            out_keep[i, at, lanes] = jnp.where(swap, odd, even)
-            out_send[i, at, lanes] = jnp.where(swap, even, odd)
+            out_keep[q, i, :, lanes] = jnp.where(swap, odd, even)
+            out_send[q, i, :, lanes] = jnp.where(swap, even, odd)
 
 
 def splat(value):
@@ -108,7 +111,8 @@
 
 
 def over_slices(slices, one):
-    lax.fori_loop(0, slices, one, 0, unroll=UNROLL)
+    for s in range(slices):
+        one(s, 0)
 
 
 def interior_kernel(
@@ -139,8 +143,16 @@
     through_ref[...] = jnp.ones_like(through_ref)
     sum_ref[...] = jnp.zeros_like(sum_ref)
     inside = jnp.where(block > 0, 1, 0)
-    above = jnp.maximum(block - 1, 0)
-    mask = [splat(occ[0, block, t]) for t in range(tiles)]
+    per = rows // BLK
+    above = jnp.maximum(per * block - 1, 0)
+
+    def mask_of(t):
+        parts = [
+            jnp.broadcast_to(splat(occ[0, per * block + b, t]), (BLK, LANES)) for b in range(per)
+        ]
+        return jnp.concatenate(parts, axis=0)
+
+    mask = [mask_of(t) for t in range(tiles)]
     lead_mask = [splat(occ[0, above, t] * inside) for t in range(tiles)]
     state = (through_ref, sum_ref)
     refs = (frac_vertical, extinction, slice_total)
@@ -160,18 +172,19 @@
     over_slices(slices, one)
     swap = lax.axis_index("depth") % 2 == 1
     for t in range(tiles - 1):
-        finish(state, gain[0], swap, out_keep, out_send, t)
+        finish(state, gain[...], swap, out_keep, out_send, t)
 
 
 def small_specs():
-    return [pl.BlockSpec(memory_space=SMEM)] * 6
+    return [pl.BlockSpec(memory_space=SMEM)] * 5 + [whole()]
 
 
 def interior(density, small, rank, slice_total):
     _, slices, rows, cols = density.shape
-    step = BLK
+    step = 2 * BLK
     width = cols - LANES
-    image = jax.ShapeDtypeStruct((2, rows // 2, width), F32)
+    pieces = step // (2 * PIECE)
+    image = jax.ShapeDtypeStruct((rows // (2 * PIECE), 2, PIECE, width), F32)
     return pl.pallas_call(
         functools.partial(interior_kernel, slice_total),
         grid=(rows // step,),
@@ -184,7 +197,7 @@
             ),
         ],
         out_specs=[
-            pl.BlockSpec((2, step // 2, width), lambda b: (0, b, 0))
+            pl.BlockSpec((pieces, 2, PIECE, width), lambda b: (b, 0, 0, 0))
         ]
         * 2
         + [
@@ -273,7 +286,7 @@
 
     over_slices(slices, one)
     swap = lax.axis_index("depth") % 2 == 1
-    finish(state, gain[0], swap, out_keep, out_send, 0)
+    finish(state, gain[...], swap, out_keep, out_send, 0)
 
 
 def border(density, small, weights, halos, above, start, blocks, slice_total):
@@ -294,14 +307,15 @@
     halo = pl.BlockSpec((slices, step // 2, LANES), lambda i: (0, 0, 0))
     last_rows = above[0].shape[1] // 16 - 1
     halo_lead = pl.BlockSpec((slices, 16, LANES), lambda i: (0, last_rows, 0))
-    image = jax.ShapeDtypeStruct((2, step // 2, LANES), F32)
+    shape = (step // (2 * PIECE), 2, PIECE, LANES)
+    image = jax.ShapeDtypeStruct(shape, F32)
     return pl.pallas_call(
         functools.partial(border_kernel, start, slice_total),
         grid=(1,),
         in_specs=small_specs()
         + [pl.BlockSpec((slices, 2 * LANES, LANES), lambda i: (0, 0, 0))]
         + [body(0), body(last), lead(0), lead(last), halo, halo, halo_lead, halo_lead],
-        out_specs=[pl.BlockSpec((2, step // 2, LANES), lambda i: (0, 0, 0))] * 2,
+        out_specs=[pl.BlockSpec(shape, lambda i: (0, 0, 0, 0))] * 2,
         out_shape=[image, image],
         scratch_shapes=[pltpu.VMEM((step, LANES), F32)] * 2,
         compiler_params=pltpu.CompilerParams(vmem_limit_bytes=32 * 2**20),
@@ -317,14 +331,13 @@
 def over_cores(keep, send, flags):
     count = lax.axis_size("depth")
     other = lax.ppermute(send, "depth", [(i, i ^ 1) for i in range(count)])
-    return jnp.stack(over(keep, other, flags[0, : keep.shape[2]]))
-
-
-def over_chips(image, flags):
+    front = flags[0, : keep.shape[3]]
+    return jnp.stack(over((keep[:, 0], keep[:, 1]), (other[:, 0], other[:, 1]), front), axis=1)
+
+
+def over_chips(pieces, flags):
     count = lax.axis_size("depth")
     chips = count // 2
-    width = image.shape[2]
-    pieces = image.reshape(2, chips, PIECE, width).transpose(1, 0, 2, 3)
     pieces = (pieces * WIRE_SCALE).astype(WIRE)
     groups = [[2 * i + core for i in range(chips)] for core in range(2)]
     pieces = lax.all_to_all(
@@ -347,9 +360,9 @@
     slice_total = lax.axis_size("depth") * slices
     lat = lax.axis_size("lat")
     density = pltpu.with_memory_space_constraint(density, pltpu.HBM)
-    small = (occupancy, shear_offsets, frac_lateral, frac_vertical, extinction, slab_gain)
+    small = (occupancy, shear_offsets, frac_lateral, frac_vertical, extinction, slab_gain[None])
     blocks = rows // BLK
-    half = blocks // 2
+    half = blocks - TAIL
     rightwards = [(x, x + 1) for x in range(lat - 1)]
     leftwards = [(x, (x - 1) % lat) for x in range(lat)]
     halos = []
@@ -363,9 +376,9 @@
     send, top = lax.optimization_barrier((send, top))
     inner = over_cores(keep, send, flags)
     bottom = border(density, small, weights, halos[1], halos[0], half, blocks - half, slice_total)
-    keep, send = (jnp.concatenate(p, axis=1) for p in zip(top, bottom))
+    keep, send = (jnp.concatenate(p, axis=0) for p in zip(top, bottom))
     edge = over_cores(keep, send, flags)
-    color, alpha = over_chips(jnp.concatenate([edge, inner], axis=2), flags)
+    color, alpha = over_chips(jnp.concatenate([edge, inner], axis=3), flags)
     image = jnp.stack([color, alpha])
     moved = lax.ppermute(image[:, :, :LANES], "lat", [(x, (x + 1) % lat) for x in range(lat)])
     lane = jnp.arange(LANES, dtype=jnp.int32)

time: 65.1 us -> 64.4 us (0.989)
  local copies, waits for them, and re-layouts: 1 us -> 0.1 us
  other arithmetic: 1.45 us -> 2.22 us
    convert_element_type x1 -> x0, local copies, waits for them, and re-layouts: 0.92 us -> none  [over_chips(): pieces = (pieces * WIRE_SCALE).astype(WIRE)]
    convert_element_type x1, other arithmetic: 0.09 us -> 0.9 us  [over_chips(): pieces = (pieces * WIRE_SCALE).astype(WIRE)]
  transfers between devices with their start and end apart: 8 -> 8, of which waited for: 3 -> 3; matrix products, arithmetic and copies ran while one was open for 0% -> 0% of each run, Pallas kernels for 35% -> 34%
where the time goes in v11:
time: 64.4 us; the launch traced here: 64 us
  Pallas kernels  25.1 us (39%)
  starting transfers between devices  18.6 us (29%)
  waiting for transfers between devices  16.4 us (25%)
  other arithmetic  2.22 us (3%)
  between operations  1.53 us (2%)
    all_to_all x1, waiting for transfers between devices, over_chips(): lax.all_to_all(pieces, 'depth', 0, 0, axis_index_groups=groups, tiled=True)  11.9 us
    pallas_call x1, Pallas kernels, interior(): pl.pallas_call(functools.partial(interior_kernel, slice_total), grid=(row...  11.5 us
    all_to_all x1, starting transfers between devices, over_chips(): lax.all_to_all(pieces, 'depth', 0, 0, axis_index_groups=groups, tiled=True)  8.06 us
    pallas_call x2, Pallas kernels, border(): pl.pallas_call(functools.partial(border_kernel, start, slice_total), grid...  7.05 us
    pallas_call x2, Pallas kernels, edge_strips(): pl.pallas_call(functools.partial(strips_kernel, first), grid=(blocks,), i...  6.59 us
    ppermute x2, starting transfers between devices, shards(): lax.ppermute(to_right, 'lat', rightwards)  4.64 us
    ppermute x2, starting transfers between devices, shards(): lax.ppermute(to_left, 'lat', leftwards)  3.61 us
    ppermute x1, waiting for transfers between devices, shards(): lax.ppermute(image[:, :, :LANES], 'lat', [(x, (x + 1) % lat) for x in ran...  3.37 us
  transfers between devices with their start and end apart: 8, of which 3 were waited for; matrix products, arithmetic and copies ran while one was open for 0% of the time, Pallas kernels for 34%

profile of v11, /device:TPU:0, one launch (start us, length us, event | category | flops | bytes accessed | tf_op | source)
XLA Modules:
  0.0 64.0 jit_solution(3480267289021878575)
XLA Ops:
  0.6 3.3 %edge_strips0.1 = (bf16[16,128,128]{2,1,0:T(8,128)(2,1)}, bf16[16,128,128]{2,1,0:T(8,128)(2,1)}) custom-call(s32[1,4,4]{2,1,0:T(4,128)} %occ.9, bf16[1,16,512,512]{3,2,1,0:T(8,128)(2,1)} %last_lead.3, bf16[1,16,512,512]{3,2,1,0:T(8,128)(2,1)} %last_lead.3), custom_call_target="tpu_custom_call" | custom-call | tf_op jit(solution)/shard_map/edge_strips0/pallas_call | solution.py:58
  3.9 2.9 %collective-permute-start = (bf16[16,128,128]{2,1,0:T(8,128)(2,1)}, bf16[16,128,128]{2,1,0:T(8,128)(2,1)S(1)}, u32[]{:S(2)}, u32[]{:S(2)}) collective-permute-start(bf16[16,128,128]{2,1,0:T(8,128)(2,1)} %get-tuple-element.19), channel_id=1, source_target_pairs={{0,3},{1,0},{2,1},{3,2},{4,7},{5,4},{6,5},{7,6},{8,11},{9,8},{10,9... | collective-permute-start | bytes 1572872 | tf_op jit(solution)/shard_map/ppermute | solution.py:372
  6.8 0.0 copy-start.4
  6.8 0.0 copy-start.5
  6.8 1.5 %collective-permute-start.1 = (bf16[16,128,128]{2,1,0:T(8,128)(2,1)}, bf16[16,128,128]{2,1,0:T(8,128)(2,1)S(1)}, u32[]{:S(2)}, u32[]{:S(2)}) collective-permute-start(bf16[16,128,128]{2,1,0:T(8,128)(2,1)} %get-tuple-element.20), channel_id=1, source_target_pairs={{0,1},{1,2},{2,3},{4,5},{5,6},{6,7},{8,9},{9,10},{10,11},{12,13},{... | collective-permute-start | bytes 1572872 | tf_op jit(solution)/shard_map/ppermute | solution.py:372
  8.3 3.3 %edge_strips2.1 = (bf16[16,128,128]{2,1,0:T(8,128)(2,1)}, bf16[16,128,128]{2,1,0:T(8,128)(2,1)}) custom-call(s32[1,4,4]{2,1,0:T(4,128)} %occ.9, bf16[1,16,512,512]{3,2,1,0:T(8,128)(2,1)} %last_lead.3, bf16[1,16,512,512]{3,2,1,0:T(8,128)(2,1)} %last_lead.3), custom_call_target="tpu_custom_call" | custom-call | tf_op jit(solution)/shard_map/edge_strips2/pallas_call | solution.py:58
  11.6 0.8 %collective-permute-start.2 = (bf16[16,128,128]{2,1,0:T(8,128)(2,1)}, bf16[16,128,128]{2,1,0:T(8,128)(2,1)S(1)}, u32[]{:S(2)}, u32[]{:S(2)}) collective-permute-start(bf16[16,128,128]{2,1,0:T(8,128)(2,1)} %get-tuple-element.24), channel_id=1, source_target_pairs={{0,3},{1,0},{2,1},{3,2},{4,7},{5,4},{6,5},{7,6},{8,11},{9,8},{10,9... | collective-permute-start | bytes 1572872 | tf_op jit(solution)/shard_map/ppermute | solution.py:372
  12.3 3.2 %collective-permute-start.3 = (bf16[16,128,128]{2,1,0:T(8,128)(2,1)}, bf16[16,128,128]{2,1,0:T(8,128)(2,1)S(1)}, u32[]{:S(2)}, u32[]{:S(2)}) collective-permute-start(bf16[16,128,128]{2,1,0:T(8,128)(2,1)} %get-tuple-element.25), channel_id=1, source_target_pairs={{0,1},{1,2},{2,3},{4,5},{5,6},{6,7},{8,9},{9,10},{10,11},{12,13},{... | collective-permute-start | bytes 1572872 | tf_op jit(solution)/shard_map/ppermute | solution.py:372
  16.2 0.0 copy-done
  16.2 0.0 copy-done.1
  16.2 0.0 copy-done.2
  16.2 11.5 %interior.1 = (f32[16,2,16,384]{3,2,1,0:T(8,128)S(1)}, f32[16,2,16,384]{3,2,1,0:T(8,128)S(1)}, bf16[16,256,128]{2,1,0:T(8,128)(2,1)S(1)}, f32[16,512]{1,0:T(8,128)S(1)}) custom-call(s32[1,4,4]{2,1,0:T(4,128)S(1)} %copy-done, s32[1,16]{1,0:T(1,128)S(1)} %copy-done.1, f32[1,16]{1,0:T(1,128)S(1)} %copy-done.2, f32[1,16]{1,0:T(1,128)S(1)} %copy-done.3, ...), custom_call_target="tpu_custom_call" | custom-call | tf_op jit(solution)/shard_map/interior/pallas_call | solution.py:188
  27.8 0.0 collective-permute-done.right_ref.right_lead
  27.8 0.0 collective-permute-done.1.left_ref.left_lead
  27.8 3.5 %border0.1 = (f32[8,2,16,128]{3,2,1,0:T(8,128)S(1)}, f32[8,2,16,128]{3,2,1,0:T(8,128)S(1)}) custom-call(s32[1,4,4]{2,1,0:T(4,128)S(1)} %copy-done, s32[1,16]{1,0:T(1,128)S(1)} %copy-done.1, f32[1,16]{1,0:T(1,128)S(1)} %copy-done.2, f32[1,16]{1,0:T(1,128)S(1)} %copy-done.3, f32[1,16]{1,0:T(1,128)S(1)} %copy-done.4, f32[1,1]{1,0:T(1,128)} %bitcast.316.gain, ...), custom_call_target="tpu_custom_call" | custom-call | tf_op jit(solution)/shard_map/border0/pallas_call | solution.py:312
  31.3 0.1 collective-permute-start.5
  31.4 0.0 collective-permute-done.2.right_ref
  31.4 0.0 collective-permute-done.3.left_ref
  31.4 3.5 %border2.1 = (f32[8,2,16,128]{3,2,1,0:T(8,128)S(1)}, f32[8,2,16,128]{3,2,1,0:T(8,128)S(1)}) custom-call(s32[1,4,4]{2,1,0:T(4,128)S(1)} %copy-done, s32[1,16]{1,0:T(1,128)S(1)} %copy-done.1, f32[1,16]{1,0:T(1,128)S(1)} %copy-done.2, f32[1,16]{1,0:T(1,128)S(1)} %copy-done.3, f32[1,16]{1,0:T(1,128)S(1)} %copy-done.4, f32[1,1]{1,0:T(1,128)} %bitcast.317.gain, ...), custom_call_target="tpu_custom_call" | custom-call | tf_op jit(solution)/shard_map/border2/pallas_call | solution.py:312
  35.0 0.5 collective-permute-start.4
  35.6 1.1 %collective-permute-done.4 = f32[16,2,16,128]{3,2,1,0:T(8,128)S(1)} collective-permute-done((f32[16,2,16,128]{3,2,1,0:T(8,128)S(1)}, f32[16,2,16,128]{3,2,1,0:T(8,128)S(1)}, u32[]{:S(2)}, u32[]{:S(2)}) %collective-permute-start.4) | collective-permute-done | bytes 262176 | tf_op jit(solution)/shard_map/ppermute | solution.py:333
  36.7 0.0 collective-permute-done.5
  36.8 0.1 fusion.1
  36.9 0.9 %fusion = f16[16,2,16,512]{3,2,1,0:T(8,128)(2,1)} fusion(f32[16,1,16,384]{3,2,1,0:T(8,128)S(1)} %get-tuple-element.36, f32[16,1,16,384]{3,2,1,0:T(8,128)S(1)} %get-tuple-element.35, f32[16,1,16,128]{3,2,1,0:T(8,128)S(1)} %get-tuple-element.38, f32[16,1,16,128]{3,2,1,0:T(8,128)S(1)} %get-tuple-element.37), kind=kLoop, calls=%fused_computation.1 | loop fusion | flops 1310720 | bytes 1572864 | tf_op jit(solution)/shard_map/convert_element_type | solution.py:341
  37.8 8.1 %all-to-all-start = ((f16[16,2,16,512]{3,2,1,0:T(8,128)(2,1)}), f16[16,2,16,512]{3,2,1,0:T(8,128)(2,1)S(1)}, u32[]{:S(2)}, u32[]{:S(2)}) async-start(f16[16,2,16,512]{3,2,1,0:T(8,128)(2,1)} %fusion), calls=%async_computation | async-start | bytes 1048576 | tf_op jit(solution)/shard_map/all_to_all | solution.py:343
  46.0 11.9 %all-to-all-done = f16[16,2,16,512]{3,2,1,0:T(8,128)(2,1)S(1)} async-done(((f16[16,2,16,512]{3,2,1,0:T(8,128)(2,1)}), f16[16,2,16,512]{3,2,1,0:T(8,128)(2,1)S(1)}, u32[]{:S(2)}, u32[]{:S(2)}) %all-to-all-start) | async-done | bytes 524320 | tf_op jit(solution)/shard_map/all_to_all | solution.py:343
  57.9 0.2 convert_multiply_fusion
  58.0 0.1 multiply_add_fusion.2
  58.1 0.2 fusion.10
  58.3 1.6 %collective-permute-start.6 = (f32[2,16,128]{2,1,0:T(8,128)S(1)}, f32[2,16,128]{2,1,0:T(8,128)S(1)}, u32[]{:S(2)}, u32[]{:S(2)}) collective-permute-start(f32[2,16,128]{2,1,0:T(8,128)S(1)} %pad_maximum_fusion.3), channel_id=1, source_target_pairs={{0,1},{1,2},{2,3},{3,0},{4,5},{5,6},{6,7},{7,4},{8,9},{9,10},{10,1... | collective-permute-start | bytes 49160 | tf_op jit(solution)/shard_map/ppermute | solution.py:383
  60.0 3.4 %collective-permute-done.6 = f32[2,16,128]{2,1,0:T(8,128)S(1)} collective-permute-done((f32[2,16,128]{2,1,0:T(8,128)S(1)}, f32[2,16,128]{2,1,0:T(8,128)S(1)}, u32[]{:S(2)}, u32[]{:S(2)}) %collective-permute-start.6) | collective-permute-done | bytes 16416 | tf_op jit(solution)/shard_map/ppermute | solution.py:383
  63.4 0.6 pad_maximum_fusion.1
  (23 shorter events, 0.2 us)
Async XLA Ops:
  3.9 23.8 %collective-permute-start = (bf16[16,128,128]{2,1,0:T(8,128)(2,1)}, bf16[16,128,128]{2,1,0:T(8,128)(2,1)S(1)}, u32[]{:S(2)}, u32[]{:S(2)}) collective-permute-start(bf16[16,128,128]{2,1,0:T(8,128)(2,1)} %get-tuple-element.19), channel_id=1, source_target_pairs={{0,3},{1,0},{2,1},{3,2},{4,7},{5,4},{6,5},{7,6},{8,11},{9,8},{10,9... | collective-permute-start | bytes 1572872 | tf_op jit(solution)/shard_map/ppermute | solution.py:372
  6.8 9.4 %copy-start = (s32[1,4,4]{2,1,0:T(4,128)S(1)}, s32[1,4,4]{2,1,0:T(4,128)}, u32[]{:S(2)}) copy-start(s32[1,4,4]{2,1,0:T(4,128)} %occ.9) | copy-start | bytes 196
  6.8 9.4 %copy-start.1 = (s32[1,16]{1,0:T(1,128)S(1)}, s32[1,16]{1,0:T(1,128)}, u32[]{:S(2)}) copy-start(s32[1,16]{1,0:T(1,128)} %offset.5) | copy-start | bytes 196
  6.8 9.4 %copy-start.2 = (f32[1,16]{1,0:T(1,128)S(1)}, f32[1,16]{1,0:T(1,128)}, u32[]{:S(2)}) copy-start(f32[1,16]{1,0:T(1,128)} %frac_lateral.5) | copy-start | bytes 196
  6.8 9.4 %copy-start.3 = (f32[1,16]{1,0:T(1,128)S(1)}, f32[1,16]{1,0:T(1,128)}, u32[]{:S(2)}) copy-start(f32[1,16]{1,0:T(1,128)} %frac_vertical.5) | copy-start | bytes 196
  6.8 9.4 %copy-start.4 = (f32[1,16]{1,0:T(1,128)S(1)}, f32[1,16]{1,0:T(1,128)}, u32[]{:S(2)}) copy-start(f32[1,16]{1,0:T(1,128)} %extinction.5) | copy-start | bytes 196
  6.8 9.4 %copy-start.5 = (s32[32]{0:T(128)S(1)}, s32[32]{0:T(128)}, u32[]{:S(2)}) copy-start(s32[32]{0:T(128)} %rank.1) | copy-start | bytes 388
  6.8 21.0 %collective-permute-start.1 = (bf16[16,128,128]{2,1,0:T(8,128)(2,1)}, bf16[16,128,128]{2,1,0:T(8,128)(2,1)S(1)}, u32[]{:S(2)}, u32[]{:S(2)}) collective-permute-start(bf16[16,128,128]{2,1,0:T(8,128)(2,1)} %get-tuple-element.20), channel_id=1, source_target_pairs={{0,1},{1,2},{2,3},{4,5},{5,6},{6,7},{8,9},{9,10},{10,11},{12,13},{... | collective-permute-start | bytes 1572872 | tf_op jit(solution)/shard_map/ppermute | solution.py:372
  11.6 19.8 %collective-permute-start.2 = (bf16[16,128,128]{2,1,0:T(8,128)(2,1)}, bf16[16,128,128]{2,1,0:T(8,128)(2,1)S(1)}, u32[]{:S(2)}, u32[]{:S(2)}) collective-permute-start(bf16[16,128,128]{2,1,0:T(8,128)(2,1)} %get-tuple-element.24), channel_id=1, source_target_pairs={{0,3},{1,0},{2,1},{3,2},{4,7},{5,4},{6,5},{7,6},{8,11},{9,8},{10,9... | collective-permute-start | bytes 1572872 | tf_op jit(solution)/shard_map/ppermute | solution.py:372
  12.3 19.1 %collective-permute-start.3 = (bf16[16,128,128]{2,1,0:T(8,128)(2,1)}, bf16[16,128,128]{2,1,0:T(8,128)(2,1)S(1)}, u32[]{:S(2)}, u32[]{:S(2)}) collective-permute-start(bf16[16,128,128]{2,1,0:T(8,128)(2,1)} %get-tuple-element.25), channel_id=1, source_target_pairs={{0,1},{1,2},{2,3},{4,5},{5,6},{6,7},{8,9},{9,10},{10,11},{12,13},{... | collective-permute-start | bytes 1572872 | tf_op jit(solution)/shard_map/ppermute | solution.py:372
  31.3 5.5 %collective-permute-start.5 = (f32[16,2,16,384]{3,2,1,0:T(8,128)S(1)}, f32[16,2,16,384]{3,2,1,0:T(8,128)S(1)}, u32[]{:S(2)}, u32[]{:S(2)}) collective-permute-start(f32[16,2,16,384]{3,2,1,0:T(8,128)S(1)} %get-tuple-element.31), channel_id=1, source_target_pairs={{0,4},{4,0},{8,12},{12,8},{16,20},{20,16},{24,28},{28,24},{32,36},... | collective-permute-start | bytes 2359304 | tf_op jit(solution)/shard_map/ppermute | solution.py:333
  35.0 1.7 %collective-permute-start.4 = (f32[16,2,16,128]{3,2,1,0:T(8,128)S(1)}, f32[16,2,16,128]{3,2,1,0:T(8,128)S(1)}, u32[]{:S(2)}, u32[]{:S(2)}) collective-permute-start(f32[16,2,16,128]{3,2,1,0:T(8,128)S(1)} %pad_maximum_fusion), channel_id=1, source_target_pairs={{0,4},{4,0},{8,12},{12,8},{16,20},{20,16},{24,28},{28,24},{32,36},... | collective-permute-start | bytes 786440 | tf_op jit(solution)/shard_map/ppermute | solution.py:333
  37.8 20.1 %all-to-all-start = ((f16[16,2,16,512]{3,2,1,0:T(8,128)(2,1)}), f16[16,2,16,512]{3,2,1,0:T(8,128)(2,1)S(1)}, u32[]{:S(2)}, u32[]{:S(2)}) async-start(f16[16,2,16,512]{3,2,1,0:T(8,128)(2,1)} %fusion), calls=%async_computation | async-start | bytes 1048576 | tf_op jit(solution)/shard_map/all_to_all | solution.py:343
  58.3 5.0 %collective-permute-start.6 = (f32[2,16,128]{2,1,0:T(8,128)S(1)}, f32[2,16,128]{2,1,0:T(8,128)S(1)}, u32[]{:S(2)}, u32[]{:S(2)}) collective-permute-start(f32[2,16,128]{2,1,0:T(8,128)S(1)} %pad_maximum_fusion.3), channel_id=1, source_target_pairs={{0,1},{1,2},{2,3},{3,0},{4,5},{5,6},{6,7},{7,4},{8,9},{9,10},{10,1... | collective-permute-start | bytes 49160 | tf_op jit(solution)/shard_map/ppermute | solution.py:383

commit v12 on v11

--- a/solution.py
+++ b/solution.py
@@ -16,6 +16,7 @@
 WIRE = jnp.float16
 WIRE_SCALE = 4096.0
 TAIL = 2
+PARTS = 2
 LOG2E = math.log2(math.e)
 SMEM = pltpu.SMEM
 F32 = jnp.float32
@@ -119,11 +120,12 @@
     slice_total, occ, offset, frac_lateral, frac_vertical, extinction, gain, rank,
     x_ref, lead_ref, out_keep, out_send, weights, flags, through_ref, sum_ref,
 ):
-    block = pl.program_id(0)
-    slices, rows = x_ref.shape[1], x_ref.shape[2]
+    block, part = pl.program_id(0), pl.program_id(1)
+    slices, rows = weights.shape[0], x_ref.shape[2]
+    count = x_ref.shape[1]
     tiles = x_ref.shape[3] // LANES
 
-    @pl.when(block == 0)
+    @pl.when((block == 0) & (part == 0))
     def _():
         k = lax.broadcasted_iota(jnp.int32, (2 * LANES, LANES), 0)
         n = lax.broadcasted_iota(jnp.int32, (2 * LANES, LANES), 1)
@@ -140,8 +142,11 @@
         for i, flag in enumerate(in_front):
             flags[i : i + 1] = jnp.full((1, flags.shape[1]), jnp.where(flag, 1.0, 0.0), F32)
 
-    through_ref[...] = jnp.ones_like(through_ref)
-    sum_ref[...] = jnp.zeros_like(sum_ref)
+    @pl.when(part == 0)
+    def _():
+        through_ref[...] = jnp.ones_like(through_ref)
+        sum_ref[...] = jnp.zeros_like(sum_ref)
+
     inside = jnp.where(block > 0, 1, 0)
     per = rows // BLK
     above = jnp.maximum(per * block - 1, 0)
@@ -157,22 +162,26 @@
     state = (through_ref, sum_ref)
     refs = (frac_vertical, extinction, slice_total)
 
-    def one(s, _):
+    def one(u, _):
+        s = part * count + u
         parts = []
         for t in range(tiles):
             lanes = slice(t * LANES, (t + 1) * LANES)
-            lead = lead_ref[0, s, :, lanes] * lead_mask[t]
-            parts.append(jnp.concatenate([lead, x_ref[0, s, :, lanes] * mask[t]], axis=0))
+            lead = lead_ref[0, u, :, lanes] * lead_mask[t]
+            parts.append(jnp.concatenate([lead, x_ref[0, u, :, lanes] * mask[t]], axis=0))
         for t in range(1, tiles):
             pair = jnp.concatenate([parts[t - 1], parts[t]], axis=1)
             x = jnp.dot(pair, weights[s], preferred_element_type=F32)
             shade(s, x[8:], (t - 1) * rows, state, refs)
         return 0
 
-    over_slices(slices, one)
-    swap = lax.axis_index("depth") % 2 == 1
-    for t in range(tiles - 1):
-        finish(state, gain[...], swap, out_keep, out_send, t)
+    over_slices(count, one)
+
+    @pl.when(part == pl.num_programs(1) - 1)
+    def _():
+        swap = lax.axis_index("depth") % 2 == 1
+        for t in range(tiles - 1):
+            finish(state, gain[...], swap, out_keep, out_send, t)
 
 
 def small_specs():
@@ -187,22 +196,23 @@
     image = jax.ShapeDtypeStruct((rows // (2 * PIECE), 2, PIECE, width), F32)
     return pl.pallas_call(
         functools.partial(interior_kernel, slice_total),
-        grid=(rows // step,),
+        grid=(rows // step, PARTS),
         in_specs=small_specs()
         + [pl.BlockSpec(memory_space=SMEM)]
         + [
-            pl.BlockSpec((1, slices, step, cols), lambda b: (0, 0, b, 0)),
+            pl.BlockSpec((1, slices // PARTS, step, cols), lambda b, g: (0, g, b, 0)),
             pl.BlockSpec(
-                (1, slices, 16, cols), lambda b: (0, 0, jnp.maximum(b * (step // 16) - 1, 0), 0)
+                (1, slices // PARTS, 16, cols),
+                lambda b, g: (0, g, jnp.maximum(b * (step // 16) - 1, 0), 0),
             ),
         ],
         out_specs=[
-            pl.BlockSpec((pieces, 2, PIECE, width), lambda b: (b, 0, 0, 0))
+            pl.BlockSpec((pieces, 2, PIECE, width), lambda b, g: (b, 0, 0, 0))
         ]
         * 2
         + [
-            pl.BlockSpec((slices, 2 * LANES, LANES), lambda b: (0, 0, 0)),
-            pl.BlockSpec((16, cols), lambda b: (0, 0)),
+            pl.BlockSpec((slices, 2 * LANES, LANES), lambda b, g: (0, 0, 0)),
+            pl.BlockSpec((16, cols), lambda b, g: (0, 0)),
         ],
         out_shape=[
             image,

time: 64.4 us -> 64.3 us (level)
  no operation moved by 1% of the time
where the time goes in v12:
time: 64.3 us; the launch traced here: 63.9 us
  Pallas kernels  25 us (39%)
  starting transfers between devices  18.7 us (29%)
  waiting for transfers between devices  16.4 us (26%)
  other arithmetic  2.22 us (3%)
  between operations  1.53 us (2%)
    all_to_all x1, waiting for transfers between devices, over_chips(): lax.all_to_all(pieces, 'depth', 0, 0, axis_index_groups=groups, tiled=True)  11.9 us
    pallas_call x1, Pallas kernels, interior(): pl.pallas_call(functools.partial(interior_kernel, slice_total), grid=(row...  11.4 us
    all_to_all x1, starting transfers between devices, over_chips(): lax.all_to_all(pieces, 'depth', 0, 0, axis_index_groups=groups, tiled=True)  8.06 us
    pallas_call x2, Pallas kernels, border(): pl.pallas_call(functools.partial(border_kernel, start, slice_total), grid...  7.05 us
    pallas_call x2, Pallas kernels, edge_strips(): pl.pallas_call(functools.partial(strips_kernel, first), grid=(blocks,), i...  6.59 us
    ppermute x2, starting transfers between devices, shards(): lax.ppermute(to_right, 'lat', rightwards)  4.64 us
    ppermute x2, starting transfers between devices, shards(): lax.ppermute(to_left, 'lat', leftwards)  3.61 us
    ppermute x1, waiting for transfers between devices, shards(): lax.ppermute(image[:, :, :LANES], 'lat', [(x, (x + 1) % lat) for x in ran...  3.3 us
  transfers between devices with their start and end apart: 8, of which 3 were waited for; matrix products, arithmetic and copies ran while one was open for 0% of the time, Pallas kernels for 34%

profile of v12, /device:TPU:0, one launch (start us, length us, event | category | flops | bytes accessed | tf_op | source)
XLA Modules:
  0.0 63.9 jit_solution(7145297152927185887)
XLA Ops:
  0.6 3.3 %edge_strips0.1 = (bf16[16,128,128]{2,1,0:T(8,128)(2,1)}, bf16[16,128,128]{2,1,0:T(8,128)(2,1)}) custom-call(s32[1,4,4]{2,1,0:T(4,128)} %occ.9, bf16[1,16,512,512]{3,2,1,0:T(8,128)(2,1)} %last_lead.3, bf16[1,16,512,512]{3,2,1,0:T(8,128)(2,1)} %last_lead.3), custom_call_target="tpu_custom_call" | custom-call | tf_op jit(solution)/shard_map/edge_strips0/pallas_call | solution.py:59
  3.9 2.9 %collective-permute-start = (bf16[16,128,128]{2,1,0:T(8,128)(2,1)}, bf16[16,128,128]{2,1,0:T(8,128)(2,1)S(1)}, u32[]{:S(2)}, u32[]{:S(2)}) collective-permute-start(bf16[16,128,128]{2,1,0:T(8,128)(2,1)} %get-tuple-element.19), channel_id=1, source_target_pairs={{0,3},{1,0},{2,1},{3,2},{4,7},{5,4},{6,5},{7,6},{8,11},{9,8},{10,9... | collective-permute-start | bytes 1572872 | tf_op jit(solution)/shard_map/ppermute | solution.py:382
  6.8 0.0 copy-start.4
  6.8 0.0 copy-start.5
  6.8 1.5 %collective-permute-start.1 = (bf16[16,128,128]{2,1,0:T(8,128)(2,1)}, bf16[16,128,128]{2,1,0:T(8,128)(2,1)S(1)}, u32[]{:S(2)}, u32[]{:S(2)}) collective-permute-start(bf16[16,128,128]{2,1,0:T(8,128)(2,1)} %get-tuple-element.20), channel_id=1, source_target_pairs={{0,1},{1,2},{2,3},{4,5},{5,6},{6,7},{8,9},{9,10},{10,11},{12,13},{... | collective-permute-start | bytes 1572872 | tf_op jit(solution)/shard_map/ppermute | solution.py:382
  8.3 3.3 %edge_strips2.1 = (bf16[16,128,128]{2,1,0:T(8,128)(2,1)}, bf16[16,128,128]{2,1,0:T(8,128)(2,1)}) custom-call(s32[1,4,4]{2,1,0:T(4,128)} %occ.9, bf16[1,16,512,512]{3,2,1,0:T(8,128)(2,1)} %last_lead.3, bf16[1,16,512,512]{3,2,1,0:T(8,128)(2,1)} %last_lead.3), custom_call_target="tpu_custom_call" | custom-call | tf_op jit(solution)/shard_map/edge_strips2/pallas_call | solution.py:59
  11.6 0.8 %collective-permute-start.2 = (bf16[16,128,128]{2,1,0:T(8,128)(2,1)}, bf16[16,128,128]{2,1,0:T(8,128)(2,1)S(1)}, u32[]{:S(2)}, u32[]{:S(2)}) collective-permute-start(bf16[16,128,128]{2,1,0:T(8,128)(2,1)} %get-tuple-element.24), channel_id=1, source_target_pairs={{0,3},{1,0},{2,1},{3,2},{4,7},{5,4},{6,5},{7,6},{8,11},{9,8},{10,9... | collective-permute-start | bytes 1572872 | tf_op jit(solution)/shard_map/ppermute | solution.py:382
  12.3 3.2 %collective-permute-start.3 = (bf16[16,128,128]{2,1,0:T(8,128)(2,1)}, bf16[16,128,128]{2,1,0:T(8,128)(2,1)S(1)}, u32[]{:S(2)}, u32[]{:S(2)}) collective-permute-start(bf16[16,128,128]{2,1,0:T(8,128)(2,1)} %get-tuple-element.25), channel_id=1, source_target_pairs={{0,1},{1,2},{2,3},{4,5},{5,6},{6,7},{8,9},{9,10},{10,11},{12,13},{... | collective-permute-start | bytes 1572872 | tf_op jit(solution)/shard_map/ppermute | solution.py:382
  16.2 0.0 copy-done
  16.2 0.0 copy-done.1
  16.2 0.0 copy-done.2
  16.2 11.4 %interior.1 = (f32[16,2,16,384]{3,2,1,0:T(8,128)S(1)}, f32[16,2,16,384]{3,2,1,0:T(8,128)S(1)}, bf16[16,256,128]{2,1,0:T(8,128)(2,1)S(1)}, f32[16,512]{1,0:T(8,128)S(1)}) custom-call(s32[1,4,4]{2,1,0:T(4,128)S(1)} %copy-done, s32[1,16]{1,0:T(1,128)S(1)} %copy-done.1, f32[1,16]{1,0:T(1,128)S(1)} %copy-done.2, f32[1,16]{1,0:T(1,128)S(1)} %copy-done.3, ...), custom_call_target="tpu_custom_call" | custom-call | tf_op jit(solution)/shard_map/interior/pallas_call | solution.py:197
  27.7 0.0 collective-permute-done.right_ref.right_lead
  27.7 0.0 collective-permute-done.1.left_ref.left_lead
  27.7 3.5 %border0.1 = (f32[8,2,16,128]{3,2,1,0:T(8,128)S(1)}, f32[8,2,16,128]{3,2,1,0:T(8,128)S(1)}) custom-call(s32[1,4,4]{2,1,0:T(4,128)S(1)} %copy-done, s32[1,16]{1,0:T(1,128)S(1)} %copy-done.1, f32[1,16]{1,0:T(1,128)S(1)} %copy-done.2, f32[1,16]{1,0:T(1,128)S(1)} %copy-done.3, f32[1,16]{1,0:T(1,128)S(1)} %copy-done.4, f32[1,1]{1,0:T(1,128)} %bitcast.316.gain, ...), custom_call_target="tpu_custom_call" | custom-call | tf_op jit(solution)/shard_map/border0/pallas_call | solution.py:322
  31.2 0.1 collective-permute-start.5
  31.3 0.0 collective-permute-done.2.right_ref
  31.3 0.0 collective-permute-done.3.left_ref
  31.3 3.5 %border2.1 = (f32[8,2,16,128]{3,2,1,0:T(8,128)S(1)}, f32[8,2,16,128]{3,2,1,0:T(8,128)S(1)}) custom-call(s32[1,4,4]{2,1,0:T(4,128)S(1)} %copy-done, s32[1,16]{1,0:T(1,128)S(1)} %copy-done.1, f32[1,16]{1,0:T(1,128)S(1)} %copy-done.2, f32[1,16]{1,0:T(1,128)S(1)} %copy-done.3, f32[1,16]{1,0:T(1,128)S(1)} %copy-done.4, f32[1,1]{1,0:T(1,128)} %bitcast.317.gain, ...), custom_call_target="tpu_custom_call" | custom-call | tf_op jit(solution)/shard_map/border2/pallas_call | solution.py:322
  34.9 0.6 collective-permute-start.4
  35.5 1.1 %collective-permute-done.4 = f32[16,2,16,128]{3,2,1,0:T(8,128)S(1)} collective-permute-done((f32[16,2,16,128]{3,2,1,0:T(8,128)S(1)}, f32[16,2,16,128]{3,2,1,0:T(8,128)S(1)}, u32[]{:S(2)}, u32[]{:S(2)}) %collective-permute-start.4) | collective-permute-done | bytes 262176 | tf_op jit(solution)/shard_map/ppermute | solution.py:343
  36.7 0.0 collective-permute-done.5
  36.7 0.1 fusion.1
  36.8 0.9 %fusion = f16[16,2,16,512]{3,2,1,0:T(8,128)(2,1)} fusion(f32[16,1,16,384]{3,2,1,0:T(8,128)S(1)} %get-tuple-element.36, f32[16,1,16,384]{3,2,1,0:T(8,128)S(1)} %get-tuple-element.35, f32[16,1,16,128]{3,2,1,0:T(8,128)S(1)} %get-tuple-element.38, f32[16,1,16,128]{3,2,1,0:T(8,128)S(1)} %get-tuple-element.37), kind=kLoop, calls=%fused_computation.1 | loop fusion | flops 1310720 | bytes 1572864 | tf_op jit(solution)/shard_map/convert_element_type | solution.py:351
  37.7 8.1 %all-to-all-start = ((f16[16,2,16,512]{3,2,1,0:T(8,128)(2,1)}), f16[16,2,16,512]{3,2,1,0:T(8,128)(2,1)S(1)}, u32[]{:S(2)}, u32[]{:S(2)}) async-start(f16[16,2,16,512]{3,2,1,0:T(8,128)(2,1)} %fusion), calls=%async_computation | async-start | bytes 1048576 | tf_op jit(solution)/shard_map/all_to_all | solution.py:353
  45.9 11.9 %all-to-all-done = f16[16,2,16,512]{3,2,1,0:T(8,128)(2,1)S(1)} async-done(((f16[16,2,16,512]{3,2,1,0:T(8,128)(2,1)}), f16[16,2,16,512]{3,2,1,0:T(8,128)(2,1)S(1)}, u32[]{:S(2)}, u32[]{:S(2)}) %all-to-all-start) | async-done | bytes 524320 | tf_op jit(solution)/shard_map/all_to_all | solution.py:353
  57.8 0.2 convert_multiply_fusion
  58.0 0.1 multiply_add_fusion.2
  58.0 0.2 fusion.10
  58.3 1.7 %collective-permute-start.6 = (f32[2,16,128]{2,1,0:T(8,128)S(1)}, f32[2,16,128]{2,1,0:T(8,128)S(1)}, u32[]{:S(2)}, u32[]{:S(2)}) collective-permute-start(f32[2,16,128]{2,1,0:T(8,128)S(1)} %pad_maximum_fusion.3), channel_id=1, source_target_pairs={{0,1},{1,2},{2,3},{3,0},{4,5},{5,6},{6,7},{7,4},{8,9},{9,10},{10,1... | collective-permute-start | bytes 49160 | tf_op jit(solution)/shard_map/ppermute | solution.py:393
  60.0 3.3 %collective-permute-done.6 = f32[2,16,128]{2,1,0:T(8,128)S(1)} collective-permute-done((f32[2,16,128]{2,1,0:T(8,128)S(1)}, f32[2,16,128]{2,1,0:T(8,128)S(1)}, u32[]{:S(2)}, u32[]{:S(2)}) %collective-permute-start.6) | collective-permute-done | bytes 16416 | tf_op jit(solution)/shard_map/ppermute | solution.py:393
  63.3 0.6 pad_maximum_fusion.1
  (23 shorter events, 0.2 us)
Async XLA Ops:
  3.9 23.8 %collective-permute-start = (bf16[16,128,128]{2,1,0:T(8,128)(2,1)}, bf16[16,128,128]{2,1,0:T(8,128)(2,1)S(1)}, u32[]{:S(2)}, u32[]{:S(2)}) collective-permute-start(bf16[16,128,128]{2,1,0:T(8,128)(2,1)} %get-tuple-element.19), channel_id=1, source_target_pairs={{0,3},{1,0},{2,1},{3,2},{4,7},{5,4},{6,5},{7,6},{8,11},{9,8},{10,9... | collective-permute-start | bytes 1572872 | tf_op jit(solution)/shard_map/ppermute | solution.py:382
  6.8 9.4 %copy-start = (s32[1,4,4]{2,1,0:T(4,128)S(1)}, s32[1,4,4]{2,1,0:T(4,128)}, u32[]{:S(2)}) copy-start(s32[1,4,4]{2,1,0:T(4,128)} %occ.9) | copy-start | bytes 196
  6.8 9.4 %copy-start.1 = (s32[1,16]{1,0:T(1,128)S(1)}, s32[1,16]{1,0:T(1,128)}, u32[]{:S(2)}) copy-start(s32[1,16]{1,0:T(1,128)} %offset.5) | copy-start | bytes 196
  6.8 9.4 %copy-start.2 = (f32[1,16]{1,0:T(1,128)S(1)}, f32[1,16]{1,0:T(1,128)}, u32[]{:S(2)}) copy-start(f32[1,16]{1,0:T(1,128)} %frac_lateral.5) | copy-start | bytes 196
  6.8 9.4 %copy-start.3 = (f32[1,16]{1,0:T(1,128)S(1)}, f32[1,16]{1,0:T(1,128)}, u32[]{:S(2)}) copy-start(f32[1,16]{1,0:T(1,128)} %frac_vertical.5) | copy-start | bytes 196
  6.8 9.4 %copy-start.4 = (f32[1,16]{1,0:T(1,128)S(1)}, f32[1,16]{1,0:T(1,128)}, u32[]{:S(2)}) copy-start(f32[1,16]{1,0:T(1,128)} %extinction.5) | copy-start | bytes 196
  6.8 9.4 %copy-start.5 = (s32[32]{0:T(128)S(1)}, s32[32]{0:T(128)}, u32[]{:S(2)}) copy-start(s32[32]{0:T(128)} %rank.1) | copy-start | bytes 388
  6.8 20.9 %collective-permute-start.1 = (bf16[16,128,128]{2,1,0:T(8,128)(2,1)}, bf16[16,128,128]{2,1,0:T(8,128)(2,1)S(1)}, u32[]{:S(2)}, u32[]{:S(2)}) collective-permute-start(bf16[16,128,128]{2,1,0:T(8,128)(2,1)} %get-tuple-element.20), channel_id=1, source_target_pairs={{0,1},{1,2},{2,3},{4,5},{5,6},{6,7},{8,9},{9,10},{10,11},{12,13},{... | collective-permute-start | bytes 1572872 | tf_op jit(solution)/shard_map/ppermute | solution.py:382
  11.6 19.7 %collective-permute-start.2 = (bf16[16,128,128]{2,1,0:T(8,128)(2,1)}, bf16[16,128,128]{2,1,0:T(8,128)(2,1)S(1)}, u32[]{:S(2)}, u32[]{:S(2)}) collective-permute-start(bf16[16,128,128]{2,1,0:T(8,128)(2,1)} %get-tuple-element.24), channel_id=1, source_target_pairs={{0,3},{1,0},{2,1},{3,2},{4,7},{5,4},{6,5},{7,6},{8,11},{9,8},{10,9... | collective-permute-start | bytes 1572872 | tf_op jit(solution)/shard_map/ppermute | solution.py:382
  12.3 19.0 %collective-permute-start.3 = (bf16[16,128,128]{2,1,0:T(8,128)(2,1)}, bf16[16,128,128]{2,1,0:T(8,128)(2,1)S(1)}, u32[]{:S(2)}, u32[]{:S(2)}) collective-permute-start(bf16[16,128,128]{2,1,0:T(8,128)(2,1)} %get-tuple-element.25), channel_id=1, source_target_pairs={{0,1},{1,2},{2,3},{4,5},{5,6},{6,7},{8,9},{9,10},{10,11},{12,13},{... | collective-permute-start | bytes 1572872 | tf_op jit(solution)/shard_map/ppermute | solution.py:382
  31.2 5.5 %collective-permute-start.5 = (f32[16,2,16,384]{3,2,1,0:T(8,128)S(1)}, f32[16,2,16,384]{3,2,1,0:T(8,128)S(1)}, u32[]{:S(2)}, u32[]{:S(2)}) collective-permute-start(f32[16,2,16,384]{3,2,1,0:T(8,128)S(1)} %get-tuple-element.31), channel_id=1, source_target_pairs={{0,4},{4,0},{8,12},{12,8},{16,20},{20,16},{24,28},{28,24},{32,36},... | collective-permute-start | bytes 2359304 | tf_op jit(solution)/shard_map/ppermute | solution.py:343
  34.9 1.7 %collective-permute-start.4 = (f32[16,2,16,128]{3,2,1,0:T(8,128)S(1)}, f32[16,2,16,128]{3,2,1,0:T(8,128)S(1)}, u32[]{:S(2)}, u32[]{:S(2)}) collective-permute-start(f32[16,2,16,128]{3,2,1,0:T(8,128)S(1)} %pad_maximum_fusion), channel_id=1, source_target_pairs={{0,4},{4,0},{8,12},{12,8},{16,20},{20,16},{24,28},{28,24},{32,36},... | collective-permute-start | bytes 786440 | tf_op jit(solution)/shard_map/ppermute | solution.py:343
  37.7 20.1 %all-to-all-start = ((f16[16,2,16,512]{3,2,1,0:T(8,128)(2,1)}), f16[16,2,16,512]{3,2,1,0:T(8,128)(2,1)S(1)}, u32[]{:S(2)}, u32[]{:S(2)}) async-start(f16[16,2,16,512]{3,2,1,0:T(8,128)(2,1)} %fusion), calls=%async_computation | async-start | bytes 1048576 | tf_op jit(solution)/shard_map/all_to_all | solution.py:353
  58.3 5.0 %collective-permute-start.6 = (f32[2,16,128]{2,1,0:T(8,128)S(1)}, f32[2,16,128]{2,1,0:T(8,128)S(1)}, u32[]{:S(2)}, u32[]{:S(2)}) collective-permute-start(f32[2,16,128]{2,1,0:T(8,128)S(1)} %pad_maximum_fusion.3), channel_id=1, source_target_pairs={{0,1},{1,2},{2,3},{3,0},{4,5},{5,6},{6,7},{7,4},{8,9},{9,10},{10,1... | collective-permute-start | bytes 49160 | tf_op jit(solution)/shard_map/ppermute | solution.py:393
